TPU v7x, 32 devices: a whole 2x2x4 slice. The times are simulated.
32 devices in a mesh: dp: 8 (over z, y), seq: 4 (over x, core).
Axes of the slice: x: 2, y: 2, z: 4, core: 2. Of those that a mesh axis runs over, the one named last changes fastest.
Arguments:
- block_in: bfloat16 [16, 1024, 512], P('dp', 'seq'), may hold values from -6 to 6
- cotangent: bfloat16 [16, 1024, 512], P('dp', 'seq'), may hold values from -6 to 6
- ln_gain: float32 [512], P('dp'), may hold values from 0.5 to 1.5
- ln_bias: float32 [512], P('dp'), may hold values from -3 to 3
- lambda_log: float32 [64], P('dp'), may hold values from -1 to 0.3
- lambda_imag: float32 [64], P('dp'), may hold values from -30 to 30
- dss_weight: float32 [2, 64, 512], P(None, None, 'dp'), may hold values from -1.5 to 1.5
- log_step: float32 [512], P('dp'), may hold values from -8 to -2
- skip_gain: float32 [512], P('dp'), may hold values from -4 to 4
- lin_weight: bfloat16 [512, 1024], P(None, 'dp'), may hold values from -0.5 to 0.5
- lin_bias: float32 [1024], P('dp'), may hold values from -3 to 3
- doc_lengths: int32 [16, 4], P('dp'), may hold values from 1 to 800, 1024 in all within a row
Outputs:
- block_out: bfloat16 [16, 1024, 512], P('dp', 'seq')
- grad_block_in: bfloat16 [16, 1024, 512], P('dp', 'seq')
- grad_ln_gain: float32 [512], P('dp')
- grad_ln_bias: float32 [512], P('dp')
- grad_lambda_log: float32 [64], P('dp')
- grad_lambda_imag: float32 [64], P('dp')
- grad_dss_weight: float32 [2, 64, 512], P(None, None, 'dp')
- grad_log_step: float32 [512], P('dp')
- grad_skip_gain: float32 [512], P('dp')
- grad_lin_weight: float32 [512, 1024], P(None, 'dp')
- grad_lin_bias: float32 [1024], P('dp')
Inputs may be any that keep to these rules, and one draw needn't show every extreme that they name: `doc_lengths`: each row sums to 1024.
All inputs are finite; a program needn't handle non-finite values.
Results may differ from a plain program's by a relative error of at most 0.0076.
Values may be sent and summed in bfloat16 or wider, within the bound.
No kernel may reach another device: no remote copies, remote signals or barrier semaphores. Data moves between devices by JAX's collectives and lax.ppermute only.
A program may use at most 448 MiB of HBM per device.

v0:
```python
from functools import partial

import jax
import jax.numpy as jnp
from jax import lax
from jax.sharding import PartitionSpec as P

MICRO = 2


ln_eps = 1e-05
highest = lax.Precision.HIGHEST


def entering(x, axis, combine, identity, reverse):
    length, place = (lax.axis_size(axis), lax.axis_index(axis))
    everything = jax.tree.map(lambda part: lax.all_gather(part, axis), x)
    start = jax.tree.map(
        lambda part, zero: jnp.broadcast_to(jnp.asarray(zero, part.dtype), part.shape), x, identity
    )

    def turn(k, before):
        at = length - 1 - k if reverse else k
        reached = at > place if reverse else at < place
        new = combine(before, jax.tree.map(lambda part: part[at], everything))
        return jax.tree.map(lambda a, b: jnp.where(reached, a, b), new, before)

    return lax.fori_loop(0, length, turn, start)


def layer_norm(values, gain_vec, bias_vec):
    centre = values - jnp.mean(values, axis=-1, keepdims=True)
    spread = jnp.mean(centre * centre, axis=-1, keepdims=True)
    return centre * lax.rsqrt(spread + ln_eps) * gain_vec + bias_vec


def exact_gelu(values):
    return jax.nn.gelu(values, approximate=False)


def power_pair(real_rate, imag_rate, exponent):
    magnitude = jnp.exp(exponent * real_rate)
    phase_val = exponent * imag_rate
    return (magnitude * jnp.cos(phase_val), magnitude * jnp.sin(phase_val))


def state_rates(rate_log, freq_imag, step_log):
    step_size = jnp.exp(step_log)
    real_rate = -jnp.exp(rate_log)[:, None] * step_size[None, :]
    imag_rate = freq_imag[:, None] * step_size[None, :]
    return (real_rate, imag_rate)


def output_coeffs(state_weight, real_rate, imag_rate, length):
    half_sine = jnp.sin(0.5 * imag_rate)
    one_re = 2.0 * half_sine * half_sine - jnp.expm1(real_rate) * jnp.cos(imag_rate)
    one_im = -jnp.exp(real_rate) * jnp.sin(imag_rate)
    far_re, far_im = power_pair(real_rate, imag_rate, float(length))
    den_re = 1.0 - far_re
    den_im = -far_im
    num_re = state_weight[0] * one_re - state_weight[1] * one_im
    num_im = state_weight[0] * one_im + state_weight[1] * one_re
    norm_sq = den_re * den_re + den_im * den_im
    coef_re = (num_re * den_re + num_im * den_im) / norm_sq
    coef_im = (num_im * den_re - num_re * den_im) / norm_sq
    return (coef_re, coef_im)


def make_tables(rate_log, freq_imag, state_weight, step_log, block, group, length):
    real_rate, imag_rate = state_rates(rate_log, freq_imag, step_log)
    coef_re, coef_im = output_coeffs(state_weight, real_rate, imag_rate, length)
    offsets = jnp.arange(block, dtype=jnp.float32)[:, None, None]
    lag_re, lag_im = power_pair(real_rate, imag_rate, offsets)
    kernel_head = jnp.sum(coef_re * lag_re - coef_im * lag_im, axis=1)
    next_re, next_im = power_pair(real_rate, imag_rate, offsets + 1.0)
    carry_re = coef_re * next_re - coef_im * next_im
    carry_im = coef_re * next_im + coef_im * next_re
    tail_re, tail_im = power_pair(real_rate, imag_rate, float(block - 1) - offsets)
    jump_re, jump_im = power_pair(real_rate, imag_rate, float(block))
    leap_re, leap_im = power_pair(real_rate, imag_rate, float(group))
    return (kernel_head, carry_re, carry_im, tail_re, tail_im, jump_re, jump_im, leap_re, leap_im)


def carried_value(carry_re, carry_im, state_re, state_im):
    return jnp.einsum("tnh,mnh->mth", carry_re, state_re, precision=highest) - jnp.einsum(
        "tnh,mnh->mth", carry_im, state_im, precision=highest
    )


def local_pass(normed, pieces, skip_vec, segs, seg_prev):
    kernel_head, carry_re, carry_im, tail_re, tail_im, jump_re, jump_im = pieces
    count, group, width = normed.shape
    block = kernel_head.shape[0]
    blocks = group // block
    lag_index = (
        jnp.arange(block, dtype=jnp.int32)[:, None] - jnp.arange(block, dtype=jnp.int32)[None, :]
    )
    causal = lag_index >= 0
    toeplitz_base = kernel_head[jnp.maximum(lag_index, 0)]
    u_blocks = normed.reshape(count, blocks, block, width).transpose(1, 0, 2, 3)
    seg_blocks = segs.reshape(count, blocks, block).transpose(1, 0, 2)
    before = jnp.concatenate(
        [seg_prev[:, None], segs[:, block - 1 :: block][:, : blocks - 1]], axis=1
    ).transpose(1, 0)

    def local_advance(state, items):
        state_re, state_im = state
        u_blk, seg_blk, seg_before = items
        same_doc = ((seg_blk[:, :, None] == seg_blk[:, None, :]) & causal[None]).astype(jnp.float32)
        inner = jnp.einsum("mtj,tjh,mjh->mth", same_doc, toeplitz_base, u_blk, precision=highest)
        follows = (seg_blk == seg_before[:, None]).astype(jnp.float32)
        out_blk = (
            inner
            + follows[:, :, None] * carried_value(carry_re, carry_im, state_re, state_im)
            + skip_vec * u_blk
        )
        last_seg = seg_blk[:, -1]
        ending = (seg_blk == last_seg[:, None]).astype(jnp.float32)
        weighted = ending[:, :, None] * u_blk
        fresh_re = jnp.einsum("jnh,mjh->mnh", tail_re, weighted, precision=highest)
        fresh_im = jnp.einsum("jnh,mjh->mnh", tail_im, weighted, precision=highest)
        keeps = (last_seg == seg_before).astype(jnp.float32)[:, None, None]
        next_re = keeps * (jump_re * state_re - jump_im * state_im) + fresh_re
        next_im = keeps * (jump_re * state_im + jump_im * state_re) + fresh_im
        return ((next_re, next_im), out_blk)

    zero_state = jnp.zeros((count,) + jump_re.shape, jnp.float32)
    (end_re, end_im), outputs = lax.scan(
        jax.checkpoint(local_advance), (zero_state, zero_state), (u_blocks, seg_blocks, before)
    )
    return (outputs.transpose(1, 0, 2, 3).reshape(count, group, width), end_re, end_im)


def carry_pass(pieces, start_re, start_im, segs, seg_prev):
    carry_re, carry_im, jump_re, jump_im = pieces
    count, group = segs.shape
    block = carry_re.shape[0]
    seg_blocks = segs.reshape(count, group // block, block).transpose(1, 0, 2)

    def carry_advance(state, seg_blk):
        state_re, state_im = state
        follows = (seg_blk == seg_prev[:, None]).astype(jnp.float32)
        out_blk = follows[:, :, None] * carried_value(carry_re, carry_im, state_re, state_im)
        keeps = (seg_blk[:, -1] == seg_prev).astype(jnp.float32)[:, None, None]
        next_re = keeps * (jump_re * state_re - jump_im * state_im)
        next_im = keeps * (jump_re * state_im + jump_im * state_re)
        return ((next_re, next_im), out_blk)

    final_state, outputs = lax.scan(jax.checkpoint(carry_advance), (start_re, start_im), seg_blocks)
    return outputs.transpose(1, 0, 2, 3).reshape(count, group, carry_re.shape[2])


def forward_combine(earlier, later):
    prod_re = earlier[0] * later[0] - earlier[1] * later[1]
    prod_im = earlier[0] * later[1] + earlier[1] * later[0]
    sum_re = later[0] * earlier[2] - later[1] * earlier[3] + later[2]
    sum_im = later[0] * earlier[3] + later[1] * earlier[2] + later[3]
    return (prod_re, prod_im, sum_re, sum_im)


def backward_combine(earlier, later):
    prod_re = earlier[0] * later[0] - earlier[1] * later[1]
    prod_im = earlier[0] * later[1] + earlier[1] * later[0]
    sum_re = later[0] * earlier[2] + later[1] * earlier[3] + later[2]
    sum_im = later[0] * earlier[3] - later[1] * earlier[2] + later[3]
    return (prod_re, prod_im, sum_re, sum_im)


def segment_ids(lengths, positions):
    ends = jnp.cumsum(lengths, axis=-1)
    return jnp.sum((positions[None, :, None] >= ends[:, None, :]).astype(jnp.int32), axis=-1)


def on_device(
    block_in,
    cotangent,
    ln_gain,
    ln_bias,
    lambda_log,
    lambda_imag,
    dss_weight,
    log_step,
    skip_gain,
    lin_weight,
    lin_bias,
    doc_lengths,
):
    full_gain, full_bias, rate_log, freq_imag, state_weight, step_log, skip_vec, bias_full = (
        lax.all_gather(ln_gain, "dp", axis=0, tiled=True),
        lax.all_gather(ln_bias, "dp", axis=0, tiled=True),
        lax.all_gather(lambda_log, "dp", axis=0, tiled=True),
        lax.all_gather(lambda_imag, "dp", axis=0, tiled=True),
        lax.all_gather(dss_weight, "dp", axis=2, tiled=True),
        lax.all_gather(log_step, "dp", axis=0, tiled=True),
        lax.all_gather(skip_gain, "dp", axis=0, tiled=True),
        lax.all_gather(lin_bias, "dp", axis=0, tiled=True),
    )
    seq_count, group, width = block_in.shape
    length = group * lax.axis_size("seq")
    block = min(64, group)
    tables, tables_back = jax.vjp(
        partial(make_tables, block=block, group=group, length=length),
        rate_log,
        freq_imag,
        state_weight,
        step_log,
    )
    kernel_head, carry_re, carry_im, tail_re, tail_im, jump_re, jump_im, leap_re, leap_im = tables
    local_pieces = (kernel_head, carry_re, carry_im, tail_re, tail_im, jump_re, jump_im)
    carry_pieces = (carry_re, carry_im, jump_re, jump_im)
    group_start = lax.axis_index("seq") * group
    positions = group_start + jnp.arange(group, dtype=jnp.int32)
    seg_all = segment_ids(doc_lengths, positions)
    seg_prev_all = segment_ids(doc_lengths, jnp.reshape(group_start - 1, (1,)))[:, 0]
    per_micro = seq_count // MICRO
    table_totals = [jnp.zeros_like(entry) for entry in tables]
    gain_total = jnp.zeros((width,), jnp.float32)
    normb_total = jnp.zeros((width,), jnp.float32)
    skip_total = jnp.zeros((width,), jnp.float32)
    weight_total = jnp.zeros((width, 2 * width), jnp.float32)
    linb_total = jnp.zeros((2 * width,), jnp.float32)
    out_parts = []
    grad_parts = []
    for micro_idx in range(MICRO):
        picked = slice(micro_idx * per_micro, (micro_idx + 1) * per_micro)
        inputs = block_in[picked].astype(jnp.float32)
        segs = seg_all[picked]
        seg_prev = seg_prev_all[picked]
        normed, norm_back = jax.vjp(layer_norm, inputs, full_gain, full_bias)
        (inner_out, end_re, end_im), local_back = jax.vjp(
            partial(local_pass, segs=segs, seg_prev=seg_prev), normed, local_pieces, skip_vec
        )
        flag_vec = (segs[:, -1] == seg_prev).astype(jnp.float32)
        keeps = flag_vec[:, None, None]
        ones_state = jnp.ones_like(end_re)
        zero_state = jnp.zeros_like(end_re)
        mult_re = keeps * leap_re
        mult_im = keeps * leap_im
        prefix = entering(
            (mult_re, mult_im, end_re, end_im),
            "seq",
            forward_combine,
            (ones_state, zero_state, zero_state, zero_state),
            False,
        )
        start_re, start_im = (prefix[2], prefix[3])
        carried_out, carry_back = jax.vjp(
            partial(carry_pass, segs=segs, seg_prev=seg_prev), carry_pieces, start_re, start_im
        )
        conv_out = inner_out + carried_out
        activated, gelu_back = jax.vjp(exact_gelu, conv_out)
        act_low = activated.astype(jnp.bfloat16).reshape(-1, width)
        pre = jnp.dot(
            act_low,
            lax.all_gather(lin_weight, "dp", axis=1, tiled=True),
            preferred_element_type=jnp.float32,
        )
        pre = pre + bias_full
        first_half = pre[:, :width]
        gate_val = jax.nn.sigmoid(pre[:, width:])
        flat_in = inputs.reshape(-1, width)
        out_parts.append(
            (flat_in + first_half * gate_val).astype(jnp.bfloat16).reshape(per_micro, group, width)
        )
        d_out = cotangent[picked].astype(jnp.float32).reshape(-1, width)
        d_first = d_out * gate_val
        d_second = d_out * first_half * gate_val * (1.0 - gate_val)
        d_pre = jnp.concatenate([d_first, d_second], axis=1).astype(jnp.bfloat16)
        linb_total = linb_total + jnp.sum(d_pre.astype(jnp.float32), axis=0)
        weight_total = weight_total + lax.dot_general(
            act_low, d_pre, (((0,), (0,)), ((), ())), preferred_element_type=jnp.float32
        )
        d_act = lax.dot_general(
            d_pre,
            lax.all_gather(lin_weight, "dp", axis=1, tiled=True),
            (((1,), (1,)), ((), ())),
            preferred_element_type=jnp.float32,
        )
        d_conv = gelu_back(d_act.reshape(conv_out.shape))[0]
        d_carry_pieces, adj_re, adj_im = carry_back(d_conv)
        suffix = entering(
            (mult_re, mult_im, adj_re, adj_im),
            "seq",
            backward_combine,
            (ones_state, zero_state, zero_state, zero_state),
            True,
        )
        later_re, later_im = (suffix[2], suffix[3])
        d_normed, d_local_pieces, d_skip = local_back((d_conv, later_re, later_im))
        for index_val, grad_val in zip((0, 1, 2, 3, 4, 5, 6), d_local_pieces):
            table_totals[index_val] = table_totals[index_val] + grad_val
        for index_val, grad_val in zip((1, 2, 5, 6), d_carry_pieces):
            table_totals[index_val] = table_totals[index_val] + grad_val
        table_totals[7] = table_totals[7] + jnp.sum(
            keeps * (later_re * start_re + later_im * start_im), axis=0
        )
        table_totals[8] = table_totals[8] + jnp.sum(
            keeps * (later_im * start_re - later_re * start_im), axis=0
        )
        skip_total = skip_total + d_skip
        d_inputs, d_gain, d_bias = norm_back(d_normed)
        gain_total = gain_total + d_gain
        normb_total = normb_total + d_bias
        grad_parts.append(
            (d_out + d_inputs.reshape(-1, width))
            .astype(jnp.bfloat16)
            .reshape(per_micro, group, width)
        )
    grad_rate, grad_freq, grad_state, grad_step = tables_back(tuple(table_totals))
    grads = (
        gain_total,
        normb_total,
        grad_rate,
        grad_freq,
        grad_state,
        grad_step,
        skip_total,
        weight_total,
        linb_total,
    )
    owned = (
        lax.psum_scatter(grads[0], "dp", scatter_dimension=0, tiled=True),
        lax.psum_scatter(grads[1], "dp", scatter_dimension=0, tiled=True),
        lax.psum_scatter(grads[2], "dp", scatter_dimension=0, tiled=True),
        lax.psum_scatter(grads[3], "dp", scatter_dimension=0, tiled=True),
        lax.psum_scatter(grads[4], "dp", scatter_dimension=2, tiled=True),
        lax.psum_scatter(grads[5], "dp", scatter_dimension=0, tiled=True),
        lax.psum_scatter(grads[6], "dp", scatter_dimension=0, tiled=True),
        lax.psum_scatter(grads[7], "dp", scatter_dimension=1, tiled=True),
        lax.psum_scatter(grads[8], "dp", scatter_dimension=0, tiled=True),
    )
    owned = lax.psum(
        (owned[0], owned[1], owned[2], owned[3], owned[4], owned[5], owned[6], owned[7], owned[8]),
        "seq",
    )
    block_out = jnp.concatenate(out_parts, axis=0)
    grad_block_in = jnp.concatenate(grad_parts, axis=0)
    return (
        block_out,
        grad_block_in,
        owned[0],
        owned[1],
        owned[2],
        owned[3],
        owned[4],
        owned[5],
        owned[6],
        owned[7],
        owned[8],
    )


def solution(mesh):
    placed = (
        P("dp", "seq", None),
        P("dp", "seq", None),
        P("dp"),
        P("dp"),
        P("dp"),
        P("dp"),
        P(None, None, "dp"),
        P("dp"),
        P("dp"),
        P(None, "dp"),
        P("dp"),
        P("dp", None),
    )
    return jax.shard_map(
        on_device,
        mesh=mesh,
        in_specs=placed,
        out_specs=(
            P("dp", "seq", None),
            P("dp", "seq", None),
            P("dp"),
            P("dp"),
            P("dp"),
            P("dp"),
            P(None, None, "dp"),
            P("dp"),
            P("dp"),
            P(None, "dp"),
            P("dp"),
        ),
        check_vma=False,
    )
```

profile of v0, /device:TPU:0, one launch (start us, length us, event | category | flops | bytes accessed | tf_op | source)
XLA Modules:
  0.0 3111.9 jit_solution(8030803023528631233)
XLA Ops:
  119.1 34.5 %subtract_reduce_fusion = f32[64,512]{1,0:T(8,128)S(1)} fusion(f32[64,512]{1,0:T(8,128)} %get-tuple-element.8907, f32[64,512]{1,0:T(8,128)} %get-tuple-element.8903, f32[64,512]{1,0:T(8,128)} %get-tuple-element.8905, f32[64,512]{1,0:T(8,128)S(1)} %get-tuple-element.8904), kind=kLoop, calls=%fused_computation.498 | loop fusion | flops 16744448 | bytes 655360 | tf_op jit(solution)/shard_map/jvp()/reduce_sum | solution.py:74
  173.5 320.0 %while.289 = (s32[]{:T(128)}, f32[1,64,512]{2,1,0:T(8,128)S(1)}, f32[1,64,512]{2,1,0:T(8,128)S(1)}, f32[4,1,64,512]{3,2,1,0:T(8,128)}, f32[4,1,64,512]{3,2,1,0:T...) while((s32[]{:T(128)}, f32[1,64,512]{2,1,0:T(8,128)S(1)}, ...), condition=%wide.region_15.16_spmd.clone.clone.clone, body=%wide.region_14.15_spmd.clone.clone.clone.sunk | while | flops 53137668 | bytes 13410079 | solution.py:128
  183.3 33.1 %fusion.588 = (f32[512,64]{0,1:T(8,128)S(1)}, f32[512,64]{0,1:T(8,128)S(1)}) fusion(f32[512,64]{0,1:T(8,128)S(1)} %fusion.587, f32[64,512]{1,0:T(8,128)} %get-tuple-element.8486, f32[64,512]{1,0:T(8,128)S(1)} %get-tuple-element.8485, f32[64]{0:T(128)S(1)} %get-tuple-element.8487), kind=kLoop, calls=%fused_computation.208.clone.1 | loop fusion | flops 16711680 | bytes 655616 | tf_op jit(solution)/shard_map/jvp()/while/body/eval_jaxpr/jnh,mjh->mnh/dot_general | solution.py:121
  217.6 35.2 %multiply_reduce_fusion.55 = (f32[512,64]{0,1:T(8,128)S(1)}, f32[512,64]{0,1:T(8,128)S(1)}) fusion(f32[512,64]{0,1:T(8,128)S(1)} %get-tuple-element.8040, f32[64,512]{1,0:T(8,128)} %get-tuple-element.8490, f32[64]{0:T(128)S(1)} %get-tuple-element.8489, f32[64,512]{1,0:T(8,128)} %get-tuple-element.8488, f32[64,512]{1,0:T(8,128)} %get-tuple-element.8486, ...), kind=kLoop, calls=%fused_computation.211.clone.1 | loop fusion | flops 29294592 | bytes 1048832 | tf_op jit(solution)/shard_map/jvp()/while/body/eval_jaxpr/tnh,mnh->mth/dot_general | solution.py:85
  263.2 33.1 %fusion.588 = (f32[512,64]{0,1:T(8,128)S(1)}, f32[512,64]{0,1:T(8,128)S(1)}) fusion(f32[512,64]{0,1:T(8,128)S(1)} %fusion.587, f32[64,512]{1,0:T(8,128)} %get-tuple-element.8486, f32[64,512]{1,0:T(8,128)S(1)} %get-tuple-element.8485, f32[64]{0:T(128)S(1)} %get-tuple-element.8487), kind=kLoop, calls=%fused_computation.208.clone.1 | loop fusion | flops 16711680 | bytes 655616 | tf_op jit(solution)/shard_map/jvp()/while/body/eval_jaxpr/jnh,mjh->mnh/dot_general | solution.py:121
  297.6 35.2 %multiply_reduce_fusion.55 = (f32[512,64]{0,1:T(8,128)S(1)}, f32[512,64]{0,1:T(8,128)S(1)}) fusion(f32[512,64]{0,1:T(8,128)S(1)} %get-tuple-element.8040, f32[64,512]{1,0:T(8,128)} %get-tuple-element.8490, f32[64]{0:T(128)S(1)} %get-tuple-element.8489, f32[64,512]{1,0:T(8,128)} %get-tuple-element.8488, f32[64,512]{1,0:T(8,128)} %get-tuple-element.8486, ...), kind=kLoop, calls=%fused_computation.211.clone.1 | loop fusion | flops 29294592 | bytes 1048832 | tf_op jit(solution)/shard_map/jvp()/while/body/eval_jaxpr/tnh,mnh->mth/dot_general | solution.py:85
  343.2 33.1 %fusion.588 = (f32[512,64]{0,1:T(8,128)S(1)}, f32[512,64]{0,1:T(8,128)S(1)}) fusion(f32[512,64]{0,1:T(8,128)S(1)} %fusion.587, f32[64,512]{1,0:T(8,128)} %get-tuple-element.8486, f32[64,512]{1,0:T(8,128)S(1)} %get-tuple-element.8485, f32[64]{0:T(128)S(1)} %get-tuple-element.8487), kind=kLoop, calls=%fused_computation.208.clone.1 | loop fusion | flops 16711680 | bytes 655616 | tf_op jit(solution)/shard_map/jvp()/while/body/eval_jaxpr/jnh,mjh->mnh/dot_general | solution.py:121
  377.6 35.2 %multiply_reduce_fusion.55 = (f32[512,64]{0,1:T(8,128)S(1)}, f32[512,64]{0,1:T(8,128)S(1)}) fusion(f32[512,64]{0,1:T(8,128)S(1)} %get-tuple-element.8040, f32[64,512]{1,0:T(8,128)} %get-tuple-element.8490, f32[64]{0:T(128)S(1)} %get-tuple-element.8489, f32[64,512]{1,0:T(8,128)} %get-tuple-element.8488, f32[64,512]{1,0:T(8,128)} %get-tuple-element.8486, ...), kind=kLoop, calls=%fused_computation.211.clone.1 | loop fusion | flops 29294592 | bytes 1048832 | tf_op jit(solution)/shard_map/jvp()/while/body/eval_jaxpr/tnh,mnh->mth/dot_general | solution.py:85
  423.1 33.1 %fusion.588 = (f32[512,64]{0,1:T(8,128)S(1)}, f32[512,64]{0,1:T(8,128)S(1)}) fusion(f32[512,64]{0,1:T(8,128)S(1)} %fusion.587, f32[64,512]{1,0:T(8,128)} %get-tuple-element.8486, f32[64,512]{1,0:T(8,128)S(1)} %get-tuple-element.8485, f32[64]{0:T(128)S(1)} %get-tuple-element.8487), kind=kLoop, calls=%fused_computation.208.clone.1 | loop fusion | flops 16711680 | bytes 655616 | tf_op jit(solution)/shard_map/jvp()/while/body/eval_jaxpr/jnh,mjh->mnh/dot_general | solution.py:121
  457.5 35.2 %multiply_reduce_fusion.55 = (f32[512,64]{0,1:T(8,128)S(1)}, f32[512,64]{0,1:T(8,128)S(1)}) fusion(f32[512,64]{0,1:T(8,128)S(1)} %get-tuple-element.8040, f32[64,512]{1,0:T(8,128)} %get-tuple-element.8490, f32[64]{0:T(128)S(1)} %get-tuple-element.8489, f32[64,512]{1,0:T(8,128)} %get-tuple-element.8488, f32[64,512]{1,0:T(8,128)} %get-tuple-element.8486, ...), kind=kLoop, calls=%fused_computation.211.clone.1 | loop fusion | flops 29294592 | bytes 1048832 | tf_op jit(solution)/shard_map/jvp()/while/body/eval_jaxpr/tnh,mnh->mth/dot_general | solution.py:85
  497.4 330.4 %while.288 = (s32[]{:T(128)}, f32[1,64,512]{2,1,0:T(8,128)S(1)}, f32[1,64,512]{2,1,0:T(8,128)S(1)}, f32[4,1,64,512]{3,2,1,0:T(8,128)}, f32[4,1,64,512]{3,2,1,0:T...) while((s32[]{:T(128)}, f32[1,64,512]{2,1,0:T(8,128)S(1)}, ...), condition=%wide.region_7.8_spmd.clone.clone.clone, body=%wide.region_6.7_spmd.clone.clone.clone.sunk | while | flops 53137668 | bytes 13410079 | solution.py:128
  551.5 35.2 %multiply_reduce_fusion.53 = (f32[512,64]{0,1:T(8,128)S(1)}, f32[512,64]{0,1:T(8,128)S(1)}) fusion(f32[512,64]{0,1:T(8,128)S(1)} %get-tuple-element.8008, f32[64,512]{1,0:T(8,128)} %get-tuple-element.8340, f32[64]{0:T(128)S(1)} %get-tuple-element.8339, f32[64,512]{1,0:T(8,128)} %get-tuple-element.8338, f32[64,512]{1,0:T(8,128)} %get-tuple-element.8336, ...), kind=kLoop, calls=%fused_computation.155.clone.1 | loop fusion | flops 29294592 | bytes 1048832 | tf_op jit(solution)/shard_map/jvp()/while/body/eval_jaxpr/tnh,mnh->mth/dot_general | solution.py:85
  631.5 35.2 %multiply_reduce_fusion.53 = (f32[512,64]{0,1:T(8,128)S(1)}, f32[512,64]{0,1:T(8,128)S(1)}) fusion(f32[512,64]{0,1:T(8,128)S(1)} %get-tuple-element.8008, f32[64,512]{1,0:T(8,128)} %get-tuple-element.8340, f32[64]{0:T(128)S(1)} %get-tuple-element.8339, f32[64,512]{1,0:T(8,128)} %get-tuple-element.8338, f32[64,512]{1,0:T(8,128)} %get-tuple-element.8336, ...), kind=kLoop, calls=%fused_computation.155.clone.1 | loop fusion | flops 29294592 | bytes 1048832 | tf_op jit(solution)/shard_map/jvp()/while/body/eval_jaxpr/tnh,mnh->mth/dot_general | solution.py:85
  677.0 33.1 %fusion.583 = (f32[512,64]{0,1:T(8,128)S(1)}, f32[512,64]{0,1:T(8,128)S(1)}) fusion(f32[512,64]{0,1:T(8,128)S(1)} %fusion.582, f32[64,512]{1,0:T(8,128)} %get-tuple-element.8336, f32[64,512]{1,0:T(8,128)S(1)} %get-tuple-element.8335, f32[64]{0:T(128)S(1)} %get-tuple-element.8337), kind=kLoop, calls=%fused_computation.152.clone.1 | loop fusion | flops 16711680 | bytes 655616 | tf_op jit(solution)/shard_map/jvp()/while/body/eval_jaxpr/jnh,mjh->mnh/dot_general | solution.py:121
  711.4 35.2 %multiply_reduce_fusion.53 = (f32[512,64]{0,1:T(8,128)S(1)}, f32[512,64]{0,1:T(8,128)S(1)}) fusion(f32[512,64]{0,1:T(8,128)S(1)} %get-tuple-element.8008, f32[64,512]{1,0:T(8,128)} %get-tuple-element.8340, f32[64]{0:T(128)S(1)} %get-tuple-element.8339, f32[64,512]{1,0:T(8,128)} %get-tuple-element.8338, f32[64,512]{1,0:T(8,128)} %get-tuple-element.8336, ...), kind=kLoop, calls=%fused_computation.155.clone.1 | loop fusion | flops 29294592 | bytes 1048832 | tf_op jit(solution)/shard_map/jvp()/while/body/eval_jaxpr/tnh,mnh->mth/dot_general | solution.py:85
  791.3 35.2 %multiply_reduce_fusion.53 = (f32[512,64]{0,1:T(8,128)S(1)}, f32[512,64]{0,1:T(8,128)S(1)}) fusion(f32[512,64]{0,1:T(8,128)S(1)} %get-tuple-element.8008, f32[64,512]{1,0:T(8,128)} %get-tuple-element.8340, f32[64]{0:T(128)S(1)} %get-tuple-element.8339, f32[64,512]{1,0:T(8,128)} %get-tuple-element.8338, f32[64,512]{1,0:T(8,128)} %get-tuple-element.8336, ...), kind=kLoop, calls=%fused_computation.155.clone.1 | loop fusion | flops 29294592 | bytes 1048832 | tf_op jit(solution)/shard_map/jvp()/while/body/eval_jaxpr/tnh,mnh->mth/dot_general | solution.py:85
  854.3 164.1 %while.286 = (s32[]{:T(128)}, f32[1,64,512]{2,1,0:T(8,128)S(1)}, f32[1,64,512]{2,1,0:T(8,128)S(1)}, f32[4,1,64,512]{3,2,1,0:T(8,128)}, f32[4,1,64,512]{3,2,1,0:T...) while((s32[]{:T(128)}, f32[1,64,512]{2,1,0:T(8,128)S(1)}, ...), condition=%wide.region_11.12_spmd.clone.clone, body=%wide.region_10.11_spmd.clone.clone.sunk | while | flops 29819012 | bytes 2494939 | solution.py:149
  858.0 35.2 %multiply_reduce_fusion.50 = (f32[512,64]{0,1:T(8,128)S(1)}, f32[512,64]{0,1:T(8,128)S(1)}) fusion(f32[512,64]{0,1:T(8,128)S(1)} %bitcast.1484, f32[64,512]{1,0:T(8,128)} %get-tuple-element.8425, f32[64,512]{1,0:T(8,128)} %get-tuple-element.8423, f32[64,512]{1,0:T(8,128)S(1)} %get-tuple-element.8422, f32[64]{0:T(128)S(1)} %get-tuple-element.8424, ...), kind=kLoop, calls=%fused_computation.91.clone.1 | loop fusion | flops 29294592 | bytes 1048832 | tf_op jit(solution)/shard_map/jvp()/while/body/eval_jaxpr/tnh,mnh->mth/dot_general | solution.py:85
  899.1 35.2 %multiply_reduce_fusion.50 = (f32[512,64]{0,1:T(8,128)S(1)}, f32[512,64]{0,1:T(8,128)S(1)}) fusion(f32[512,64]{0,1:T(8,128)S(1)} %bitcast.1484, f32[64,512]{1,0:T(8,128)} %get-tuple-element.8425, f32[64,512]{1,0:T(8,128)} %get-tuple-element.8423, f32[64,512]{1,0:T(8,128)S(1)} %get-tuple-element.8422, f32[64]{0:T(128)S(1)} %get-tuple-element.8424, ...), kind=kLoop, calls=%fused_computation.91.clone.1 | loop fusion | flops 29294592 | bytes 1048832 | tf_op jit(solution)/shard_map/jvp()/while/body/eval_jaxpr/tnh,mnh->mth/dot_general | solution.py:85
  940.2 35.2 %multiply_reduce_fusion.50 = (f32[512,64]{0,1:T(8,128)S(1)}, f32[512,64]{0,1:T(8,128)S(1)}) fusion(f32[512,64]{0,1:T(8,128)S(1)} %bitcast.1484, f32[64,512]{1,0:T(8,128)} %get-tuple-element.8425, f32[64,512]{1,0:T(8,128)} %get-tuple-element.8423, f32[64,512]{1,0:T(8,128)S(1)} %get-tuple-element.8422, f32[64]{0:T(128)S(1)} %get-tuple-element.8424, ...), kind=kLoop, calls=%fused_computation.91.clone.1 | loop fusion | flops 29294592 | bytes 1048832 | tf_op jit(solution)/shard_map/jvp()/while/body/eval_jaxpr/tnh,mnh->mth/dot_general | solution.py:85
  981.2 35.2 %multiply_reduce_fusion.50 = (f32[512,64]{0,1:T(8,128)S(1)}, f32[512,64]{0,1:T(8,128)S(1)}) fusion(f32[512,64]{0,1:T(8,128)S(1)} %bitcast.1484, f32[64,512]{1,0:T(8,128)} %get-tuple-element.8425, f32[64,512]{1,0:T(8,128)} %get-tuple-element.8423, f32[64,512]{1,0:T(8,128)S(1)} %get-tuple-element.8422, f32[64]{0:T(128)S(1)} %get-tuple-element.8424, ...), kind=kLoop, calls=%fused_computation.91.clone.1 | loop fusion | flops 29294592 | bytes 1048832 | tf_op jit(solution)/shard_map/jvp()/while/body/eval_jaxpr/tnh,mnh->mth/dot_general | solution.py:85
  1040.3 164.3 %while.287 = (s32[]{:T(128)}, f32[1,64,512]{2,1,0:T(8,128)S(1)}, f32[1,64,512]{2,1,0:T(8,128)S(1)}, f32[4,1,64,512]{3,2,1,0:T(8,128)}, f32[4,1,64,512]{3,2,1,0:T...) while((s32[]{:T(128)}, f32[1,64,512]{2,1,0:T(8,128)S(1)}, ...), condition=%wide.region_19.20_spmd.clone.clone, body=%wide.region_18.19_spmd.clone.clone.sunk | while | flops 29819012 | bytes 2494683 | solution.py:149
  1044.2 35.2 %multiply_reduce_fusion.51 = (f32[512,64]{0,1:T(8,128)S(1)}, f32[512,64]{0,1:T(8,128)S(1)}) fusion(f32[512,64]{0,1:T(8,128)S(1)} %bitcast.1485, f32[64,512]{1,0:T(8,128)} %get-tuple-element.8575, f32[64,512]{1,0:T(8,128)} %get-tuple-element.8573, f32[64,512]{1,0:T(8,128)S(1)} %get-tuple-element.8572, f32[64]{0:T(128)S(1)} %get-tuple-element.8574, ...), kind=kLoop, calls=%fused_computation.118.clone.1 | loop fusion | flops 29294592 | bytes 1048832 | tf_op jit(solution)/shard_map/jvp()/while/body/eval_jaxpr/tnh,mnh->mth/dot_general | solution.py:85
  1085.2 35.2 %multiply_reduce_fusion.51 = (f32[512,64]{0,1:T(8,128)S(1)}, f32[512,64]{0,1:T(8,128)S(1)}) fusion(f32[512,64]{0,1:T(8,128)S(1)} %bitcast.1485, f32[64,512]{1,0:T(8,128)} %get-tuple-element.8575, f32[64,512]{1,0:T(8,128)} %get-tuple-element.8573, f32[64,512]{1,0:T(8,128)S(1)} %get-tuple-element.8572, f32[64]{0:T(128)S(1)} %get-tuple-element.8574, ...), kind=kLoop, calls=%fused_computation.118.clone.1 | loop fusion | flops 29294592 | bytes 1048832 | tf_op jit(solution)/shard_map/jvp()/while/body/eval_jaxpr/tnh,mnh->mth/dot_general | solution.py:85
  1126.4 35.2 %multiply_reduce_fusion.51 = (f32[512,64]{0,1:T(8,128)S(1)}, f32[512,64]{0,1:T(8,128)S(1)}) fusion(f32[512,64]{0,1:T(8,128)S(1)} %bitcast.1485, f32[64,512]{1,0:T(8,128)} %get-tuple-element.8575, f32[64,512]{1,0:T(8,128)} %get-tuple-element.8573, f32[64,512]{1,0:T(8,128)S(1)} %get-tuple-element.8572, f32[64]{0:T(128)S(1)} %get-tuple-element.8574, ...), kind=kLoop, calls=%fused_computation.118.clone.1 | loop fusion | flops 29294592 | bytes 1048832 | tf_op jit(solution)/shard_map/jvp()/while/body/eval_jaxpr/tnh,mnh->mth/dot_general | solution.py:85
  1167.3 35.2 %multiply_reduce_fusion.51 = (f32[512,64]{0,1:T(8,128)S(1)}, f32[512,64]{0,1:T(8,128)S(1)}) fusion(f32[512,64]{0,1:T(8,128)S(1)} %bitcast.1485, f32[64,512]{1,0:T(8,128)} %get-tuple-element.8575, f32[64,512]{1,0:T(8,128)} %get-tuple-element.8573, f32[64,512]{1,0:T(8,128)S(1)} %get-tuple-element.8572, f32[64]{0:T(128)S(1)} %get-tuple-element.8574, ...), kind=kLoop, calls=%fused_computation.118.clone.1 | loop fusion | flops 29294592 | bytes 1048832 | tf_op jit(solution)/shard_map/jvp()/while/body/eval_jaxpr/tnh,mnh->mth/dot_general | solution.py:85
  1242.2 269.7 %while.292 = (s32[]{:T(128)}, f32[64,64,512]{2,1,0:T(8,128)}, f32[64,64,512]{2,1,0:T(8,128)}, f32[64,512]{1,0:T(8,128)}, f32[64,512]{1,0:T(8,128)}, /*index=5*/f...) while((s32[]{:T(128)}, f32[64,64,512]{2,1,0:T(8,128)}, ...), condition=%wide.region_30.31_spmd.clone.clone.clone, body=%wide.region_29.30_spmd.clone.clone.clone.sunk | while | flops 42991748 | bytes 190190000 | solution.py:149
  1250.0 33.4 %multiply_add_fusion.15 = (f32[64,64,512]{2,1,0:T(8,128)S(1)}, f32[64,64,512]{2,1,0:T(8,128)S(1)}) fusion(f32[64,512]{1,0:T(8,128)} %get-tuple-element.8840, f32[64,512]{1,0:T(8,128)} %get-tuple-element.8838, f32[64,512]{1,0:T(8,128)S(1)} %get-tuple-element.8837, f32[64]{0:T(128)S(1)} %get-tuple-element.8839, f32[64,512]{1,0:T(8,128)} %get-tuple-element.8836), kind=kLoop, calls=%fused_computation.357.clone.1 | loop fusion | flops 20971520 | bytes 17301760 | tf_op jit(solution)/shard_map/jvp()/add | solution.py:77
  1317.8 33.4 %multiply_add_fusion.15 = (f32[64,64,512]{2,1,0:T(8,128)S(1)}, f32[64,64,512]{2,1,0:T(8,128)S(1)}) fusion(f32[64,512]{1,0:T(8,128)} %get-tuple-element.8840, f32[64,512]{1,0:T(8,128)} %get-tuple-element.8838, f32[64,512]{1,0:T(8,128)S(1)} %get-tuple-element.8837, f32[64]{0:T(128)S(1)} %get-tuple-element.8839, f32[64,512]{1,0:T(8,128)} %get-tuple-element.8836), kind=kLoop, calls=%fused_computation.357.clone.1 | loop fusion | flops 20971520 | bytes 17301760 | tf_op jit(solution)/shard_map/jvp()/add | solution.py:77
  1385.5 33.4 %multiply_add_fusion.15 = (f32[64,64,512]{2,1,0:T(8,128)S(1)}, f32[64,64,512]{2,1,0:T(8,128)S(1)}) fusion(f32[64,512]{1,0:T(8,128)} %get-tuple-element.8840, f32[64,512]{1,0:T(8,128)} %get-tuple-element.8838, f32[64,512]{1,0:T(8,128)S(1)} %get-tuple-element.8837, f32[64]{0:T(128)S(1)} %get-tuple-element.8839, f32[64,512]{1,0:T(8,128)} %get-tuple-element.8836), kind=kLoop, calls=%fused_computation.357.clone.1 | loop fusion | flops 20971520 | bytes 17301760 | tf_op jit(solution)/shard_map/jvp()/add | solution.py:77
  1453.3 33.4 %multiply_add_fusion.15 = (f32[64,64,512]{2,1,0:T(8,128)S(1)}, f32[64,64,512]{2,1,0:T(8,128)S(1)}) fusion(f32[64,512]{1,0:T(8,128)} %get-tuple-element.8840, f32[64,512]{1,0:T(8,128)} %get-tuple-element.8838, f32[64,512]{1,0:T(8,128)S(1)} %get-tuple-element.8837, f32[64]{0:T(128)S(1)} %get-tuple-element.8839, f32[64,512]{1,0:T(8,128)} %get-tuple-element.8836), kind=kLoop, calls=%fused_computation.357.clone.1 | loop fusion | flops 20971520 | bytes 17301760 | tf_op jit(solution)/shard_map/jvp()/add | solution.py:77
  1536.3 495.8 %while.293 = (s32[]{:T(128)}, f32[64,64,512]{2,1,0:T(8,128)}, f32[64,64,512]{2,1,0:T(8,128)}, f32[64,64,512]{2,1,0:T(8,128)}, f32[512]{0:T(512)S(1)}, /*index=5*...) while((s32[]{:T(128)}, f32[64,64,512]{2,1,0:T(8,128)}, ...), condition=%wide.region_35.36_spmd.clone.clone.clone, body=%wide.region_33.35_spmd.clone.clone.clone.sunk | while | flops 87151360 | bytes 345448416 | solution.py:128
  1542.9 67.2 %fusion.600 = (f32[64,64,512]{2,1,0:T(8,128)}, f32[64,64,512]{2,1,0:T(8,128)}, f32[64,64,512]{2,1,0:T(8,128)}, f32[64,64,512]{2,1,0:T(8,128)}) fusion(f32[64]{0:T(128)} %get-tuple-element.8972, f32[64,512]{1,0:T(8,128)} %get-tuple-element.8969, f32[64,512]{1,0:T(8,128)S(1)} %get-tuple-element.8968, f32[64,512]{1,0:T(8,128)} %get-tuple-element.8971, ...), kind=kLoop, calls=%fused_computation.392.clone.1 | loop fusion | flops 29360128 | bytes 34079232 | tf_op jit(solution)/shard_map/jvp()/mul | solution.py:44
  1661.0 67.2 %fusion.600 = (f32[64,64,512]{2,1,0:T(8,128)}, f32[64,64,512]{2,1,0:T(8,128)}, f32[64,64,512]{2,1,0:T(8,128)}, f32[64,64,512]{2,1,0:T(8,128)}) fusion(f32[64]{0:T(128)} %get-tuple-element.8972, f32[64,512]{1,0:T(8,128)} %get-tuple-element.8969, f32[64,512]{1,0:T(8,128)S(1)} %get-tuple-element.8968, f32[64,512]{1,0:T(8,128)} %get-tuple-element.8971, ...), kind=kLoop, calls=%fused_computation.392.clone.1 | loop fusion | flops 29360128 | bytes 34079232 | tf_op jit(solution)/shard_map/jvp()/mul | solution.py:44
  1786.7 67.2 %fusion.600 = (f32[64,64,512]{2,1,0:T(8,128)}, f32[64,64,512]{2,1,0:T(8,128)}, f32[64,64,512]{2,1,0:T(8,128)}, f32[64,64,512]{2,1,0:T(8,128)}) fusion(f32[64]{0:T(128)} %get-tuple-element.8972, f32[64,512]{1,0:T(8,128)} %get-tuple-element.8969, f32[64,512]{1,0:T(8,128)S(1)} %get-tuple-element.8968, f32[64,512]{1,0:T(8,128)} %get-tuple-element.8971, ...), kind=kLoop, calls=%fused_computation.392.clone.1 | loop fusion | flops 29360128 | bytes 34079232 | tf_op jit(solution)/shard_map/jvp()/mul | solution.py:44
  1912.3 67.2 %fusion.600 = (f32[64,64,512]{2,1,0:T(8,128)}, f32[64,64,512]{2,1,0:T(8,128)}, f32[64,64,512]{2,1,0:T(8,128)}, f32[64,64,512]{2,1,0:T(8,128)}) fusion(f32[64]{0:T(128)} %get-tuple-element.8972, f32[64,512]{1,0:T(8,128)} %get-tuple-element.8969, f32[64,512]{1,0:T(8,128)S(1)} %get-tuple-element.8968, f32[64,512]{1,0:T(8,128)} %get-tuple-element.8971, ...), kind=kLoop, calls=%fused_computation.392.clone.1 | loop fusion | flops 29360128 | bytes 34079232 | tf_op jit(solution)/shard_map/jvp()/mul | solution.py:44
  2035.0 269.3 %while.290 = (s32[]{:T(128)}, f32[64,64,512]{2,1,0:T(8,128)}, f32[64,64,512]{2,1,0:T(8,128)}, f32[64,512]{1,0:T(8,128)}, f32[64,512]{1,0:T(8,128)}, /*index=5*/f...) while((s32[]{:T(128)}, f32[64,64,512]{2,1,0:T(8,128)}, ...), condition=%wide.region_21.22_spmd.clone.clone.clone, body=%wide.region_20.21_spmd.clone.clone.clone.sunk | while | flops 42991748 | bytes 190190000 | solution.py:149
  2042.3 33.4 %multiply_add_fusion.14 = (f32[64,64,512]{2,1,0:T(8,128)S(1)}, f32[64,64,512]{2,1,0:T(8,128)S(1)}) fusion(f32[64,512]{1,0:T(8,128)} %get-tuple-element.8639, f32[64,512]{1,0:T(8,128)} %get-tuple-element.8637, f32[64,512]{1,0:T(8,128)S(1)} %get-tuple-element.8636, f32[64]{0:T(128)S(1)} %get-tuple-element.8638, f32[64,512]{1,0:T(8,128)} %get-tuple-element.8635), kind=kLoop, calls=%fused_computation.261.clone.1 | loop fusion | flops 20971520 | bytes 17301760 | tf_op jit(solution)/shard_map/jvp()/add | solution.py:77
  2110.0 33.4 %multiply_add_fusion.14 = (f32[64,64,512]{2,1,0:T(8,128)S(1)}, f32[64,64,512]{2,1,0:T(8,128)S(1)}) fusion(f32[64,512]{1,0:T(8,128)} %get-tuple-element.8639, f32[64,512]{1,0:T(8,128)} %get-tuple-element.8637, f32[64,512]{1,0:T(8,128)S(1)} %get-tuple-element.8636, f32[64]{0:T(128)S(1)} %get-tuple-element.8638, f32[64,512]{1,0:T(8,128)} %get-tuple-element.8635), kind=kLoop, calls=%fused_computation.261.clone.1 | loop fusion | flops 20971520 | bytes 17301760 | tf_op jit(solution)/shard_map/jvp()/add | solution.py:77
  2177.8 33.4 %multiply_add_fusion.14 = (f32[64,64,512]{2,1,0:T(8,128)S(1)}, f32[64,64,512]{2,1,0:T(8,128)S(1)}) fusion(f32[64,512]{1,0:T(8,128)} %get-tuple-element.8639, f32[64,512]{1,0:T(8,128)} %get-tuple-element.8637, f32[64,512]{1,0:T(8,128)S(1)} %get-tuple-element.8636, f32[64]{0:T(128)S(1)} %get-tuple-element.8638, f32[64,512]{1,0:T(8,128)} %get-tuple-element.8635), kind=kLoop, calls=%fused_computation.261.clone.1 | loop fusion | flops 20971520 | bytes 17301760 | tf_op jit(solution)/shard_map/jvp()/add | solution.py:77
  2245.6 33.4 %multiply_add_fusion.14 = (f32[64,64,512]{2,1,0:T(8,128)S(1)}, f32[64,64,512]{2,1,0:T(8,128)S(1)}) fusion(f32[64,512]{1,0:T(8,128)} %get-tuple-element.8639, f32[64,512]{1,0:T(8,128)} %get-tuple-element.8637, f32[64,512]{1,0:T(8,128)S(1)} %get-tuple-element.8636, f32[64]{0:T(128)S(1)} %get-tuple-element.8638, f32[64,512]{1,0:T(8,128)} %get-tuple-element.8635), kind=kLoop, calls=%fused_computation.261.clone.1 | loop fusion | flops 20971520 | bytes 17301760 | tf_op jit(solution)/shard_map/jvp()/add | solution.py:77
  2328.4 488.5 %while.291 = (s32[]{:T(128)}, f32[64,64,512]{2,1,0:T(8,128)}, f32[64,64,512]{2,1,0:T(8,128)}, f32[64,64,512]{2,1,0:T(8,128)}, f32[512]{0:T(512)S(1)}, /*index=5*...) while((s32[]{:T(128)}, f32[64,64,512]{2,1,0:T(8,128)}, ...), condition=%wide.region_26.27_spmd.clone.clone.clone, body=%wide.region_24.26_spmd.clone.clone.clone.sunk | while | flops 87151360 | bytes 311894208 | solution.py:128
  2334.9 66.8 %fusion.593 = (f32[64,64,512]{2,1,0:T(8,128)}, f32[64,64,512]{2,1,0:T(8,128)}, f32[64,64,512]{2,1,0:T(8,128)S(1)}, f32[64,64,512]{2,1,0:T(8,128)}) fusion(f32[64]{0:T(128)} %get-tuple-element.8771, f32[64,512]{1,0:T(8,128)} %get-tuple-element.8768, f32[64,512]{1,0:T(8,128)S(1)} %get-tuple-element.8767, f32[64,512]{1,0:T(8,128)} %get-tuple-element.8770, ...), kind=kLoop, calls=%fused_computation.296.clone.1 | loop fusion | flops 29360128 | bytes 34079232 | tf_op jit(solution)/shard_map/jvp()/mul | solution.py:44
  2451.4 66.8 %fusion.593 = (f32[64,64,512]{2,1,0:T(8,128)}, f32[64,64,512]{2,1,0:T(8,128)}, f32[64,64,512]{2,1,0:T(8,128)S(1)}, f32[64,64,512]{2,1,0:T(8,128)}) fusion(f32[64]{0:T(128)} %get-tuple-element.8771, f32[64,512]{1,0:T(8,128)} %get-tuple-element.8768, f32[64,512]{1,0:T(8,128)S(1)} %get-tuple-element.8767, f32[64,512]{1,0:T(8,128)} %get-tuple-element.8770, ...), kind=kLoop, calls=%fused_computation.296.clone.1 | loop fusion | flops 29360128 | bytes 34079232 | tf_op jit(solution)/shard_map/jvp()/mul | solution.py:44
  2575.2 66.8 %fusion.593 = (f32[64,64,512]{2,1,0:T(8,128)}, f32[64,64,512]{2,1,0:T(8,128)}, f32[64,64,512]{2,1,0:T(8,128)S(1)}, f32[64,64,512]{2,1,0:T(8,128)}) fusion(f32[64]{0:T(128)} %get-tuple-element.8771, f32[64,512]{1,0:T(8,128)} %get-tuple-element.8768, f32[64,512]{1,0:T(8,128)S(1)} %get-tuple-element.8767, f32[64,512]{1,0:T(8,128)} %get-tuple-element.8770, ...), kind=kLoop, calls=%fused_computation.296.clone.1 | loop fusion | flops 29360128 | bytes 34079232 | tf_op jit(solution)/shard_map/jvp()/mul | solution.py:44
  2699.1 66.8 %fusion.593 = (f32[64,64,512]{2,1,0:T(8,128)}, f32[64,64,512]{2,1,0:T(8,128)}, f32[64,64,512]{2,1,0:T(8,128)S(1)}, f32[64,64,512]{2,1,0:T(8,128)}) fusion(f32[64]{0:T(128)} %get-tuple-element.8771, f32[64,512]{1,0:T(8,128)} %get-tuple-element.8768, f32[64,512]{1,0:T(8,128)S(1)} %get-tuple-element.8767, f32[64,512]{1,0:T(8,128)} %get-tuple-element.8770, ...), kind=kLoop, calls=%fused_computation.296.clone.1 | loop fusion | flops 29360128 | bytes 34079232 | tf_op jit(solution)/shard_map/jvp()/mul | solution.py:44
  2870.7 121.4 %fusion.230 = (f32[64,512]{1,0:T(8,128)}, f32[64,512]{1,0:T(8,128)}, f32[64,512]{1,0:T(8,128)S(1)}, f32[64,512]{1,0:T(8,128)S(1)}, f32[64,512]{1,0:T(8,128)}, /*...) fusion(f32[64,512]{1,0:T(8,128)} %get-tuple-element.8905, ...), kind=kLoop, calls=%fused_computation.465 | loop fusion | flops 169476096 | bytes 103023104 | tf_op jit(solution)/shard_map/transpose(jvp())/reduce_sum | solution.py:43
  3014.9 34.7 %all-reduce.17 = (f32[512]{0:T(512)S(1)}, f32[512]{0:T(512)S(1)}, f32[64]{0:T(128)S(1)}, f32[64]{0:T(128)S(1)}, f32[512]{0:T(512)S(1)}, /*index=5*/f32[512]{0:T(512)S(1)}, f32[1024]{0:T(1024)S(1)}) all-reduce(f32[512]{0:T(512)S(1)} %add.653, f32[512]{0:T(512)S(1)} %add.654, ...), channel_id=10, replica_groups=mesh['dp'=8,'seq'=4] {'dp'}, use_global_device_ids=true, to_apply=%region_40.41.clone | all-reduce | flops 3200 | bytes 25600
  (1126 shorter events, 1336.2 us)
Async XLA Ops:
  7.2 1221.6 %all-gather.11.cloned.1.call-start = ((), (), s32[]{:S(2)}) async-start(), calls=%async_computation.2 | async-start | bytes 1179648 | tf_op jit(solution)/shard_map/all_gather | solution.py:255
  7.9 3005.7 %reduce-scatter.5.cloned.1.call-start = ((), (), s32[]{:S(2)}) async-start(), calls=%async_computation.3 | async-start | bytes 2359296 | tf_op jit(solution)/shard_map/reduce_scatter | solution.py:329
  48.2 122.3 %copy-start.64 = (f32[256]{0:T(256)}, f32[256]{0:T(256)S(1)}, u32[]{:S(2)}) copy-start(f32[256]{0:T(256)S(1)} %get-tuple-element.6685) | copy-start | bytes 3076
  48.3 122.3 %copy-start.66 = (f32[256]{0:T(256)}, f32[256]{0:T(256)S(1)}, u32[]{:S(2)}) copy-start(f32[256]{0:T(256)S(1)} %get-tuple-element.6686) | copy-start | bytes 3076
  84.5 86.1 %copy-start.52 = (f32[1,64,512]{2,1,0:T(8,128)}, f32[1,64,512]{2,1,0:T(8,128)S(1)}, u32[]{:S(2)}) copy-start(f32[1,64,512]{2,1,0:T(8,128)S(1)} %copy.376) | copy-start | bytes 393220
  84.6 86.0 %copy-start.53 = (f32[1,64,512]{2,1,0:T(8,128)}, f32[1,64,512]{2,1,0:T(8,128)S(1)}, u32[]{:S(2)}) copy-start(f32[1,64,512]{2,1,0:T(8,128)S(1)} %copy.377) | copy-start | bytes 393220
  173.5 320.6 %copy-start.86 = (s32[1,4]{1,0:T(1,128)S(1)}, s32[1,4]{1,0:T(1,128)}, u32[]{:S(2)}) copy-start(s32[1,4]{1,0:T(1,128)} %slice.128) | copy-start | bytes 52
  497.4 345.5 %copy-start.23 = (f32[1,64,512]{2,1,0:T(8,128)S(1)}, f32[1,64,512]{2,1,0:T(8,128)}, u32[]{:S(2)}) copy-start(f32[1,64,512]{2,1,0:T(8,128)} %custom-call.3) | copy-start | bytes 393220
  1040.2 166.6 %copy-start.81 = (f32[128]{0:T(128)S(1)}, f32[128]{0:T(128)}, u32[]{:S(2)}) copy-start(f32[128]{0:T(128)} %param.46) | copy-start | bytes 1540
  1040.2 182.9 %copy-start.55 = (f32[4,1,64,512]{3,2,1,0:T(8,128)S(1)}, f32[4,1,64,512]{3,2,1,0:T(8,128)}, u32[]{:S(2)}) copy-start(f32[4,1,64,512]{3,2,1,0:T(8,128)} %get-tuple-element.2935) | copy-start | bytes 1572868
  1040.2 182.9 %copy-start.56 = (f32[4,1,64,512]{3,2,1,0:T(8,128)S(1)}, f32[4,1,64,512]{3,2,1,0:T(8,128)}, u32[]{:S(2)}) copy-start(f32[4,1,64,512]{3,2,1,0:T(8,128)} %get-tuple-element.2940) | copy-start | bytes 1572868
  1239.7 1830.4 %reduce-scatter.7.cloned.1.call-start = ((), (), s32[]{:S(2)}) async-start(), calls=%async_computation.5 | async-start | bytes 294912
  1242.2 294.1 %copy-start.58 = (f32[1,1,512]{2,1,0:T(1,128)S(1)}, f32[1,1,512]{2,1,0:T(1,128)}, u32[]{:S(2)}) copy-start(f32[1,1,512]{2,1,0:T(1,128)} %copy-done.57) | copy-start | bytes 6148
  1536.3 495.8 %copy-start.14 = (bf16[512,1024]{1,0:T(8,128)(2,1)S(1)}, bf16[512,1024]{1,0:T(8,128)(2,1)}, u32[]{:S(2)}) copy-start(bf16[512,1024]{1,0:T(8,128)(2,1)} %all-gather.11.cloned.1.call-done) | copy-start | bytes 3145732
  1541.2 72.1 %slice-start = ((s8[8388608]{0:T(1024)(128)(4,1)}), s8[4194304]{0:T(1024)(128)(4,1)S(1)}, s32[]{:S(2)}) async-start(s8[8388608]{0:T(1024)(128)(4,1)} %bitcast.1440), calls=%async_computation.6 | async-start | bytes 8388608 | tf_op jit(solution)/shard_map/transpose(jvp())/while
  1542.8 70.4 %slice-start.1 = ((s8[8388608]{0:T(1024)(128)(4,1)}), s8[4194304]{0:T(1024)(128)(4,1)S(1)}, s32[]{:S(2)}) async-start(s8[8388608]{0:T(1024)(128)(4,1)} %bitcast.1440), calls=%async_computation.7 | async-start | bytes 8388608 | tf_op jit(solution)/shard_map/transpose(jvp())/while
  1659.4 72.1 %slice-start = ((s8[8388608]{0:T(1024)(128)(4,1)}), s8[4194304]{0:T(1024)(128)(4,1)S(1)}, s32[]{:S(2)}) async-start(s8[8388608]{0:T(1024)(128)(4,1)} %bitcast.1440), calls=%async_computation.6 | async-start | bytes 8388608 | tf_op jit(solution)/shard_map/transpose(jvp())/while
  1661.0 70.4 %slice-start.1 = ((s8[8388608]{0:T(1024)(128)(4,1)}), s8[4194304]{0:T(1024)(128)(4,1)S(1)}, s32[]{:S(2)}) async-start(s8[8388608]{0:T(1024)(128)(4,1)} %bitcast.1440), calls=%async_computation.7 | async-start | bytes 8388608 | tf_op jit(solution)/shard_map/transpose(jvp())/while
  1785.0 72.1 %slice-start = ((s8[8388608]{0:T(1024)(128)(4,1)}), s8[4194304]{0:T(1024)(128)(4,1)S(1)}, s32[]{:S(2)}) async-start(s8[8388608]{0:T(1024)(128)(4,1)} %bitcast.1440), calls=%async_computation.6 | async-start | bytes 8388608 | tf_op jit(solution)/shard_map/transpose(jvp())/while
  1786.7 70.4 %slice-start.1 = ((s8[8388608]{0:T(1024)(128)(4,1)}), s8[4194304]{0:T(1024)(128)(4,1)S(1)}, s32[]{:S(2)}) async-start(s8[8388608]{0:T(1024)(128)(4,1)} %bitcast.1440), calls=%async_computation.7 | async-start | bytes 8388608 | tf_op jit(solution)/shard_map/transpose(jvp())/while
  1910.7 72.1 %slice-start = ((s8[8388608]{0:T(1024)(128)(4,1)}), s8[4194304]{0:T(1024)(128)(4,1)S(1)}, s32[]{:S(2)}) async-start(s8[8388608]{0:T(1024)(128)(4,1)} %bitcast.1440), calls=%async_computation.6 | async-start | bytes 8388608 | tf_op jit(solution)/shard_map/transpose(jvp())/while
  1912.3 70.4 %slice-start.1 = ((s8[8388608]{0:T(1024)(128)(4,1)}), s8[4194304]{0:T(1024)(128)(4,1)S(1)}, s32[]{:S(2)}) async-start(s8[8388608]{0:T(1024)(128)(4,1)} %bitcast.1440), calls=%async_computation.7 | async-start | bytes 8388608 | tf_op jit(solution)/shard_map/transpose(jvp())/while
  2035.0 293.5 %copy-start.59 = (f32[512]{0:T(512)S(1)}, f32[512]{0:T(512)}, u32[]{:S(2)}) copy-start(f32[512]{0:T(512)} %custom-call.19) | copy-start | bytes 6148
  2110.0 45.8 %slice-start.10 = ((s8[8388608]{0:T(1024)(128)(4,1)}), s8[4194304]{0:T(1024)(128)(4,1)S(1)}, s32[]{:S(2)}) async-start(s8[8388608]{0:T(1024)(128)(4,1)} %bitcast.1450), calls=%async_computation.16 | async-start | bytes 8388608 | tf_op jit(solution)/shard_map/transpose(jvp())/while
  2177.8 45.8 %slice-start.10 = ((s8[8388608]{0:T(1024)(128)(4,1)}), s8[4194304]{0:T(1024)(128)(4,1)S(1)}, s32[]{:S(2)}) async-start(s8[8388608]{0:T(1024)(128)(4,1)} %bitcast.1450), calls=%async_computation.16 | async-start | bytes 8388608 | tf_op jit(solution)/shard_map/transpose(jvp())/while
  2245.6 45.8 %slice-start.10 = ((s8[8388608]{0:T(1024)(128)(4,1)}), s8[4194304]{0:T(1024)(128)(4,1)S(1)}, s32[]{:S(2)}) async-start(s8[8388608]{0:T(1024)(128)(4,1)} %bitcast.1450), calls=%async_computation.16 | async-start | bytes 8388608 | tf_op jit(solution)/shard_map/transpose(jvp())/while
  2333.3 71.7 %slice-start.2 = ((s8[8388608]{0:T(1024)(128)(4,1)}), s8[4194304]{0:T(1024)(128)(4,1)S(1)}, s32[]{:S(2)}) async-start(s8[8388608]{0:T(1024)(128)(4,1)} %bitcast.1442), calls=%async_computation.8 | async-start | bytes 8388608 | tf_op jit(solution)/shard_map/transpose(jvp())/while
  2334.9 70.1 %slice-start.3 = ((s8[8388608]{0:T(1024)(128)(4,1)}), s8[4194304]{0:T(1024)(128)(4,1)S(1)}, s32[]{:S(2)}) async-start(s8[8388608]{0:T(1024)(128)(4,1)} %bitcast.1442), calls=%async_computation.9 | async-start | bytes 8388608 | tf_op jit(solution)/shard_map/transpose(jvp())/while
  2449.7 71.7 %slice-start.2 = ((s8[8388608]{0:T(1024)(128)(4,1)}), s8[4194304]{0:T(1024)(128)(4,1)S(1)}, s32[]{:S(2)}) async-start(s8[8388608]{0:T(1024)(128)(4,1)} %bitcast.1442), calls=%async_computation.8 | async-start | bytes 8388608 | tf_op jit(solution)/shard_map/transpose(jvp())/while
  2451.3 70.1 %slice-start.3 = ((s8[8388608]{0:T(1024)(128)(4,1)}), s8[4194304]{0:T(1024)(128)(4,1)S(1)}, s32[]{:S(2)}) async-start(s8[8388608]{0:T(1024)(128)(4,1)} %bitcast.1442), calls=%async_computation.9 | async-start | bytes 8388608 | tf_op jit(solution)/shard_map/transpose(jvp())/while
  2573.6 71.7 %slice-start.2 = ((s8[8388608]{0:T(1024)(128)(4,1)}), s8[4194304]{0:T(1024)(128)(4,1)S(1)}, s32[]{:S(2)}) async-start(s8[8388608]{0:T(1024)(128)(4,1)} %bitcast.1442), calls=%async_computation.8 | async-start | bytes 8388608 | tf_op jit(solution)/shard_map/transpose(jvp())/while
  2575.2 70.1 %slice-start.3 = ((s8[8388608]{0:T(1024)(128)(4,1)}), s8[4194304]{0:T(1024)(128)(4,1)S(1)}, s32[]{:S(2)}) async-start(s8[8388608]{0:T(1024)(128)(4,1)} %bitcast.1442), calls=%async_computation.9 | async-start | bytes 8388608 | tf_op jit(solution)/shard_map/transpose(jvp())/while
  2697.5 71.7 %slice-start.2 = ((s8[8388608]{0:T(1024)(128)(4,1)}), s8[4194304]{0:T(1024)(128)(4,1)S(1)}, s32[]{:S(2)}) async-start(s8[8388608]{0:T(1024)(128)(4,1)} %bitcast.1442), calls=%async_computation.8 | async-start | bytes 8388608 | tf_op jit(solution)/shard_map/transpose(jvp())/while
  2699.1 70.1 %slice-start.3 = ((s8[8388608]{0:T(1024)(128)(4,1)}), s8[4194304]{0:T(1024)(128)(4,1)S(1)}, s32[]{:S(2)}) async-start(s8[8388608]{0:T(1024)(128)(4,1)} %bitcast.1442), calls=%async_computation.9 | async-start | bytes 8388608 | tf_op jit(solution)/shard_map/transpose(jvp())/while
  2870.5 130.2 %copy-start.17 = (f32[1,64,512]{2,1,0:T(8,128)S(1)}, f32[1,64,512]{2,1,0:T(8,128)}, u32[]{:S(2)}) copy-start(f32[1,64,512]{2,1,0:T(8,128)} %get-tuple-element.8692) | copy-start | bytes 393220
  2870.5 130.2 %copy-start.18 = (f32[1,64,512]{2,1,0:T(8,128)S(1)}, f32[1,64,512]{2,1,0:T(8,128)}, u32[]{:S(2)}) copy-start(f32[1,64,512]{2,1,0:T(8,128)} %get-tuple-element.8691) | copy-start | bytes 393220
  2870.6 130.2 %copy-start.20 = (f32[1,64,512]{2,1,0:T(8,128)S(1)}, f32[1,64,512]{2,1,0:T(8,128)}, u32[]{:S(2)}) copy-start(f32[1,64,512]{2,1,0:T(8,128)} %copy-done.19) | copy-start | bytes 393220
  2870.6 130.2 %copy-start.22 = (f32[1,64,512]{2,1,0:T(8,128)S(1)}, f32[1,64,512]{2,1,0:T(8,128)}, u32[]{:S(2)}) copy-start(f32[1,64,512]{2,1,0:T(8,128)} %copy-done.21) | copy-start | bytes 393220
  2870.6 130.2 %copy-start.25 = (f32[1,64,512]{2,1,0:T(8,128)S(1)}, f32[1,64,512]{2,1,0:T(8,128)}, u32[]{:S(2)}) copy-start(f32[1,64,512]{2,1,0:T(8,128)} %copy-done.24) | copy-start | bytes 393220
  2870.6 130.2 %copy-start.26 = (f32[1,64,512]{2,1,0:T(8,128)S(1)}, f32[1,64,512]{2,1,0:T(8,128)}, u32[]{:S(2)}) copy-start(f32[1,64,512]{2,1,0:T(8,128)} %get-tuple-element.8374) | copy-start | bytes 393220
  2870.6 130.2 %copy-start.27 = (f32[1,64,512]{2,1,0:T(8,128)S(1)}, f32[1,64,512]{2,1,0:T(8,128)}, u32[]{:S(2)}) copy-start(f32[1,64,512]{2,1,0:T(8,128)} %get-tuple-element.8893) | copy-start | bytes 393220
  2870.6 130.2 %copy-start.28 = (f32[1,64,512]{2,1,0:T(8,128)S(1)}, f32[1,64,512]{2,1,0:T(8,128)}, u32[]{:S(2)}) copy-start(f32[1,64,512]{2,1,0:T(8,128)} %get-tuple-element.8892) | copy-start | bytes 393220
  2870.6 130.2 %copy-start.31 = (f32[64,512]{1,0:T(8,128)S(1)}, f32[64,512]{1,0:T(8,128)}, u32[]{:S(2)}) copy-start(f32[64,512]{1,0:T(8,128)} %get-tuple-element.2965) | copy-start | bytes 393220
  2870.6 130.2 %copy-start.34 = (f32[64,512]{1,0:T(8,128)S(1)}, f32[64,512]{1,0:T(8,128)}, u32[]{:S(2)}) copy-start(f32[64,512]{1,0:T(8,128)} %get-tuple-element.2969) | copy-start | bytes 393220
  2870.6 130.2 %copy-start.35 = (f32[64,512]{1,0:T(8,128)S(1)}, f32[64,512]{1,0:T(8,128)}, u32[]{:S(2)}) copy-start(f32[64,512]{1,0:T(8,128)} %get-tuple-element.2966) | copy-start | bytes 393220
  2870.6 130.2 %copy-start.36 = (f32[64,512]{1,0:T(8,128)S(1)}, f32[64,512]{1,0:T(8,128)}, u32[]{:S(2)}) copy-start(f32[64,512]{1,0:T(8,128)} %get-tuple-element.2970) | copy-start | bytes 393220
  2870.7 130.2 %copy-start.39 = (f32[64,512]{1,0:T(8,128)S(1)}, f32[64,512]{1,0:T(8,128)}, u32[]{:S(2)}) copy-start(f32[64,512]{1,0:T(8,128)} %get-tuple-element.2967) | copy-start | bytes 393220
  3010.3 93.0 %all-reduce.22.cloned.1.call-start = ((), (), s32[]{:S(2)}) async-start(), calls=%async_computation.4 | async-start | bytes 524288 | tf_op jit(solution)/shard_map/psum | solution.py:332
  (174 other events, 1849.1 us)
Sparse Core Ops, SparseCore 0:
  10.1 43.4 all-gather.10
  1239.8 66.2 reduce-scatter.4
  3010.4 59.6 reduce-scatter.6
  3072.3 31.0 all-reduce.21
where the time goes:
time: 3120 us; the launch traced here: 3110 us
  other arithmetic  2500 us (80%)
  local copies, waits for them, and re-layouts  270 us (9%)
  blocking collectives  208 us (7%)
  loops' own time  57.7 us (2%)
  waiting for transfers between devices  40.4 us (1%)
    dot_general x32, other arithmetic, carried_value(): jnp.einsum('tnh,mnh->mth', carry_im, state_im, precision=highest)  642 us
    mul x24, other arithmetic, power_pair(): return (magnitude * jnp.cos(phase_val), magnitude * jnp.sin(phase_val))  551 us
    add x8, other arithmetic, make_tables(): carry_im = coef_re * next_im + coef_im * next_re  267 us
    dot_general x8, other arithmetic, local_advance(): fresh_im = jnp.einsum('jnh,mjh->mnh', tail_im, weighted, precision=highest)  265 us
    add_any x40, other arithmetic, local_pass(): lax.scan(jax.checkpoint(local_advance), (zero_state, zero_state), (u_bloc...  197 us
    reduce_sum x1, other arithmetic, power_pair(): phase_val = exponent * imag_rate  121 us
    while x312, local copies, waits for them, and re-layouts  93.6 us
    all_gather x12, blocking collectives, entering(): everything = jax.tree.map(lambda part: lax.all_gather(part, axis), x)  89 us
  transfers between devices with their start and end apart: 4, of which 2 were waited for; matrix products, arithmetic and copies ran while one was open for 86% of the time, Pallas kernels for 0%

commit v1 on v0

v1 whole, which is shorter than its diff:
```python
from functools import partial

import jax
import jax.numpy as jnp
import numpy as np
from jax import lax
from jax.experimental import pallas as pl
from jax.experimental.pallas import tpu as pltpu
from jax.sharding import PartitionSpec as P

f32, bf16, i32 = jnp.float32, jnp.bfloat16, jnp.int32
ln_eps = 1e-05
DOCMAX = 800
FINE = 8
COARSE = 10
LANES = 128
NN = (((1,), (0,)), ((), ()))
NT = (((1,), (1,)), ((), ()))
TN = (((0,), (0,)), ((), ()))
VM = pl.BlockSpec(memory_space=pltpu.VMEM)
SM = pl.BlockSpec(memory_space=pltpu.SMEM)


def dot(a, b, dims=NN):
    return lax.dot_general(a, b, dims, preferred_element_type=f32)


def exact_dot(a, b, dims=NN):
    return lax.dot_general(a, b, dims, precision=lax.Precision.HIGHEST, preferred_element_type=f32)


def shape(dims, dtype=f32):
    return jax.ShapeDtypeStruct(dims, dtype)


def call(body, out, specs, scratch=(), name=None, mib=8):
    return pl.pallas_call(
        body,
        out_shape=out,
        in_specs=specs,
        scratch_shapes=list(scratch),
        cost_estimate=pl.CostEstimate(flops=1000, bytes_accessed=1000, transcendentals=0),
        compiler_params=pltpu.CompilerParams(vmem_limit_bytes=mib * 2**20),
        name=name,
    )


def dft_tables(block):
    k = np.arange(block)[:, None]
    j = np.arange(block)[None, :]
    theta = np.pi * (((2 * k + 1) * j) % (4 * block)) / (2 * block)
    full = np.concatenate([np.cos(theta), -np.sin(theta)], axis=0)
    high = full.astype(jnp.bfloat16)
    low = (full - high.astype(np.float64)).astype(jnp.bfloat16)
    return high, low, np.ascontiguousarray(high.T), np.ascontiguousarray(low.T)


def channel_order(width, ndp, nseq):
    sub = width // ndp // nseq
    return np.arange(width).reshape(ndp, nseq, sub).transpose(1, 0, 2).reshape(-1)


def iota(dims, axis):
    return lax.broadcasted_iota(i32, dims, axis)


def cmul(ar, ai, br, bi):
    return ar * br - ai * bi, ar * bi + ai * br


def small_expm1(a):
    poly = jnp.full_like(a, 1.0)
    for k in range(9, 1, -1):
        poly = 1.0 + poly * a * (1.0 / k)
    return jnp.where(jnp.abs(a) < 0.5, a * poly, jnp.exp(a) - 1.0)


def state_terms(rate_log, freq, step_log, length):
    step = jnp.exp(step_log)
    a = -jnp.exp(rate_log) * step
    b = freq * step
    half = jnp.sin(0.5 * b)
    cos_b, sin_b, mag = jnp.cos(b), jnp.sin(b), jnp.exp(a)
    one_re = 2.0 * half * half - small_expm1(a) * cos_b
    one_im = -mag * sin_b
    far = jnp.exp(length * a)
    far_re, far_im = far * jnp.cos(length * b), far * jnp.sin(length * b)
    den_re, den_im = 1.0 - far_re, -far_im
    inv = 1.0 / (den_re * den_re + den_im * den_im)
    g_re = (one_re * den_re + one_im * den_im) * inv
    g_im = (one_im * den_re - one_re * den_im) * inv
    return a, b, mag * cos_b, mag * sin_b, one_re, one_im, far_re, far_im, den_re, den_im, inv, g_re, g_im


TERMS = 13


def rows8(zr, zi):
    dims = (8, zr.shape[-1])
    at = iota(dims, 0)
    r1, i1 = jnp.broadcast_to(zr, dims), jnp.broadcast_to(zi, dims)
    r2, i2 = cmul(r1, i1, r1, i1)
    r4, i4 = cmul(r2, i2, r2, i2)
    p = (jnp.where(at & 1 > 0, r1, 1.0), jnp.where(at & 1 > 0, i1, 0.0))
    p = cmul(*p, jnp.where(at & 2 > 0, r2, 1.0), jnp.where(at & 2 > 0, i2, 0.0))
    p = cmul(*p, jnp.where(at & 4 > 0, r4, 1.0), jnp.where(at & 4 > 0, i4, 0.0))
    return p, cmul(r4, i4, r4, i4)


def powers(wr, wi):
    pows = [None, (wr, wi)]
    for v in range(2, COARSE + 1):
        pows.append(cmul(*pows[v // 2], *pows[v - v // 2]))
    return pows


def halves(x):
    hi = x.astype(bf16)
    return hi, (x - hi.astype(f32)).astype(bf16)


def split3(hi_ref, lo_ref, x):
    x_hi, x_lo = halves(x)
    return dot(hi_ref[...], x_hi) + (dot(hi_ref[...], x_lo) + dot(lo_ref[...], x_hi))


def signs(block, lanes):
    return jnp.where(iota((block, lanes), 0) & 1 > 0, -1.0, 1.0)


def moved(x, by):
    return x if by % LANES == 0 else pltpu.roll(x, by % LANES, 1)


def pack_kernel(sub, me_ref, w_ref, step_ref, skip_ref, gain_ref, bias_ref, lam_ref, imag_ref, lb_ref, o_ref):
    own, per, cols = step_ref.shape[1], lam_ref.shape[1], lb_ref.shape[1]
    groups = LANES // sub
    height = w_ref.shape[0] // groups
    pick = (iota((own, LANES), 0) == me_ref[0] * sub + iota((own, LANES), 1) % sub).astype(f32)
    w = exact_dot(w_ref[...], pick)
    vec = exact_dot(jnp.concatenate([step_ref[...], skip_ref[...], gain_ref[...], bias_ref[...]] * 2, axis=0), pick)
    group = iota((1, LANES), 1) // sub
    main = jnp.zeros((height, LANES), f32)
    row = jnp.zeros((1, LANES), f32)
    for u in range(groups):
        main = jnp.where(group == u, w[u * height : (u + 1) * height], main)
        if u < 4:
            row = jnp.where(group == u, vec[u : u + 1], row)
    spot, lane = iota((per, LANES), 0), iota((per, LANES), 1)
    rates = exact_dot(jnp.broadcast_to(lam_ref[...], (8, per)), (lane == spot).astype(f32)) + exact_dot(
        jnp.broadcast_to(imag_ref[...], (8, per)), (lane == spot + per).astype(f32)
    )
    o_ref[0] = jnp.zeros(o_ref.shape[1:], f32)
    o_ref[0, 0:height] = main
    o_ref[0, height : height + 1] = row
    o_ref[0, height + 1 : height + 2] = rates[0:1]
    o_ref[0, height + 2 : height + 3, 0:cols] = lb_ref[...]
    for i in range(1, o_ref.shape[0]):
        o_ref[i] = o_ref[0]


def lag_kernel(sub, length, shared_ref, f_ref, fl_ref, kh_ref, w_ref, vec_ref, term_ref, k_scr, z_scr, kf_scr):
    ndp = shared_ref.shape[0]
    n_w, lanes = w_ref.shape
    nstate = n_w // 2
    per = nstate // ndp
    groups = LANES // sub
    height = n_w // groups
    block = f_ref.shape[1]
    group = iota((1, LANES), 1) // sub
    for u in range(groups):
        acc = jnp.zeros(shared_ref.shape[1:], f32)
        for i in range(ndp):
            acc = jnp.where(group == i, moved(shared_ref[i], (i - u) * sub), acc)
        w_ref[u * height : (u + 1) * height] = acc[0:height]
        if u < 4:
            vec_ref[u : u + 1] = acc[height : height + 1]
    vec_ref[4:8] = jnp.zeros((4, lanes), f32)
    rows = jnp.concatenate([shared_ref[i, height + 1 : height + 2] for i in range(ndp)], axis=0)
    spread = exact_dot((iota((nstate, ndp), 0) // per == iota((nstate, ndp), 1)).astype(f32), rows)
    lane, state = iota((nstate, lanes), 1), iota((nstate, lanes), 0)
    lam = jnp.sum(jnp.where(lane == state % per, spread, 0.0), axis=1, keepdims=True)
    imag = jnp.sum(jnp.where(lane == state % per + per, spread, 0.0), axis=1, keepdims=True)
    terms = state_terms(lam, imag, vec_ref[0:1], float(length))
    for slot, value in enumerate(terms):
        term_ref[slot] = value
    z_scr[0], z_scr[1] = cmul(w_ref[0:nstate], w_ref[nstate:], terms[11], terms[12])
    k_scr[...] = jnp.zeros_like(k_scr)

    def pair(m, _):
        ready = []
        for n in (2 * m, 2 * m + 1):
            (fr, fi), w = rows8(term_ref[2, pl.ds(n, 1), :], term_ref[3, pl.ds(n, 1), :])
            cr = jnp.broadcast_to(z_scr[0, pl.ds(n, 1), :], (8, lanes))
            ci = jnp.broadcast_to(z_scr[1, pl.ds(n, 1), :], (8, lanes))
            ready.append([cmul(fr, fi, cr, ci), powers(*w)])
        for u in range(DOCMAX // FINE // COARSE):
            for v in range(COARSE):
                at = (u * COARSE + v) * FINE
                total = k_scr[at : at + FINE]
                for (xr, xi), pows in ready:
                    total = total + (xr * pows[v][0] - xi * pows[v][1] if v else xr)
                k_scr[at : at + FINE] = total
            for one in ready:
                one[0] = cmul(*one[0], *one[1][COARSE])
        return 0

    lax.fori_loop(0, nstate // 2, pair, 0)
    k_scr[0:1] += vec_ref[1:2]
    parts = length // block
    for p in range(parts):
        kf_scr[p] = split3(f_ref, fl_ref, k_scr[p * block : (p + 1) * block])
    sign = signs(block, lanes)
    for p in range(parts):
        re, im = kf_scr[p, :block], kf_scr[p, block:]
        if p:
            re = re - sign * kf_scr[p - 1, block:]
            im = im + sign * kf_scr[p - 1, :block]
        kh_ref[p, :block] = re * (1.0 / block)
        kh_ref[p, block:] = im * (1.0 / block)


def ln_kernel(me_ref, x_ref, p_ref, *o_refs):
    count, block, width = x_ref.shape
    wide = o_refs[0].shape[-1]
    x = x_ref[...].astype(f32).reshape(count * block, width)
    centre = x - jnp.mean(x, axis=-1, keepdims=True)
    spread = jnp.mean(centre * centre, axis=-1, keepdims=True)
    hi, lo = halves(centre * lax.rsqrt(spread + ln_eps))
    for d, o_ref in enumerate(o_refs):
        c = me_ref[0] ^ d
        cols = p_ref[:, pl.ds(pl.multiple_of(c * wide, wide), wide)]
        o_ref[...] = (dot(hi, cols) + dot(lo, cols)).reshape(count, block, wide)


def ln_back_kernel(me_ref, g0, g1, g2, g3, x_ref, c_ref, p_ref, o_ref):
    count, block, width = x_ref.shape
    wide = g0.shape[-1]
    tokens = count * block
    g = jnp.zeros((tokens, width), f32)
    for d, g_ref in enumerate((g0, g1, g2, g3)):
        c = me_ref[0] ^ d
        cols = p_ref[:, pl.ds(pl.multiple_of(c * wide, wide), wide)]
        g = g + dot(g_ref[...].reshape(tokens, wide), cols, NT)
    x = x_ref[...].astype(f32).reshape(tokens, width)
    centre = x - jnp.mean(x, axis=-1, keepdims=True)
    inv = lax.rsqrt(jnp.mean(centre * centre, axis=-1, keepdims=True) + ln_eps)
    hat = centre * inv
    mean_g = jnp.mean(g, axis=-1, keepdims=True)
    mean_gx = jnp.mean(g * hat, axis=-1, keepdims=True)
    cot = c_ref[...].astype(f32).reshape(tokens, width)
    o_ref[...] = (cot + inv * (g - mean_g - hat * mean_gx)).astype(bf16).reshape(o_ref.shape)


def doc_ends(len_ref, s):
    ends = []
    for d in range(len_ref.shape[1]):
        ends.append(len_ref[s, d] + (ends[-1] if ends else 0))
    return ends


def places(len_ref, s, b, block, parts):
    lo, hi = b * block, b * block + block
    ends = doc_ends(len_ref, s)
    h_start, t_start, h_end, t_end = 0, 0, parts * block, parts * block
    for end in ends:
        h_start = jnp.maximum(h_start, jnp.where(end <= lo, end, 0))
        t_start = jnp.maximum(t_start, jnp.where(end < hi, end, 0))
        h_end = jnp.minimum(h_end, jnp.where(end > lo, end, parts * block))
        t_end = jnp.minimum(t_end, jnp.where(end >= hi, end, parts * block))
    head = jnp.minimum(h_end, hi) - lo
    tail = jnp.maximum(t_start, lo) - lo
    return head, tail, h_start // block, (t_end - 1) // block


def middles(len_ref, count, block, body):
    docs = len_ref.shape[1]
    if docs < 3:
        return

    def one(item, _):
        s, d = item // (docs - 2), item % (docs - 2) + 1
        start = 0
        for e in range(docs):
            start = start + jnp.where(e < d, len_ref[s, e], 0)
        end = start + len_ref[s, d]
        b = start // block

        @pl.when((start > b * block) & (end < (b + 1) * block))
        def _():
            body(s, b, start - b * block, end - b * block)

        return 0

    lax.fori_loop(0, count * (docs - 2), one, 0)


def spectra(head, tail, x, f_ref, fl_ref, exact=False):
    rows = iota(x.shape, 0)
    both = jnp.concatenate([jnp.where(rows < head, x, 0.0), jnp.where(rows >= tail, x, 0.0)], axis=1)
    if exact:
        both = both.astype(bf16)
        return dot(f_ref[...], both) + dot(fl_ref[...], both)
    return split3(f_ref, fl_ref, both)


def conv_kernel(me_ref, len_ref, x0, x1, x2, x3, vec_ref, kh_ref, f_ref, fl_ref, ft_ref, ftl_ref,
                o0, o1, o2, o3, s_ref, u_scr, y_scr, out_scr):
    count, block, lanes = x0.shape
    parts = kh_ref.shape[0]
    gain, bias = vec_ref[2:3], vec_ref[3:4]
    for d, x_ref in enumerate((x0, x1, x2, x3)):
        for s in range(count):
            u_scr[s, me_ref[0] ^ d] = x_ref[s] * gain + bias

    def forward(item, _):
        s, b = item // parts, item % parts
        head, tail, _, _ = places(len_ref, s, b, block, parts)
        s_ref[item] = spectra(head, tail, u_scr[s, b], f_ref, fl_ref)
        return 0

    lax.fori_loop(0, count * parts, forward, 0)

    def output(item, _):
        s, b = item // parts, item % parts
        head, tail, first, _ = places(len_ref, s, b, block, parts)
        kr, ki = kh_ref[0, :block], kh_ref[0, block:]
        for cols in (slice(0, lanes), slice(lanes, 2 * lanes)):
            sr, si = s_ref[item, :block, cols], s_ref[item, block:, cols]
            y_scr[:block, cols], y_scr[block:, cols] = cmul(kr, ki, sr, si)

        def add(e, _):
            p = b - e
            sr, si = s_ref[item - p, :block, lanes:], s_ref[item - p, block:, lanes:]
            re, im = cmul(kh_ref[p, :block], kh_ref[p, block:], sr, si)
            y_scr[:block, :lanes] += re
            y_scr[block:, :lanes] += im
            return 0

        lax.fori_loop(first, b, add, 0)
        y = split3(ft_ref, ftl_ref, y_scr[...])
        rows = iota((block, lanes), 0)
        out_scr[s, b] = jnp.where(rows < head, y[:, :lanes], jnp.where(rows >= tail, y[:, lanes:], 0.0))
        return 0

    lax.fori_loop(0, count * parts, output, 0)

    def middle(s, b, start, end):
        rows = iota((block, lanes), 0)
        keep = (rows >= start) & (rows < end)
        spec = split3(f_ref, fl_ref, jnp.where(keep, u_scr[s, b], 0.0))
        re, im = cmul(kh_ref[0, :block], kh_ref[0, block:], spec[:block], spec[block:])
        y = split3(ft_ref, ftl_ref, jnp.concatenate([re, im], axis=0))
        out_scr[s, b] = jnp.where(keep, y, out_scr[s, b])

    middles(len_ref, count, block, middle)
    for d, o_ref in enumerate((o0, o1, o2, o3)):
        for s in range(count):
            o_ref[s] = out_scr[s, me_ref[0] ^ d].astype(bf16)


def back_kernel(me_ref, len_ref, x0, x1, x2, x3, c0, c1, c2, c3, s_ref, vec_ref, kh_ref,
                f_ref, fl_ref, ft_ref, ftl_ref, g0, g1, g2, g3, dkh_ref, dvec_ref,
                v_scr, sv_scr, y_scr, du_scr):
    count, block, lanes = x0.shape
    parts = kh_ref.shape[0]
    gain, bias = vec_ref[2:3], vec_ref[3:4]
    for d, c_ref in enumerate((c0, c1, c2, c3)):
        for s in range(count):
            v_scr[s, me_ref[0] ^ d] = c_ref[s].astype(f32)
    dkh_ref[...] = jnp.zeros_like(dkh_ref)

    def forward(item, _):
        s, b = item // parts, item % parts
        head, tail, _, _ = places(len_ref, s, b, block, parts)
        sv_scr[item] = spectra(head, tail, v_scr[s, b], f_ref, fl_ref, exact=True)
        return 0

    lax.fori_loop(0, count * parts, forward, 0)

    def source(item, _):
        s, b = item // parts, item % parts
        head, tail, _, last = places(len_ref, s, b, block, parts)
        kr, ki = kh_ref[0, :block], kh_ref[0, block:]
        two = jnp.where(tail > 0, 1.0, 0.0)
        for side in (0, 1):
            cols = slice(side * lanes, (side + 1) * lanes)
            vr, vi = sv_scr[item, :block, cols], sv_scr[item, block:, cols]
            y_scr[:block, cols], y_scr[block:, cols] = cmul(kr, -ki, vr, vi)
            re, im = cmul(vr, vi, s_ref[item, :block, cols], -s_ref[item, block:, cols])
            dkh_ref[0, :block] += re * two if side else re
            dkh_ref[0, block:] += im * two if side else im

        def add(e, _):
            p = e - b
            vr, vi = sv_scr[item + p, :block, :lanes], sv_scr[item + p, block:, :lanes]
            re, im = cmul(kh_ref[p, :block], -kh_ref[p, block:], vr, vi)
            y_scr[:block, lanes:] += re
            y_scr[block:, lanes:] += im
            re, im = cmul(vr, vi, s_ref[item, :block, lanes:], -s_ref[item, block:, lanes:])
            dkh_ref[p, :block] += re
            dkh_ref[p, block:] += im
            return 0

        lax.fori_loop(b + 1, last + 1, add, 0)
        y = split3(ft_ref, ftl_ref, y_scr[...])
        rows = iota((block, lanes), 0)
        du_scr[s, b] = jnp.where(rows >= tail, y[:, lanes:], jnp.where(rows < head, y[:, :lanes], 0.0))
        return 0

    lax.fori_loop(0, count * parts, source, 0)

    def middle(s, b, start, end):
        rows = iota((block, lanes), 0)
        keep = (rows >= start) & (rows < end)
        v = jnp.where(keep, v_scr[s, b], 0.0).astype(bf16)
        sv = dot(f_ref[...], v) + dot(fl_ref[...], v)
        u = jnp.zeros((block, lanes), f32)
        for d, x_ref in enumerate((x0, x1, x2, x3)):
            u = jnp.where(b == me_ref[0] ^ d, x_ref[s], u)
        su = split3(f_ref, fl_ref, jnp.where(keep, u * gain + bias, 0.0))
        re, im = cmul(sv[:block], sv[block:], su[:block], -su[block:])
        dkh_ref[0, :block] += re
        dkh_ref[0, block:] += im
        re, im = cmul(kh_ref[0, :block], -kh_ref[0, block:], sv[:block], sv[block:])
        y = split3(ft_ref, ftl_ref, jnp.concatenate([re, im], axis=0))
        du_scr[s, b] = jnp.where(keep, y, du_scr[s, b])

    middles(len_ref, count, block, middle)
    d_gain = jnp.zeros((1, lanes), f32)
    d_bias = jnp.zeros((1, lanes), f32)
    for d, (x_ref, g_ref) in enumerate(zip((x0, x1, x2, x3), (g0, g1, g2, g3))):
        for s in range(count):
            du = du_scr[s, me_ref[0] ^ d]
            d_bias += jnp.sum(du, axis=0, keepdims=True)
            d_gain += jnp.sum(du * x_ref[s], axis=0, keepdims=True)
            g_ref[s] = (du * gain).astype(bf16)
    dvec_ref[0:1] = d_gain
    dvec_ref[1:2] = d_bias


def dense_kernel(me_ref, q0, q1, q2, q3, x_ref, c_ref, w_ref, lb_ref,
                 out_ref, act_ref, dpre_ref, dlb_ref, d0, d1, d2, d3, slope_scr, dact_scr):
    count, block, wide = q0.shape
    tokens, width = act_ref.shape
    for d, q_ref in enumerate((q0, q1, q2, q3)):
        cols = pl.ds(pl.multiple_of((me_ref[0] ^ d) * wide, wide), wide)
        v = q_ref[...].reshape(tokens, wide).astype(f32)
        cdf = 0.5 * (1.0 + lax.erf(v * np.float32(1.0 / np.sqrt(2.0))))
        act_ref[:, cols] = (v * cdf).astype(bf16)
        slope_scr[:, cols] = cdf + v * (jnp.exp(-0.5 * v * v) * np.float32(1.0 / np.sqrt(2.0 * np.pi)))
    pre = dot(act_ref[...], w_ref[...]) + lb_ref[...]
    first = pre[:, :width]
    gate = 1.0 / (1.0 + jnp.exp(-pre[:, width:]))
    x = x_ref[...].reshape(tokens, width).astype(f32)
    out_ref[...] = (x + first * gate).astype(bf16).reshape(out_ref.shape)
    cot = c_ref[...].reshape(tokens, width).astype(f32)
    d_first = cot * gate
    d_second = d_first * first * (1.0 - gate)
    d_pre = jnp.concatenate([d_first, d_second], axis=1).astype(bf16)
    dpre_ref[...] = d_pre
    dlb_ref[...] = jnp.sum(d_pre.astype(f32), axis=0, keepdims=True)
    dact_scr[...] = dot(d_pre, w_ref[...], NT)
    for d, o_ref in enumerate((d0, d1, d2, d3)):
        cols = pl.ds(pl.multiple_of((me_ref[0] ^ d) * wide, wide), wide)
        o_ref[...] = (dact_scr[:, cols] * slope_scr[:, cols]).astype(bf16).reshape(o_ref.shape)


def weight_kernel(act_ref, dpre_ref, dw_ref):
    part = dw_ref.shape[-1]
    full = dot(act_ref[...], dpre_ref[...], TN)
    for i in range(dw_ref.shape[0]):
        dw_ref[i] = full[:, i * part : (i + 1) * part].astype(bf16)


def state_grad_kernel(sub, length, w_ref, term_ref, dkh_ref, dvec_ref, dlb_ref, ft_ref, ftl_ref, o_ref,
                      dk_scr, f_scr, dw_scr):
    ndp = o_ref.shape[0]
    n_w, lanes = w_ref.shape
    nstate = n_w // 2
    per = nstate // ndp
    groups = LANES // sub
    height = n_w // groups
    parts, twice, _ = dkh_ref.shape
    block = twice // 2
    sign = signs(block, lanes)
    for p in range(parts):
        re, im = dkh_ref[p, :block], dkh_ref[p, block:]
        if p + 1 < parts:
            re = re + sign * dkh_ref[p + 1, block:]
            im = im - sign * dkh_ref[p + 1, :block]
        dk_scr[p * block : (p + 1) * block] = split3(
            ft_ref, ftl_ref, jnp.concatenate([re, im], axis=0)
        ) * (1.0 / block)
    at8 = iota((8, lanes), 0).astype(f32)

    def one(n, _):
        (fr, fi), w = rows8(term_ref[2, pl.ds(n, 1), :], term_ref[3, pl.ds(n, 1), :])
        pows = powers(*w)
        zero = jnp.zeros((8, lanes), f32)
        s_re, s_im, e_re, e_im, h_re, h_im = (zero,) * 6
        for u in range(DOCMAX // FINE // COARSE - 1, -1, -1):
            t_re, t_im, o_re, o_im = (zero,) * 4
            for v in range(COARSE - 1, 0, -1):
                at = (u * COARSE + v) * FINE
                dk = dk_scr[at : at + FINE]
                t_re = t_re + dk * pows[v][0]
                t_im = t_im + dk * pows[v][1]
                o_re = o_re + t_re
                o_im = o_im + t_im
            t_re = t_re + dk_scr[u * COARSE * FINE : u * COARSE * FINE + FINE]
            e_re, e_im = cmul(e_re, e_im, *pows[COARSE])
            s_re, s_im = cmul(s_re, s_im, *pows[COARSE])
            h_re, h_im = cmul(h_re, h_im, *pows[COARSE])
            e_re, e_im = e_re + s_re, e_im + s_im
            s_re, s_im = s_re + t_re, s_im + t_im
            h_re, h_im = h_re + o_re, h_im + o_im
        m_re = (FINE * COARSE) * e_re + FINE * h_re + at8 * s_re
        m_im = (FINE * COARSE) * e_im + FINE * h_im + at8 * s_im
        s_re, s_im = cmul(s_re, s_im, fr, fi)
        m_re, m_im = cmul(m_re, m_im, fr, fi)
        for slot, value in enumerate((s_re, s_im, m_re, m_im)):
            f_scr[slot, pl.ds(n, 1), :] = jnp.sum(value, axis=0, keepdims=True)
        return 0

    lax.fori_loop(0, nstate, one, 0)
    a, b, z_re, z_im, one_re, one_im, far_re, far_im, den_re, den_im, inv, g_re, g_im = (
        term_ref[slot] for slot in range(TERMS)
    )
    f0, f1 = (f_scr[0], f_scr[1]), (f_scr[2], f_scr[3])
    gf_re, gf_im = cmul(g_re, g_im, *f0)
    dw_scr[0:nstate] = gf_re
    dw_scr[nstate:] = -gf_im
    inv_one = 1.0 / (one_re * one_re + one_im * one_im)
    near_re, near_im = cmul(z_re, z_im, one_re * inv_one, -one_im * inv_one)
    far_re, far_im = cmul(far_re, far_im, den_re * inv, -den_im * inv)
    q_re, q_im = cmul(length * far_re - near_re, length * far_im - near_im, *f0)
    c_re, c_im = cmul(w_ref[0:nstate], w_ref[nstate:], g_re, g_im)
    y_re, y_im = cmul(c_re, c_im, q_re + f1[0], q_im + f1[1])
    by_a = a * y_re
    by_step = by_a - b * y_im
    step = jnp.exp(dvec_ref[2:3])
    by_imag = -step * y_im
    d_step = jnp.sum(by_step, axis=0, keepdims=True)
    lane, state = iota((nstate, lanes), 1), iota((nstate, lanes), 0)
    col_a = jnp.sum(by_a, axis=1, keepdims=True)
    col_b = jnp.sum(by_imag, axis=1, keepdims=True)
    grid = jnp.where(lane == state % per, col_a, jnp.where(lane == state % per + per, col_b, 0.0))
    rates = exact_dot((iota((ndp, nstate), 0) == iota((ndp, nstate), 1) // per).astype(f32), grid)
    vecs = (d_step, dk_scr[0:1], dvec_ref[0:1], dvec_ref[1:2])
    group = iota((1, LANES), 1) // sub
    cols = dlb_ref.shape[1] // ndp
    for i in range(ndp):
        main = jnp.zeros((height, LANES), f32)
        row = jnp.zeros((1, LANES), f32)
        for u in range(groups):
            main = jnp.where(group == u, moved(dw_scr[u * height : (u + 1) * height], (u - i) * sub), main)
            if u < 4:
                row = jnp.where(group == u, moved(jnp.broadcast_to(vecs[u], (8, LANES)), (u - i) * sub)[0:1], row)
        o_ref[i] = jnp.zeros(o_ref.shape[1:], f32)
        o_ref[i, 0:height] = main
        o_ref[i, height : height + 1] = row
        o_ref[i, height + 1 : height + 2] = rates[i : i + 1]
        o_ref[i, height + 2 : height + 3, 0:cols] = dlb_ref[:, i * cols : (i + 1) * cols]


def sum_kernel(x_ref, o_ref):
    total = x_ref[0].astype(f32)
    for i in range(1, x_ref.shape[0]):
        total = total + x_ref[i].astype(f32)
    o_ref[...] = total


def last_kernel(sub, me_ref, m0, m1, m2, m3, w0, w1, w2, w3, w_ref, step_ref, skip_ref, gain_ref, bias_ref,
                lam_ref, imag_ref, lb_ref, dw_ref):
    n_w, own = w_ref.shape
    groups = LANES // sub
    height = n_w // groups
    per, cols = lam_ref.shape[1], lb_ref.shape[1]
    group = iota((1, LANES), 1) // sub
    parts = (m0, m1, m2, m3)
    for u in range(groups):
        acc = jnp.zeros(m0.shape, f32)
        for d, m_ref in enumerate(parts):
            c = me_ref[0] ^ d
            acc = jnp.where(group == c, pltpu.roll(m_ref[...], (c - u) * sub + LANES, 1), acc)
        w_ref[u * height : (u + 1) * height] = acc[0:height, 0:own]
        if u < 4:
            (step_ref, skip_ref, gain_ref, bias_ref)[u][...] = acc[height : height + 1, 0:own]
    total = m0[...] + m1[...] + m2[...] + m3[...]
    lam_ref[...] = total[height + 1 : height + 2, 0:per]
    imag_ref[...] = pltpu.roll(total, LANES - per, 1)[height + 1 : height + 2, 0:per]
    lb_ref[...] = total[height + 2 : height + 3, 0:cols]
    nseq = len(parts)
    width = w0.shape[0]
    span = width // nseq
    for c in range(nseq):
        rows = slice(c * span, (c + 1) * span)
        whole = w0[rows].astype(f32) + w1[rows].astype(f32) + w2[rows].astype(f32) + w3[rows].astype(f32)
        for i in range(span // sub):
            at = (i * nseq + c) * sub
            dw_ref[at : at + sub] = whole[i * sub : (i + 1) * sub]


def trade(parts, axis):
    n = len(parts)
    return [parts[0]] + [lax.ppermute(parts[d], axis, [(i, i ^ d) for i in range(n)]) for d in range(1, n)]


def after(values, first):
    tied = lax.optimization_barrier((tuple(values), first))
    return list(tied[0])


def on_device(block_in, cotangent, ln_gain, ln_bias, lambda_log, lambda_imag, dss_weight, log_step, skip_gain,
              lin_weight, lin_bias, doc_lengths):
    ndp, nseq = lax.axis_size("dp"), lax.axis_size("seq")
    count, block, width = block_in.shape
    length = block * nseq
    own = ln_gain.shape[0]
    sub = own // nseq
    wide = width // nseq
    per = lambda_log.shape[0]
    nstate = per * ndp
    n_w = 2 * nstate
    cols = lin_weight.shape[1]
    tokens = count * block
    me = jnp.reshape(lax.axis_index("seq"), (1,)).astype(i32)
    perm = np.zeros((width, width), np.float32)
    perm[channel_order(width, ndp, nseq), np.arange(width)] = 1.0
    perm = jnp.asarray(perm, bf16)
    f_hi, f_lo, ft_hi, ft_lo = (jnp.asarray(t) for t in dft_tables(block))
    rows = -(-(n_w * sub // LANES + 3) // 8) * 8

    def row(v):
        return v.reshape(1, -1)

    packed = call(partial(pack_kernel, sub), shape((ndp, rows, LANES)), [SM] + [VM] * 8, name="pack")(
        me, dss_weight.reshape(n_w, own), row(log_step), row(skip_gain), row(ln_gain), row(ln_bias),
        row(lambda_log), row(lambda_imag), row(lin_bias)
    )
    shared = lax.all_to_all(packed, "dp", 0, 0, tiled=True)

    piece, piece32 = shape((count, block, wide), bf16), shape((count, block, wide))
    hats = call(ln_kernel, [piece32] * nseq, [SM, VM, VM], name="layer_norm")(me, block_in, perm)
    hats = trade(hats, "seq")

    (lin_late,) = after([lin_weight], shared[0, 0, 0])
    w_lin = lax.all_to_all(jnp.broadcast_to(lin_late[None], (ndp, width, cols)), "dp", 0, 0, tiled=True)
    w_lin = w_lin.reshape(ndp, ndp, nseq, sub, cols).transpose(2, 1, 3, 0, 4).reshape(width, 2 * width)
    bias_full = shared[:, n_w * sub // LANES + 2, :cols].reshape(1, 2 * width)

    spec = (nseq, 2 * block, wide)
    kh, w_all, vec, terms = call(
        partial(lag_kernel, sub, length), [shape(spec), shape((n_w, wide)), shape((8, wide)), shape((TERMS, nstate, wide))],
        [VM] * 3, scratch=[pltpu.VMEM((length, wide), f32), pltpu.VMEM((2, nstate, wide), f32), pltpu.VMEM(spec, f32)],
        name="lag_kernel",
    )(shared, f_hi, f_lo)

    blocks4 = (count, nseq, block, wide)
    sides = (count * nseq, 2 * block, 2 * wide)
    out = call(
        conv_kernel, [piece] * nseq + [shape(sides)], [SM, SM] + [VM] * (nseq + 6),
        scratch=[pltpu.VMEM(blocks4, f32), pltpu.VMEM(sides[1:], f32), pltpu.VMEM(blocks4, f32)],
        name="doc_conv", mib=16,
    )(me, doc_lengths, *hats, vec, kh, f_hi, f_lo, ft_hi, ft_lo)
    convs, spectra_u = trade(out[:nseq], "seq"), out[nseq]

    out = call(
        dense_kernel,
        [shape((count, block, width), bf16), shape((tokens, width), bf16), shape((tokens, 2 * width), bf16),
         shape((1, 2 * width))] + [piece] * nseq,
        [SM] + [VM] * (nseq + 4),
        scratch=[pltpu.VMEM((tokens, width), f32), pltpu.VMEM((tokens, width), f32)],
        name="gated_linear", mib=20,
    )(me, *convs, block_in, cotangent, w_lin, bias_full)
    block_out, act, d_pre, d_lin_bias = out[:4]
    d_convs = trade(out[4:], "seq")

    dw_parts = call(weight_kernel, shape((ndp, width, cols), bf16), [VM, VM], name="weight_grad")(act, d_pre)
    dw_parts = lax.all_to_all(dw_parts, "dp", 0, 0, tiled=True)

    out = call(
        back_kernel, [piece] * nseq + [shape(spec), shape((2, wide))],
        [SM, SM] + [VM] * (2 * nseq + 7),
        scratch=[pltpu.VMEM(blocks4, f32), pltpu.VMEM(sides, f32), pltpu.VMEM(sides[1:], f32), pltpu.VMEM(blocks4, f32)],
        name="doc_conv_grad", mib=24,
    )(me, doc_lengths, *hats, *d_convs, spectra_u, vec, kh, f_hi, f_lo, ft_hi, ft_lo)
    g_own, dkh, d_norm = out[:nseq], out[nseq], out[nseq + 1]
    gs = trade(g_own, "seq")

    small = call(
        partial(state_grad_kernel, sub, length), shape((ndp, rows, LANES)), [VM] * 7,
        scratch=[pltpu.VMEM((length, wide), f32), pltpu.VMEM((4, nstate, wide), f32), pltpu.VMEM((n_w, wide), f32)],
        name="state_grad",
    )(w_all, terms, dkh, jnp.concatenate([d_norm, vec[0:1]], axis=0), d_lin_bias, ft_hi, ft_lo)
    small, dw_parts = lax.optimization_barrier((small, dw_parts))
    small = lax.all_to_all(small, "dp", 0, 0, tiled=True)

    grad_in = call(
        ln_back_kernel, shape((count, block, width), bf16), [SM] + [VM] * (nseq + 3), name="layer_norm_grad", mib=12,
    )(me, *gs, block_in, cotangent, perm)

    dw_own = call(sum_kernel, shape((width, cols)), [VM], name="weight_sum")(dw_parts)
    dws = trade([dw_own] * nseq, "seq")
    small = call(sum_kernel, shape((rows, LANES)), [VM], name="small_sum")(small)
    smalls = trade([small] * nseq, "seq")
    d_w, d_step, d_skip, d_gain, d_bias, d_lam, d_imag, d_lb, dw = call(
        partial(last_kernel, sub),
        [shape((n_w, own))] + [shape((1, own))] * 4 + [shape((1, per))] * 2 + [shape((1, cols)), shape((width, cols))],
        [SM] + [VM] * (2 * nseq), name="last",
    )(me, *smalls, *dws)
    return (
        block_out, grad_in, d_gain.reshape(own), d_bias.reshape(own), d_lam.reshape(per), d_imag.reshape(per),
        d_w.reshape(2, nstate, own), d_step.reshape(own), d_skip.reshape(own), dw, d_lb.reshape(cols),
    )


def solution(mesh):
    placed = (
        P("dp", "seq", None), P("dp", "seq", None), P("dp"), P("dp"), P("dp"), P("dp"),
        P(None, None, "dp"), P("dp"), P("dp"), P(None, "dp"), P("dp"), P("dp", None),
    )
    return jax.shard_map(
        on_device,
        mesh=mesh,
        in_specs=placed,
        out_specs=(
            P("dp", "seq", None), P("dp", "seq", None), P("dp"), P("dp"), P("dp"), P("dp"),
            P(None, None, "dp"), P("dp"), P("dp"), P(None, "dp"), P("dp"),
        ),
        check_vma=False,
    )
```

time: 3120 us -> 150 us (0.05)
  other arithmetic: 2500 us -> 0.01 us
  local copies, waits for them, and re-layouts: 270 us -> 30 us
  blocking collectives: 208 us -> 0 us
  loops' own time: 57.7 us -> 0 us
  Pallas kernels: 0 us -> 52.9 us
  starting transfers between devices: 0.16 us -> 33.7 us
    dot_general x64 -> x0, other arithmetic: 1020 us -> none  [the longest x32 642 us: carried_value(): jnp.einsum('tnh,mnh->mth', carry_im, state_im, precision=highest)]
    mul x57 -> x0, other arithmetic: 580 us -> none  [the longest x24 551 us: power_pair(): return (magnitude * jnp.cos(phase_val), magnitude * jnp.sin(phase_val))]
    add_any x74 -> x0, other arithmetic: 292 us -> none  [the longest x40 197 us: local_pass(): lax.scan(jax.checkpoint(local_advance), (zero_state, zero_state), (u_bloc...]
    add x23 -> x0, other arithmetic: 272 us -> none  [the longest x8 267 us: make_tables(): carry_im = coef_re * next_im + coef_im * next_re]
    reduce_sum x14 -> x0, other arithmetic: 166 us -> none  [the longest x1 121 us: power_pair(): phase_val = exponent * imag_rate]
    all_gather x14 -> x0, blocking collectives: 137 us -> none  [the longest x12 89 us: entering(): everything = jax.tree.map(lambda part: lax.all_gather(part, axis), x)]
    while x312 -> x0, local copies, waits for them, and re-layouts: 93.6 us -> none
    squeeze x88 -> x0, local copies, waits for them, and re-layouts: 83.1 us -> none  [local_pass(): lax.scan(jax.checkpoint(local_advance), (zero_state, zero_state), (u_bloc...]
  transfers between devices with their start and end apart: 4 -> 22, of which waited for: 2 -> 9; matrix products, arithmetic and copies ran while one was open for 86% -> 2% of each run, Pallas kernels for 0% -> 32%
where the time goes in v1:
time: 150 us; the launch traced here: 147 us
  Pallas kernels  52.9 us (35%)
  starting transfers between devices  33.7 us (22%)
  local copies, waits for them, and re-layouts  30 us (20%)
  waiting for transfers between devices  29.9 us (20%)
    unnamed x89, local copies, waits for them, and re-layouts  25.5 us
    ppermute x18, waiting for transfers between devices, trade(): lax.ppermute(parts[d], axis, [(i, i ^ d) for i in range(n)])  16.1 us
    pallas_call x1, Pallas kernels, on_device(): call(back_kernel, [piece] * nseq + [shape(spec), shape((2, wide))], [SM,...  13.7 us
    pallas_call x1, Pallas kernels, on_device(): call(conv_kernel, [piece] * nseq + [shape(sides)], [SM, SM] + [VM] * (nse...  12.4 us
    ppermute x18, starting transfers between devices, trade(): lax.ppermute(parts[d], axis, [(i, i ^ d) for i in range(n)])  12.2 us
    pallas_call x1, Pallas kernels, on_device(): call(partial(state_grad_kernel, sub, length), shape((ndp, rows, LANES)),...  10.8 us
    all_to_all x1, starting transfers between devices, on_device(): shared = lax.all_to_all(packed, 'dp', 0, 0, tiled=True)  7.28 us
    all_to_all x1, waiting for transfers between devices, on_device(): shared = lax.all_to_all(packed, 'dp', 0, 0, tiled=True)  7.12 us
  transfers between devices with their start and end apart: 22, of which 9 were waited for; matrix products, arithmetic and copies ran while one was open for 2% of the time, Pallas kernels for 32%

profile of v1, /device:TPU:0, one launch (start us, length us, event | category | flops | bytes accessed | tf_op | source)
XLA Modules:
  0.0 147.4 jit_solution(4915720090105450724)
XLA Ops:
  0.7 0.9 copy-done.30
  1.6 0.7 copy-done.32
  6.2 0.9 pack.1
  7.1 7.3 %all-to-all-start = ((f32[8,24,128]{2,1,0:T(8,128)}), f32[8,24,128]{2,1,0:T(8,128)S(1)}, u32[]{:S(2)}, u32[]{:S(2)}) async-start(f32[8,24,128]{2,1,0:T(8,128)} %pack.1), calls=%async_computation | async-start | bytes 196608 | tf_op jit(solution)/shard_map/all_to_all | solution.py:642
  14.4 7.1 %all-to-all-done.shared_ref = f32[8,24,128]{2,1,0:T(8,128)S(1)} async-done(((f32[8,24,128]{2,1,0:T(8,128)}), f32[8,24,128]{2,1,0:T(8,128)S(1)}, u32[]{:S(2)}, u32[]{:S(2)}) %all-to-all-start) | async-done | bytes 98336 | tf_op jit(solution)/shard_map/all_to_all | solution.py:642
  21.5 2.0 %broadcast_in_dim.2 = bf16[8,512,128]{2,1,0:T(8,128)(2,1)} broadcast(bf16[512,128]{1,0:T(8,128)(2,1)} %param.26), dimensions={1,2} | broadcast | bytes 1179648 | tf_op jit(solution)/shard_map/broadcast_in_dim | solution.py:649
  23.6 4.2 %all-to-all-start.1 = ((bf16[8,512,128]{2,1,0:T(8,128)(2,1)}), bf16[8,512,128]{2,1,0:T(8,128)(2,1)}, u32[]{:S(2)}, u32[]{:S(2)}) async-start(bf16[8,512,128]{2,1,0:T(8,128)(2,1)} %broadcast_in_dim.2), calls=%async_computation.1 | async-start | bytes 2097152 | tf_op jit(solution)/shard_map/all_to_all | solution.py:649
  27.8 1.0 copy-done
  28.9 1.0 copy-done.12
  29.9 1.5 %layer_norm.1 = (f32[2,256,128]{2,1,0:T(8,128)S(1)}, f32[2,256,128]{2,1,0:T(8,128)S(1)}, f32[2,256,128]{2,1,0:T(8,128)S(1)}, f32[2,256,128]{2,1,0:T(8,128)S(1)}) custom-call(s32[1]{0:T(128)} %bitcast.me_ref, bf16[2,256,512]{2,1,0:T(8,128)(2,1)S(1)} %copy-done, bf16[512,512]{1,0:T(8,128)(2,1)S(1)} %copy-done.12), custom_call_target="tpu_custom_call" | custom-call | flops 1000 | bytes 1000 | tf_op jit(solution)/shard_map/layer_norm/pallas_call | solution.py:645
  31.5 1.6 %collective-permute-start.1 = (f32[2,256,128]{2,1,0:T(8,128)S(1)}, f32[2,256,128]{2,1,0:T(8,128)S(1)}, u32[]{:S(2)}, u32[]{:S(2)}) collective-permute-start(f32[2,256,128]{2,1,0:T(8,128)S(1)} %get-tuple-element.51), channel_id=1, source_target_pairs={{0,2},{1,3},{2,0},{3,1},{4,6},{5,7},{6,4},{7,5},{8,10},{9,11},{10,... | collective-permute-start | bytes 786440 | tf_op jit(solution)/shard_map/ppermute | solution.py:607
  33.4 6.3 %lag_kernel.1 = (f32[4,512,128]{2,1,0:T(8,128)S(1)}, f32[128,128]{1,0:T(8,128)S(1)}, f32[8,128]{1,0:T(8,128)S(1)}, f32[13,64,128]{2,1,0:T(8,128)S(1)}) custom-call(f32[8,24,128]{2,1,0:T(8,128)S(1)} %all-to-all-done.shared_ref, bf16[512,256]{1,0:T(8,128)(2,1)S(1)} %copy-done.7, bf16[512,256]{1,0:T(8,128)(2,1)S(1)} %copy-done.8), custom_call_target="tpu_custom_call" | custom-call | flops 1000 | bytes 1000 | tf_op jit(solution)/shard_map/lag_kernel/pallas_call | solution.py:654
  39.7 0.7 copy-done.22
  41.1 4.3 %collective-permute-done.2.x3 = f32[2,256,128]{2,1,0:T(8,128)S(1)} collective-permute-done((f32[2,256,128]{2,1,0:T(8,128)S(1)}, f32[2,256,128]{2,1,0:T(8,128)S(1)}, u32[]{:S(2)}, u32[]{:S(2)}) %collective-permute-start.2) | collective-permute-done | bytes 262176 | tf_op jit(solution)/shard_map/ppermute | solution.py:607
  45.4 12.4 %doc_conv.1 = (bf16[2,256,128]{2,1,0:T(8,128)(2,1)S(1)}, bf16[2,256,128]{2,1,0:T(8,128)(2,1)}, bf16[2,256,128]{2,1,0:T(8,128)(2,1)}, bf16[2,256,128]{2,1,0:T(8,128)(2,1)}, f32[8,512,256]{2,1,0:T(8,128)S(1)}) custom-call(s32[1]{0:T(128)} %bitcast.me_ref, s32[2,4]{1,0:T(2,128)S(1)} %copy-done.31, f32[2,256,128]{2,1,0:T(8,128)S(1)} %get-tuple-element.49.x0, ...), custom_call_target="tpu_custom_call" | custom-call | flops 1000 | bytes 1000 | tf_op jit(solution)/shard_map/doc_conv/pallas_call | solution.py:662
  57.9 2.0 %copy-done.3 = f32[8,512,256]{2,1,0:T(8,128)} copy-done((f32[8,512,256]{2,1,0:T(8,128)}, f32[8,512,256]{2,1,0:T(8,128)S(1)}, u32[]{:S(2)}) %copy-start.3) | copy-done | bytes 4194328
  60.5 0.7 collective-permute-start.3
  61.2 1.5 %collective-permute-start.4 = (bf16[2,256,128]{2,1,0:T(8,128)(2,1)}, bf16[2,256,128]{2,1,0:T(8,128)(2,1)}, u32[]{:S(2)}, u32[]{:S(2)}) collective-permute-start(bf16[2,256,128]{2,1,0:T(8,128)(2,1)} %get-tuple-element.57), channel_id=1, source_target_pairs={{0,2},{1,3},{2,0},{3,1},{4,6},{5,7},{6,4},{7,5},{8,10},{9,11},{10,... | collective-permute-start | bytes 393224 | tf_op jit(solution)/shard_map/ppermute | solution.py:607
  62.7 2.4 %copy.28 = bf16[4,8,16,8,128]{4,3,2,1,0:T(8,128)(2,1)S(1)} copy(bf16[4,8,16,8,128]{4,2,0,1,3:T(8,128)(2,1)} %bitcast.10) | data formatting | bytes 2097152 | tf_op jit(solution)/shard_map/transpose | solution.py:650
  65.4 2.4 %collective-permute-done.4.q2 = bf16[2,256,128]{2,1,0:T(8,128)(2,1)} collective-permute-done((bf16[2,256,128]{2,1,0:T(8,128)(2,1)}, bf16[2,256,128]{2,1,0:T(8,128)(2,1)}, u32[]{:S(2)}, u32[]{:S(2)}) %collective-permute-start.4) | collective-permute-done | bytes 131104 | tf_op jit(solution)/shard_map/ppermute | solution.py:607
  67.8 1.0 collective-permute-done.5.q3
  68.9 3.8 %gated_linear.1 = (bf16[2,256,512]{2,1,0:T(8,128)(2,1)}, bf16[512,512]{1,0:T(8,128)(2,1)S(1)}, bf16[512,1024]{1,0:T(8,128)(2,1)S(1)}, f32[1,1024]{1,0:T(1,128)S(...) custom-call(s32[1]{0:T(128)} %bitcast.me_ref, ...), custom_call_target="tpu_custom_call" | custom-call | flops 1000 | bytes 1000 | tf_op jit(solution)/shard_map/gated_linear/pallas_call | solution.py:669
  73.5 0.7 weight_grad.1
  74.2 1.0 copy-done.2
  75.2 4.8 %all-to-all-start.2 = ((bf16[8,512,128]{2,1,0:T(8,128)(2,1)}), bf16[8,512,128]{2,1,0:T(8,128)(2,1)S(1)}, u32[]{:S(2)}, u32[]{:S(2)}) async-start(bf16[8,512,128]{2,1,0:T(8,128)(2,1)} %copy-done.2), calls=%async_computation.2 | async-start | bytes 2097152 | tf_op jit(solution)/shard_map/all_to_all | solution.py:681
  80.4 1.5 %collective-permute-start.7 = (bf16[2,256,128]{2,1,0:T(8,128)(2,1)}, bf16[2,256,128]{2,1,0:T(8,128)(2,1)S(1)}, u32[]{:S(2)}, u32[]{:S(2)}) collective-permute-start(bf16[2,256,128]{2,1,0:T(8,128)(2,1)} %copy-done.42), channel_id=1, source_target_pairs={{0,2},{1,3},{2,0},{3,1},{4,6},{5,7},{6,4},{7,5},{8,10},{9,11},{10,... | collective-permute-start | bytes 393224 | tf_op jit(solution)/shard_map/ppermute | solution.py:607
  81.9 5.1 %collective-permute-done.7.c2 = bf16[2,256,128]{2,1,0:T(8,128)(2,1)S(1)} collective-permute-done((bf16[2,256,128]{2,1,0:T(8,128)(2,1)}, bf16[2,256,128]{2,1,0:T(8,128)(2,1)S(1)}, u32[]{:S(2)}, u32[]{:S(2)}) %collective-permute-start.7) | collective-permute-done | bytes 131104 | tf_op jit(solution)/shard_map/ppermute | solution.py:607
  87.0 1.1 collective-permute-done.8.c3
  88.1 2.2 %copy-done.4 = f32[8,512,256]{2,1,0:T(8,128)S(1)} copy-done((f32[8,512,256]{2,1,0:T(8,128)S(1)}, f32[8,512,256]{2,1,0:T(8,128)}, u32[]{:S(2)}) %copy-start.4) | copy-done | bytes 4194328
  90.3 0.9 copy-done.9
  91.2 0.9 copy-done.15
  92.2 0.9 copy-done.17
  93.1 0.9 copy-done.19
  94.1 0.9 copy-done.21
  95.0 13.7 %doc_conv_grad.1 = (bf16[2,256,128]{2,1,0:T(8,128)(2,1)S(1)}, bf16[2,256,128]{2,1,0:T(8,128)(2,1)S(1)}, bf16[2,256,128]{2,1,0:T(8,128)(2,1)}, bf16[2,256,128]{2,...) custom-call(s32[1]{0:T(128)} %bitcast.me_ref, s32[2,4]{1,0:T(2,128)S(1)} %copy-done.31, ...), custom_call_target="tpu_custom_call" | custom-call | flops 1000 | bytes 1000 | tf_op jit(solution)/shard_map/doc_conv_grad/pallas_call | solution.py:683
  110.6 1.4 collective-permute-start.10
  112.1 10.8 %state_grad.1 = f32[8,24,128]{2,1,0:T(8,128)} custom-call(f32[128,128]{1,0:T(8,128)S(1)} %copy-done.29, f32[13,64,128]{2,1,0:T(8,128)S(1)} %copy-done.23, f32[4,512,128]{2,1,0:T(8,128)S(1)} %get-tuple-element.71.dkh_ref, f32[3,128]{1,0:T(4,128)S(1)} %pad_maximum_fusion.dvec_ref, f32[1,1024]{1,0:T(1,128)S(1)} %get-tuple-element.73.dlb_ref, ...), custom_call_target="tpu_custom_call" | custom-call | flops 1000 | bytes 1000 | tf_op jit(solution)/shard_map/state_grad/pallas_call | solution.py:692
  123.0 0.8 collective-permute-start.15
  124.4 0.9 collective-permute-start.17
  125.2 5.2 %all-to-all-start.3 = ((f32[8,24,128]{2,1,0:T(8,128)}), f32[8,24,128]{2,1,0:T(8,128)S(1)}, u32[]{:S(2)}, u32[]{:S(2)}) async-start(f32[8,24,128]{2,1,0:T(8,128)} %state_grad.1), calls=%async_computation.3 | async-start | bytes 196608 | tf_op jit(solution)/shard_map/all_to_all | solution.py:698
  131.1 6.6 %all-to-all-done.3.x_ref = f32[8,24,128]{2,1,0:T(8,128)S(1)} async-done(((f32[8,24,128]{2,1,0:T(8,128)}), f32[8,24,128]{2,1,0:T(8,128)S(1)}, u32[]{:S(2)}, u32[]{:S(2)}) %all-to-all-start.3) | async-done | bytes 98336 | tf_op jit(solution)/shard_map/all_to_all | solution.py:698
  137.8 1.9 %collective-permute-done.11.g3 = bf16[2,256,128]{2,1,0:T(8,128)(2,1)S(1)} collective-permute-done((bf16[2,256,128]{2,1,0:T(8,128)(2,1)}, bf16[2,256,128]{2,1,0:T(8,128)(2,1)S(1)}, u32[]{:S(2)}, u32[]{:S(2)}) %collective-permute-start.11) | collective-permute-done | bytes 131104 | tf_op jit(solution)/shard_map/ppermute | solution.py:607
  139.7 0.7 collective-permute-start.12
  141.7 1.0 copy-done.11
  142.8 1.0 copy-done.13
  143.8 0.9 copy-done.25
  144.7 1.8 %layer_norm_grad.1 = bf16[2,256,512]{2,1,0:T(8,128)(2,1)} custom-call(s32[1]{0:T(128)} %bitcast.me_ref, bf16[2,256,128]{2,1,0:T(8,128)(2,1)S(1)} %copy-done.25, bf16[2,256,128]{2,1,0:T(8,128)(2,1)S(1)} %collective-permute-done.9.g1, bf16[2,256,128]{2,1,0:T(8,128)(2,1)S(1)} %collective-permute-done.10.g2, ...), custom_call_target="tpu_custom_call" | custom-call | flops 1000 | bytes 1000 | tf_op jit(solution)/shard_map/layer_norm_grad/pallas_call | solution.py:700
  146.5 0.9 last.1
  (102 shorter events, 11.9 us)
Async XLA Ops:
  0.6 32.7 %copy-start.7 = (bf16[512,256]{1,0:T(8,128)(2,1)S(1)}, bf16[512,256]{1,0:T(8,128)(2,1)}, u32[]{:S(2)}) copy-start(bf16[512,256]{1,0:T(8,128)(2,1)} %constant.15.clone.f_ref) | copy-start | bytes 786436
  0.7 32.7 %copy-start.8 = (bf16[512,256]{1,0:T(8,128)(2,1)S(1)}, bf16[512,256]{1,0:T(8,128)(2,1)}, u32[]{:S(2)}) copy-start(bf16[512,256]{1,0:T(8,128)(2,1)} %constant.16.clone.fl_ref) | copy-start | bytes 786436
  0.7 44.7 %copy-start.5 = (bf16[256,512]{1,0:T(8,128)(2,1)S(1)}, bf16[256,512]{1,0:T(8,128)(2,1)}, u32[]{:S(2)}) copy-start(bf16[256,512]{1,0:T(8,128)(2,1)} %constant.17.clone.ft_ref) | copy-start | bytes 786436
  0.7 44.7 %copy-start.6 = (bf16[256,512]{1,0:T(8,128)(2,1)S(1)}, bf16[256,512]{1,0:T(8,128)(2,1)}, u32[]{:S(2)}) copy-start(bf16[256,512]{1,0:T(8,128)(2,1)} %constant.18.clone.ftl_ref) | copy-start | bytes 786436
  6.2 39.2 %copy-start.31 = (s32[2,4]{1,0:T(2,128)S(1)}, s32[2,4]{1,0:T(2,128)}, u32[]{:S(2)}) copy-start(s32[2,4]{1,0:T(2,128)} %len_ref.3) | copy-start | bytes 100
  7.1 14.4 %all-to-all-start = ((f32[8,24,128]{2,1,0:T(8,128)}), f32[8,24,128]{2,1,0:T(8,128)S(1)}, u32[]{:S(2)}, u32[]{:S(2)}) async-start(f32[8,24,128]{2,1,0:T(8,128)} %pack.1), calls=%async_computation | async-start | bytes 196608 | tf_op jit(solution)/shard_map/all_to_all | solution.py:642
  23.6 39.1 %all-to-all-start.1 = ((bf16[8,512,128]{2,1,0:T(8,128)(2,1)}), bf16[8,512,128]{2,1,0:T(8,128)(2,1)}, u32[]{:S(2)}, u32[]{:S(2)}) async-start(bf16[8,512,128]{2,1,0:T(8,128)(2,1)} %broadcast_in_dim.2), calls=%async_computation.1 | async-start | bytes 2097152 | tf_op jit(solution)/shard_map/all_to_all | solution.py:649
  27.8 1.0 copy-start
  28.9 1.0 copy-start.12
  31.4 41.3 %copy-start.14 = (f32[2,256,128]{2,1,0:T(8,128)}, f32[2,256,128]{2,1,0:T(8,128)S(1)}, u32[]{:S(2)}) copy-start(f32[2,256,128]{2,1,0:T(8,128)S(1)} %get-tuple-element.49.x0) | copy-start | bytes 786436
  31.4 37.5 %copy-start.1 = (bf16[2,256,512]{2,1,0:T(8,128)(2,1)S(1)}, bf16[2,256,512]{2,1,0:T(8,128)(2,1)}, u32[]{:S(2)}) copy-start(bf16[2,256,512]{2,1,0:T(8,128)(2,1)} %x_ref.5) | copy-start | bytes 1572868
  31.4 37.5 %copy-start.10 = (bf16[2,256,512]{2,1,0:T(8,128)(2,1)S(1)}, bf16[2,256,512]{2,1,0:T(8,128)(2,1)}, u32[]{:S(2)}) copy-start(bf16[2,256,512]{2,1,0:T(8,128)(2,1)} %c_ref.3) | copy-start | bytes 1572868
  31.4 9.6 %collective-permute-start = (f32[2,256,128]{2,1,0:T(8,128)S(1)}, f32[2,256,128]{2,1,0:T(8,128)S(1)}, u32[]{:S(2)}, u32[]{:S(2)}) collective-permute-start(f32[2,256,128]{2,1,0:T(8,128)S(1)} %get-tuple-element.50), channel_id=1, source_target_pairs={{0,1},{1,0},{2,3},{3,2},{4,5},{5,4},{6,7},{7,6},{8,9},{9,8},{10,11... | collective-permute-start | bytes 786440 | tf_op jit(solution)/shard_map/ppermute | solution.py:607
  31.5 9.5 %collective-permute-start.1 = (f32[2,256,128]{2,1,0:T(8,128)S(1)}, f32[2,256,128]{2,1,0:T(8,128)S(1)}, u32[]{:S(2)}, u32[]{:S(2)}) collective-permute-start(f32[2,256,128]{2,1,0:T(8,128)S(1)} %get-tuple-element.51), channel_id=1, source_target_pairs={{0,2},{1,3},{2,0},{3,1},{4,6},{5,7},{6,4},{7,5},{8,10},{9,11},{10,... | collective-permute-start | bytes 786440 | tf_op jit(solution)/shard_map/ppermute | solution.py:607
  33.1 12.3 %collective-permute-start.2 = (f32[2,256,128]{2,1,0:T(8,128)S(1)}, f32[2,256,128]{2,1,0:T(8,128)S(1)}, u32[]{:S(2)}, u32[]{:S(2)}) collective-permute-start(f32[2,256,128]{2,1,0:T(8,128)S(1)} %get-tuple-element.52), channel_id=1, source_target_pairs={{0,3},{1,2},{2,1},{3,0},{4,7},{5,6},{6,5},{7,4},{8,11},{9,10},{10,... | collective-permute-start | bytes 786440 | tf_op jit(solution)/shard_map/ppermute | solution.py:607
  41.0 16.8 %copy-start.16 = (f32[2,256,128]{2,1,0:T(8,128)}, f32[2,256,128]{2,1,0:T(8,128)S(1)}, u32[]{:S(2)}) copy-start(f32[2,256,128]{2,1,0:T(8,128)S(1)} %collective-permute-done.x1) | copy-start | bytes 786436
  41.1 19.4 %copy-start.18 = (f32[2,256,128]{2,1,0:T(8,128)}, f32[2,256,128]{2,1,0:T(8,128)S(1)}, u32[]{:S(2)}) copy-start(f32[2,256,128]{2,1,0:T(8,128)S(1)} %collective-permute-done.1.x2) | copy-start | bytes 786436
  45.4 15.8 %copy-start.20 = (f32[2,256,128]{2,1,0:T(8,128)}, f32[2,256,128]{2,1,0:T(8,128)S(1)}, u32[]{:S(2)}) copy-start(f32[2,256,128]{2,1,0:T(8,128)S(1)} %collective-permute-done.2.x3) | copy-start | bytes 786436
  57.9 2.0 %copy-start.3 = (f32[8,512,256]{2,1,0:T(8,128)}, f32[8,512,256]{2,1,0:T(8,128)S(1)}, u32[]{:S(2)}) copy-start(f32[8,512,256]{2,1,0:T(8,128)S(1)} %get-tuple-element.64.s_ref) | copy-start | bytes 12582916
  60.5 8.4 %copy-start.27 = (bf16[2,256,128]{2,1,0:T(8,128)(2,1)S(1)}, bf16[2,256,128]{2,1,0:T(8,128)(2,1)}, u32[]{:S(2)}) copy-start(bf16[2,256,128]{2,1,0:T(8,128)(2,1)} %copy-done.26) | copy-start | bytes 393220
  60.5 4.9 %collective-permute-start.3 = (bf16[2,256,128]{2,1,0:T(8,128)(2,1)}, bf16[2,256,128]{2,1,0:T(8,128)(2,1)S(1)}, u32[]{:S(2)}, u32[]{:S(2)}) collective-permute-start(bf16[2,256,128]{2,1,0:T(8,128)(2,1)} %get-tuple-element.56), channel_id=1, source_target_pairs={{0,1},{1,0},{2,3},{3,2},{4,5},{5,4},{6,7},{7,6},{8,9},{9,8},{10,11... | collective-permute-start | bytes 393224 | tf_op jit(solution)/shard_map/ppermute | solution.py:607
  61.2 6.7 %collective-permute-start.4 = (bf16[2,256,128]{2,1,0:T(8,128)(2,1)}, bf16[2,256,128]{2,1,0:T(8,128)(2,1)}, u32[]{:S(2)}, u32[]{:S(2)}) collective-permute-start(bf16[2,256,128]{2,1,0:T(8,128)(2,1)} %get-tuple-element.57), channel_id=1, source_target_pairs={{0,2},{1,3},{2,0},{3,1},{4,6},{5,7},{6,4},{7,5},{8,10},{9,11},{10,... | collective-permute-start | bytes 393224 | tf_op jit(solution)/shard_map/ppermute | solution.py:607
  62.7 6.2 %collective-permute-start.5 = (bf16[2,256,128]{2,1,0:T(8,128)(2,1)}, bf16[2,256,128]{2,1,0:T(8,128)(2,1)}, u32[]{:S(2)}, u32[]{:S(2)}) collective-permute-start(bf16[2,256,128]{2,1,0:T(8,128)(2,1)} %get-tuple-element.58), channel_id=1, source_target_pairs={{0,3},{1,2},{2,1},{3,0},{4,7},{5,6},{6,5},{7,4},{8,11},{9,10},{10,... | collective-permute-start | bytes 393224 | tf_op jit(solution)/shard_map/ppermute | solution.py:607
  74.2 1.0 copy-start.2
  75.2 47.7 %all-to-all-start.2 = ((bf16[8,512,128]{2,1,0:T(8,128)(2,1)}), bf16[8,512,128]{2,1,0:T(8,128)(2,1)S(1)}, u32[]{:S(2)}, u32[]{:S(2)}) async-start(bf16[8,512,128]{2,1,0:T(8,128)(2,1)} %copy-done.2), calls=%async_computation.2 | async-start | bytes 2097152 | tf_op jit(solution)/shard_map/all_to_all | solution.py:681
  80.0 1.9 %collective-permute-start.6 = (bf16[2,256,128]{2,1,0:T(8,128)(2,1)}, bf16[2,256,128]{2,1,0:T(8,128)(2,1)S(1)}, u32[]{:S(2)}, u32[]{:S(2)}) collective-permute-start(bf16[2,256,128]{2,1,0:T(8,128)(2,1)} %copy-done.43), channel_id=1, source_target_pairs={{0,1},{1,0},{2,3},{3,2},{4,5},{5,4},{6,7},{7,6},{8,9},{9,8},{10,11... | collective-permute-start | bytes 393224 | tf_op jit(solution)/shard_map/ppermute | solution.py:607
  80.4 6.6 %collective-permute-start.7 = (bf16[2,256,128]{2,1,0:T(8,128)(2,1)}, bf16[2,256,128]{2,1,0:T(8,128)(2,1)S(1)}, u32[]{:S(2)}, u32[]{:S(2)}) collective-permute-start(bf16[2,256,128]{2,1,0:T(8,128)(2,1)} %copy-done.42), channel_id=1, source_target_pairs={{0,2},{1,3},{2,0},{3,1},{4,6},{5,7},{6,4},{7,5},{8,10},{9,11},{10,... | collective-permute-start | bytes 393224 | tf_op jit(solution)/shard_map/ppermute | solution.py:607
  81.9 6.2 %collective-permute-start.8 = (bf16[2,256,128]{2,1,0:T(8,128)(2,1)}, bf16[2,256,128]{2,1,0:T(8,128)(2,1)S(1)}, u32[]{:S(2)}, u32[]{:S(2)}) collective-permute-start(bf16[2,256,128]{2,1,0:T(8,128)(2,1)} %copy-done.41), channel_id=1, source_target_pairs={{0,3},{1,2},{2,1},{3,0},{4,7},{5,6},{6,5},{7,4},{8,11},{9,10},{10,... | collective-permute-start | bytes 393224 | tf_op jit(solution)/shard_map/ppermute | solution.py:607
  88.1 2.2 %copy-start.4 = (f32[8,512,256]{2,1,0:T(8,128)S(1)}, f32[8,512,256]{2,1,0:T(8,128)}, u32[]{:S(2)}) copy-start(f32[8,512,256]{2,1,0:T(8,128)} %copy-done.3) | copy-start | bytes 12582916
  90.3 0.9 copy-start.9
  91.2 0.9 copy-start.15
  92.2 0.9 copy-start.17
  93.1 0.9 copy-start.19
  94.1 0.9 copy-start.21
  95.0 17.1 %copy-start.23 = (f32[13,64,128]{2,1,0:T(8,128)S(1)}, f32[13,64,128]{2,1,0:T(8,128)}, u32[]{:S(2)}) copy-start(f32[13,64,128]{2,1,0:T(8,128)} %copy-done.22) | copy-start | bytes 1277956
  95.0 17.1 %copy-start.29 = (f32[128,128]{1,0:T(8,128)S(1)}, f32[128,128]{1,0:T(8,128)}, u32[]{:S(2)}) copy-start(f32[128,128]{1,0:T(8,128)} %copy-done.28) | copy-start | bytes 196612
  110.6 20.3 %collective-permute-start.10 = (bf16[2,256,128]{2,1,0:T(8,128)(2,1)}, bf16[2,256,128]{2,1,0:T(8,128)(2,1)S(1)}, u32[]{:S(2)}, u32[]{:S(2)}) collective-permute-start(bf16[2,256,128]{2,1,0:T(8,128)(2,1)} %get-tuple-element.67), channel_id=1, source_target_pairs={{0,2},{1,3},{2,0},{3,1},{4,6},{5,7},{6,4},{7,5},{8,10},{9,11},{10,... | collective-permute-start | bytes 393224 | tf_op jit(solution)/shard_map/ppermute | solution.py:607
  123.0 23.5 %collective-permute-start.15 = (f32[512,128]{1,0:T(8,128)S(1)}, f32[512,128]{1,0:T(8,128)S(1)}, u32[]{:S(2)}, u32[]{:S(2)}) collective-permute-start(f32[512,128]{1,0:T(8,128)S(1)} %weight_sum.1.w0), channel_id=1, source_target_pairs={{0,1},{1,0},{2,3},{3,2},{4,5},{5,4},{6,7},{7,6},{8,9},{9,8},{10,11... | collective-permute-start | bytes 786440 | tf_op jit(solution)/shard_map/ppermute | solution.py:607
  123.8 22.7 %collective-permute-start.16 = (f32[512,128]{1,0:T(8,128)S(1)}, f32[512,128]{1,0:T(8,128)S(1)}, u32[]{:S(2)}, u32[]{:S(2)}) collective-permute-start(f32[512,128]{1,0:T(8,128)S(1)} %weight_sum.1.w0), channel_id=1, source_target_pairs={{0,2},{1,3},{2,0},{3,1},{4,6},{5,7},{6,4},{7,5},{8,10},{9,11},{10,... | collective-permute-start | bytes 786440 | tf_op jit(solution)/shard_map/ppermute | solution.py:607
  124.4 22.2 %collective-permute-start.17 = (f32[512,128]{1,0:T(8,128)S(1)}, f32[512,128]{1,0:T(8,128)S(1)}, u32[]{:S(2)}, u32[]{:S(2)}) collective-permute-start(f32[512,128]{1,0:T(8,128)S(1)} %weight_sum.1.w0), channel_id=1, source_target_pairs={{0,3},{1,2},{2,1},{3,0},{4,7},{5,6},{6,5},{7,4},{8,11},{9,10},{10,... | collective-permute-start | bytes 786440 | tf_op jit(solution)/shard_map/ppermute | solution.py:607
  125.2 12.5 %all-to-all-start.3 = ((f32[8,24,128]{2,1,0:T(8,128)}), f32[8,24,128]{2,1,0:T(8,128)S(1)}, u32[]{:S(2)}, u32[]{:S(2)}) async-start(f32[8,24,128]{2,1,0:T(8,128)} %state_grad.1), calls=%async_computation.3 | async-start | bytes 196608 | tf_op jit(solution)/shard_map/all_to_all | solution.py:698
  130.4 9.3 %collective-permute-start.11 = (bf16[2,256,128]{2,1,0:T(8,128)(2,1)}, bf16[2,256,128]{2,1,0:T(8,128)(2,1)S(1)}, u32[]{:S(2)}, u32[]{:S(2)}) collective-permute-start(bf16[2,256,128]{2,1,0:T(8,128)(2,1)} %copy-done.40), channel_id=1, source_target_pairs={{0,3},{1,2},{2,1},{3,0},{4,7},{5,6},{6,5},{7,4},{8,11},{9,10},{10,... | collective-permute-start | bytes 393224 | tf_op jit(solution)/shard_map/ppermute | solution.py:607
  131.0 9.4 %collective-permute-start.9 = (bf16[2,256,128]{2,1,0:T(8,128)(2,1)}, bf16[2,256,128]{2,1,0:T(8,128)(2,1)S(1)}, u32[]{:S(2)}, u32[]{:S(2)}) collective-permute-start(bf16[2,256,128]{2,1,0:T(8,128)(2,1)} %copy-done.39), channel_id=1, source_target_pairs={{0,1},{1,0},{2,3},{3,2},{4,5},{5,4},{6,7},{7,6},{8,9},{9,8},{10,11... | collective-permute-start | bytes 393224 | tf_op jit(solution)/shard_map/ppermute | solution.py:607
  139.7 1.5 %collective-permute-start.12 = (f32[24,128]{1,0:T(8,128)S(1)}, f32[24,128]{1,0:T(8,128)S(1)}, u32[]{:S(2)}, u32[]{:S(2)}) collective-permute-start(f32[24,128]{1,0:T(8,128)S(1)} %small_sum.1.m0), channel_id=1, source_target_pairs={{0,1},{1,0},{2,3},{3,2},{4,5},{5,4},{6,7},{7,6},{8,9},{9,8},{10,11... | collective-permute-start | bytes 36872 | tf_op jit(solution)/shard_map/ppermute | solution.py:607
  140.4 6.1 %collective-permute-start.13 = (f32[24,128]{1,0:T(8,128)S(1)}, f32[24,128]{1,0:T(8,128)S(1)}, u32[]{:S(2)}, u32[]{:S(2)}) collective-permute-start(f32[24,128]{1,0:T(8,128)S(1)} %small_sum.1.m0), channel_id=1, source_target_pairs={{0,2},{1,3},{2,0},{3,1},{4,6},{5,7},{6,4},{7,5},{8,10},{9,11},{10,... | collective-permute-start | bytes 36872 | tf_op jit(solution)/shard_map/ppermute | solution.py:607
  141.2 5.3 %collective-permute-start.14 = (f32[24,128]{1,0:T(8,128)S(1)}, f32[24,128]{1,0:T(8,128)S(1)}, u32[]{:S(2)}, u32[]{:S(2)}) collective-permute-start(f32[24,128]{1,0:T(8,128)S(1)} %small_sum.1.m0), channel_id=1, source_target_pairs={{0,3},{1,2},{2,1},{3,0},{4,7},{5,6},{6,5},{7,4},{8,11},{9,10},{10,... | collective-permute-start | bytes 36872 | tf_op jit(solution)/shard_map/ppermute | solution.py:607
  141.7 1.0 copy-start.11
  142.8 1.0 copy-start.13
  (18 other events, 12.5 us)

commit v2 on v1

v2 whole, which is shorter than its diff:
```python
from functools import partial

import jax
import jax.numpy as jnp
import numpy as np
from jax import lax
from jax.experimental import pallas as pl
from jax.experimental.pallas import tpu as pltpu
from jax.sharding import PartitionSpec as P

f32, bf16, i32 = jnp.float32, jnp.bfloat16, jnp.int32
ln_eps = 1e-05
DOCMAX = 800
FINE = 8
COARSE = 10
LANES = 128
NN = (((1,), (0,)), ((), ()))
NT = (((1,), (1,)), ((), ()))
TN = (((0,), (0,)), ((), ()))
VM = pl.BlockSpec(memory_space=pltpu.VMEM)
AN = pl.BlockSpec(memory_space=pl.ANY)
DMA = pltpu.SemaphoreType.DMA


def dot(a, b, dims=NN):
    return lax.dot_general(a, b, dims, preferred_element_type=f32)


def exact_dot(a, b, dims=NN):
    return lax.dot_general(a, b, dims, precision=lax.Precision.HIGHEST, preferred_element_type=f32)


def shape(dims, dtype=f32):
    return jax.ShapeDtypeStruct(dims, dtype)


def call(body, out, specs, scratch=(), name=None, mib=8, outs=None, us=0, keep=()):
    inputs, kept = len(specs), len(keep)

    def whole(*refs):
        body(*refs[:inputs], *refs[inputs + kept :])

    kernel = pl.pallas_call(
        whole,
        out_shape=out,
        in_specs=list(specs) + [AN] * kept,
        out_specs=outs if outs is not None else jax.tree.map(lambda _: VM, out),
        scratch_shapes=list(scratch),
        cost_estimate=pl.CostEstimate(flops=int(us * 1.15e9), bytes_accessed=1000, transcendentals=0),
        compiler_params=pltpu.CompilerParams(vmem_limit_bytes=mib * 2**20),
        name=name,
    )
    return lambda *args: kernel(*args, *keep)


def iota(dims, axis):
    return lax.broadcasted_iota(i32, dims, axis)


def cmul(ar, ai, br, bi):
    return ar * br - ai * bi, ar * bi + ai * br


def small_expm1(a):
    poly = jnp.full_like(a, 1.0)
    for k in range(9, 1, -1):
        poly = 1.0 + poly * a * (1.0 / k)
    return jnp.where(jnp.abs(a) < 0.5, a * poly, jnp.exp(a) - 1.0)


def state_terms(rate_log, freq, step_log, length):
    step = jnp.exp(step_log)
    a = -jnp.exp(rate_log) * step
    b = freq * step
    half = jnp.sin(0.5 * b)
    cos_b, sin_b, mag = jnp.cos(b), jnp.sin(b), jnp.exp(a)
    one_re = 2.0 * half * half - small_expm1(a) * cos_b
    one_im = -mag * sin_b
    far = jnp.exp(length * a)
    far_re, far_im = far * jnp.cos(length * b), far * jnp.sin(length * b)
    den_re, den_im = 1.0 - far_re, -far_im
    inv = 1.0 / (den_re * den_re + den_im * den_im)
    g_re = (one_re * den_re + one_im * den_im) * inv
    g_im = (one_im * den_re - one_re * den_im) * inv
    return a, b, mag * cos_b, mag * sin_b, one_re, one_im, far_re, far_im, den_re, den_im, inv, g_re, g_im


TERMS = 13


def rows8(zr, zi):
    dims = (8, zr.shape[-1])
    at = iota(dims, 0)
    r1, i1 = jnp.broadcast_to(zr, dims), jnp.broadcast_to(zi, dims)
    r2, i2 = cmul(r1, i1, r1, i1)
    r4, i4 = cmul(r2, i2, r2, i2)
    p = (jnp.where(at & 1 > 0, r1, 1.0), jnp.where(at & 1 > 0, i1, 0.0))
    p = cmul(*p, jnp.where(at & 2 > 0, r2, 1.0), jnp.where(at & 2 > 0, i2, 0.0))
    p = cmul(*p, jnp.where(at & 4 > 0, r4, 1.0), jnp.where(at & 4 > 0, i4, 0.0))
    return p, cmul(r4, i4, r4, i4)


def powers(wr, wi):
    pows = [None, (wr, wi)]
    for v in range(2, COARSE + 1):
        pows.append(cmul(*pows[v // 2], *pows[v - v // 2]))
    return pows


def halves(x):
    hi = x.astype(bf16)
    return hi, (x - hi.astype(f32)).astype(bf16)


def stack3(ref, cols, x):
    height = x.shape[0]
    hi, lo = halves(x)
    ref[0:height, cols] = hi
    ref[height : 2 * height, cols] = lo
    ref[2 * height : 3 * height, cols] = hi


def signs(block, lanes):
    return jnp.where(iota((block, lanes), 0) & 1 > 0, -1.0, 1.0)


def table_kernel(f_ref, ft_ref):
    block = ft_ref.shape[0]
    for ref, flip in ((f_ref, 0), (ft_ref, 1)):
        k, j = iota((block, block), flip), iota((block, block), 1 - flip)
        theta = (((2 * k + 1) * j) % (4 * block)).astype(f32) * np.float32(np.pi / (2 * block))
        for half, value in ((0, jnp.cos(theta)), (1, -jnp.sin(theta))):
            hi, lo = halves(value)
            for third, part in enumerate((hi, hi, lo)):
                if flip:
                    at = (2 * third + half) * block
                    ref[:, at : at + block] = part
                else:
                    ref[half * block : (half + 1) * block, third * block : (third + 1) * block] = part


def moved(x, by):
    return x if by % LANES == 0 else pltpu.roll(x, by % LANES, 1)


def pack_kernel(sub, w_ref, step_ref, skip_ref, gain_ref, bias_ref, lam_ref, imag_ref, lb_ref, o_ref):
    own, per, cols = step_ref.shape[1], lam_ref.shape[1], lb_ref.shape[1]
    groups = LANES // sub
    height = w_ref.shape[0] // groups
    pick = (iota((own, LANES), 0) == lax.axis_index("seq") * sub + iota((own, LANES), 1) % sub).astype(f32)
    w = exact_dot(w_ref[...], pick)
    vec = exact_dot(jnp.concatenate([step_ref[...], skip_ref[...], gain_ref[...], bias_ref[...]] * 2, axis=0), pick)
    group = iota((1, LANES), 1) // sub
    main = jnp.zeros((height, LANES), f32)
    row = jnp.zeros((1, LANES), f32)
    for u in range(groups):
        main = jnp.where(group == u, w[u * height : (u + 1) * height], main)
        if u < 4:
            row = jnp.where(group == u, vec[u : u + 1], row)
    spot, lane = iota((per, LANES), 0), iota((per, LANES), 1)
    rates = exact_dot(jnp.broadcast_to(lam_ref[...], (8, per)), (lane == spot).astype(f32)) + exact_dot(
        jnp.broadcast_to(imag_ref[...], (8, per)), (lane == spot + per).astype(f32)
    )
    o_ref[...] = jnp.zeros(o_ref.shape, f32)
    o_ref[0, 0:height] = main
    o_ref[0, height : height + 1] = row
    o_ref[0, height + 1 : height + 2] = rates[0:1]
    o_ref[0, height + 2 : height + 3, 0:cols] = lb_ref[...]


def lag_kernel(sub, length, masks, n_parts, *refs):
    pieces, refs = refs[:n_parts], refs[n_parts:]
    f_ref, kh_ref, vec_ref, w_out, term_out, w_ref, term_ref, k_scr, z_scr, rhs_scr, kf_scr, sems = refs
    slots = [piece.at[t] for piece in pieces for t in range(piece.shape[0])]
    ndp = len(slots)
    me = lax.axis_index("dp")
    n_w, lanes = w_ref.shape
    nstate = n_w // 2
    per = nstate // ndp
    groups = LANES // sub
    height = n_w // groups
    block = f_ref.shape[0] // 2
    group = iota((1, LANES), 1) // sub
    for u in range(groups):
        acc = jnp.zeros(slots[0].shape, f32)
        for t in range(ndp):
            i = me ^ masks[t]
            acc = jnp.where(group == i, pltpu.roll(slots[t][...], (i - u) * sub + LANES * ndp, 1), acc)
        w_ref[u * height : (u + 1) * height] = acc[0:height]
        if u < 4:
            vec_ref[u : u + 1] = acc[height : height + 1]
    vec_ref[4:8] = jnp.zeros((4, lanes), f32)
    rows = jnp.concatenate([slot[height + 1 : height + 2] for slot in slots], axis=0)
    source = jnp.zeros((nstate, ndp), i32)
    for t in range(ndp):
        source = jnp.where(iota((nstate, ndp), 1) == t, me ^ masks[t], source)
    spread = exact_dot((iota((nstate, ndp), 0) // per == source).astype(f32), rows)
    lane, state = iota((nstate, lanes), 1), iota((nstate, lanes), 0)
    lam = jnp.sum(jnp.where(lane == state % per, spread, 0.0), axis=1, keepdims=True)
    imag = jnp.sum(jnp.where(lane == state % per + per, spread, 0.0), axis=1, keepdims=True)
    terms = state_terms(lam, imag, vec_ref[0:1], float(length))
    for slot, value in enumerate(terms):
        term_ref[slot] = value
    saves = [pltpu.make_async_copy(w_ref, w_out, sems.at[0]), pltpu.make_async_copy(term_ref, term_out, sems.at[1])]
    for save in saves:
        save.start()
    z_scr[0], z_scr[1] = cmul(w_ref[0:nstate], w_ref[nstate:], terms[11], terms[12])
    k_scr[...] = jnp.zeros_like(k_scr)

    def pair(m, _):
        ready = []
        for n in (2 * m, 2 * m + 1):
            (fr, fi), w = rows8(term_ref[2, pl.ds(n, 1), :], term_ref[3, pl.ds(n, 1), :])
            cr = jnp.broadcast_to(z_scr[0, pl.ds(n, 1), :], (8, lanes))
            ci = jnp.broadcast_to(z_scr[1, pl.ds(n, 1), :], (8, lanes))
            ready.append([cmul(fr, fi, cr, ci), powers(*w)])
        for u in range(DOCMAX // FINE // COARSE):
            for v in range(COARSE):
                at = (u * COARSE + v) * FINE
                total = k_scr[at : at + FINE]
                for (xr, xi), pows in ready:
                    total = total + (xr * pows[v][0] - xi * pows[v][1] if v else xr)
                k_scr[at : at + FINE] = total
            for one in ready:
                one[0] = cmul(*one[0], *one[1][COARSE])
        return 0

    lax.fori_loop(0, nstate // 2, pair, 0)
    k_scr[0:1] += vec_ref[1:2]
    parts = length // block
    for p in range(parts):
        stack3(rhs_scr, slice(p * lanes, (p + 1) * lanes), k_scr[p * block : (p + 1) * block])
    kf_scr[...] = dot(f_ref[...], rhs_scr[...])
    sign = signs(block, lanes)
    for p in range(parts):
        here, past = slice(p * lanes, (p + 1) * lanes), slice((p - 1) * lanes, p * lanes)
        re, im = kf_scr[:block, here], kf_scr[block:, here]
        if p:
            re = re - sign * kf_scr[block:, past]
            im = im + sign * kf_scr[:block, past]
        kh_ref[p, :block] = re * (1.0 / block)
        kh_ref[p, block:] = im * (1.0 / block)
    for save in saves:
        save.wait()


def members(own, sub, c, width, wide):
    lane = iota((1, wide), 1)
    return (iota((width, wide), 0) == (lane // sub) * own + c * sub + lane % sub).astype(f32).astype(bf16)


def ln_kernel(own, sub, x_any, *refs):
    *o_refs, x_ref, sems = refs
    count, block, width = x_ref.shape
    wide = o_refs[0].shape[-1]
    copies = [pltpu.make_async_copy(x_any.at[s], x_ref.at[s], sems.at[s]) for s in range(count)]
    for copy in copies:
        copy.start()
    places = [members(own, sub, lax.axis_index("seq") ^ d, width, wide) for d in range(len(o_refs))]
    for s in range(count):
        copies[s].wait()
        x = x_ref[s].astype(f32)
        centre = x - jnp.mean(x, axis=-1, keepdims=True)
        spread = jnp.mean(centre * centre, axis=-1, keepdims=True)
        hi, lo = halves(centre * lax.rsqrt(spread + ln_eps))
        for o_ref, cols in zip(o_refs, places):
            o_ref[s] = dot(hi, cols) + dot(lo, cols)


def ln_back_kernel(own, sub, g0, g1, g2, g3, x_ref, c_ref, o_ref):
    count, block, width = x_ref.shape
    wide = g0.shape[-1]
    tokens = count * block
    g = jnp.zeros((tokens, width), f32)
    for d, g_ref in enumerate((g0, g1, g2, g3)):
        cols = members(own, sub, lax.axis_index("seq") ^ d, width, wide)
        g = g + dot(g_ref[...].reshape(tokens, wide), cols, NT)
    x = x_ref[...].astype(f32).reshape(tokens, width)
    centre = x - jnp.mean(x, axis=-1, keepdims=True)
    inv = lax.rsqrt(jnp.mean(centre * centre, axis=-1, keepdims=True) + ln_eps)
    hat = centre * inv
    mean_g = jnp.mean(g, axis=-1, keepdims=True)
    mean_gx = jnp.mean(g * hat, axis=-1, keepdims=True)
    cot = c_ref[...].astype(f32).reshape(tokens, width)
    o_ref[...] = (cot + inv * (g - mean_g - hat * mean_gx)).astype(bf16).reshape(o_ref.shape)


def segments(len_ref, cut_ref, block, parts):
    count, docs = len_ref.shape
    last = parts + docs - 1
    for s in range(count):
        ends = []
        for d in range(docs - 1):
            ends.append(len_ref[s, d] + (ends[-1] if ends else 0))
        cut_ref[s, 0] = 0
        cut_ref[s, last] = parts * block
        for d, end in enumerate(ends):
            rank = 1 + d
            for k in range(1, parts):
                rank = rank + jnp.where(end > k * block, 1, 0)
            cut_ref[s, rank] = end
        for k in range(1, parts):
            rank = k
            for end in ends:
                rank = rank + jnp.where(end <= k * block, 1, 0)
            cut_ref[s, rank] = k * block


def document(len_ref, s, at):
    start, end, total = 0, 0, 0
    for d in range(len_ref.shape[1]):
        total = total + len_ref[s, d]
        start = jnp.where(total <= at, total, start)
    total = 0
    end = 1 << 30
    for d in range(len_ref.shape[1]):
        total = total + len_ref[s, d]
        end = jnp.minimum(end, jnp.where(total > at, total, 1 << 30))
    return start, end


def within(cut_ref, s, j, block, lanes):
    start, end = cut_ref[s, j], cut_ref[s, j + 1]
    b = start // block
    rows = b * block + iota((block, lanes), 0)
    return b, (rows >= start) & (rows < end)


def column(j, s, count, lanes):
    return pl.ds(pl.multiple_of((j * count + s) * lanes, lanes), lanes)


CHUNK = 64


def arrivals(x_refs, x_scr, len_ref, len_scr, sems):
    me = lax.axis_index("seq")
    copies = [pltpu.make_async_copy(len_ref, len_scr, sems.at[0])]
    for d, x_ref in enumerate(x_refs):
        for s in range(x_ref.shape[0]):
            copies.append(pltpu.make_async_copy(x_ref.at[s], x_scr.at[s, me ^ d], sems.at[len(copies)]))
    return copies


def split_rows(y_scr, rows, cols, value, block, half):
    hi, lo = halves(value)
    for third, part in enumerate((hi, lo, hi)):
        at = (2 * third + half) * block
        y_scr[at + rows.start : at + rows.stop, cols] = part


def row_chunks(block):
    for r in range(0, block, CHUNK):
        yield slice(r, r + CHUNK), slice(block + r, block + r + CHUNK)


def conv_kernel(x0, x1, x2, x3, len_ref, vec_ref, kh_ref, f_ref, ft_ref,
                o0, o1, o2, o3, s_out, x_out, len_scr, cut_ref, x_scr, rhs_scr, s_scr, acc_scr, y_scr, out_scr, sems):
    count, block, lanes = x0.shape
    parts = kh_ref.shape[0]
    me = lax.axis_index("seq")
    copies = arrivals((x0, x1, x2, x3), x_scr, len_ref, len_scr, sems)
    for copy in copies:
        copy.start()
    for copy in copies:
        copy.wait()
    segments(len_scr, cut_ref, block, parts)
    gain, bias = vec_ref[2:3], vec_ref[3:4]
    items = cut_ref.shape[1] - 1
    for j in range(items):
        for s in range(count):
            b, keep = within(cut_ref, s, j, block, lanes)
            cols = slice((j * count + s) * lanes, (j * count + s + 1) * lanes)
            stack3(rhs_scr, cols, jnp.where(keep, x_scr[s, b] * gain + bias, 0.0))
    s_scr[...] = dot(f_ref[...], rhs_scr[...])
    saves = [pltpu.make_async_copy(s_scr, s_out, sems.at[len(copies)]),
             pltpu.make_async_copy(x_scr, x_out, sems.at[len(copies) + 1])]
    for save in saves:
        save.start()

    def own(j, _):
        for s in range(count):
            cols = column(j, s, count, lanes)
            for re, im in row_chunks(block):
                acc_scr[re, cols], acc_scr[im, cols] = cmul(
                    kh_ref[0, re], kh_ref[0, im], s_scr[re, cols], s_scr[im, cols]
                )
            start, _ = document(len_scr, s, cut_ref[s, j])
            b = cut_ref[s, j] // block
            first = j
            for i in range(items):
                first = first - jnp.where((i < j) & (cut_ref[s, i] >= start), 1, 0)

            def add(i, _):
                p = b - cut_ref[s, i] // block
                there = column(i, s, count, lanes)
                for re, im in row_chunks(block):
                    more = cmul(kh_ref[p, re], kh_ref[p, im], s_scr[re, there], s_scr[im, there])
                    acc_scr[re, cols] += more[0]
                    acc_scr[im, cols] += more[1]
                return 0

            lax.fori_loop(first, j, add, 0)
            for re, im in row_chunks(block):
                split_rows(y_scr, re, cols, acc_scr[re, cols], block, 0)
                split_rows(y_scr, re, cols, acc_scr[im, cols], block, 1)
        return 0

    lax.fori_loop(0, items, own, 0)
    acc_scr[0:block] = dot(ft_ref[...], y_scr[...])
    for j in range(items):
        for s in range(count):
            b, keep = within(cut_ref, s, j, block, lanes)
            cols = slice((j * count + s) * lanes, (j * count + s + 1) * lanes)
            out_scr[s, b] = jnp.where(keep, acc_scr[0:block, cols], out_scr[s, b])
    for d, o_ref in enumerate((o0, o1, o2, o3)):
        for s in range(count):
            o_ref[s] = out_scr[s, me ^ d].astype(bf16)
    for save in saves:
        save.wait()


def back_kernel(c0, c1, c2, c3, x_ref, len_ref, s_ref, vec_ref, kh_ref, f_ref, ft_ref,
                g0, g1, g2, g3, dkh_ref, dvec_ref,
                len_scr, cut_ref, v_scr, x_scr, rhs_scr, s_scr, sv_scr, acc_scr, y_scr, du_scr, sems):
    count, block, lanes = c0.shape
    parts = kh_ref.shape[0]
    me = lax.axis_index("seq")
    copies = arrivals((c0, c1, c2, c3), v_scr, len_ref, len_scr, sems)
    later = [pltpu.make_async_copy(s_ref, s_scr, sems.at[len(copies)]),
             pltpu.make_async_copy(x_ref, x_scr, sems.at[len(copies) + 1])]
    for copy in copies + later:
        copy.start()
    dkh_ref[...] = jnp.zeros_like(dkh_ref)
    for copy in copies:
        copy.wait()
    segments(len_scr, cut_ref, block, parts)
    items = cut_ref.shape[1] - 1
    for j in range(items):
        for s in range(count):
            b, keep = within(cut_ref, s, j, block, lanes)
            v = jnp.where(keep, v_scr[s, b].astype(f32), 0.0).astype(bf16)
            cols = slice((j * count + s) * lanes, (j * count + s + 1) * lanes)
            rhs_scr[0:block, cols] = v
            rhs_scr[block:, cols] = v
    sv_scr[...] = dot(f_ref[:, block:], rhs_scr[...])
    later[0].wait()

    def own(j, _):
        for s in range(count):
            cols = column(j, s, count, lanes)
            for re, im in row_chunks(block):
                vr, vi, ur, ui = sv_scr[re, cols], sv_scr[im, cols], s_scr[re, cols], s_scr[im, cols]
                kr, ki = kh_ref[0, re], kh_ref[0, im]
                acc_scr[re, cols] = kr * vr + ki * vi
                acc_scr[im, cols] = kr * vi - ki * vr
                dkh_ref[0, re] += vr * ur + vi * ui
                dkh_ref[0, im] += vi * ur - vr * ui
            _, end = document(len_scr, s, cut_ref[s, j])
            b = cut_ref[s, j] // block
            last = j
            for i in range(items):
                last = last + jnp.where((i > j) & (cut_ref[s, i] < end), 1, 0)

            def add(i, _):
                p = cut_ref[s, i] // block - b
                there = column(i, s, count, lanes)
                for re, im in row_chunks(block):
                    vr, vi, ur, ui = sv_scr[re, there], sv_scr[im, there], s_scr[re, cols], s_scr[im, cols]
                    kr, ki = kh_ref[p, re], kh_ref[p, im]
                    acc_scr[re, cols] += kr * vr + ki * vi
                    acc_scr[im, cols] += kr * vi - ki * vr
                    dkh_ref[p, re] += vr * ur + vi * ui
                    dkh_ref[p, im] += vi * ur - vr * ui
                return 0

            lax.fori_loop(j + 1, last + 1, add, 0)
            for re, im in row_chunks(block):
                split_rows(y_scr, re, cols, acc_scr[re, cols], block, 0)
                split_rows(y_scr, re, cols, acc_scr[im, cols], block, 1)
        return 0

    lax.fori_loop(0, items, own, 0)
    acc_scr[0:block] = dot(ft_ref[...], y_scr[...])
    for j in range(items):
        for s in range(count):
            b, keep = within(cut_ref, s, j, block, lanes)
            cols = slice((j * count + s) * lanes, (j * count + s + 1) * lanes)
            du_scr[s, b] = jnp.where(keep, acc_scr[0:block, cols], du_scr[s, b])
    for copy in later[1:]:
        copy.wait()
    gain = vec_ref[2:3]
    d_gain = jnp.zeros((8, lanes), f32)
    d_bias = jnp.zeros((8, lanes), f32)
    for d, g_ref in enumerate((g0, g1, g2, g3)):
        for s in range(count):
            for r in range(0, block, CHUNK):
                du = du_scr[s, me ^ d, r : r + CHUNK]
                d_bias += jnp.sum(du.reshape(CHUNK // 8, 8, lanes), axis=0)
                d_gain += jnp.sum((du * x_scr[s, me ^ d, r : r + CHUNK]).reshape(CHUNK // 8, 8, lanes), axis=0)
                g_ref[s, r : r + CHUNK] = (du * gain).astype(bf16)
    dvec_ref[0:1] = jnp.sum(d_gain, axis=0, keepdims=True)
    dvec_ref[1:2] = jnp.sum(d_bias, axis=0, keepdims=True)
    dvec_ref[2:3] = vec_ref[0:1]


def normal_cdf(v, bell):
    t = 1.0 / (1.0 + np.float32(0.3275911 / np.sqrt(2.0)) * jnp.abs(v))
    tail = t * (0.127414796 + t * (-0.142248368 + t * (0.7107068705 + t * (-0.7265760135 + t * 0.5307027145)))) * bell
    return jnp.where(v < 0.0, tail, 1.0 - tail)


def dense_kernel(q0, q1, q2, q3, x_any, c_any, w_ref, lb_ref,
                 out_ref, act_ref, dpre_ref, dlb_ref, d0, d1, d2, d3, x_ref, c_ref, slope_scr, pre_scr, dact_scr, sems):
    count, block, wide = q0.shape
    width = act_ref.shape[1]
    me = lax.axis_index("seq")
    copies = [pltpu.make_async_copy(x_any, x_ref, sems.at[0]), pltpu.make_async_copy(c_any, c_ref, sems.at[1])]
    for copy in copies:
        copy.start()

    def cols_of(d):
        return pl.ds(pl.multiple_of((me ^ d) * wide, wide), wide)

    def sequence(s, lb_sum):
        def slope(r, _):
            rows = pl.ds(pl.multiple_of(r * CHUNK, CHUNK), CHUNK)
            flat = pl.ds(pl.multiple_of(s * block + r * CHUNK, CHUNK), CHUNK)
            for d, q_ref in enumerate((q0, q1, q2, q3)):
                v = q_ref[s, rows].astype(f32)
                bell = jnp.exp(-0.5 * v * v)
                cdf = normal_cdf(v, bell)
                act_ref[flat, cols_of(d)] = (v * cdf).astype(bf16)
                slope_scr[rows, cols_of(d)] = cdf + v * (bell * np.float32(1.0 / np.sqrt(2.0 * np.pi)))
            return 0

        lax.fori_loop(0, block // CHUNK, slope, 0)
        whole = pl.ds(pl.multiple_of(s * block, block), block)
        pre_scr[...] = dot(act_ref[whole, :], w_ref[...])

        @pl.when(s == 0)
        def _():
            for copy in copies:
                copy.wait()

        def gate(r, total):
            rows = pl.ds(pl.multiple_of(r * 32, 32), 32)
            flat = pl.ds(pl.multiple_of(s * block + r * 32, 32), 32)
            first = pre_scr[rows, 0:width] + lb_ref[:, 0:width]
            sig = 1.0 / (1.0 + jnp.exp(-(pre_scr[rows, width:] + lb_ref[:, width:])))
            out_ref[s, rows] = (x_ref[s, rows].astype(f32) + first * sig).astype(bf16)
            d_first = c_ref[s, rows].astype(f32) * sig
            d_second = d_first * first * (1.0 - sig)
            d_pre = jnp.concatenate([d_first, d_second], axis=1).astype(bf16)
            dpre_ref[flat, :] = d_pre
            return total + jnp.sum(d_pre.astype(f32).reshape(4, 8, 2 * width), axis=0)

        lb_sum = lax.fori_loop(0, block // 32, gate, lb_sum)
        dact_scr[...] = dot(dpre_ref[whole, :], w_ref[...], NT)
        for d, o_ref in enumerate((d0, d1, d2, d3)):
            o_ref[s] = (dact_scr[:, cols_of(d)] * slope_scr[:, cols_of(d)]).astype(bf16)
        return lb_sum

    lb_sum = lax.fori_loop(0, count, sequence, jnp.zeros((8, 2 * width), f32))
    dlb_ref[...] = jnp.sum(lb_sum, axis=0, keepdims=True)


def rows_kernel(sub, nseq, masks, shared_ref, *refs):
    *w_refs, o_ref, lb_ref = refs
    cols = w_refs[0].shape[-1]
    span = o_ref.shape[0] // nseq
    me = lax.axis_index("dp")
    bias_row = shared_ref.shape[1] - 8 + 2
    t = 0
    for w_ref in w_refs:
        for slot in range(w_ref.shape[0]):
            at = pl.ds(pl.multiple_of((me ^ masks[t]) * cols, cols), cols)
            lb_ref[:, at] = shared_ref[t, bias_row : bias_row + 1, 0:cols]
            t += 1
            for c in range(nseq):
                for i in range(span // sub):
                    o_ref[c * span + i * sub : c * span + (i + 1) * sub, at] = w_ref[
                        slot, (i * nseq + c) * sub : (i * nseq + c + 1) * sub
                    ]


def weight_kernel(act_ref, dpre_ref, *o_refs):
    ndp = len(o_refs)
    part = o_refs[0].shape[1]
    for d, o_ref in enumerate(o_refs):
        at = pl.ds(pl.multiple_of((lax.axis_index("dp") ^ d) * part, part), part)
        o_ref[...] = dot(act_ref[...], dpre_ref[:, at], TN).astype(bf16)


def sum_all_kernel(*refs):
    *x_refs, o_ref = refs
    total = x_refs[0][...].astype(f32)
    for x_ref in x_refs[1:]:
        total = total + x_ref[...].astype(f32)
    o_ref[...] = total.astype(o_ref.dtype)


def state_grad_kernel(sub, length, w_any, term_any, dkh_ref, dvec_ref, dlb_ref, ft_ref, o_ref,
                      w_ref, term_ref, dk_scr, f_scr, dw_scr, y_scr, sems):
    loads = [pltpu.make_async_copy(w_any, w_ref, sems.at[0]), pltpu.make_async_copy(term_any, term_ref, sems.at[1])]
    for load in loads:
        load.start()
    ndp = o_ref.shape[0]
    n_w, lanes = w_ref.shape
    nstate = n_w // 2
    per = nstate // ndp
    groups = LANES // sub
    height = n_w // groups
    parts, twice, _ = dkh_ref.shape
    block = twice // 2
    sign = signs(block, lanes)
    for p in range(parts):
        re, im = dkh_ref[p, :block], dkh_ref[p, block:]
        if p + 1 < parts:
            re = re + sign * dkh_ref[p + 1, block:]
            im = im - sign * dkh_ref[p + 1, :block]
        stack3(y_scr, slice(p * lanes, (p + 1) * lanes), jnp.concatenate([re, im], axis=0))
    all_lags = dot(ft_ref[...], y_scr[...]) * (1.0 / block)
    for p in range(parts):
        dk_scr[p * block : (p + 1) * block] = all_lags[:, p * lanes : (p + 1) * lanes]
    at8 = iota((8, lanes), 0).astype(f32)
    for load in loads:
        load.wait()

    def one(n, _):
        (fr, fi), w = rows8(term_ref[2, pl.ds(n, 1), :], term_ref[3, pl.ds(n, 1), :])
        pows = powers(*w)
        zero = jnp.zeros((8, lanes), f32)
        s_re, s_im, e_re, e_im, h_re, h_im = (zero,) * 6
        for u in range(DOCMAX // FINE // COARSE - 1, -1, -1):
            t_re, t_im, o_re, o_im = (zero,) * 4
            for v in range(COARSE - 1, 0, -1):
                at = (u * COARSE + v) * FINE
                dk = dk_scr[at : at + FINE]
                t_re = t_re + dk * pows[v][0]
                t_im = t_im + dk * pows[v][1]
                o_re = o_re + t_re
                o_im = o_im + t_im
            t_re = t_re + dk_scr[u * COARSE * FINE : u * COARSE * FINE + FINE]
            e_re, e_im = cmul(e_re, e_im, *pows[COARSE])
            s_re, s_im = cmul(s_re, s_im, *pows[COARSE])
            h_re, h_im = cmul(h_re, h_im, *pows[COARSE])
            e_re, e_im = e_re + s_re, e_im + s_im
            s_re, s_im = s_re + t_re, s_im + t_im
            h_re, h_im = h_re + o_re, h_im + o_im
        m_re = (FINE * COARSE) * e_re + FINE * h_re + at8 * s_re
        m_im = (FINE * COARSE) * e_im + FINE * h_im + at8 * s_im
        s_re, s_im = cmul(s_re, s_im, fr, fi)
        m_re, m_im = cmul(m_re, m_im, fr, fi)
        for slot, value in enumerate((s_re, s_im, m_re, m_im)):
            f_scr[slot, pl.ds(n, 1), :] = jnp.sum(value, axis=0, keepdims=True)
        return 0

    lax.fori_loop(0, nstate, one, 0)
    a, b, z_re, z_im, one_re, one_im, far_re, far_im, den_re, den_im, inv, g_re, g_im = (
        term_ref[slot] for slot in range(TERMS)
    )
    f0, f1 = (f_scr[0], f_scr[1]), (f_scr[2], f_scr[3])
    gf_re, gf_im = cmul(g_re, g_im, *f0)
    dw_scr[0:nstate] = gf_re
    dw_scr[nstate:] = -gf_im
    inv_one = 1.0 / (one_re * one_re + one_im * one_im)
    near_re, near_im = cmul(z_re, z_im, one_re * inv_one, -one_im * inv_one)
    far_re, far_im = cmul(far_re, far_im, den_re * inv, -den_im * inv)
    q_re, q_im = cmul(length * far_re - near_re, length * far_im - near_im, *f0)
    c_re, c_im = cmul(w_ref[0:nstate], w_ref[nstate:], g_re, g_im)
    y_re, y_im = cmul(c_re, c_im, q_re + f1[0], q_im + f1[1])
    by_a = a * y_re
    by_step = by_a - b * y_im
    step = jnp.exp(dvec_ref[2:3])
    by_imag = -step * y_im
    d_step = jnp.sum(by_step, axis=0, keepdims=True)
    lane, state = iota((nstate, lanes), 1), iota((nstate, lanes), 0)
    col_a = jnp.sum(by_a, axis=1, keepdims=True)
    col_b = jnp.sum(by_imag, axis=1, keepdims=True)
    grid = jnp.where(lane == state % per, col_a, jnp.where(lane == state % per + per, col_b, 0.0))
    rates = exact_dot((iota((ndp, nstate), 0) == iota((ndp, nstate), 1) // per).astype(f32), grid)
    vecs = (d_step, dk_scr[0:1], dvec_ref[0:1], dvec_ref[1:2])
    group = iota((1, LANES), 1) // sub
    cols = dlb_ref.shape[1] // ndp
    for i in range(ndp):
        main = jnp.zeros((height, LANES), f32)
        row = jnp.zeros((1, LANES), f32)
        for u in range(groups):
            main = jnp.where(group == u, moved(dw_scr[u * height : (u + 1) * height], (u - i) * sub), main)
            if u < 4:
                row = jnp.where(group == u, moved(jnp.broadcast_to(vecs[u], (8, LANES)), (u - i) * sub)[0:1], row)
        o_ref[i] = jnp.zeros(o_ref.shape[1:], f32)
        o_ref[i, 0:height] = main
        o_ref[i, height : height + 1] = row
        o_ref[i, height + 1 : height + 2] = rates[i : i + 1]
        o_ref[i, height + 2 : height + 3, 0:cols] = dlb_ref[:, i * cols : (i + 1) * cols]


def sum_kernel(x_ref, o_ref):
    total = x_ref[0].astype(f32)
    for i in range(1, x_ref.shape[0]):
        total = total + x_ref[i].astype(f32)
    o_ref[...] = total.astype(o_ref.dtype)


def last_kernel(sub, m0, m1, m2, m3, w0, w1, w2, w3, w_ref, step_ref, skip_ref, gain_ref, bias_ref,
                lam_ref, imag_ref, lb_ref, dw_ref):
    n_w, own = w_ref.shape
    groups = LANES // sub
    height = n_w // groups
    per, cols = lam_ref.shape[1], lb_ref.shape[1]
    group = iota((1, LANES), 1) // sub
    parts = (m0, m1, m2, m3)
    for u in range(groups):
        acc = jnp.zeros(m0.shape, f32)
        for d, m_ref in enumerate(parts):
            c = lax.axis_index("seq") ^ d
            acc = jnp.where(group == c, pltpu.roll(m_ref[...], (c - u) * sub + LANES, 1), acc)
        w_ref[u * height : (u + 1) * height] = acc[0:height, 0:own]
        if u < 4:
            (step_ref, skip_ref, gain_ref, bias_ref)[u][...] = acc[height : height + 1, 0:own]
    total = m0[...] + m1[...] + m2[...] + m3[...]
    lam_ref[...] = total[height + 1 : height + 2, 0:per]
    imag_ref[...] = pltpu.roll(total, LANES - per, 1)[height + 1 : height + 2, 0:per]
    lb_ref[...] = total[height + 2 : height + 3, 0:cols]
    nseq = len(parts)
    width = w0.shape[0]
    span = width // nseq
    for c in range(nseq):
        rows = slice(c * span, (c + 1) * span)
        whole = w0[rows].astype(f32) + w1[rows].astype(f32) + w2[rows].astype(f32) + w3[rows].astype(f32)
        for i in range(span // sub):
            at = (i * nseq + c) * sub
            dw_ref[at : at + sub] = whole[i * sub : (i + 1) * sub]


def swap(x, axis, by):
    n = lax.axis_size(axis)
    return jax.tree.map(lambda v: lax.ppermute(v, axis, [(i, i ^ by) for i in range(n)]), x)


def trade(parts, axis):
    return [parts[0]] + [swap(parts[d], axis, d) for d in range(1, len(parts))]


def tie(*values):
    return lax.optimization_barrier(values)


def on_device(block_in, cotangent, ln_gain, ln_bias, lambda_log, lambda_imag, dss_weight, log_step, skip_gain,
              lin_weight, lin_bias, doc_lengths):
    ndp, nseq = lax.axis_size("dp"), lax.axis_size("seq")
    count, block, width = block_in.shape
    length = block * nseq
    own = ln_gain.shape[0]
    sub = own // nseq
    wide = width // nseq
    per = lambda_log.shape[0]
    nstate = per * ndp
    n_w = 2 * nstate
    cols = lin_weight.shape[1]
    tokens = count * block
    height = n_w * sub // LANES
    rows = height + 8
    steps = [1 << k for k in reversed(range(ndp.bit_length() - 1))]
    masks = [0]
    for step in steps:
        masks += [mask ^ step for mask in masks]

    def row(v):
        return v.reshape(1, -1)

    packed = call(partial(pack_kernel, sub), shape((1, rows, LANES)), [VM] * 8, name="pack", mib=60, us=2)(
        dss_weight.reshape(n_w, own), row(log_step), row(skip_gain), row(ln_gain), row(ln_bias),
        row(lambda_log), row(lambda_imag), row(lin_bias)
    )

    piece, piece32 = shape((count, block, wide), bf16), shape((count, block, wide))
    shared, shared_parts = packed, [packed]
    w_slots = [lin_weight[None]]
    f_table = hats = None
    for number, step in enumerate(steps):
        if number == 2:
            shared, hats[1] = tie(shared, hats[1])
        more = swap(shared, "dp", step)
        if number == 0:
            f_table, ft_table = call(
                table_kernel, [shape((2 * block, 3 * block), bf16), shape((block, 6 * block), bf16)], [], name="tables", us=2
            )()
            more, f_table, ft_table, x_late = tie(more, f_table, ft_table, block_in)
        elif number == 1:
            hats = call(
                partial(ln_kernel, own, sub), [piece32] * nseq, [AN],
                scratch=[pltpu.VMEM((count, block, width), bf16), DMA((count,))], name="layer_norm", us=2,
            )(x_late)
            more, *hats = tie(more, *hats)
            hats = trade(hats, "seq")
        shared_parts.append(more)
        if number < len(steps) - 1:
            shared = jnp.concatenate([shared, more], axis=0)

    w_more = swap(w_slots[0], "dp", steps[0])

    spec = (nseq, 2 * block, wide)
    kh, vec, w_all, terms = call(
        partial(lag_kernel, sub, length, masks, len(shared_parts)),
        [shape(spec), shape((8, wide)), shape((n_w, wide)), shape((TERMS, nstate, wide))],
        [VM] * (len(shared_parts) + 1), outs=[VM, VM, AN, AN],
        scratch=[pltpu.VMEM((n_w, wide), f32), pltpu.VMEM((TERMS, nstate, wide), f32),
                 pltpu.VMEM((length, wide), f32), pltpu.VMEM((2, nstate, wide), f32),
                 pltpu.VMEM((3 * block, nseq * wide), bf16), pltpu.VMEM((2 * block, nseq * wide), f32), DMA((2,))],
        name="lag_kernel", us=6, keep=[ft_table],
    )(*shared_parts, f_table)

    kh, w_more = tie(kh, w_more)
    w_late = jnp.concatenate([w_slots[0], w_more], axis=0)
    ahead = steps[1:]
    if len(ahead) == 2:
        w_slots = [w_late, swap(w_late, "dp", ahead[0]), swap(w_late, "dp", ahead[1])]
    else:
        w_slots = [w_late]
        for step in ahead:
            w_slots = [jnp.concatenate(w_slots + [swap(slot, "dp", step) for slot in w_slots], axis=0)]

    blocks4 = (count, nseq, block, wide)
    items = nseq + doc_lengths.shape[1] - 1
    lens = pltpu.SMEM(doc_lengths.shape, i32)
    cuts = pltpu.SMEM((count, items + 1), i32)
    across = items * count * wide
    *convs, spectra_u, x_blocks = call(
        conv_kernel, [piece] * nseq + [shape((2 * block, across)), shape(blocks4)],
        [AN] * (nseq + 1) + [VM] * 4, outs=[VM] * nseq + [AN, AN],
        scratch=[lens, cuts, pltpu.VMEM(blocks4, f32), pltpu.VMEM((3 * block, across), bf16),
                 pltpu.VMEM((2 * block, across), f32), pltpu.VMEM((2 * block, across), f32),
                 pltpu.VMEM((6 * block, across), bf16), pltpu.VMEM(blocks4, f32), DMA((count * nseq + 3,))],
        name="doc_conv", mib=24, us=7, keep=[w_all, terms],
    )(*hats, doc_lengths, vec, kh, f_table, ft_table)
    keep = [w_all, terms, vec, kh, f_table, ft_table, spectra_u, x_blocks]
    if len(ahead) == 2:
        *convs, w_slots[1], w_slots[2] = tie(*convs, w_slots[1], w_slots[2])
        w_slots.append(swap(w_slots[1], "dp", ahead[1]))
    convs = trade(convs, "seq")
    if cols % LANES == 0 and sub % 16 == 0:
        shared = jnp.concatenate([shared, shared_parts[-1]], axis=0)
        shared, convs[1] = tie(shared, convs[1])
        w_lin, bias_full = call(
            partial(rows_kernel, sub, nseq, masks), [shape((width, 2 * width), bf16), shape((1, 2 * width))],
            [VM] * (1 + len(w_slots)), name="linear_rows", us=1, keep=keep,
        )(shared, *w_slots)
    else:
        shared = jnp.concatenate([shared, shared_parts[-1]], axis=0)
        place = jnp.asarray([masks.index(i) for i in range(ndp)])[lax.axis_index("dp") ^ jnp.arange(ndp)]
        w_lin = jnp.take(jnp.concatenate(w_slots, axis=0), place, axis=0)
        w_lin = w_lin.reshape(ndp, ndp, nseq, sub, cols).transpose(2, 1, 3, 0, 4).reshape(width, 2 * width)
        bias_full = jnp.take(shared[:, height + 2, :cols], place, axis=0).reshape(1, 2 * width)

    block_out, act, d_pre, d_lin_bias, *d_convs = call(
        dense_kernel,
        [shape((count, block, width), bf16), shape((tokens, width), bf16), shape((tokens, 2 * width), bf16),
         shape((1, 2 * width))] + [piece] * nseq,
        [VM] * nseq + [AN, AN, VM, VM],
        scratch=[pltpu.VMEM((count, block, width), bf16), pltpu.VMEM((count, block, width), bf16),
                 pltpu.VMEM((block, width), f32), pltpu.VMEM((block, 2 * width), f32), pltpu.VMEM((block, width), f32), DMA((2,))],
        name="gated_linear", mib=16, us=5, keep=keep,
    )(*convs, block_in, cotangent, w_lin, bias_full)
    d_convs = trade(d_convs, "seq")

    act, d_pre, d_convs[1] = tie(act, d_pre, d_convs[1])
    if cols % LANES == 0:
        dw_parts = call(
            weight_kernel, [shape((width, cols), bf16)] * ndp, [VM, VM], name="weight_grad", us=1, keep=keep
        )(act, d_pre)
        dw_parts = trade(dw_parts, "dp")
    else:
        full = lax.dot_general(act, d_pre, TN, preferred_element_type=f32).astype(bf16)
        full = full.reshape(width, ndp, cols).transpose(1, 0, 2)
        dw_parts = list(lax.all_to_all(full, "dp", 0, 0, tiled=True))

    out = call(
        back_kernel, [piece] * nseq + [shape(spec), shape((3, wide))],
        [AN] * (nseq + 3) + [VM] * 4,
        scratch=[lens, cuts, pltpu.VMEM(blocks4, bf16), pltpu.VMEM(blocks4, f32),
                 pltpu.VMEM((2 * block, across), bf16), pltpu.VMEM((2 * block, across), f32),
                 pltpu.VMEM((2 * block, across), f32), pltpu.VMEM((2 * block, across), f32),
                 pltpu.VMEM((6 * block, across), bf16), pltpu.VMEM(blocks4, f32), DMA((count * nseq + 3,))],
        name="doc_conv_grad", mib=30, us=8, keep=[w_all, terms],
    )(*d_convs, x_blocks, doc_lengths, spectra_u, vec, kh, f_table, ft_table)
    g_own, dkh, d_norm = out[:nseq], out[nseq], out[nseq + 1]
    gs = trade(g_own, "seq")

    small = call(
        partial(state_grad_kernel, sub, length), shape((ndp, rows, LANES)), [AN, AN] + [VM] * 4,
        scratch=[pltpu.VMEM((n_w, wide), f32), pltpu.VMEM((TERMS, nstate, wide), f32),
                 pltpu.VMEM((length, wide), f32), pltpu.VMEM((4, nstate, wide), f32), pltpu.VMEM((n_w, wide), f32),
                 pltpu.VMEM((6 * block, nseq * wide), bf16), DMA((2,))],
        name="state_grad", mib=10, us=10,
    )(w_all, terms, dkh, d_norm, d_lin_bias, ft_table)
    small, dw_parts, gs = tie(small, tuple(dw_parts), tuple(gs))
    small = lax.all_to_all(small, "dp", 0, 0, tiled=True)
    dw_own = call(sum_all_kernel, shape((width, cols), bf16), [VM] * ndp, name="weight_sum")(*dw_parts)
    dws = trade([dw_own] * nseq, "seq")
    gs, dws[1] = tie(gs, dws[1])
    grad_in = call(
        partial(ln_back_kernel, own, sub), shape((count, block, width), bf16), [VM] * (nseq + 2),
        name="layer_norm_grad", mib=12,
    )(*gs, block_in, cotangent)
    small, grad_in, *dws = tie(small, grad_in, *dws)
    small = call(sum_kernel, shape((rows, LANES)), [VM], name="small_sum", us=0.5)(small)
    smalls = trade([small] * nseq, "seq")
    d_w, d_step, d_skip, d_gain, d_bias, d_lam, d_imag, d_lb, dw = call(
        partial(last_kernel, sub),
        [shape((n_w, own))] + [shape((1, own))] * 4 + [shape((1, per))] * 2 + [shape((1, cols)), shape((width, cols))],
        [VM] * (2 * nseq), name="last", us=1,
    )(*smalls, *dws)
    return (
        block_out, grad_in, d_gain.reshape(own), d_bias.reshape(own), d_lam.reshape(per), d_imag.reshape(per),
        d_w.reshape(2, nstate, own), d_step.reshape(own), d_skip.reshape(own), dw, d_lb.reshape(cols),
    )


def solution(mesh):
    placed = (
        P("dp", "seq", None), P("dp", "seq", None), P("dp"), P("dp"), P("dp"), P("dp"),
        P(None, None, "dp"), P("dp"), P("dp"), P(None, "dp"), P("dp"), P("dp", None),
    )
    return jax.shard_map(
        on_device,
        mesh=mesh,
        in_specs=placed,
        out_specs=(
            P("dp", "seq", None), P("dp", "seq", None), P("dp"), P("dp"), P("dp"), P("dp"),
            P(None, None, "dp"), P("dp"), P("dp"), P(None, "dp"), P("dp"),
        ),
        check_vma=False,
    )
```

time: 150 us -> 107 us (0.71); the launches traced: 147 us -> 107 us
  local copies, waits for them, and re-layouts: 30 us -> 0.72 us
  waiting for transfers between devices: 29.9 us -> 18.3 us
  Pallas kernels: 52.9 us -> 48.4 us
  starting transfers between devices: 33.7 us -> 38.2 us
    unnamed x89 -> x10, local copies, waits for them, and re-layouts: 25.5 us -> 0.72 us
    ppermute x18 -> x32, starting transfers between devices: 12.2 us -> 34.5 us  [swap(): lax.ppermute(v, axis, [(i, i ^ by) for i in range(n)])]
    all_to_all x3 -> x0, starting transfers between devices: 16.4 us -> none  [the longest x1 7.28 us: on_device(): shared = lax.all_to_all(packed, 'dp', 0, 0, tiled=True)]
    all_to_all x3 -> x0, waiting for transfers between devices: 7.13 us -> none  [the longest x1 7.12 us: on_device(): shared = lax.all_to_all(packed, 'dp', 0, 0, tiled=True)]
    all_to_all x1, waiting for transfers between devices: 6.64 us -> 0.01 us  [on_device(): small = lax.all_to_all(small, 'dp', 0, 0, tiled=True)]
    pallas_call x12 -> x14, Pallas kernels: 52.9 us -> 48.4 us  [call(): return lambda *args: kernel(*args, *keep)]
    transpose x1 -> x0, local copies, waits for them, and re-layouts: 2.44 us -> none  [on_device(): w_lin.reshape(ndp, ndp, nseq, sub, cols).transpose(2, 1, 3, 0, 4)]
    ppermute x18 -> x32, waiting for transfers between devices: 16.1 us -> 18.3 us  [swap(): lax.ppermute(v, axis, [(i, i ^ by) for i in range(n)])]
  transfers between devices with their start and end apart: 22 -> 33, of which waited for: 9 -> 9; matrix products, arithmetic and copies ran while one was open for 2% -> 0% of each run, Pallas kernels for 32% -> 38%
where the time goes in v2:
time: 107 us
  Pallas kernels  48.4 us (45%)
  starting transfers between devices  38.2 us (36%)
  waiting for transfers between devices  18.3 us (17%)
    pallas_call x14, Pallas kernels, call(): return lambda *args: kernel(*args, *keep)  48.4 us
    ppermute x32, starting transfers between devices, swap(): lax.ppermute(v, axis, [(i, i ^ by) for i in range(n)])  34.5 us
    ppermute x32, waiting for transfers between devices, swap(): lax.ppermute(v, axis, [(i, i ^ by) for i in range(n)])  18.3 us
    all_to_all x1, starting transfers between devices, on_device(): small = lax.all_to_all(small, 'dp', 0, 0, tiled=True)  3.75 us
  transfers between devices with their start and end apart: 33, of which 9 were waited for; matrix products, arithmetic and copies ran while one was open for 0% of the time, Pallas kernels for 38%

profile of v2, /device:TPU:0, one launch (start us, length us, event | category | flops | bytes accessed | tf_op | source)
XLA Modules:
  0.0 106.6 jit_solution(5098909286914949408)
XLA Ops:
  0.6 1.8 %pack.1.refs_0_ = f32[1,24,128]{2,1,0:T(8,128)} custom-call(f32[128,64]{1,0:T(8,128)} %bitcast.19, f32[1,64]{1,0:T(1,128)} %bitcast.20, f32[1,64]{1,0:T(1,128)} %bitcast.21, f32[1,64]{1,0:T(1,128)} %bitcast.22, f32[1,64]{1,0:T(1,128)} %bitcast.23, f32[1,8]{1,0:T(1,128)} %bitcast.24, f32[1,8]{1,0:T(1,128)} %bitcast.25, f32[1,128]{1,0:T(1,128)} %bitcast.26), custom_call_target="tpu_custom_call" | custom-call | flops 2300000000 | bytes 1000 | tf_op jit(solution)/shard_map/pack/pallas_call | solution.py:53
  2.4 4.0 %collective-permute-start = (f32[1,24,128]{2,1,0:T(8,128)}, f32[1,24,128]{2,1,0:T(8,128)S(1)}, u32[]{:S(2)}, u32[]{:S(2)}) collective-permute-start(f32[1,24,128]{2,1,0:T(8,128)} %pack.1.refs_0_), channel_id=1, source_target_pairs={{0,16},{4,20},{8,24},{12,28},{16,0},{20,4},{24,8},{28,12},{1,17},{... | collective-permute-start | bytes 36872 | tf_op jit(solution)/shard_map/ppermute | solution.py:740
  6.4 2.2 %tables.1 = (bf16[512,768]{1,0:T(8,128)(2,1)S(1)}, bf16[256,1536]{1,0:T(8,128)(2,1)S(1)}) custom-call(), custom_call_target="tpu_custom_call" | custom-call | flops 2300000000 | bytes 1000 | tf_op jit(solution)/shard_map/tables/pallas_call | solution.py:53
  8.7 1.6 %collective-permute-start.1 = (f32[2,24,128]{2,1,0:T(8,128)S(1)}, f32[2,24,128]{2,1,0:T(8,128)S(1)}, u32[]{:S(2)}, u32[]{:S(2)}) collective-permute-start(f32[2,24,128]{2,1,0:T(8,128)S(1)} %pad_maximum_fusion.3), channel_id=1, source_target_pairs={{0,8},{4,12},{8,0},{12,4},{16,24},{20,28},{24,16},{28,20},{1,9},{5... | collective-permute-start | bytes 73736 | tf_op jit(solution)/shard_map/ppermute | solution.py:740
  10.4 2.0 %layer_norm.1 = (f32[2,256,128]{2,1,0:T(8,128)S(1)}, f32[2,256,128]{2,1,0:T(8,128)S(1)}, f32[2,256,128]{2,1,0:T(8,128)S(1)}, f32[2,256,128]{2,1,0:T(8,128)S(1)}) custom-call(bf16[2,256,512]{2,1,0:T(8,128)(2,1)S(1)} %copy-done), custom_call_target="tpu_custom_call" | custom-call | flops 2300000000 | bytes 1000 | tf_op jit(solution)/shard_map/layer_norm/pallas_call | solution.py:53
  12.6 1.5 %collective-permute-done.2.refs_1_ = f32[2,256,128]{2,1,0:T(8,128)S(1)} collective-permute-done((f32[2,256,128]{2,1,0:T(8,128)S(1)}, f32[2,256,128]{2,1,0:T(8,128)S(1)}, u32[]{:S(2)}, u32[]{:S(2)}) %collective-permute-start.2) | collective-permute-done | bytes 262176 | tf_op jit(solution)/shard_map/ppermute | solution.py:740
  14.2 1.5 %collective-permute-start.5 = (f32[4,24,128]{2,1,0:T(8,128)S(1)}, f32[4,24,128]{2,1,0:T(8,128)S(1)}, u32[]{:S(2)}, u32[]{:S(2)}) collective-permute-start(f32[4,24,128]{2,1,0:T(8,128)S(1)} %pad_maximum_fusion.2), channel_id=1, source_target_pairs={{0,4},{4,0},{8,12},{12,8},{16,20},{20,16},{24,28},{28,24},{1,5},{5... | collective-permute-start | bytes 147464 | tf_op jit(solution)/shard_map/ppermute | solution.py:740
  15.7 2.5 %collective-permute-start.6 = (bf16[1,512,128]{2,1,0:T(8,128)(2,1)S(1)}, bf16[1,512,128]{2,1,0:T(8,128)(2,1)S(1)}, u32[]{:S(2)}, u32[]{:S(2)}) collective-permute-start(bf16[1,512,128]{2,1,0:T(8,128)(2,1)S(1)} %bitcast.17), channel_id=1, source_target_pairs={{0,16},{4,20},{8,24},{12,28},{16,0},{20,4},{24,8},{28,12},{1,17},{... | collective-permute-start | bytes 393224 | tf_op jit(solution)/shard_map/ppermute | solution.py:740
  18.2 1.5 %collective-permute-start.3 = (f32[2,256,128]{2,1,0:T(8,128)S(1)}, f32[2,256,128]{2,1,0:T(8,128)S(1)}, u32[]{:S(2)}, u32[]{:S(2)}) collective-permute-start(f32[2,256,128]{2,1,0:T(8,128)S(1)} %get-tuple-element.120), channel_id=1, source_target_pairs={{0,2},{1,3},{2,0},{3,1},{4,6},{5,7},{6,4},{7,5},{8,10},{9,11},{10,... | collective-permute-start | bytes 786440 | tf_op jit(solution)/shard_map/ppermute | solution.py:740
  19.7 6.3 %lag_kernel.1 = (f32[4,512,128]{2,1,0:T(8,128)S(1)}, f32[8,128]{1,0:T(8,128)S(1)}, f32[128,128]{1,0:T(8,128)S(1)}, f32[13,64,128]{2,1,0:T(8,128)S(1)}) custom-call(f32[1,24,128]{2,1,0:T(8,128)S(1)} %copy-done.2, f32[1,24,128]{2,1,0:T(8,128)S(1)} %collective-permute-done.refs_1_, f32[2,24,128]{2,1,0:T(8,128)S(1)} %collective-permute-done.1.refs_2_, ...), custom_call_target="tpu_custom_call" | custom-call | flops 6899999744 | bytes 1000 | tf_op jit(solution)/shard_map/lag_kernel/pallas_call | solution.py:53
  26.1 0.6 collective-permute-start.8
  26.6 1.6 %collective-permute-start.7 = (bf16[2,512,128]{2,1,0:T(8,128)(2,1)S(1)}, bf16[2,512,128]{2,1,0:T(8,128)(2,1)S(1)}, u32[]{:S(2)}, u32[]{:S(2)}) collective-permute-start(bf16[2,512,128]{2,1,0:T(8,128)(2,1)S(1)} %pad_maximum_fusion.refs_1_), channel_id=1, source_target_pairs={{0,8},{4,12},{8,0},{12,4},{16,24},{20,28},{24,16},{28,20},{1,9},{5... | collective-permute-start | bytes 786440 | tf_op jit(solution)/shard_map/ppermute | solution.py:740
  28.2 2.4 %collective-permute-done.4.refs_3_ = f32[2,256,128]{2,1,0:T(8,128)S(1)} collective-permute-done((f32[2,256,128]{2,1,0:T(8,128)S(1)}, f32[2,256,128]{2,1,0:T(8,128)S(1)}, u32[]{:S(2)}, u32[]{:S(2)}) %collective-permute-start.4) | collective-permute-done | bytes 262176 | tf_op jit(solution)/shard_map/ppermute | solution.py:740
  30.6 7.9 %doc_conv.1 = (bf16[2,256,128]{2,1,0:T(8,128)(2,1)S(1)}, bf16[2,256,128]{2,1,0:T(8,128)(2,1)S(1)}, bf16[2,256,128]{2,1,0:T(8,128)(2,1)S(1)}, bf16[2,256,128]{2,1...) custom-call(f32[2,256,128]{2,1,0:T(8,128)S(1)} %get-tuple-element.116.refs_0_, ...), custom_call_target="tpu_custom_call" | custom-call | flops 8049999872 | bytes 1000 | tf_op jit(solution)/shard_map/doc_conv/pallas_call | solution.py:53
  38.5 0.6 collective-permute-start.12
  39.1 0.8 collective-permute-start.9
  39.9 1.5 %collective-permute-start.10 = (bf16[2,256,128]{2,1,0:T(8,128)(2,1)S(1)}, bf16[2,256,128]{2,1,0:T(8,128)(2,1)S(1)}, u32[]{:S(2)}, u32[]{:S(2)}) collective-permute-start(bf16[2,256,128]{2,1,0:T(8,128)(2,1)S(1)} %get-tuple-element.138), channel_id=1, source_target_pairs={{0,2},{1,3},{2,0},{3,1},{4,6},{5,7},{6,4},{7,5},{8,10},{9,11},{10,... | collective-permute-start | bytes 393224 | tf_op jit(solution)/shard_map/ppermute | solution.py:740
  41.4 6.2 %collective-permute-done.12.refs_4_ = bf16[2,512,128]{2,1,0:T(8,128)(2,1)S(1)} collective-permute-done((bf16[2,512,128]{2,1,0:T(8,128)(2,1)S(1)}, bf16[2,512,128]{2,1,0:T(8,128)(2,1)S(1)}, u32[]{:S(2)}, u32[]{:S(2)}) %collective-permute-start.12) | collective-permute-done | bytes 262176 | tf_op jit(solution)/shard_map/ppermute | solution.py:740
  47.6 0.3 linear_rows.1
  48.0 0.7 copy-done.1
  48.7 4.9 %gated_linear.1 = (bf16[2,256,512]{2,1,0:T(8,128)(2,1)}, bf16[512,512]{1,0:T(8,128)(2,1)S(1)}, bf16[512,1024]{1,0:T(8,128)(2,1)S(1)}, f32[1,1024]{1,0:T(1,128)S(...) custom-call(bf16[2,256,128]{2,1,0:T(8,128)(2,1)S(1)} %get-tuple-elem, ...), custom_call_target="tpu_custom_call" | custom-call | flops 5750000128 | bytes 1000 | tf_op jit(solution)/shard_map/gated_linear/pallas_call | solution.py:53
  53.7 1.0 collective-permute-start.14
  54.8 0.7 collective-permute-start.15
  55.5 1.3 %weight_grad.1 = (bf16[512,128]{1,0:T(8,128)(2,1)S(1)}, bf16[512,128]{1,0:T(8,128)(2,1)S(1)}, bf16[512,128]{1,0:T(8,128)(2,1)S(1)}, bf16[512,128]{1,0:T(8,128)(2...) custom-call(bf16[512,512]{1,0:T(8,128)(2,1)S(1)} %get-tuple-element., ...), custom_call_target="tpu_custom_call" | custom-call | flops 1150000000 | bytes 1000 | tf_op jit(solution)/shard_map/weight_grad/pallas_call | solution.py:53
  56.8 0.6 collective-permute-start.16
  57.4 1.6 %collective-permute-start.17 = (bf16[512,128]{1,0:T(8,128)(2,1)S(1)}, bf16[512,128]{1,0:T(8,128)(2,1)S(1)}, u32[]{:S(2)}, u32[]{:S(2)}) collective-permute-start(bf16[512,128]{1,0:T(8,128)(2,1)S(1)} %get-tuple-element.162), channel_id=1, source_target_pairs={{0,8},{4,12},{8,0},{12,4},{16,24},{20,28},{24,16},{28,20},{1,9},{5... | collective-permute-start | bytes 393224 | tf_op jit(solution)/shard_map/ppermute | solution.py:740
  59.0 1.4 %collective-permute-start.18 = (bf16[512,128]{1,0:T(8,128)(2,1)S(1)}, bf16[512,128]{1,0:T(8,128)(2,1)S(1)}, u32[]{:S(2)}, u32[]{:S(2)}) collective-permute-start(bf16[512,128]{1,0:T(8,128)(2,1)S(1)} %get-tuple-element.163), channel_id=1, source_target_pairs={{0,12},{4,8},{8,4},{12,0},{16,28},{20,24},{24,20},{28,16},{1,13},{... | collective-permute-start | bytes 393224 | tf_op jit(solution)/shard_map/ppermute | solution.py:740
  60.4 0.4 collective-permute-start.19
  60.8 1.0 collective-permute-done.15.refs_3_
  61.8 1.5 %collective-permute-start.20 = (bf16[512,128]{1,0:T(8,128)(2,1)S(1)}, bf16[512,128]{1,0:T(8,128)(2,1)S(1)}, u32[]{:S(2)}, u32[]{:S(2)}) collective-permute-start(bf16[512,128]{1,0:T(8,128)(2,1)S(1)} %get-tuple-element.165), channel_id=1, source_target_pairs={{0,20},{4,16},{8,28},{12,24},{16,4},{20,0},{24,12},{28,8},{1,21},{... | collective-permute-start | bytes 393224 | tf_op jit(solution)/shard_map/ppermute | solution.py:740
  63.2 8.0 %doc_conv_grad.1 = (bf16[2,256,128]{2,1,0:T(8,128)(2,1)S(1)}, bf16[2,256,128]{2,1,0:T(8,128)(2,1)S(1)}, bf16[2,256,128]{2,1,0:T(8,128)(2,1)S(1)}, bf16[2,256,128...) custom-call(bf16[2,256,128]{2,1,0:T(8,128)(2,1)S(1)} %get-tuple-element.148.refs_0_, ...), custom_call_target="tpu_custom_call" | custom-call | flops 9200000000 | bytes 1000 | tf_op jit(solution)/shard_map/doc_conv_grad/pallas_call | solution.py:53
  71.3 2.3 %collective-permute-start.21 = (bf16[512,128]{1,0:T(8,128)(2,1)S(1)}, bf16[512,128]{1,0:T(8,128)(2,1)S(1)}, u32[]{:S(2)}, u32[]{:S(2)}) collective-permute-start(bf16[512,128]{1,0:T(8,128)(2,1)S(1)} %get-tuple-element.166), channel_id=1, source_target_pairs={{0,24},{4,28},{8,16},{12,20},{16,8},{20,12},{24,0},{28,4},{1,25},{... | collective-permute-start | bytes 393224 | tf_op jit(solution)/shard_map/ppermute | solution.py:740
  73.5 2.6 %collective-permute-start.22 = (bf16[512,128]{1,0:T(8,128)(2,1)S(1)}, bf16[512,128]{1,0:T(8,128)(2,1)S(1)}, u32[]{:S(2)}, u32[]{:S(2)}) collective-permute-start(bf16[512,128]{1,0:T(8,128)(2,1)S(1)} %get-tuple-element.167), channel_id=1, source_target_pairs={{0,28},{4,24},{8,20},{12,16},{16,12},{20,8},{24,4},{28,0},{1,29},{... | collective-permute-start | bytes 393224 | tf_op jit(solution)/shard_map/ppermute | solution.py:740
  76.1 0.8 collective-permute-start.24
  77.0 1.0 collective-permute-start.25
  78.0 10.8 %state_grad.1 = f32[8,24,128]{2,1,0:T(8,128)} custom-call(f32[128,128]{1,0:T(8,128)S(1)} %get-tuple-element.128.refs_9_.refs_5_.refs_8_.refs_11_.refs_0_.refs_2_, f32[13,64,128]{2,1,0:T(8,128)S(1)} %get-tuple-element.129.refs_10_.refs_6_.refs_9_.refs_12_.refs_1_.refs_3_, f32[4,512,128]{2,1,0:T(8,128)S(1)} %get-tuple-element.155.refs_2_, ...), custom_call_target="tpu_custom_call" | custom-call | flops 11500000256 | bytes 1000 | tf_op jit(solution)/shard_map/state_grad/pallas_call | solution.py:53
  88.9 3.8 %all-to-all-start = ((f32[8,24,128]{2,1,0:T(8,128)}), f32[8,24,128]{2,1,0:T(8,128)S(1)}, u32[]{:S(2)}, u32[]{:S(2)}) async-start(f32[8,24,128]{2,1,0:T(8,128)} %state_grad.1), calls=%async_computation | async-start | bytes 196608 | tf_op jit(solution)/shard_map/all_to_all | solution.py:900
  92.9 1.0 collective-permute-start.28
  94.0 1.0 collective-permute-start.27
  95.0 1.8 %layer_norm_grad.1 = bf16[2,256,512]{2,1,0:T(8,128)(2,1)} custom-call(bf16[2,256,128]{2,1,0:T(8,128)(2,1)S(1)} %get-tuple-element.185.refs_0_, bf16[2,256,128]{2,1,0:T(8,128)(2,1)S(1)} %collective-permute-done.23.refs_1_, bf16[2,256,128]{2,1,0:T(8,128)(2,1)S(1)} %collective-permute-done.24.refs_2_, bf16[2,256,128]{2,1,0:T(8,128)(2,1)S(1)} %collective-permute-done.25.refs_3_, ...), custom_call_target="tpu_custom_call" | custom-call | bytes 1000 | tf_op jit(solution)/shard_map/layer_norm_grad/pallas_call | solution.py:53
  96.8 1.3 %collective-permute-done.28.refs_7_ = bf16[512,128]{1,0:T(8,128)(2,1)S(1)} collective-permute-done((bf16[512,128]{1,0:T(8,128)(2,1)S(1)}, bf16[512,128]{1,0:T(8,128)(2,1)S(1)}, u32[]{:S(2)}, u32[]{:S(2)}) %collective-permute-start.28) | collective-permute-done | bytes 131104 | tf_op jit(solution)/shard_map/ppermute | solution.py:740
  98.1 3.4 %collective-permute-done.27.refs_6_ = bf16[512,128]{1,0:T(8,128)(2,1)S(1)} collective-permute-done((bf16[512,128]{1,0:T(8,128)(2,1)S(1)}, bf16[512,128]{1,0:T(8,128)(2,1)S(1)}, u32[]{:S(2)}, u32[]{:S(2)}) %collective-permute-start.27) | collective-permute-done | bytes 131104 | tf_op jit(solution)/shard_map/ppermute | solution.py:740
  101.5 0.4 collective-permute-start.31
  102.0 0.8 collective-permute-start.30
  102.8 0.7 collective-permute-start.29
  103.5 1.3 %collective-permute-done.31.refs_3_ = f32[24,128]{1,0:T(8,128)S(1)} collective-permute-done((f32[24,128]{1,0:T(8,128)S(1)}, f32[24,128]{1,0:T(8,128)S(1)}, u32[]{:S(2)}, u32[]{:S(2)}) %collective-permute-start.31) | collective-permute-done | bytes 12320 | tf_op jit(solution)/shard_map/ppermute | solution.py:740
  104.7 0.9 collective-permute-done.30.refs_2_
  105.7 0.9 last.1
  (46 shorter events, 0.8 us)
Async XLA Ops:
  2.4 6.3 %copy-start.2 = (f32[1,24,128]{2,1,0:T(8,128)S(1)}, f32[1,24,128]{2,1,0:T(8,128)}, u32[]{:S(2)}) copy-start(f32[1,24,128]{2,1,0:T(8,128)} %pack.1.refs_0_) | copy-start | bytes 36868
  2.4 8.0 %copy-start = (bf16[2,256,512]{2,1,0:T(8,128)(2,1)S(1)}, bf16[2,256,512]{2,1,0:T(8,128)(2,1)}, u32[]{:S(2)}) copy-start(bf16[2,256,512]{2,1,0:T(8,128)(2,1)} %refs_4_.5) | copy-start | bytes 1572868
  2.4 6.3 %collective-permute-start = (f32[1,24,128]{2,1,0:T(8,128)}, f32[1,24,128]{2,1,0:T(8,128)S(1)}, u32[]{:S(2)}, u32[]{:S(2)}) collective-permute-start(f32[1,24,128]{2,1,0:T(8,128)} %pack.1.refs_0_), channel_id=1, source_target_pairs={{0,16},{4,20},{8,24},{12,28},{16,0},{20,4},{24,8},{28,12},{1,17},{... | collective-permute-start | bytes 36872 | tf_op jit(solution)/shard_map/ppermute | solution.py:740
  8.7 7.0 %copy-start.4 = (bf16[512,128]{1,0:T(8,128)(2,1)S(1)}, bf16[512,128]{1,0:T(8,128)(2,1)}, u32[]{:S(2)}) copy-start(bf16[512,128]{1,0:T(8,128)(2,1)} %param.21) | copy-start | bytes 393220
  8.7 3.9 %collective-permute-start.1 = (f32[2,24,128]{2,1,0:T(8,128)S(1)}, f32[2,24,128]{2,1,0:T(8,128)S(1)}, u32[]{:S(2)}, u32[]{:S(2)}) collective-permute-start(f32[2,24,128]{2,1,0:T(8,128)S(1)} %pad_maximum_fusion.3), channel_id=1, source_target_pairs={{0,8},{4,12},{8,0},{12,4},{16,24},{20,28},{24,16},{28,20},{1,9},{5... | collective-permute-start | bytes 73736 | tf_op jit(solution)/shard_map/ppermute | solution.py:740
  12.6 1.5 %collective-permute-start.2 = (f32[2,256,128]{2,1,0:T(8,128)S(1)}, f32[2,256,128]{2,1,0:T(8,128)S(1)}, u32[]{:S(2)}, u32[]{:S(2)}) collective-permute-start(f32[2,256,128]{2,1,0:T(8,128)S(1)} %get-tuple-element.118), channel_id=1, source_target_pairs={{0,1},{1,0},{2,3},{3,2},{4,5},{5,4},{6,7},{7,6},{8,9},{9,8},{10,11... | collective-permute-start | bytes 786440 | tf_op jit(solution)/shard_map/ppermute | solution.py:740
  14.2 5.6 %collective-permute-start.5 = (f32[4,24,128]{2,1,0:T(8,128)S(1)}, f32[4,24,128]{2,1,0:T(8,128)S(1)}, u32[]{:S(2)}, u32[]{:S(2)}) collective-permute-start(f32[4,24,128]{2,1,0:T(8,128)S(1)} %pad_maximum_fusion.2), channel_id=1, source_target_pairs={{0,4},{4,0},{8,12},{12,8},{16,20},{20,16},{24,28},{28,24},{1,5},{5... | collective-permute-start | bytes 147464 | tf_op jit(solution)/shard_map/ppermute | solution.py:740
  15.7 15.0 %copy-start.3 = (s32[2,4]{1,0:T(2,128)S(1)}, s32[2,4]{1,0:T(2,128)}, u32[]{:S(2)}) copy-start(s32[2,4]{1,0:T(2,128)} %refs_5_.4) | copy-start | bytes 100
  15.7 10.3 %collective-permute-start.6 = (bf16[1,512,128]{2,1,0:T(8,128)(2,1)S(1)}, bf16[1,512,128]{2,1,0:T(8,128)(2,1)S(1)}, u32[]{:S(2)}, u32[]{:S(2)}) collective-permute-start(bf16[1,512,128]{2,1,0:T(8,128)(2,1)S(1)} %bitcast.17), channel_id=1, source_target_pairs={{0,16},{4,20},{8,24},{12,28},{16,0},{20,4},{24,8},{28,12},{1,17},{... | collective-permute-start | bytes 393224 | tf_op jit(solution)/shard_map/ppermute | solution.py:740
  18.2 10.0 %collective-permute-start.3 = (f32[2,256,128]{2,1,0:T(8,128)S(1)}, f32[2,256,128]{2,1,0:T(8,128)S(1)}, u32[]{:S(2)}, u32[]{:S(2)}) collective-permute-start(f32[2,256,128]{2,1,0:T(8,128)S(1)} %get-tuple-element.120), channel_id=1, source_target_pairs={{0,2},{1,3},{2,0},{3,1},{4,6},{5,7},{6,4},{7,5},{8,10},{9,11},{10,... | collective-permute-start | bytes 786440 | tf_op jit(solution)/shard_map/ppermute | solution.py:740
  19.7 10.9 %collective-permute-start.4 = (f32[2,256,128]{2,1,0:T(8,128)S(1)}, f32[2,256,128]{2,1,0:T(8,128)S(1)}, u32[]{:S(2)}, u32[]{:S(2)}) collective-permute-start(f32[2,256,128]{2,1,0:T(8,128)S(1)} %get-tuple-element.121), channel_id=1, source_target_pairs={{0,3},{1,2},{2,1},{3,0},{4,7},{5,6},{6,5},{7,4},{8,11},{9,10},{10,... | collective-permute-start | bytes 786440 | tf_op jit(solution)/shard_map/ppermute | solution.py:740
  26.1 12.5 %collective-permute-start.8 = (bf16[2,512,128]{2,1,0:T(8,128)(2,1)S(1)}, bf16[2,512,128]{2,1,0:T(8,128)(2,1)S(1)}, u32[]{:S(2)}, u32[]{:S(2)}) collective-permute-start(bf16[2,512,128]{2,1,0:T(8,128)(2,1)S(1)} %pad_maximum_fusion.refs_1_), channel_id=1, source_target_pairs={{0,4},{4,0},{8,12},{12,8},{16,20},{20,16},{24,28},{28,24},{1,5},{5... | collective-permute-start | bytes 786440 | tf_op jit(solution)/shard_map/ppermute | solution.py:740
  26.6 11.9 %collective-permute-start.7 = (bf16[2,512,128]{2,1,0:T(8,128)(2,1)S(1)}, bf16[2,512,128]{2,1,0:T(8,128)(2,1)S(1)}, u32[]{:S(2)}, u32[]{:S(2)}) collective-permute-start(bf16[2,512,128]{2,1,0:T(8,128)(2,1)S(1)} %pad_maximum_fusion.refs_1_), channel_id=1, source_target_pairs={{0,8},{4,12},{8,0},{12,4},{16,24},{20,28},{24,16},{28,20},{1,9},{5... | collective-permute-start | bytes 786440 | tf_op jit(solution)/shard_map/ppermute | solution.py:740
  38.5 9.1 %collective-permute-start.12 = (bf16[2,512,128]{2,1,0:T(8,128)(2,1)S(1)}, bf16[2,512,128]{2,1,0:T(8,128)(2,1)S(1)}, u32[]{:S(2)}, u32[]{:S(2)}) collective-permute-start(bf16[2,512,128]{2,1,0:T(8,128)(2,1)S(1)} %collective-permute-done.7.refs_2_), channel_id=1, source_target_pairs={{0,4},{4,0},{8,12},{12,8},{16,20},{20,16},{24,28},{28,24},{1,5},{5... | collective-permute-start | bytes 786440 | tf_op jit(solution)/shard_map/ppermute | solution.py:740
  39.1 2.3 %collective-permute-start.9 = (bf16[2,256,128]{2,1,0:T(8,128)(2,1)S(1)}, bf16[2,256,128]{2,1,0:T(8,128)(2,1)S(1)}, u32[]{:S(2)}, u32[]{:S(2)}) collective-permute-start(bf16[2,256,128]{2,1,0:T(8,128)(2,1)S(1)} %get-tuple-element.136), channel_id=1, source_target_pairs={{0,1},{1,0},{2,3},{3,2},{4,5},{5,4},{6,7},{7,6},{8,9},{9,8},{10,11... | collective-permute-start | bytes 393224 | tf_op jit(solution)/shard_map/ppermute | solution.py:740
  39.9 8.0 %collective-permute-start.10 = (bf16[2,256,128]{2,1,0:T(8,128)(2,1)S(1)}, bf16[2,256,128]{2,1,0:T(8,128)(2,1)S(1)}, u32[]{:S(2)}, u32[]{:S(2)}) collective-permute-start(bf16[2,256,128]{2,1,0:T(8,128)(2,1)S(1)} %get-tuple-element.138), channel_id=1, source_target_pairs={{0,2},{1,3},{2,0},{3,1},{4,6},{5,7},{6,4},{7,5},{8,10},{9,11},{10,... | collective-permute-start | bytes 393224 | tf_op jit(solution)/shard_map/ppermute | solution.py:740
  41.4 6.5 %collective-permute-start.11 = (bf16[2,256,128]{2,1,0:T(8,128)(2,1)S(1)}, bf16[2,256,128]{2,1,0:T(8,128)(2,1)S(1)}, u32[]{:S(2)}, u32[]{:S(2)}) collective-permute-start(bf16[2,256,128]{2,1,0:T(8,128)(2,1)S(1)} %get-tuple-element.139), channel_id=1, source_target_pairs={{0,3},{1,2},{2,1},{3,0},{4,7},{5,6},{6,5},{7,4},{8,11},{9,10},{10,... | collective-permute-start | bytes 393224 | tf_op jit(solution)/shard_map/ppermute | solution.py:740
  47.6 1.0 copy-start.1
  53.5 1.9 %collective-permute-start.13 = (bf16[2,256,128]{2,1,0:T(8,128)(2,1)S(1)}, bf16[2,256,128]{2,1,0:T(8,128)(2,1)S(1)}, u32[]{:S(2)}, u32[]{:S(2)}) collective-permute-start(bf16[2,256,128]{2,1,0:T(8,128)(2,1)S(1)} %get-tuple-element.151), channel_id=1, source_target_pairs={{0,1},{1,0},{2,3},{3,2},{4,5},{5,4},{6,7},{7,6},{8,9},{9,8},{10,11... | collective-permute-start | bytes 393224 | tf_op jit(solution)/shard_map/ppermute | solution.py:740
  53.7 6.6 %collective-permute-start.14 = (bf16[2,256,128]{2,1,0:T(8,128)(2,1)S(1)}, bf16[2,256,128]{2,1,0:T(8,128)(2,1)S(1)}, u32[]{:S(2)}, u32[]{:S(2)}) collective-permute-start(bf16[2,256,128]{2,1,0:T(8,128)(2,1)S(1)} %get-tuple-element.153), channel_id=1, source_target_pairs={{0,2},{1,3},{2,0},{3,1},{4,6},{5,7},{6,4},{7,5},{8,10},{9,11},{10,... | collective-permute-start | bytes 393224 | tf_op jit(solution)/shard_map/ppermute | solution.py:740
  54.8 7.0 %collective-permute-start.15 = (bf16[2,256,128]{2,1,0:T(8,128)(2,1)S(1)}, bf16[2,256,128]{2,1,0:T(8,128)(2,1)S(1)}, u32[]{:S(2)}, u32[]{:S(2)}) collective-permute-start(bf16[2,256,128]{2,1,0:T(8,128)(2,1)S(1)} %get-tuple-element.154), channel_id=1, source_target_pairs={{0,3},{1,2},{2,1},{3,0},{4,7},{5,6},{6,5},{7,4},{8,11},{9,10},{10,... | collective-permute-start | bytes 393224 | tf_op jit(solution)/shard_map/ppermute | solution.py:740
  56.8 14.5 %collective-permute-start.16 = (bf16[512,128]{1,0:T(8,128)(2,1)S(1)}, bf16[512,128]{1,0:T(8,128)(2,1)S(1)}, u32[]{:S(2)}, u32[]{:S(2)}) collective-permute-start(bf16[512,128]{1,0:T(8,128)(2,1)S(1)} %get-tuple-element.161), channel_id=1, source_target_pairs={{0,4},{4,0},{8,12},{12,8},{16,20},{20,16},{24,28},{28,24},{1,5},{5... | collective-permute-start | bytes 393224 | tf_op jit(solution)/shard_map/ppermute | solution.py:740
  57.4 16.2 %collective-permute-start.17 = (bf16[512,128]{1,0:T(8,128)(2,1)S(1)}, bf16[512,128]{1,0:T(8,128)(2,1)S(1)}, u32[]{:S(2)}, u32[]{:S(2)}) collective-permute-start(bf16[512,128]{1,0:T(8,128)(2,1)S(1)} %get-tuple-element.162), channel_id=1, source_target_pairs={{0,8},{4,12},{8,0},{12,4},{16,24},{20,28},{24,16},{28,20},{1,9},{5... | collective-permute-start | bytes 393224 | tf_op jit(solution)/shard_map/ppermute | solution.py:740
  59.0 17.1 %collective-permute-start.18 = (bf16[512,128]{1,0:T(8,128)(2,1)S(1)}, bf16[512,128]{1,0:T(8,128)(2,1)S(1)}, u32[]{:S(2)}, u32[]{:S(2)}) collective-permute-start(bf16[512,128]{1,0:T(8,128)(2,1)S(1)} %get-tuple-element.163), channel_id=1, source_target_pairs={{0,12},{4,8},{8,4},{12,0},{16,28},{20,24},{24,20},{28,16},{1,13},{... | collective-permute-start | bytes 393224 | tf_op jit(solution)/shard_map/ppermute | solution.py:740
  60.4 15.8 %collective-permute-start.19 = (bf16[512,128]{1,0:T(8,128)(2,1)S(1)}, bf16[512,128]{1,0:T(8,128)(2,1)S(1)}, u32[]{:S(2)}, u32[]{:S(2)}) collective-permute-start(bf16[512,128]{1,0:T(8,128)(2,1)S(1)} %get-tuple-element.164), channel_id=1, source_target_pairs={{0,16},{4,20},{8,24},{12,28},{16,0},{20,4},{24,8},{28,12},{1,17},{... | collective-permute-start | bytes 393224 | tf_op jit(solution)/shard_map/ppermute | solution.py:740
  61.8 15.2 %collective-permute-start.20 = (bf16[512,128]{1,0:T(8,128)(2,1)S(1)}, bf16[512,128]{1,0:T(8,128)(2,1)S(1)}, u32[]{:S(2)}, u32[]{:S(2)}) collective-permute-start(bf16[512,128]{1,0:T(8,128)(2,1)S(1)} %get-tuple-element.165), channel_id=1, source_target_pairs={{0,20},{4,16},{8,28},{12,24},{16,4},{20,0},{24,12},{28,8},{1,21},{... | collective-permute-start | bytes 393224 | tf_op jit(solution)/shard_map/ppermute | solution.py:740
  71.3 17.6 %collective-permute-start.21 = (bf16[512,128]{1,0:T(8,128)(2,1)S(1)}, bf16[512,128]{1,0:T(8,128)(2,1)S(1)}, u32[]{:S(2)}, u32[]{:S(2)}) collective-permute-start(bf16[512,128]{1,0:T(8,128)(2,1)S(1)} %get-tuple-element.166), channel_id=1, source_target_pairs={{0,24},{4,28},{8,16},{12,20},{16,8},{20,12},{24,0},{28,4},{1,25},{... | collective-permute-start | bytes 393224 | tf_op jit(solution)/shard_map/ppermute | solution.py:740
  73.5 15.3 %collective-permute-start.22 = (bf16[512,128]{1,0:T(8,128)(2,1)S(1)}, bf16[512,128]{1,0:T(8,128)(2,1)S(1)}, u32[]{:S(2)}, u32[]{:S(2)}) collective-permute-start(bf16[512,128]{1,0:T(8,128)(2,1)S(1)} %get-tuple-element.167), channel_id=1, source_target_pairs={{0,28},{4,24},{8,20},{12,16},{16,12},{20,8},{24,4},{28,0},{1,29},{... | collective-permute-start | bytes 393224 | tf_op jit(solution)/shard_map/ppermute | solution.py:740
  76.1 12.7 %collective-permute-start.23 = (bf16[2,256,128]{2,1,0:T(8,128)(2,1)S(1)}, bf16[2,256,128]{2,1,0:T(8,128)(2,1)S(1)}, u32[]{:S(2)}, u32[]{:S(2)}) collective-permute-start(bf16[2,256,128]{2,1,0:T(8,128)(2,1)S(1)} %get-tuple-element.169), channel_id=1, source_target_pairs={{0,1},{1,0},{2,3},{3,2},{4,5},{5,4},{6,7},{7,6},{8,9},{9,8},{10,11... | collective-permute-start | bytes 393224 | tf_op jit(solution)/shard_map/ppermute | solution.py:740
  76.1 12.7 %collective-permute-start.24 = (bf16[2,256,128]{2,1,0:T(8,128)(2,1)S(1)}, bf16[2,256,128]{2,1,0:T(8,128)(2,1)S(1)}, u32[]{:S(2)}, u32[]{:S(2)}) collective-permute-start(bf16[2,256,128]{2,1,0:T(8,128)(2,1)S(1)} %get-tuple-element.170), channel_id=1, source_target_pairs={{0,2},{1,3},{2,0},{3,1},{4,6},{5,7},{6,4},{7,5},{8,10},{9,11},{10,... | collective-permute-start | bytes 393224 | tf_op jit(solution)/shard_map/ppermute | solution.py:740
  77.0 11.9 %collective-permute-start.25 = (bf16[2,256,128]{2,1,0:T(8,128)(2,1)S(1)}, bf16[2,256,128]{2,1,0:T(8,128)(2,1)S(1)}, u32[]{:S(2)}, u32[]{:S(2)}) collective-permute-start(bf16[2,256,128]{2,1,0:T(8,128)(2,1)S(1)} %get-tuple-element.171), channel_id=1, source_target_pairs={{0,3},{1,2},{2,1},{3,0},{4,7},{5,6},{6,5},{7,4},{8,11},{9,10},{10,... | collective-permute-start | bytes 393224 | tf_op jit(solution)/shard_map/ppermute | solution.py:740
  88.9 12.6 %all-to-all-start = ((f32[8,24,128]{2,1,0:T(8,128)}), f32[8,24,128]{2,1,0:T(8,128)S(1)}, u32[]{:S(2)}, u32[]{:S(2)}) async-start(f32[8,24,128]{2,1,0:T(8,128)} %state_grad.1), calls=%async_computation | async-start | bytes 196608 | tf_op jit(solution)/shard_map/all_to_all | solution.py:900
  92.8 2.2 %collective-permute-start.26 = (bf16[512,128]{1,0:T(8,128)(2,1)S(1)}, bf16[512,128]{1,0:T(8,128)(2,1)S(1)}, u32[]{:S(2)}, u32[]{:S(2)}) collective-permute-start(bf16[512,128]{1,0:T(8,128)(2,1)S(1)} %weight_sum.1.refs_4_), channel_id=1, source_target_pairs={{0,1},{1,0},{2,3},{3,2},{4,5},{5,4},{6,7},{7,6},{8,9},{9,8},{10,11... | collective-permute-start | bytes 393224 | tf_op jit(solution)/shard_map/ppermute | solution.py:740
  92.9 5.2 %collective-permute-start.28 = (bf16[512,128]{1,0:T(8,128)(2,1)S(1)}, bf16[512,128]{1,0:T(8,128)(2,1)S(1)}, u32[]{:S(2)}, u32[]{:S(2)}) collective-permute-start(bf16[512,128]{1,0:T(8,128)(2,1)S(1)} %weight_sum.1.refs_4_), channel_id=1, source_target_pairs={{0,3},{1,2},{2,1},{3,0},{4,7},{5,6},{6,5},{7,4},{8,11},{9,10},{10,... | collective-permute-start | bytes 393224 | tf_op jit(solution)/shard_map/ppermute | solution.py:740
  94.0 7.6 %collective-permute-start.27 = (bf16[512,128]{1,0:T(8,128)(2,1)S(1)}, bf16[512,128]{1,0:T(8,128)(2,1)S(1)}, u32[]{:S(2)}, u32[]{:S(2)}) collective-permute-start(bf16[512,128]{1,0:T(8,128)(2,1)S(1)} %weight_sum.1.refs_4_), channel_id=1, source_target_pairs={{0,2},{1,3},{2,0},{3,1},{4,6},{5,7},{6,4},{7,5},{8,10},{9,11},{10,... | collective-permute-start | bytes 393224 | tf_op jit(solution)/shard_map/ppermute | solution.py:740
  101.5 3.2 %collective-permute-start.31 = (f32[24,128]{1,0:T(8,128)S(1)}, f32[24,128]{1,0:T(8,128)S(1)}, u32[]{:S(2)}, u32[]{:S(2)}) collective-permute-start(f32[24,128]{1,0:T(8,128)S(1)} %small_sum.1.refs_0_), channel_id=1, source_target_pairs={{0,3},{1,2},{2,1},{3,0},{4,7},{5,6},{6,5},{7,4},{8,11},{9,10},{10,... | collective-permute-start | bytes 36872 | tf_op jit(solution)/shard_map/ppermute | solution.py:740
  102.0 3.7 %collective-permute-start.30 = (f32[24,128]{1,0:T(8,128)S(1)}, f32[24,128]{1,0:T(8,128)S(1)}, u32[]{:S(2)}, u32[]{:S(2)}) collective-permute-start(f32[24,128]{1,0:T(8,128)S(1)} %small_sum.1.refs_0_), channel_id=1, source_target_pairs={{0,2},{1,3},{2,0},{3,1},{4,6},{5,7},{6,4},{7,5},{8,10},{9,11},{10,... | collective-permute-start | bytes 36872 | tf_op jit(solution)/shard_map/ppermute | solution.py:740
  102.8 2.9 %collective-permute-start.29 = (f32[24,128]{1,0:T(8,128)S(1)}, f32[24,128]{1,0:T(8,128)S(1)}, u32[]{:S(2)}, u32[]{:S(2)}) collective-permute-start(f32[24,128]{1,0:T(8,128)S(1)} %small_sum.1.refs_0_), channel_id=1, source_target_pairs={{0,1},{1,0},{2,3},{3,2},{4,5},{5,4},{6,7},{7,6},{8,9},{9,8},{10,11... | collective-permute-start | bytes 36872 | tf_op jit(solution)/shard_map/ppermute | solution.py:740

commit v3 on v2

--- a/solution.py
+++ b/solution.py
@@ -124,19 +124,14 @@
     return jnp.where(iota((block, lanes), 0) & 1 > 0, -1.0, 1.0)
 
 
-def table_kernel(f_ref, ft_ref):
-    block = ft_ref.shape[0]
-    for ref, flip in ((f_ref, 0), (ft_ref, 1)):
-        k, j = iota((block, block), flip), iota((block, block), 1 - flip)
-        theta = (((2 * k + 1) * j) % (4 * block)).astype(f32) * np.float32(np.pi / (2 * block))
-        for half, value in ((0, jnp.cos(theta)), (1, -jnp.sin(theta))):
-            hi, lo = halves(value)
-            for third, part in enumerate((hi, hi, lo)):
-                if flip:
-                    at = (2 * third + half) * block
-                    ref[:, at : at + block] = part
-                else:
-                    ref[half * block : (half + 1) * block, third * block : (third + 1) * block] = part
+def dft_tables(block):
+    k, j = np.arange(block)[:, None], np.arange(block)[None, :]
+    theta = np.pi * (((2 * k + 1) * j) % (4 * block)) / (2 * block)
+    full = np.concatenate([np.cos(theta), -np.sin(theta)], axis=0)
+    high = full.astype(jnp.bfloat16)
+    low = (full - high.astype(np.float64)).astype(jnp.bfloat16)
+    return (jnp.asarray(np.concatenate([high, high, low], axis=1)),
+            jnp.asarray(np.concatenate([high.T, high.T, low.T], axis=1)))
 
 
 def moved(x, by):
@@ -170,7 +165,7 @@
 
 def lag_kernel(sub, length, masks, n_parts, *refs):
     pieces, refs = refs[:n_parts], refs[n_parts:]
-    f_ref, kh_ref, vec_ref, w_out, term_out, w_ref, term_ref, k_scr, z_scr, rhs_scr, kf_scr, sems = refs
+    f_ref, kh_ref, vec_ref, w_ref, term_ref, k_scr, z_scr, rhs_scr, kf_scr = refs
     slots = [piece.at[t] for piece in pieces for t in range(piece.shape[0])]
     ndp = len(slots)
     me = lax.axis_index("dp")
@@ -201,9 +196,6 @@
     terms = state_terms(lam, imag, vec_ref[0:1], float(length))
     for slot, value in enumerate(terms):
         term_ref[slot] = value
-    saves = [pltpu.make_async_copy(w_ref, w_out, sems.at[0]), pltpu.make_async_copy(term_ref, term_out, sems.at[1])]
-    for save in saves:
-        save.start()
     z_scr[0], z_scr[1] = cmul(w_ref[0:nstate], w_ref[nstate:], terms[11], terms[12])
     k_scr[...] = jnp.zeros_like(k_scr)
 
@@ -240,8 +232,6 @@
             im = im + sign * kf_scr[:block, past]
         kh_ref[p, :block] = re * (1.0 / block)
         kh_ref[p, block:] = im * (1.0 / block)
-    for save in saves:
-        save.wait()
 
 
 def members(own, sub, c, width, wide):
@@ -333,13 +323,10 @@
 CHUNK = 64
 
 
-def arrivals(x_refs, x_scr, len_ref, len_scr, sems):
-    me = lax.axis_index("seq")
-    copies = [pltpu.make_async_copy(len_ref, len_scr, sems.at[0])]
-    for d, x_ref in enumerate(x_refs):
-        for s in range(x_ref.shape[0]):
-            copies.append(pltpu.make_async_copy(x_ref.at[s], x_scr.at[s, me ^ d], sems.at[len(copies)]))
-    return copies
+def lengths_in(len_ref, len_scr, sem):
+    copy = pltpu.make_async_copy(len_ref, len_scr, sem)
+    copy.start()
+    copy.wait()
 
 
 def split_rows(y_scr, rows, cols, value, block, half):
@@ -355,15 +342,14 @@
 
 
 def conv_kernel(x0, x1, x2, x3, len_ref, vec_ref, kh_ref, f_ref, ft_ref,
-                o0, o1, o2, o3, s_out, x_out, len_scr, cut_ref, x_scr, rhs_scr, s_scr, acc_scr, y_scr, out_scr, sems):
+                o0, o1, o2, o3, s_scr, x_scr, len_scr, cut_ref, rhs_scr, acc_scr, y_scr, out_scr, sem):
     count, block, lanes = x0.shape
     parts = kh_ref.shape[0]
     me = lax.axis_index("seq")
-    copies = arrivals((x0, x1, x2, x3), x_scr, len_ref, len_scr, sems)
-    for copy in copies:
-        copy.start()
-    for copy in copies:
-        copy.wait()
+    lengths_in(len_ref, len_scr, sem)
+    for d, x_ref in enumerate((x0, x1, x2, x3)):
+        for s in range(count):
+            x_scr[s, me ^ d] = x_ref[s]
     segments(len_scr, cut_ref, block, parts)
     gain, bias = vec_ref[2:3], vec_ref[3:4]
     items = cut_ref.shape[1] - 1
@@ -373,10 +359,6 @@
             cols = slice((j * count + s) * lanes, (j * count + s + 1) * lanes)
             stack3(rhs_scr, cols, jnp.where(keep, x_scr[s, b] * gain + bias, 0.0))
     s_scr[...] = dot(f_ref[...], rhs_scr[...])
-    saves = [pltpu.make_async_copy(s_scr, s_out, sems.at[len(copies)]),
-             pltpu.make_async_copy(x_scr, x_out, sems.at[len(copies) + 1])]
-    for save in saves:
-        save.start()
 
     def own(j, _):
         for s in range(count):
@@ -416,24 +398,19 @@
     for d, o_ref in enumerate((o0, o1, o2, o3)):
         for s in range(count):
             o_ref[s] = out_scr[s, me ^ d].astype(bf16)
-    for save in saves:
-        save.wait()
-
-
-def back_kernel(c0, c1, c2, c3, x_ref, len_ref, s_ref, vec_ref, kh_ref, f_ref, ft_ref,
+
+
+def back_kernel(c0, c1, c2, c3, x_scr, len_ref, s_scr, vec_ref, kh_ref, f_ref, ft_ref,
                 g0, g1, g2, g3, dkh_ref, dvec_ref,
-                len_scr, cut_ref, v_scr, x_scr, rhs_scr, s_scr, sv_scr, acc_scr, y_scr, du_scr, sems):
+                len_scr, cut_ref, v_scr, rhs_scr, sv_scr, acc_scr, y_scr, du_scr, sem):
     count, block, lanes = c0.shape
     parts = kh_ref.shape[0]
     me = lax.axis_index("seq")
-    copies = arrivals((c0, c1, c2, c3), v_scr, len_ref, len_scr, sems)
-    later = [pltpu.make_async_copy(s_ref, s_scr, sems.at[len(copies)]),
-             pltpu.make_async_copy(x_ref, x_scr, sems.at[len(copies) + 1])]
-    for copy in copies + later:
-        copy.start()
+    lengths_in(len_ref, len_scr, sem)
+    for d, c_ref in enumerate((c0, c1, c2, c3)):
+        for s in range(count):
+            v_scr[s, me ^ d] = c_ref[s]
     dkh_ref[...] = jnp.zeros_like(dkh_ref)
-    for copy in copies:
-        copy.wait()
     segments(len_scr, cut_ref, block, parts)
     items = cut_ref.shape[1] - 1
     for j in range(items):
@@ -444,7 +421,6 @@
             rhs_scr[0:block, cols] = v
             rhs_scr[block:, cols] = v
     sv_scr[...] = dot(f_ref[:, block:], rhs_scr[...])
-    later[0].wait()
 
     def own(j, _):
         for s in range(count):
@@ -487,8 +463,6 @@
             b, keep = within(cut_ref, s, j, block, lanes)
             cols = slice((j * count + s) * lanes, (j * count + s + 1) * lanes)
             du_scr[s, b] = jnp.where(keep, acc_scr[0:block, cols], du_scr[s, b])
-    for copy in later[1:]:
-        copy.wait()
     gain = vec_ref[2:3]
     d_gain = jnp.zeros((8, lanes), f32)
     d_bias = jnp.zeros((8, lanes), f32)
@@ -511,7 +485,8 @@
 
 
 def dense_kernel(q0, q1, q2, q3, x_any, c_any, w_ref, lb_ref,
-                 out_ref, act_ref, dpre_ref, dlb_ref, d0, d1, d2, d3, x_ref, c_ref, slope_scr, pre_scr, dact_scr, sems):
+                 out_ref, dlb_ref, d0, d1, d2, d3, stay_ref, send_ref,
+                 x_ref, c_ref, act_ref, dpre_ref, slope_scr, pre_scr, dact_scr, sems):
     count, block, wide = q0.shape
     width = act_ref.shape[1]
     me = lax.axis_index("seq")
@@ -563,6 +538,8 @@
 
     lb_sum = lax.fori_loop(0, count, sequence, jnp.zeros((8, 2 * width), f32))
     dlb_ref[...] = jnp.sum(lb_sum, axis=0, keepdims=True)
+    for d in range(4):
+        (send_ref if d & 1 else stay_ref)[d // 2] = dot(act_ref[:, cols_of(d)], dpre_ref[...], TN).astype(bf16)
 
 
 def rows_kernel(sub, nseq, masks, shared_ref, *refs):
@@ -571,11 +548,13 @@
     span = o_ref.shape[0] // nseq
     me = lax.axis_index("dp")
     bias_row = shared_ref.shape[1] - 8 + 2
+    for t, mask in enumerate(masks):
+        at = pl.ds(pl.multiple_of((me ^ mask) * cols, cols), cols)
+        lb_ref[:, at] = shared_ref[t, bias_row : bias_row + 1, 0:cols]
     t = 0
     for w_ref in w_refs:
         for slot in range(w_ref.shape[0]):
             at = pl.ds(pl.multiple_of((me ^ masks[t]) * cols, cols), cols)
-            lb_ref[:, at] = shared_ref[t, bias_row : bias_row + 1, 0:cols]
             t += 1
             for c in range(nseq):
                 for i in range(span // sub):
@@ -584,27 +563,31 @@
                     ]
 
 
-def weight_kernel(act_ref, dpre_ref, *o_refs):
-    ndp = len(o_refs)
-    part = o_refs[0].shape[1]
-    for d, o_ref in enumerate(o_refs):
-        at = pl.ds(pl.multiple_of((lax.axis_index("dp") ^ d) * part, part), part)
-        o_ref[...] = dot(act_ref[...], dpre_ref[:, at], TN).astype(bf16)
-
-
-def sum_all_kernel(*refs):
-    *x_refs, o_ref = refs
-    total = x_refs[0][...].astype(f32)
-    for x_ref in x_refs[1:]:
-        total = total + x_ref[...].astype(f32)
-    o_ref[...] = total.astype(o_ref.dtype)
-
-
-def state_grad_kernel(sub, length, w_any, term_any, dkh_ref, dvec_ref, dlb_ref, ft_ref, o_ref,
-                      w_ref, term_ref, dk_scr, f_scr, dw_scr, y_scr, sems):
-    loads = [pltpu.make_async_copy(w_any, w_ref, sems.at[0]), pltpu.make_async_copy(term_any, term_ref, sems.at[1])]
-    for load in loads:
-        load.start()
+def halve_kernel(mine_ref, other_ref, stay_ref, send_ref):
+    for k in range(mine_ref.shape[0]):
+        total = mine_ref[k].astype(f32) + other_ref[k].astype(f32)
+        (send_ref if k & 1 else stay_ref)[k // 2] = total.astype(stay_ref.dtype)
+
+
+def deal_kernel(mine_ref, other_ref, stay_ref, send_ref):
+    part = stay_ref.shape[2]
+    me = lax.axis_index("dp")
+    for d in range(2 * stay_ref.shape[0]):
+        cols = pl.ds(pl.multiple_of((me ^ d) * part, part), part)
+        (send_ref if d & 1 else stay_ref)[d // 2] = mine_ref[0, :, cols].astype(f32) + other_ref[0, :, cols].astype(f32)
+
+
+def merge_kernel(x_ref, mine_ref, other_ref, o_ref):
+    rows = x_ref.shape[1]
+    total = x_ref[0]
+    for i in range(1, x_ref.shape[0]):
+        total = total + x_ref[i]
+    o_ref[0:rows] = total
+    o_ref[rows:] = mine_ref[0] + other_ref[0]
+
+
+def state_grad_kernel(sub, length, w_ref, term_ref, dkh_ref, dvec_ref, dlb_ref, ft_ref, o_ref,
+                      dk_scr, f_scr, dw_scr, y_scr):
     ndp = o_ref.shape[0]
     n_w, lanes = w_ref.shape
     nstate = n_w // 2
@@ -624,8 +607,6 @@
     for p in range(parts):
         dk_scr[p * block : (p + 1) * block] = all_lags[:, p * lanes : (p + 1) * lanes]
     at8 = iota((8, lanes), 0).astype(f32)
-    for load in loads:
-        load.wait()
 
     def one(n, _):
         (fr, fi), w = rows8(term_ref[2, pl.ds(n, 1), :], term_ref[3, pl.ds(n, 1), :])
@@ -704,35 +685,35 @@
     o_ref[...] = total.astype(o_ref.dtype)
 
 
-def last_kernel(sub, m0, m1, m2, m3, w0, w1, w2, w3, w_ref, step_ref, skip_ref, gain_ref, bias_ref,
-                lam_ref, imag_ref, lb_ref, dw_ref):
+def last_kernel(sub, rows, *refs):
+    *parts, w_ref, step_ref, skip_ref, gain_ref, bias_ref, lam_ref, imag_ref, lb_ref, dw_ref = refs
     n_w, own = w_ref.shape
+    nseq = LANES * own // sub // LANES
+    parts, dws = parts[:nseq], parts[nseq:]
     groups = LANES // sub
     height = n_w // groups
     per, cols = lam_ref.shape[1], lb_ref.shape[1]
     group = iota((1, LANES), 1) // sub
-    parts = (m0, m1, m2, m3)
+    me = lax.axis_index("seq")
+    small = [part[0:rows] for part in parts]
     for u in range(groups):
-        acc = jnp.zeros(m0.shape, f32)
-        for d, m_ref in enumerate(parts):
-            c = lax.axis_index("seq") ^ d
-            acc = jnp.where(group == c, pltpu.roll(m_ref[...], (c - u) * sub + LANES, 1), acc)
+        acc = jnp.zeros((rows, LANES), f32)
+        for d, value in enumerate(small):
+            c = me ^ d
+            acc = jnp.where(group == c, pltpu.roll(value, (c - u) * sub + LANES, 1), acc)
         w_ref[u * height : (u + 1) * height] = acc[0:height, 0:own]
         if u < 4:
             (step_ref, skip_ref, gain_ref, bias_ref)[u][...] = acc[height : height + 1, 0:own]
-    total = m0[...] + m1[...] + m2[...] + m3[...]
+    total = sum(small[1:], small[0])
     lam_ref[...] = total[height + 1 : height + 2, 0:per]
     imag_ref[...] = pltpu.roll(total, LANES - per, 1)[height + 1 : height + 2, 0:per]
     lb_ref[...] = total[height + 2 : height + 3, 0:cols]
-    nseq = len(parts)
-    width = w0.shape[0]
-    span = width // nseq
-    for c in range(nseq):
-        rows = slice(c * span, (c + 1) * span)
-        whole = w0[rows].astype(f32) + w1[rows].astype(f32) + w2[rows].astype(f32) + w3[rows].astype(f32)
-        for i in range(span // sub):
-            at = (i * nseq + c) * sub
-            dw_ref[at : at + sub] = whole[i * sub : (i + 1) * sub]
+    for d in range(nseq):
+        part_ref, first = (dws[d], 0) if dws else (parts[d], rows)
+        c = me ^ d
+        for i in range((part_ref.shape[0] - first) // sub):
+            at = pl.multiple_of((i * nseq + c) * sub, sub)
+            dw_ref[pl.ds(at, sub)] = part_ref[first + i * sub : first + (i + 1) * sub]
 
 
 def swap(x, axis, by):
@@ -779,38 +760,34 @@
     piece, piece32 = shape((count, block, wide), bf16), shape((count, block, wide))
     shared, shared_parts = packed, [packed]
     w_slots = [lin_weight[None]]
-    f_table = hats = None
+    f_table, ft_table = dft_tables(block)
+    w_more = hats = None
     for number, step in enumerate(steps):
-        if number == 2:
-            shared, hats[1] = tie(shared, hats[1])
         more = swap(shared, "dp", step)
         if number == 0:
-            f_table, ft_table = call(
-                table_kernel, [shape((2 * block, 3 * block), bf16), shape((block, 6 * block), bf16)], [], name="tables", us=2
-            )()
-            more, f_table, ft_table, x_late = tie(more, f_table, ft_table, block_in)
-        elif number == 1:
+            x_late, _ = tie(block_in, packed)
             hats = call(
                 partial(ln_kernel, own, sub), [piece32] * nseq, [AN],
                 scratch=[pltpu.VMEM((count, block, width), bf16), DMA((count,))], name="layer_norm", us=2,
             )(x_late)
             more, *hats = tie(more, *hats)
+        elif number == 1:
             hats = trade(hats, "seq")
+            more, hats[1] = tie(more, hats[1])
+        elif number == 2:
+            w_more = swap(w_slots[0], "dp", steps[0])
         shared_parts.append(more)
         if number < len(steps) - 1:
             shared = jnp.concatenate([shared, more], axis=0)
-
-    w_more = swap(w_slots[0], "dp", steps[0])
 
     spec = (nseq, 2 * block, wide)
     kh, vec, w_all, terms = call(
         partial(lag_kernel, sub, length, masks, len(shared_parts)),
         [shape(spec), shape((8, wide)), shape((n_w, wide)), shape((TERMS, nstate, wide))],
-        [VM] * (len(shared_parts) + 1), outs=[VM, VM, AN, AN],
-        scratch=[pltpu.VMEM((n_w, wide), f32), pltpu.VMEM((TERMS, nstate, wide), f32),
-                 pltpu.VMEM((length, wide), f32), pltpu.VMEM((2, nstate, wide), f32),
-                 pltpu.VMEM((3 * block, nseq * wide), bf16), pltpu.VMEM((2 * block, nseq * wide), f32), DMA((2,))],
-        name="lag_kernel", us=6, keep=[ft_table],
+        [VM] * (len(shared_parts) + 1),
+        scratch=[pltpu.VMEM((length, wide), f32), pltpu.VMEM((2, nstate, wide), f32),
+                 pltpu.VMEM((3 * block, nseq * wide), bf16), pltpu.VMEM((2 * block, nseq * wide), f32)],
+        name="lag_kernel", us=0, keep=[ft_table, block_in, cotangent],
     )(*shared_parts, f_table)
 
     kh, w_more = tie(kh, w_more)
@@ -830,17 +807,17 @@
     across = items * count * wide
     *convs, spectra_u, x_blocks = call(
         conv_kernel, [piece] * nseq + [shape((2 * block, across)), shape(blocks4)],
-        [AN] * (nseq + 1) + [VM] * 4, outs=[VM] * nseq + [AN, AN],
-        scratch=[lens, cuts, pltpu.VMEM(blocks4, f32), pltpu.VMEM((3 * block, across), bf16),
-                 pltpu.VMEM((2 * block, across), f32), pltpu.VMEM((2 * block, across), f32),
-                 pltpu.VMEM((6 * block, across), bf16), pltpu.VMEM(blocks4, f32), DMA((count * nseq + 3,))],
-        name="doc_conv", mib=24, us=7, keep=[w_all, terms],
+        [VM] * nseq + [AN] + [VM] * 4,
+        scratch=[lens, cuts, pltpu.VMEM((3 * block, across), bf16), pltpu.VMEM((2 * block, across), f32),
+                 pltpu.VMEM((6 * block, across), bf16), pltpu.VMEM(blocks4, f32), DMA],
+        name="doc_conv", mib=20, us=7, keep=[w_all, terms, block_in, cotangent],
     )(*hats, doc_lengths, vec, kh, f_table, ft_table)
     keep = [w_all, terms, vec, kh, f_table, ft_table, spectra_u, x_blocks]
     if len(ahead) == 2:
         *convs, w_slots[1], w_slots[2] = tie(*convs, w_slots[1], w_slots[2])
+    convs = trade(convs, "seq")
+    if len(ahead) == 2:
         w_slots.append(swap(w_slots[1], "dp", ahead[1]))
-    convs = trade(convs, "seq")
     if cols % LANES == 0 and sub % 16 == 0:
         shared = jnp.concatenate([shared, shared_parts[-1]], axis=0)
         shared, convs[1] = tie(shared, convs[1])
@@ -855,63 +832,81 @@
         w_lin = w_lin.reshape(ndp, ndp, nseq, sub, cols).transpose(2, 1, 3, 0, 4).reshape(width, 2 * width)
         bias_full = jnp.take(shared[:, height + 2, :cols], place, axis=0).reshape(1, 2 * width)
 
-    block_out, act, d_pre, d_lin_bias, *d_convs = call(
+    group = shape((2, wide, 2 * width), bf16)
+    block_out, d_lin_bias, *d_convs, stay, send = call(
         dense_kernel,
-        [shape((count, block, width), bf16), shape((tokens, width), bf16), shape((tokens, 2 * width), bf16),
-         shape((1, 2 * width))] + [piece] * nseq,
+        [shape((count, block, width), bf16), shape((1, 2 * width))] + [piece] * nseq + [group] * 2,
         [VM] * nseq + [AN, AN, VM, VM],
         scratch=[pltpu.VMEM((count, block, width), bf16), pltpu.VMEM((count, block, width), bf16),
+                 pltpu.VMEM((tokens, width), bf16), pltpu.VMEM((tokens, 2 * width), bf16),
                  pltpu.VMEM((block, width), f32), pltpu.VMEM((block, 2 * width), f32), pltpu.VMEM((block, width), f32), DMA((2,))],
         name="gated_linear", mib=16, us=5, keep=keep,
     )(*convs, block_in, cotangent, w_lin, bias_full)
     d_convs = trade(d_convs, "seq")
 
-    act, d_pre, d_convs[1] = tie(act, d_pre, d_convs[1])
-    if cols % LANES == 0:
-        dw_parts = call(
-            weight_kernel, [shape((width, cols), bf16)] * ndp, [VM, VM], name="weight_grad", us=1, keep=keep
-        )(act, d_pre)
-        dw_parts = trade(dw_parts, "dp")
+    staged = cols % LANES == 0
+    if staged:
+        stay, send = call(
+            halve_kernel, [shape((1, wide, 2 * width), bf16)] * 2, [VM, VM], name="weight_half", keep=keep
+        )(stay, swap(send, "seq", 1))
+        d_convs[2], *_ = tie(d_convs[2], send)
+        dw_other = swap(send, "seq", 2)
     else:
-        full = lax.dot_general(act, d_pre, TN, preferred_element_type=f32).astype(bf16)
-        full = full.reshape(width, ndp, cols).transpose(1, 0, 2)
-        dw_parts = list(lax.all_to_all(full, "dp", 0, 0, tiled=True))
+        full = jnp.stack([stay[0], send[0], stay[1], send[1]])
+        full = full.reshape(nseq, wide, ndp, cols).transpose(2, 0, 1, 3)
+        dw_own = jnp.sum(lax.all_to_all(full, "dp", 0, 0, tiled=True).astype(f32), axis=0)
+        dw_own = sum(trade([dw_own[d] for d in range(nseq)], "seq"))
 
     out = call(
         back_kernel, [piece] * nseq + [shape(spec), shape((3, wide))],
-        [AN] * (nseq + 3) + [VM] * 4,
-        scratch=[lens, cuts, pltpu.VMEM(blocks4, bf16), pltpu.VMEM(blocks4, f32),
-                 pltpu.VMEM((2 * block, across), bf16), pltpu.VMEM((2 * block, across), f32),
+        [VM] * (nseq + 1) + [AN] + [VM] * 5,
+        scratch=[lens, cuts, pltpu.VMEM(blocks4, bf16), pltpu.VMEM((2 * block, across), bf16),
                  pltpu.VMEM((2 * block, across), f32), pltpu.VMEM((2 * block, across), f32),
-                 pltpu.VMEM((6 * block, across), bf16), pltpu.VMEM(blocks4, f32), DMA((count * nseq + 3,))],
-        name="doc_conv_grad", mib=30, us=8, keep=[w_all, terms],
+                 pltpu.VMEM((6 * block, across), bf16), pltpu.VMEM(blocks4, f32), DMA],
+        name="doc_conv_grad", mib=24, us=8, keep=[w_all, terms],
     )(*d_convs, x_blocks, doc_lengths, spectra_u, vec, kh, f_table, ft_table)
     g_own, dkh, d_norm = out[:nseq], out[nseq], out[nseq + 1]
-    gs = trade(g_own, "seq")
+    if staged:
+        stay, send = call(
+            deal_kernel, [shape((ndp // 2, wide, cols))] * 2, [VM, VM], name="weight_deal", us=1, keep=keep[:2]
+        )(stay, dw_other)
+        dkh, *_ = tie(dkh, send)
+        dw_other = swap(send, "dp", 1)
 
     small = call(
-        partial(state_grad_kernel, sub, length), shape((ndp, rows, LANES)), [AN, AN] + [VM] * 4,
-        scratch=[pltpu.VMEM((n_w, wide), f32), pltpu.VMEM((TERMS, nstate, wide), f32),
-                 pltpu.VMEM((length, wide), f32), pltpu.VMEM((4, nstate, wide), f32), pltpu.VMEM((n_w, wide), f32),
-                 pltpu.VMEM((6 * block, nseq * wide), bf16), DMA((2,))],
+        partial(state_grad_kernel, sub, length), shape((ndp, rows, LANES)), [VM] * 6,
+        scratch=[pltpu.VMEM((length, wide), f32), pltpu.VMEM((4, nstate, wide), f32), pltpu.VMEM((n_w, wide), f32),
+                 pltpu.VMEM((6 * block, nseq * wide), bf16)],
         name="state_grad", mib=10, us=10,
     )(w_all, terms, dkh, d_norm, d_lin_bias, ft_table)
-    small, dw_parts, gs = tie(small, tuple(dw_parts), tuple(gs))
+    small, *g_own = tie(small, *g_own)
+    if staged:
+        small, dw_other = tie(small, dw_other)
     small = lax.all_to_all(small, "dp", 0, 0, tiled=True)
-    dw_own = call(sum_all_kernel, shape((width, cols), bf16), [VM] * ndp, name="weight_sum")(*dw_parts)
-    dws = trade([dw_own] * nseq, "seq")
-    gs, dws[1] = tie(gs, dws[1])
+    gs = trade(g_own, "seq")
+    if staged:
+        step = 2
+        while step < ndp:
+            stay, send = call(
+                halve_kernel, [shape((ndp // 2 // step, wide, cols))] * 2, [VM, VM], name="weight_half"
+            )(stay, dw_other)
+            dw_other = swap(send, "dp", step)
+            step *= 2
     grad_in = call(
         partial(ln_back_kernel, own, sub), shape((count, block, width), bf16), [VM] * (nseq + 2),
         name="layer_norm_grad", mib=12,
     )(*gs, block_in, cotangent)
-    small, grad_in, *dws = tie(small, grad_in, *dws)
-    small = call(sum_kernel, shape((rows, LANES)), [VM], name="small_sum", us=0.5)(small)
-    smalls = trade([small] * nseq, "seq")
+    if staged:
+        merged = call(merge_kernel, shape((rows + wide, cols)), [VM] * 3, name="last_sums", us=0.5)(small, stay, dw_other)
+        merged = trade([merged] * nseq, "seq")
+        smalls, dws = merged, []
+    else:
+        small = call(sum_kernel, shape((rows, LANES)), [VM], name="small_sum", us=0.5)(small)
+        smalls, dws = trade([small] * nseq, "seq"), trade([dw_own] * nseq, "seq")
     d_w, d_step, d_skip, d_gain, d_bias, d_lam, d_imag, d_lb, dw = call(
-        partial(last_kernel, sub),
+        partial(last_kernel, sub, rows),
         [shape((n_w, own))] + [shape((1, own))] * 4 + [shape((1, per))] * 2 + [shape((1, cols)), shape((width, cols))],
-        [VM] * (2 * nseq), name="last", us=1,
+        [VM] * (len(smalls) + len(dws)), name="last", us=1,
     )(*smalls, *dws)
     return (
         block_out, grad_in, d_gain.reshape(own), d_bias.reshape(own), d_lam.reshape(per), d_imag.reshape(per),

time: 107 us -> 97 us (0.907)
  starting transfers between devices: 38.2 us -> 31.1 us
  Pallas kernels: 48.4 us -> 42.4 us
  waiting for transfers between devices: 18.3 us -> 22.3 us
    ppermute x32 -> x27, starting transfers between devices: 34.5 us -> 27.8 us  [swap(): lax.ppermute(v, axis, [(i, i ^ by) for i in range(n)])]
    pallas_call x14 -> x15, Pallas kernels: 48.4 us -> 42.4 us  [call(): return lambda *args: kernel(*args, *keep)]
    all_to_all x1, waiting for transfers between devices: 0.01 us -> 3.58 us  [on_device(): small = lax.all_to_all(small, 'dp', 0, 0, tiled=True)]
    ppermute x32 -> x27, waiting for transfers between devices: 18.3 us -> 18.7 us  [swap(): lax.ppermute(v, axis, [(i, i ^ by) for i in range(n)])]
  transfers between devices with their start and end apart: 33 -> 28, of which waited for: 9 -> 11; matrix products, arithmetic and copies ran while one was open for 0% -> 0% of each run, Pallas kernels for 38% -> 36%
where the time goes in v3:
time: 97 us; the launch traced here: 96.8 us
  Pallas kernels  42.4 us (44%)
  starting transfers between devices  31.1 us (32%)
  waiting for transfers between devices  22.3 us (23%)
    pallas_call x15, Pallas kernels, call(): return lambda *args: kernel(*args, *keep)  42.4 us
    ppermute x27, starting transfers between devices, swap(): lax.ppermute(v, axis, [(i, i ^ by) for i in range(n)])  27.8 us
    ppermute x27, waiting for transfers between devices, swap(): lax.ppermute(v, axis, [(i, i ^ by) for i in range(n)])  18.7 us
    all_to_all x1, waiting for transfers between devices, on_device(): small = lax.all_to_all(small, 'dp', 0, 0, tiled=True)  3.58 us
    all_to_all x1, starting transfers between devices, on_device(): small = lax.all_to_all(small, 'dp', 0, 0, tiled=True)  3.36 us
  transfers between devices with their start and end apart: 28, of which 11 were waited for; matrix products, arithmetic and copies ran while one was open for 0% of the time, Pallas kernels for 36%

profile of v3, /device:TPU:0, one launch (start us, length us, event | category | flops | bytes accessed | tf_op | source)
XLA Modules:
  0.0 96.8 jit_solution(8023082128868186243)
XLA Ops:
  0.7 1.8 %pack.1.refs_0_ = f32[1,24,128]{2,1,0:T(8,128)} custom-call(f32[128,64]{1,0:T(8,128)} %bitcast.19, f32[1,64]{1,0:T(1,128)} %bitcast.20, f32[1,64]{1,0:T(1,128)} %bitcast.21, f32[1,64]{1,0:T(1,128)} %bitcast.22, f32[1,64]{1,0:T(1,128)} %bitcast.23, f32[1,8]{1,0:T(1,128)} %bitcast.24, f32[1,8]{1,0:T(1,128)} %bitcast.25, f32[1,128]{1,0:T(1,128)} %bitcast.26), custom_call_target="tpu_custom_call" | custom-call | flops 2300000000 | bytes 1000 | tf_op jit(solution)/shard_map/pack/pallas_call | solution.py:53
  2.5 4.1 %collective-permute-start = (f32[1,24,128]{2,1,0:T(8,128)}, f32[1,24,128]{2,1,0:T(8,128)S(1)}, u32[]{:S(2)}, u32[]{:S(2)}) collective-permute-start(f32[1,24,128]{2,1,0:T(8,128)} %pack.1.refs_0_), channel_id=1, source_target_pairs={{0,16},{4,20},{8,24},{12,28},{16,0},{20,4},{24,8},{28,12},{1,17},{... | collective-permute-start | bytes 36872 | tf_op jit(solution)/shard_map/ppermute | solution.py:721
  6.6 2.0 %layer_norm.1 = (f32[2,256,128]{2,1,0:T(8,128)S(1)}, f32[2,256,128]{2,1,0:T(8,128)S(1)}, f32[2,256,128]{2,1,0:T(8,128)S(1)}, f32[2,256,128]{2,1,0:T(8,128)S(1)}) custom-call(bf16[2,256,512]{2,1,0:T(8,128)(2,1)S(1)} %copy-done.2), custom_call_target="tpu_custom_call" | custom-call | flops 2300000000 | bytes 1000 | tf_op jit(solution)/shard_map/layer_norm/pallas_call | solution.py:53
  8.7 0.1 collective-permute-start.2
  8.8 1.7 %collective-permute-start.1 = (f32[2,24,128]{2,1,0:T(8,128)S(1)}, f32[2,24,128]{2,1,0:T(8,128)S(1)}, u32[]{:S(2)}, u32[]{:S(2)}) collective-permute-start(f32[2,24,128]{2,1,0:T(8,128)S(1)} %pad_maximum_fusion.3), channel_id=1, source_target_pairs={{0,8},{4,12},{8,0},{12,4},{16,24},{20,28},{24,16},{28,20},{1,9},{5... | collective-permute-start | bytes 73736 | tf_op jit(solution)/shard_map/ppermute | solution.py:721
  10.5 2.6 %collective-permute-start.6 = (bf16[1,512,128]{2,1,0:T(8,128)(2,1)S(1)}, bf16[1,512,128]{2,1,0:T(8,128)(2,1)S(1)}, u32[]{:S(2)}, u32[]{:S(2)}) collective-permute-start(bf16[1,512,128]{2,1,0:T(8,128)(2,1)S(1)} %bitcast.17), channel_id=1, source_target_pairs={{0,16},{4,20},{8,24},{12,28},{16,0},{20,4},{24,8},{28,12},{1,17},{... | collective-permute-start | bytes 393224 | tf_op jit(solution)/shard_map/ppermute | solution.py:721
  13.1 1.5 %collective-permute-start.3 = (f32[2,256,128]{2,1,0:T(8,128)S(1)}, f32[2,256,128]{2,1,0:T(8,128)S(1)}, u32[]{:S(2)}, u32[]{:S(2)}) collective-permute-start(f32[2,256,128]{2,1,0:T(8,128)S(1)} %get-tuple-element.94), channel_id=1, source_target_pairs={{0,2},{1,3},{2,0},{3,1},{4,6},{5,7},{6,4},{7,5},{8,10},{9,11},{10,... | collective-permute-start | bytes 786440 | tf_op jit(solution)/shard_map/ppermute | solution.py:721
  14.6 1.6 %collective-permute-start.5 = (f32[4,24,128]{2,1,0:T(8,128)S(1)}, f32[4,24,128]{2,1,0:T(8,128)S(1)}, u32[]{:S(2)}, u32[]{:S(2)}) collective-permute-start(f32[4,24,128]{2,1,0:T(8,128)S(1)} %pad_maximum_fusion.2), channel_id=1, source_target_pairs={{0,4},{4,0},{8,12},{12,8},{16,20},{20,16},{24,28},{28,24},{1,5},{5... | collective-permute-start | bytes 147464 | tf_op jit(solution)/shard_map/ppermute | solution.py:721
  16.2 2.8 %collective-permute-done.5.refs_3_ = f32[4,24,128]{2,1,0:T(8,128)S(1)} collective-permute-done((f32[4,24,128]{2,1,0:T(8,128)S(1)}, f32[4,24,128]{2,1,0:T(8,128)S(1)}, u32[]{:S(2)}, u32[]{:S(2)}) %collective-permute-start.5) | collective-permute-done | bytes 49184 | tf_op jit(solution)/shard_map/ppermute | solution.py:721
  19.0 5.9 %lag_kernel.1 = (f32[4,512,128]{2,1,0:T(8,128)S(1)}, f32[8,128]{1,0:T(8,128)S(1)}, f32[128,128]{1,0:T(8,128)S(1)}, f32[13,64,128]{2,1,0:T(8,128)S(1)}) custom-call(f32[1,24,128]{2,1,0:T(8,128)S(1)} %copy-done.4, f32[1,24,128]{2,1,0:T(8,128)S(1)} %collective-permute-done.refs_1_, f32[2,24,128]{2,1,0:T(8,128)S(1)} %collective-permute-done.1.refs_2_, ...), custom_call_target="tpu_custom_call" | custom-call | bytes 1000 | tf_op jit(solution)/shard_map/lag_kernel/pallas_call | solution.py:53
  25.0 1.6 %collective-permute-start.8 = (bf16[2,512,128]{2,1,0:T(8,128)(2,1)S(1)}, bf16[2,512,128]{2,1,0:T(8,128)(2,1)S(1)}, u32[]{:S(2)}, u32[]{:S(2)}) collective-permute-start(bf16[2,512,128]{2,1,0:T(8,128)(2,1)S(1)} %pad_maximum_fusion.refs_1_), channel_id=1, source_target_pairs={{0,4},{4,0},{8,12},{12,8},{16,20},{20,16},{24,28},{28,24},{1,5},{5... | collective-permute-start | bytes 786440 | tf_op jit(solution)/shard_map/ppermute | solution.py:721
  26.6 0.4 collective-permute-start.7
  27.0 6.6 %doc_conv.1 = (bf16[2,256,128]{2,1,0:T(8,128)(2,1)S(1)}, bf16[2,256,128]{2,1,0:T(8,128)(2,1)S(1)}, bf16[2,256,128]{2,1,0:T(8,128)(2,1)S(1)}, bf16[2,256,128]{2,1...) custom-call(f32[2,256,128]{2,1,0:T(8,128)S(1)} %get-tuple-element.90.refs_0_, ...), custom_call_target="tpu_custom_call" | custom-call | flops 8049999872 | bytes 1000 | tf_op jit(solution)/shard_map/doc_conv/pallas_call | solution.py:53
  33.6 0.7 collective-permute-done.7.refs_2_
  34.3 0.5 collective-permute-start.12
  34.8 1.8 %collective-permute-start.10 = (bf16[2,256,128]{2,1,0:T(8,128)(2,1)S(1)}, bf16[2,256,128]{2,1,0:T(8,128)(2,1)S(1)}, u32[]{:S(2)}, u32[]{:S(2)}) collective-permute-start(bf16[2,256,128]{2,1,0:T(8,128)(2,1)S(1)} %get-tuple-element.110), channel_id=1, source_target_pairs={{0,2},{1,3},{2,0},{3,1},{4,6},{5,7},{6,4},{7,5},{8,10},{9,11},{10,... | collective-permute-start | bytes 393224 | tf_op jit(solution)/shard_map/ppermute | solution.py:721
  36.5 0.1 collective-permute-start.11
  36.7 4.8 %collective-permute-done.12.refs_4_ = bf16[2,512,128]{2,1,0:T(8,128)(2,1)S(1)} collective-permute-done((bf16[2,512,128]{2,1,0:T(8,128)(2,1)S(1)}, bf16[2,512,128]{2,1,0:T(8,128)(2,1)S(1)}, u32[]{:S(2)}, u32[]{:S(2)}) %collective-permute-start.12) | collective-permute-done | bytes 262176 | tf_op jit(solution)/shard_map/ppermute | solution.py:721
  41.5 0.3 linear_rows.1
  41.8 1.3 %collective-permute-done.11.refs_3_ = bf16[2,256,128]{2,1,0:T(8,128)(2,1)S(1)} collective-permute-done((bf16[2,256,128]{2,1,0:T(8,128)(2,1)S(1)}, bf16[2,256,128]{2,1,0:T(8,128)(2,1)S(1)}, u32[]{:S(2)}, u32[]{:S(2)}) %collective-permute-start.11) | collective-permute-done | bytes 131104 | tf_op jit(solution)/shard_map/ppermute | solution.py:721
  43.2 4.9 %gated_linear.1 = (bf16[2,256,512]{2,1,0:T(8,128)(2,1)}, f32[1,1024]{1,0:T(1,128)S(1)}, bf16[2,256,128]{2,1,0:T(8,128)(2,1)S(1)}, bf16[2,256,128]{2,1,0:T(8,128)...) custom-call(bf16[2,256,128]{2,1,0:T(8,128)(2,1)S(1)} %get-tuple-elem, ...), custom_call_target="tpu_custom_call" | custom-call | flops 5750000128 | bytes 1000 | tf_op jit(solution)/shard_map/gated_linear/pallas_call | solution.py:53
  48.0 0.3 collective-permute-start.15
  48.3 1.8 %collective-permute-start.14 = (bf16[2,256,128]{2,1,0:T(8,128)(2,1)S(1)}, bf16[2,256,128]{2,1,0:T(8,128)(2,1)S(1)}, u32[]{:S(2)}, u32[]{:S(2)}) collective-permute-start(bf16[2,256,128]{2,1,0:T(8,128)(2,1)S(1)} %get-tuple-element.122), channel_id=1, source_target_pairs={{0,2},{1,3},{2,0},{3,1},{4,6},{5,7},{6,4},{7,5},{8,10},{9,11},{10,... | collective-permute-start | bytes 393224 | tf_op jit(solution)/shard_map/ppermute | solution.py:721
  50.1 0.4 collective-permute-start.16
  50.5 0.1 weight_half.3
  50.6 1.8 %collective-permute-start.17 = (bf16[1,128,1024]{2,1,0:T(8,128)(2,1)S(1)}, bf16[1,128,1024]{2,1,0:T(8,128)(2,1)S(1)}, u32[]{:S(2)}, u32[]{:S(2)}) collective-permute-start(bf16[1,128,1024]{2,1,0:T(8,128)(2,1)S(1)} %get-tuple-element.125), channel_id=1, source_target_pairs={{0,2},{1,3},{2,0},{3,1},{4,6},{5,7},{6,4},{7,5},{8,10},{9,11},{10,... | collective-permute-start | bytes 786440 | tf_op jit(solution)/shard_map/ppermute | solution.py:721
  52.4 2.2 %collective-permute-done.14.refs_2_ = bf16[2,256,128]{2,1,0:T(8,128)(2,1)S(1)} collective-permute-done((bf16[2,256,128]{2,1,0:T(8,128)(2,1)S(1)}, bf16[2,256,128]{2,1,0:T(8,128)(2,1)S(1)}, u32[]{:S(2)}, u32[]{:S(2)}) %collective-permute-start.14) | collective-permute-done | bytes 131104 | tf_op jit(solution)/shard_map/ppermute | solution.py:721
  54.6 2.1 %collective-permute-done.16.refs_3_ = bf16[2,256,128]{2,1,0:T(8,128)(2,1)S(1)} collective-permute-done((bf16[2,256,128]{2,1,0:T(8,128)(2,1)S(1)}, bf16[2,256,128]{2,1,0:T(8,128)(2,1)S(1)}, u32[]{:S(2)}, u32[]{:S(2)}) %collective-permute-start.16) | collective-permute-done | bytes 131104 | tf_op jit(solution)/shard_map/ppermute | solution.py:721
  56.7 7.3 %doc_conv_grad.1 = (bf16[2,256,128]{2,1,0:T(8,128)(2,1)S(1)}, bf16[2,256,128]{2,1,0:T(8,128)(2,1)S(1)}, bf16[2,256,128]{2,1,0:T(8,128)(2,1)S(1)}, bf16[2,256,128...) custom-call(bf16[2,256,128]{2,1,0:T(8,128)(2,1)S(1)} %get-tuple-element.120.refs_0_, ...), custom_call_target="tpu_custom_call" | custom-call | flops 9200000000 | bytes 1000 | tf_op jit(solution)/shard_map/doc_conv_grad/pallas_call | solution.py:53
  64.1 0.2 weight_deal.1
  64.2 1.6 %collective-permute-start.21 = (f32[4,128,128]{2,1,0:T(8,128)S(1)}, f32[4,128,128]{2,1,0:T(8,128)S(1)}, u32[]{:S(2)}, u32[]{:S(2)}) collective-permute-start(f32[4,128,128]{2,1,0:T(8,128)S(1)} %get-tuple-element.130), channel_id=1, source_target_pairs={{0,4},{4,0},{8,12},{12,8},{16,20},{20,16},{24,28},{28,24},{1,5},{5... | collective-permute-start | bytes 786440 | tf_op jit(solution)/shard_map/ppermute | solution.py:721
  65.8 10.5 %state_grad.1 = f32[8,24,128]{2,1,0:T(8,128)} custom-call(f32[128,128]{1,0:T(8,128)S(1)} %get-tuple-element.100.refs_9_.refs_5_.refs_8_.refs_2_.refs_11_.refs_0_, f32[13,64,128]{2,1,0:T(8,128)S(1)} %get-tuple-element.101.refs_10_.refs_6_.refs_9_.refs_3_.refs_12_.refs_1_, f32[4,512,128]{2,1,0:T(8,128)S(1)} %get-tuple-element.131.refs_2_, ...), custom_call_target="tpu_custom_call" | custom-call | flops 11500000256 | bytes 1000 | tf_op jit(solution)/shard_map/state_grad/pallas_call | solution.py:53
  76.4 0.8 collective-permute-start.22
  77.2 3.4 %all-to-all-start = ((f32[8,24,128]{2,1,0:T(8,128)}), f32[8,24,128]{2,1,0:T(8,128)S(1)}, u32[]{:S(2)}, u32[]{:S(2)}) async-start(f32[8,24,128]{2,1,0:T(8,128)} %state_grad.1), calls=%async_computation | async-start | bytes 196608 | tf_op jit(solution)/shard_map/all_to_all | solution.py:885
  80.6 0.3 collective-permute-start.18
  80.8 1.3 %collective-permute-done.22.refs_1_ = f32[2,128,128]{2,1,0:T(8,128)S(1)} collective-permute-done((f32[2,128,128]{2,1,0:T(8,128)S(1)}, f32[2,128,128]{2,1,0:T(8,128)S(1)}, u32[]{:S(2)}, u32[]{:S(2)}) %collective-permute-start.22) | collective-permute-done | bytes 131104 | tf_op jit(solution)/shard_map/ppermute | solution.py:721
  82.1 1.4 %collective-permute-start.23 = (f32[1,128,128]{2,1,0:T(8,128)S(1)}, f32[1,128,128]{2,1,0:T(8,128)S(1)}, u32[]{:S(2)}, u32[]{:S(2)}) collective-permute-start(f32[1,128,128]{2,1,0:T(8,128)S(1)} %get-tuple-element.149), channel_id=1, source_target_pairs={{0,16},{4,20},{8,24},{12,28},{16,0},{20,4},{24,8},{28,12},{1,17},{... | collective-permute-start | bytes 196616 | tf_op jit(solution)/shard_map/ppermute | solution.py:721
  83.5 1.5 %collective-permute-start.19 = (bf16[2,256,128]{2,1,0:T(8,128)(2,1)S(1)}, bf16[2,256,128]{2,1,0:T(8,128)(2,1)S(1)}, u32[]{:S(2)}, u32[]{:S(2)}) collective-permute-start(bf16[2,256,128]{2,1,0:T(8,128)(2,1)S(1)} %get-tuple-element.140), channel_id=1, source_target_pairs={{0,2},{1,3},{2,0},{3,1},{4,6},{5,7},{6,4},{7,5},{8,10},{9,11},{10,... | collective-permute-start | bytes 393224 | tf_op jit(solution)/shard_map/ppermute | solution.py:721
  85.0 0.1 collective-permute-start.20
  85.1 3.6 %all-to-all-done.refs_0_ = f32[8,24,128]{2,1,0:T(8,128)S(1)} async-done(((f32[8,24,128]{2,1,0:T(8,128)}), f32[8,24,128]{2,1,0:T(8,128)S(1)}, u32[]{:S(2)}, u32[]{:S(2)}) %all-to-all-start) | async-done | bytes 98336 | tf_op jit(solution)/shard_map/all_to_all | solution.py:885
  88.7 0.8 collective-permute-done.23.refs_2_
  89.5 1.2 %collective-permute-start.26 = (f32[152,128]{1,0:T(8,128)S(1)}, f32[152,128]{1,0:T(8,128)S(1)}, u32[]{:S(2)}, u32[]{:S(2)}) collective-permute-start(f32[152,128]{1,0:T(8,128)S(1)} %last_sums.1.refs_0_), channel_id=1, source_target_pairs={{0,3},{1,2},{2,1},{3,0},{4,7},{5,6},{6,5},{7,4},{8,11},{9,10},{10,... | collective-permute-start | bytes 233480 | tf_op jit(solution)/shard_map/ppermute | solution.py:721
  90.8 0.5 collective-permute-start.25
  91.3 0.2 collective-permute-start.24
  91.5 1.8 %layer_norm_grad.1 = bf16[2,256,512]{2,1,0:T(8,128)(2,1)} custom-call(bf16[2,256,128]{2,1,0:T(8,128)(2,1)S(1)} %get-tuple-element.138.refs_0_, bf16[2,256,128]{2,1,0:T(8,128)(2,1)S(1)} %collective-permute-done.18.refs_1_, bf16[2,256,128]{2,1,0:T(8,128)(2,1)S(1)} %collective-permute-done.19.refs_2_, bf16[2,256,128]{2,1,0:T(8,128)(2,1)S(1)} %collective-permute-done.20.refs_3_, ...), custom_call_target="tpu_custom_call" | custom-call | bytes 1000 | tf_op jit(solution)/shard_map/layer_norm_grad/pallas_call | solution.py:53
  93.3 0.8 collective-permute-done.26.refs_3_
  94.1 1.8 %collective-permute-done.25.refs_2_ = f32[152,128]{1,0:T(8,128)S(1)} collective-permute-done((f32[152,128]{1,0:T(8,128)S(1)}, f32[152,128]{1,0:T(8,128)S(1)}, u32[]{:S(2)}, u32[]{:S(2)}) %collective-permute-start.25) | collective-permute-done | bytes 77856 | tf_op jit(solution)/shard_map/ppermute | solution.py:721
  95.9 0.8 last.1
  (43 shorter events, 0.2 us)
Async XLA Ops:
  0.6 6.0 %copy-start.2 = (bf16[2,256,512]{2,1,0:T(8,128)(2,1)S(1)}, bf16[2,256,512]{2,1,0:T(8,128)(2,1)}, u32[]{:S(2)}) copy-start(bf16[2,256,512]{2,1,0:T(8,128)(2,1)} %refs_4_.6) | copy-start | bytes 1572868
  2.5 6.3 %copy-start.4 = (f32[1,24,128]{2,1,0:T(8,128)S(1)}, f32[1,24,128]{2,1,0:T(8,128)}, u32[]{:S(2)}) copy-start(f32[1,24,128]{2,1,0:T(8,128)} %pack.1.refs_0_) | copy-start | bytes 36868
  2.5 8.0 %copy-start.7 = (bf16[512,128]{1,0:T(8,128)(2,1)S(1)}, bf16[512,128]{1,0:T(8,128)(2,1)}, u32[]{:S(2)}) copy-start(bf16[512,128]{1,0:T(8,128)(2,1)} %param.23) | copy-start | bytes 393220
  2.5 16.5 %copy-start = (bf16[256,1536]{1,0:T(8,128)(2,1)S(1)}, bf16[256,1536]{1,0:T(8,128)(2,1)}, u32[]{:S(2)}) copy-start(bf16[256,1536]{1,0:T(8,128)(2,1)} %constant.5.clone.refs_5_.refs_8_.refs_10_.refs_13_.refs_7_) | copy-start | bytes 2359300
  2.5 16.5 %copy-start.1 = (bf16[512,768]{1,0:T(8,128)(2,1)S(1)}, bf16[512,768]{1,0:T(8,128)(2,1)}, u32[]{:S(2)}) copy-start(bf16[512,768]{1,0:T(8,128)(2,1)} %constant.4.clone.refs_4_.refs_7_.refs_9_.refs_12_.refs_6_) | copy-start | bytes 2359300
  2.5 16.5 %copy-start.3 = (bf16[2,256,512]{2,1,0:T(8,128)(2,1)S(1)}, bf16[2,256,512]{2,1,0:T(8,128)(2,1)}, u32[]{:S(2)}) copy-start(bf16[2,256,512]{2,1,0:T(8,128)(2,1)} %refs_5_.7) | copy-start | bytes 1572868
  2.5 24.5 %copy-start.6 = (s32[2,4]{1,0:T(2,128)S(1)}, s32[2,4]{1,0:T(2,128)}, u32[]{:S(2)}) copy-start(s32[2,4]{1,0:T(2,128)} %refs_5_.6) | copy-start | bytes 100
  2.5 6.2 %collective-permute-start = (f32[1,24,128]{2,1,0:T(8,128)}, f32[1,24,128]{2,1,0:T(8,128)S(1)}, u32[]{:S(2)}, u32[]{:S(2)}) collective-permute-start(f32[1,24,128]{2,1,0:T(8,128)} %pack.1.refs_0_), channel_id=1, source_target_pairs={{0,16},{4,20},{8,24},{12,28},{16,0},{20,4},{24,8},{28,12},{1,17},{... | collective-permute-start | bytes 36872 | tf_op jit(solution)/shard_map/ppermute | solution.py:721
  8.7 5.9 %collective-permute-start.2 = (f32[2,256,128]{2,1,0:T(8,128)S(1)}, f32[2,256,128]{2,1,0:T(8,128)S(1)}, u32[]{:S(2)}, u32[]{:S(2)}) collective-permute-start(f32[2,256,128]{2,1,0:T(8,128)S(1)} %get-tuple-element.92), channel_id=1, source_target_pairs={{0,1},{1,0},{2,3},{3,2},{4,5},{5,4},{6,7},{7,6},{8,9},{9,8},{10,11... | collective-permute-start | bytes 786440 | tf_op jit(solution)/shard_map/ppermute | solution.py:721
  8.8 5.8 %collective-permute-start.1 = (f32[2,24,128]{2,1,0:T(8,128)S(1)}, f32[2,24,128]{2,1,0:T(8,128)S(1)}, u32[]{:S(2)}, u32[]{:S(2)}) collective-permute-start(f32[2,24,128]{2,1,0:T(8,128)S(1)} %pad_maximum_fusion.3), channel_id=1, source_target_pairs={{0,8},{4,12},{8,0},{12,4},{16,24},{20,28},{24,16},{28,20},{1,9},{5... | collective-permute-start | bytes 73736 | tf_op jit(solution)/shard_map/ppermute | solution.py:721
  10.5 14.4 %collective-permute-start.6 = (bf16[1,512,128]{2,1,0:T(8,128)(2,1)S(1)}, bf16[1,512,128]{2,1,0:T(8,128)(2,1)S(1)}, u32[]{:S(2)}, u32[]{:S(2)}) collective-permute-start(bf16[1,512,128]{2,1,0:T(8,128)(2,1)S(1)} %bitcast.17), channel_id=1, source_target_pairs={{0,16},{4,20},{8,24},{12,28},{16,0},{20,4},{24,8},{28,12},{1,17},{... | collective-permute-start | bytes 393224 | tf_op jit(solution)/shard_map/ppermute | solution.py:721
  13.1 13.9 %collective-permute-start.3 = (f32[2,256,128]{2,1,0:T(8,128)S(1)}, f32[2,256,128]{2,1,0:T(8,128)S(1)}, u32[]{:S(2)}, u32[]{:S(2)}) collective-permute-start(f32[2,256,128]{2,1,0:T(8,128)S(1)} %get-tuple-element.94), channel_id=1, source_target_pairs={{0,2},{1,3},{2,0},{3,1},{4,6},{5,7},{6,4},{7,5},{8,10},{9,11},{10,... | collective-permute-start | bytes 786440 | tf_op jit(solution)/shard_map/ppermute | solution.py:721
  14.6 12.4 %collective-permute-start.4 = (f32[2,256,128]{2,1,0:T(8,128)S(1)}, f32[2,256,128]{2,1,0:T(8,128)S(1)}, u32[]{:S(2)}, u32[]{:S(2)}) collective-permute-start(f32[2,256,128]{2,1,0:T(8,128)S(1)} %get-tuple-element.95), channel_id=1, source_target_pairs={{0,3},{1,2},{2,1},{3,0},{4,7},{5,6},{6,5},{7,4},{8,11},{9,10},{10,... | collective-permute-start | bytes 786440 | tf_op jit(solution)/shard_map/ppermute | solution.py:721
  14.6 4.4 %collective-permute-start.5 = (f32[4,24,128]{2,1,0:T(8,128)S(1)}, f32[4,24,128]{2,1,0:T(8,128)S(1)}, u32[]{:S(2)}, u32[]{:S(2)}) collective-permute-start(f32[4,24,128]{2,1,0:T(8,128)S(1)} %pad_maximum_fusion.2), channel_id=1, source_target_pairs={{0,4},{4,0},{8,12},{12,8},{16,20},{20,16},{24,28},{28,24},{1,5},{5... | collective-permute-start | bytes 147464 | tf_op jit(solution)/shard_map/ppermute | solution.py:721
  25.0 8.6 %collective-permute-start.8 = (bf16[2,512,128]{2,1,0:T(8,128)(2,1)S(1)}, bf16[2,512,128]{2,1,0:T(8,128)(2,1)S(1)}, u32[]{:S(2)}, u32[]{:S(2)}) collective-permute-start(bf16[2,512,128]{2,1,0:T(8,128)(2,1)S(1)} %pad_maximum_fusion.refs_1_), channel_id=1, source_target_pairs={{0,4},{4,0},{8,12},{12,8},{16,20},{20,16},{24,28},{28,24},{1,5},{5... | collective-permute-start | bytes 786440 | tf_op jit(solution)/shard_map/ppermute | solution.py:721
  26.6 7.7 %collective-permute-start.7 = (bf16[2,512,128]{2,1,0:T(8,128)(2,1)S(1)}, bf16[2,512,128]{2,1,0:T(8,128)(2,1)S(1)}, u32[]{:S(2)}, u32[]{:S(2)}) collective-permute-start(bf16[2,512,128]{2,1,0:T(8,128)(2,1)S(1)} %pad_maximum_fusion.refs_1_), channel_id=1, source_target_pairs={{0,8},{4,12},{8,0},{12,4},{16,24},{20,28},{24,16},{28,20},{1,9},{5... | collective-permute-start | bytes 786440 | tf_op jit(solution)/shard_map/ppermute | solution.py:721
  34.3 7.2 %collective-permute-start.12 = (bf16[2,512,128]{2,1,0:T(8,128)(2,1)S(1)}, bf16[2,512,128]{2,1,0:T(8,128)(2,1)S(1)}, u32[]{:S(2)}, u32[]{:S(2)}) collective-permute-start(bf16[2,512,128]{2,1,0:T(8,128)(2,1)S(1)} %collective-permute-done.7.refs_2_), channel_id=1, source_target_pairs={{0,4},{4,0},{8,12},{12,8},{16,20},{20,16},{24,28},{28,24},{1,5},{5... | collective-permute-start | bytes 786440 | tf_op jit(solution)/shard_map/ppermute | solution.py:721
  34.8 1.9 %collective-permute-start.9 = (bf16[2,256,128]{2,1,0:T(8,128)(2,1)S(1)}, bf16[2,256,128]{2,1,0:T(8,128)(2,1)S(1)}, u32[]{:S(2)}, u32[]{:S(2)}) collective-permute-start(bf16[2,256,128]{2,1,0:T(8,128)(2,1)S(1)} %get-tuple-element.108), channel_id=1, source_target_pairs={{0,1},{1,0},{2,3},{3,2},{4,5},{5,4},{6,7},{7,6},{8,9},{9,8},{10,11... | collective-permute-start | bytes 393224 | tf_op jit(solution)/shard_map/ppermute | solution.py:721
  34.8 7.1 %collective-permute-start.10 = (bf16[2,256,128]{2,1,0:T(8,128)(2,1)S(1)}, bf16[2,256,128]{2,1,0:T(8,128)(2,1)S(1)}, u32[]{:S(2)}, u32[]{:S(2)}) collective-permute-start(bf16[2,256,128]{2,1,0:T(8,128)(2,1)S(1)} %get-tuple-element.110), channel_id=1, source_target_pairs={{0,2},{1,3},{2,0},{3,1},{4,6},{5,7},{6,4},{7,5},{8,10},{9,11},{10,... | collective-permute-start | bytes 393224 | tf_op jit(solution)/shard_map/ppermute | solution.py:721
  36.5 6.6 %collective-permute-start.11 = (bf16[2,256,128]{2,1,0:T(8,128)(2,1)S(1)}, bf16[2,256,128]{2,1,0:T(8,128)(2,1)S(1)}, u32[]{:S(2)}, u32[]{:S(2)}) collective-permute-start(bf16[2,256,128]{2,1,0:T(8,128)(2,1)S(1)} %get-tuple-element.111), channel_id=1, source_target_pairs={{0,3},{1,2},{2,1},{3,0},{4,7},{5,6},{6,5},{7,4},{8,11},{9,10},{10,... | collective-permute-start | bytes 393224 | tf_op jit(solution)/shard_map/ppermute | solution.py:721
  48.0 2.4 %collective-permute-start.15 = (bf16[2,128,1024]{2,1,0:T(8,128)(2,1)S(1)}, bf16[2,128,1024]{2,1,0:T(8,128)(2,1)S(1)}, u32[]{:S(2)}, u32[]{:S(2)}) collective-permute-start(bf16[2,128,1024]{2,1,0:T(8,128)(2,1)S(1)} %get-tuple-element.124), channel_id=1, source_target_pairs={{0,1},{1,0},{2,3},{3,2},{4,5},{5,4},{6,7},{7,6},{8,9},{9,8},{10,11... | collective-permute-start | bytes 1572872 | tf_op jit(solution)/shard_map/ppermute | solution.py:721
  48.3 6.3 %collective-permute-start.14 = (bf16[2,256,128]{2,1,0:T(8,128)(2,1)S(1)}, bf16[2,256,128]{2,1,0:T(8,128)(2,1)S(1)}, u32[]{:S(2)}, u32[]{:S(2)}) collective-permute-start(bf16[2,256,128]{2,1,0:T(8,128)(2,1)S(1)} %get-tuple-element.122), channel_id=1, source_target_pairs={{0,2},{1,3},{2,0},{3,1},{4,6},{5,7},{6,4},{7,5},{8,10},{9,11},{10,... | collective-permute-start | bytes 393224 | tf_op jit(solution)/shard_map/ppermute | solution.py:721
  50.1 4.6 %collective-permute-start.13 = (bf16[2,256,128]{2,1,0:T(8,128)(2,1)S(1)}, bf16[2,256,128]{2,1,0:T(8,128)(2,1)S(1)}, u32[]{:S(2)}, u32[]{:S(2)}) collective-permute-start(bf16[2,256,128]{2,1,0:T(8,128)(2,1)S(1)} %get-tuple-element.121), channel_id=1, source_target_pairs={{0,1},{1,0},{2,3},{3,2},{4,5},{5,4},{6,7},{7,6},{8,9},{9,8},{10,11... | collective-permute-start | bytes 393224 | tf_op jit(solution)/shard_map/ppermute | solution.py:721
  50.1 6.6 %collective-permute-start.16 = (bf16[2,256,128]{2,1,0:T(8,128)(2,1)S(1)}, bf16[2,256,128]{2,1,0:T(8,128)(2,1)S(1)}, u32[]{:S(2)}, u32[]{:S(2)}) collective-permute-start(bf16[2,256,128]{2,1,0:T(8,128)(2,1)S(1)} %get-tuple-element.127), channel_id=1, source_target_pairs={{0,3},{1,2},{2,1},{3,0},{4,7},{5,6},{6,5},{7,4},{8,11},{9,10},{10,... | collective-permute-start | bytes 393224 | tf_op jit(solution)/shard_map/ppermute | solution.py:721
  50.6 13.5 %collective-permute-start.17 = (bf16[1,128,1024]{2,1,0:T(8,128)(2,1)S(1)}, bf16[1,128,1024]{2,1,0:T(8,128)(2,1)S(1)}, u32[]{:S(2)}, u32[]{:S(2)}) collective-permute-start(bf16[1,128,1024]{2,1,0:T(8,128)(2,1)S(1)} %get-tuple-element.125), channel_id=1, source_target_pairs={{0,2},{1,3},{2,0},{3,1},{4,6},{5,7},{6,4},{7,5},{8,10},{9,11},{10,... | collective-permute-start | bytes 786440 | tf_op jit(solution)/shard_map/ppermute | solution.py:721
  64.0 12.3 %copy-start.5 = (bf16[2,256,128]{2,1,0:T(8,128)(2,1)}, bf16[2,256,128]{2,1,0:T(8,128)(2,1)S(1)}, u32[]{:S(2)}) copy-start(bf16[2,256,128]{2,1,0:T(8,128)(2,1)S(1)} %get-tuple-element.139) | copy-start | bytes 393220
  64.2 12.1 %collective-permute-start.21 = (f32[4,128,128]{2,1,0:T(8,128)S(1)}, f32[4,128,128]{2,1,0:T(8,128)S(1)}, u32[]{:S(2)}, u32[]{:S(2)}) collective-permute-start(f32[4,128,128]{2,1,0:T(8,128)S(1)} %get-tuple-element.130), channel_id=1, source_target_pairs={{0,4},{4,0},{8,12},{12,8},{16,20},{20,16},{24,28},{28,24},{1,5},{5... | collective-permute-start | bytes 786440 | tf_op jit(solution)/shard_map/ppermute | solution.py:721
  76.4 5.7 %collective-permute-start.22 = (f32[2,128,128]{2,1,0:T(8,128)S(1)}, f32[2,128,128]{2,1,0:T(8,128)S(1)}, u32[]{:S(2)}, u32[]{:S(2)}) collective-permute-start(f32[2,128,128]{2,1,0:T(8,128)S(1)} %get-tuple-element.147), channel_id=1, source_target_pairs={{0,8},{4,12},{8,0},{12,4},{16,24},{20,28},{24,16},{28,20},{1,9},{5... | collective-permute-start | bytes 393224 | tf_op jit(solution)/shard_map/ppermute | solution.py:721
  77.2 11.5 %all-to-all-start = ((f32[8,24,128]{2,1,0:T(8,128)}), f32[8,24,128]{2,1,0:T(8,128)S(1)}, u32[]{:S(2)}, u32[]{:S(2)}) async-start(f32[8,24,128]{2,1,0:T(8,128)} %state_grad.1), calls=%async_computation | async-start | bytes 196608 | tf_op jit(solution)/shard_map/all_to_all | solution.py:885
  80.6 10.7 %collective-permute-start.18 = (bf16[2,256,128]{2,1,0:T(8,128)(2,1)}, bf16[2,256,128]{2,1,0:T(8,128)(2,1)S(1)}, u32[]{:S(2)}, u32[]{:S(2)}) collective-permute-start(bf16[2,256,128]{2,1,0:T(8,128)(2,1)} %copy-done.5), channel_id=1, source_target_pairs={{0,1},{1,0},{2,3},{3,2},{4,5},{5,4},{6,7},{7,6},{8,9},{9,8},{10,11... | collective-permute-start | bytes 393224 | tf_op jit(solution)/shard_map/ppermute | solution.py:721
  82.1 7.4 %collective-permute-start.23 = (f32[1,128,128]{2,1,0:T(8,128)S(1)}, f32[1,128,128]{2,1,0:T(8,128)S(1)}, u32[]{:S(2)}, u32[]{:S(2)}) collective-permute-start(f32[1,128,128]{2,1,0:T(8,128)S(1)} %get-tuple-element.149), channel_id=1, source_target_pairs={{0,16},{4,20},{8,24},{12,28},{16,0},{20,4},{24,8},{28,12},{1,17},{... | collective-permute-start | bytes 196616 | tf_op jit(solution)/shard_map/ppermute | solution.py:721
  83.5 8.0 %collective-permute-start.19 = (bf16[2,256,128]{2,1,0:T(8,128)(2,1)S(1)}, bf16[2,256,128]{2,1,0:T(8,128)(2,1)S(1)}, u32[]{:S(2)}, u32[]{:S(2)}) collective-permute-start(bf16[2,256,128]{2,1,0:T(8,128)(2,1)S(1)} %get-tuple-element.140), channel_id=1, source_target_pairs={{0,2},{1,3},{2,0},{3,1},{4,6},{5,7},{6,4},{7,5},{8,10},{9,11},{10,... | collective-permute-start | bytes 393224 | tf_op jit(solution)/shard_map/ppermute | solution.py:721
  85.0 6.5 %collective-permute-start.20 = (bf16[2,256,128]{2,1,0:T(8,128)(2,1)S(1)}, bf16[2,256,128]{2,1,0:T(8,128)(2,1)S(1)}, u32[]{:S(2)}, u32[]{:S(2)}) collective-permute-start(bf16[2,256,128]{2,1,0:T(8,128)(2,1)S(1)} %get-tuple-element.141), channel_id=1, source_target_pairs={{0,3},{1,2},{2,1},{3,0},{4,7},{5,6},{6,5},{7,4},{8,11},{9,10},{10,... | collective-permute-start | bytes 393224 | tf_op jit(solution)/shard_map/ppermute | solution.py:721
  89.5 4.6 %collective-permute-start.26 = (f32[152,128]{1,0:T(8,128)S(1)}, f32[152,128]{1,0:T(8,128)S(1)}, u32[]{:S(2)}, u32[]{:S(2)}) collective-permute-start(f32[152,128]{1,0:T(8,128)S(1)} %last_sums.1.refs_0_), channel_id=1, source_target_pairs={{0,3},{1,2},{2,1},{3,0},{4,7},{5,6},{6,5},{7,4},{8,11},{9,10},{10,... | collective-permute-start | bytes 233480 | tf_op jit(solution)/shard_map/ppermute | solution.py:721
  90.8 5.1 %collective-permute-start.25 = (f32[152,128]{1,0:T(8,128)S(1)}, f32[152,128]{1,0:T(8,128)S(1)}, u32[]{:S(2)}, u32[]{:S(2)}) collective-permute-start(f32[152,128]{1,0:T(8,128)S(1)} %last_sums.1.refs_0_), channel_id=1, source_target_pairs={{0,2},{1,3},{2,0},{3,1},{4,6},{5,7},{6,4},{7,5},{8,10},{9,11},{10,... | collective-permute-start | bytes 233480 | tf_op jit(solution)/shard_map/ppermute | solution.py:721
  91.3 4.7 %collective-permute-start.24 = (f32[152,128]{1,0:T(8,128)S(1)}, f32[152,128]{1,0:T(8,128)S(1)}, u32[]{:S(2)}, u32[]{:S(2)}) collective-permute-start(f32[152,128]{1,0:T(8,128)S(1)} %last_sums.1.refs_0_), channel_id=1, source_target_pairs={{0,1},{1,0},{2,3},{3,2},{4,5},{5,4},{6,7},{7,6},{8,9},{9,8},{10,11... | collective-permute-start | bytes 233480 | tf_op jit(solution)/shard_map/ppermute | solution.py:721

commit v4 on v3

--- a/solution.py
+++ b/solution.py
@@ -88,23 +88,33 @@
 TERMS = 13
 
 
-def rows8(zr, zi):
-    dims = (8, zr.shape[-1])
-    at = iota(dims, 0)
-    r1, i1 = jnp.broadcast_to(zr, dims), jnp.broadcast_to(zi, dims)
-    r2, i2 = cmul(r1, i1, r1, i1)
-    r4, i4 = cmul(r2, i2, r2, i2)
-    p = (jnp.where(at & 1 > 0, r1, 1.0), jnp.where(at & 1 > 0, i1, 0.0))
-    p = cmul(*p, jnp.where(at & 2 > 0, r2, 1.0), jnp.where(at & 2 > 0, i2, 0.0))
-    p = cmul(*p, jnp.where(at & 4 > 0, r4, 1.0), jnp.where(at & 4 > 0, i4, 0.0))
-    return p, cmul(r4, i4, r4, i4)
-
-
-def powers(wr, wi):
-    pows = [None, (wr, wi)]
-    for v in range(2, COARSE + 1):
-        pows.append(cmul(*pows[v // 2], *pows[v - v // 2]))
-    return pows
+POWERS = (1, 2, 4) + tuple(8 * v for v in range(1, COARSE + 1))
+
+
+def power_table(zr, zi):
+    table = {1: (zr, zi)}
+    for p in POWERS[1:]:
+        at = p // 16 * 8 if p > 8 else p // 2
+        table[p] = cmul(*table[at], *table[p - at])
+    return [table[p] for p in POWERS]
+
+
+def wide_row(ref, p, half, n):
+    return jnp.broadcast_to(ref[2 * POWERS.index(p) + half, pl.ds(n, 1), :], (8, LANES))
+
+
+def rows8(ref, n):
+    at = iota((8, LANES), 0)
+    total = None
+    for p in (1, 2, 4):
+        here = at & p > 0
+        one = jnp.where(here, wide_row(ref, p, 0, n), 1.0), jnp.where(here, wide_row(ref, p, 1, n), 0.0)
+        total = one if total is None else cmul(*total, *one)
+    return total
+
+
+def powers(ref, n):
+    return [None] + [(wide_row(ref, 8 * v, 0, n), wide_row(ref, 8 * v, 1, n)) for v in range(1, COARSE + 1)]
 
 
 def halves(x):
@@ -165,7 +175,7 @@
 
 def lag_kernel(sub, length, masks, n_parts, *refs):
     pieces, refs = refs[:n_parts], refs[n_parts:]
-    f_ref, kh_ref, vec_ref, w_ref, term_ref, k_scr, z_scr, rhs_scr, kf_scr = refs
+    f_ref, kh_ref, vec_ref, w_ref, term_ref, pow_ref, k_scr, z_scr, rhs_scr, kf_scr = refs
     slots = [piece.at[t] for piece in pieces for t in range(piece.shape[0])]
     ndp = len(slots)
     me = lax.axis_index("dp")
@@ -197,15 +207,17 @@
     for slot, value in enumerate(terms):
         term_ref[slot] = value
     z_scr[0], z_scr[1] = cmul(w_ref[0:nstate], w_ref[nstate:], terms[11], terms[12])
+    for slot, pair in enumerate(power_table(terms[2], terms[3])):
+        pow_ref[2 * slot], pow_ref[2 * slot + 1] = pair
     k_scr[...] = jnp.zeros_like(k_scr)
 
     def pair(m, _):
         ready = []
         for n in (2 * m, 2 * m + 1):
-            (fr, fi), w = rows8(term_ref[2, pl.ds(n, 1), :], term_ref[3, pl.ds(n, 1), :])
+            fr, fi = rows8(pow_ref, n)
             cr = jnp.broadcast_to(z_scr[0, pl.ds(n, 1), :], (8, lanes))
             ci = jnp.broadcast_to(z_scr[1, pl.ds(n, 1), :], (8, lanes))
-            ready.append([cmul(fr, fi, cr, ci), powers(*w)])
+            ready.append([cmul(fr, fi, cr, ci), powers(pow_ref, n)])
         for u in range(DOCMAX // FINE // COARSE):
             for v in range(COARSE):
                 at = (u * COARSE + v) * FINE
@@ -358,7 +370,8 @@
             b, keep = within(cut_ref, s, j, block, lanes)
             cols = slice((j * count + s) * lanes, (j * count + s + 1) * lanes)
             stack3(rhs_scr, cols, jnp.where(keep, x_scr[s, b] * gain + bias, 0.0))
-    s_scr[...] = dot(f_ref[...], rhs_scr[...])
+        tile = slice(j * count * lanes, (j + 1) * count * lanes)
+        s_scr[:, tile] = dot(f_ref[...], rhs_scr[:, tile])
 
     def own(j, _):
         for s in range(count):
@@ -420,7 +433,8 @@
             cols = slice((j * count + s) * lanes, (j * count + s + 1) * lanes)
             rhs_scr[0:block, cols] = v
             rhs_scr[block:, cols] = v
-    sv_scr[...] = dot(f_ref[:, block:], rhs_scr[...])
+        tile = slice(j * count * lanes, (j + 1) * count * lanes)
+        sv_scr[:, tile] = dot(f_ref[:, block:], rhs_scr[:, tile])
 
     def own(j, _):
         for s in range(count):
@@ -586,7 +600,29 @@
     o_ref[rows:] = mine_ref[0] + other_ref[0]
 
 
-def state_grad_kernel(sub, length, w_ref, term_ref, dkh_ref, dvec_ref, dlb_ref, ft_ref, o_ref,
+PAIR = 2 * FINE
+
+
+def power_kernel(pow_ref, o_ref):
+    def some(g, _):
+        rows = pl.ds(pl.multiple_of(g * 8, 8), 8)
+        at = [2 * POWERS.index(PAIR * v) for v in range(1, COARSE // 2 + 1)]
+        small = [(pow_ref[i, rows], pow_ref[i + 1, rows]) for i in at]
+        x = jnp.ones((8, LANES), f32), jnp.zeros((8, LANES), f32)
+        for u in range(DOCMAX // PAIR // (COARSE // 2)):
+            for v in range(COARSE // 2):
+                m = u * (COARSE // 2) + v
+                o_ref[2 * m, rows], o_ref[2 * m + 1, rows] = cmul(*x, *small[v - 1]) if v else x
+            x = cmul(*x, *small[-1])
+        return 0
+
+    lax.fori_loop(0, pow_ref.shape[1] // 8, some, 0)
+
+
+CHAINS = 2
+
+
+def state_grad_kernel(sub, length, w_ref, term_ref, pow_ref, far_ref, dkh_ref, dvec_ref, dlb_ref, ft_ref, o_ref,
                       dk_scr, f_scr, dw_scr, y_scr):
     ndp = o_ref.shape[0]
     n_w, lanes = w_ref.shape
@@ -609,35 +645,44 @@
     at8 = iota((8, lanes), 0).astype(f32)
 
     def one(n, _):
-        (fr, fi), w = rows8(term_ref[2, pl.ds(n, 1), :], term_ref[3, pl.ds(n, 1), :])
-        pows = powers(*w)
+        fr, fi = rows8(pow_ref, n)
         zero = jnp.zeros((8, lanes), f32)
-        s_re, s_im, e_re, e_im, h_re, h_im = (zero,) * 6
-        for u in range(DOCMAX // FINE // COARSE - 1, -1, -1):
-            t_re, t_im, o_re, o_im = (zero,) * 4
-            for v in range(COARSE - 1, 0, -1):
-                at = (u * COARSE + v) * FINE
-                dk = dk_scr[at : at + FINE]
-                t_re = t_re + dk * pows[v][0]
-                t_im = t_im + dk * pows[v][1]
-                o_re = o_re + t_re
-                o_im = o_im + t_im
-            t_re = t_re + dk_scr[u * COARSE * FINE : u * COARSE * FINE + FINE]
-            e_re, e_im = cmul(e_re, e_im, *pows[COARSE])
-            s_re, s_im = cmul(s_re, s_im, *pows[COARSE])
-            h_re, h_im = cmul(h_re, h_im, *pows[COARSE])
-            e_re, e_im = e_re + s_re, e_im + s_im
-            s_re, s_im = s_re + t_re, s_im + t_im
-            h_re, h_im = h_re + o_re, h_im + o_im
-        m_re = (FINE * COARSE) * e_re + FINE * h_re + at8 * s_re
-        m_im = (FINE * COARSE) * e_im + FINE * h_im + at8 * s_im
-        s_re, s_im = cmul(s_re, s_im, fr, fi)
-        m_re, m_im = cmul(m_re, m_im, fr, fi)
+        span = DOCMAX // PAIR // CHAINS
+        sums = []
+        for c in range(CHAINS):
+            acc = [[zero] * 4, [zero] * 4]
+            for m in range(c * span + span - 1, c * span - 1, -1):
+                if m:
+                    p_re = jnp.broadcast_to(far_ref[2 * m, pl.ds(n, 1), :], (8, lanes))
+                    p_im = jnp.broadcast_to(far_ref[2 * m + 1, pl.ds(n, 1), :], (8, lanes))
+                for h, one_acc in enumerate(acc):
+                    at = m * PAIR + h * FINE
+                    dk = dk_scr[at : at + FINE]
+                    one_acc[0] = one_acc[0] + (dk * p_re if m else dk)
+                    if m:
+                        one_acc[1] = one_acc[1] + dk * p_im
+                    if m > c * span:
+                        one_acc[2], one_acc[3] = one_acc[2] + one_acc[0], one_acc[3] + one_acc[1]
+            for one_acc in acc:
+                one_acc[2], one_acc[3] = (one_acc[2 + k] + (c * span) * one_acc[k] for k in (0, 1))
+            sums.append(acc)
+        low, high = (
+            [sum((acc[h][k] for acc in sums[1:]), sums[0][h][k]) for k in range(4)] for h in (0, 1)
+        )
+        for h, part in enumerate((low, high)):
+            for k in (0, 1):
+                part[2 + k] = PAIR * part[2 + k] + (at8 + float(h * FINE)) * part[k]
+        shift = wide_row(pow_ref, FINE, 0, n), wide_row(pow_ref, FINE, 1, n)
+        values = []
+        for k in (0, 2):
+            up = cmul(high[k], high[k + 1], *shift)
+            values.append(cmul(low[k] + up[0], low[k + 1] + up[1], fr, fi))
+        (s_re, s_im), (m_re, m_im) = values
         for slot, value in enumerate((s_re, s_im, m_re, m_im)):
             f_scr[slot, pl.ds(n, 1), :] = jnp.sum(value, axis=0, keepdims=True)
         return 0
 
-    lax.fori_loop(0, nstate, one, 0)
+    lax.fori_loop(0, nstate, one, 0, unroll=2)
     a, b, z_re, z_im, one_re, one_im, far_re, far_im, den_re, den_im, inv, g_re, g_im = (
         term_ref[slot] for slot in range(TERMS)
     )
@@ -781,9 +826,10 @@
             shared = jnp.concatenate([shared, more], axis=0)
 
     spec = (nseq, 2 * block, wide)
-    kh, vec, w_all, terms = call(
+    kh, vec, w_all, terms, pows = call(
         partial(lag_kernel, sub, length, masks, len(shared_parts)),
-        [shape(spec), shape((8, wide)), shape((n_w, wide)), shape((TERMS, nstate, wide))],
+        [shape(spec), shape((8, wide)), shape((n_w, wide)), shape((TERMS, nstate, wide)),
+         shape((2 * len(POWERS), nstate, wide))],
         [VM] * (len(shared_parts) + 1),
         scratch=[pltpu.VMEM((length, wide), f32), pltpu.VMEM((2, nstate, wide), f32),
                  pltpu.VMEM((3 * block, nseq * wide), bf16), pltpu.VMEM((2 * block, nseq * wide), f32)],
@@ -810,14 +856,18 @@
         [VM] * nseq + [AN] + [VM] * 4,
         scratch=[lens, cuts, pltpu.VMEM((3 * block, across), bf16), pltpu.VMEM((2 * block, across), f32),
                  pltpu.VMEM((6 * block, across), bf16), pltpu.VMEM(blocks4, f32), DMA],
-        name="doc_conv", mib=20, us=7, keep=[w_all, terms, block_in, cotangent],
+        name="doc_conv", mib=20, us=7, keep=[w_all, terms, pows, block_in, cotangent],
     )(*hats, doc_lengths, vec, kh, f_table, ft_table)
-    keep = [w_all, terms, vec, kh, f_table, ft_table, spectra_u, x_blocks]
+    keep = [w_all, terms, pows, vec, kh, f_table, ft_table, spectra_u, x_blocks]
     if len(ahead) == 2:
         *convs, w_slots[1], w_slots[2] = tie(*convs, w_slots[1], w_slots[2])
     convs = trade(convs, "seq")
     if len(ahead) == 2:
         w_slots.append(swap(w_slots[1], "dp", ahead[1]))
+    pows_late, _ = tie(pows, convs[1])
+    far = call(power_kernel, shape((2 * DOCMAX // PAIR, nstate, wide)), [VM], name="state_powers", mib=16, us=1, keep=keep)(pows_late)
+    convs[2], _ = tie(convs[2], far)
+    keep.append(far)
     if cols % LANES == 0 and sub % 16 == 0:
         shared = jnp.concatenate([shared, shared_parts[-1]], axis=0)
         shared, convs[1] = tie(shared, convs[1])
@@ -863,22 +913,22 @@
         scratch=[lens, cuts, pltpu.VMEM(blocks4, bf16), pltpu.VMEM((2 * block, across), bf16),
                  pltpu.VMEM((2 * block, across), f32), pltpu.VMEM((2 * block, across), f32),
                  pltpu.VMEM((6 * block, across), bf16), pltpu.VMEM(blocks4, f32), DMA],
-        name="doc_conv_grad", mib=24, us=8, keep=[w_all, terms],
+        name="doc_conv_grad", mib=24, us=8, keep=[w_all, terms, pows, far],
     )(*d_convs, x_blocks, doc_lengths, spectra_u, vec, kh, f_table, ft_table)
     g_own, dkh, d_norm = out[:nseq], out[nseq], out[nseq + 1]
     if staged:
         stay, send = call(
-            deal_kernel, [shape((ndp // 2, wide, cols))] * 2, [VM, VM], name="weight_deal", us=1, keep=keep[:2]
+            deal_kernel, [shape((ndp // 2, wide, cols))] * 2, [VM, VM], name="weight_deal", us=1, keep=[w_all, terms, pows, far]
         )(stay, dw_other)
         dkh, *_ = tie(dkh, send)
         dw_other = swap(send, "dp", 1)
 
     small = call(
-        partial(state_grad_kernel, sub, length), shape((ndp, rows, LANES)), [VM] * 6,
+        partial(state_grad_kernel, sub, length), shape((ndp, rows, LANES)), [VM] * 8,
         scratch=[pltpu.VMEM((length, wide), f32), pltpu.VMEM((4, nstate, wide), f32), pltpu.VMEM((n_w, wide), f32),
                  pltpu.VMEM((6 * block, nseq * wide), bf16)],
         name="state_grad", mib=10, us=10,
-    )(w_all, terms, dkh, d_norm, d_lin_bias, ft_table)
+    )(w_all, terms, pows, far, dkh, d_norm, d_lin_bias, ft_table)
     small, *g_own = tie(small, *g_own)
     if staged:
         small, dw_other = tie(small, dw_other)

time: 97 us -> 95 us (0.979)
  Pallas kernels: 42.4 us -> 40.8 us
    pallas_call x15 -> x16, Pallas kernels: 42.4 us -> 40.8 us  [call(): return lambda *args: kernel(*args, *keep)]
  transfers between devices with their start and end apart: 28 -> 28, of which waited for: 11 -> 12; matrix products, arithmetic and copies ran while one was open for 0% -> 0% of each run, Pallas kernels for 36% -> 35%
where the time goes in v4:
time: 95 us; the launch traced here: 94.7 us
  Pallas kernels  40.8 us (43%)
  starting transfers between devices  31.3 us (33%)
  waiting for transfers between devices  21.6 us (23%)
    pallas_call x16, Pallas kernels, call(): return lambda *args: kernel(*args, *keep)  40.8 us
    ppermute x27, starting transfers between devices, swap(): lax.ppermute(v, axis, [(i, i ^ by) for i in range(n)])  27.9 us
    ppermute x27, waiting for transfers between devices, swap(): lax.ppermute(v, axis, [(i, i ^ by) for i in range(n)])  18 us
    all_to_all x1, waiting for transfers between devices, on_device(): small = lax.all_to_all(small, 'dp', 0, 0, tiled=True)  3.58 us
    all_to_all x1, starting transfers between devices, on_device(): small = lax.all_to_all(small, 'dp', 0, 0, tiled=True)  3.36 us
  transfers between devices with their start and end apart: 28, of which 12 were waited for; matrix products, arithmetic and copies ran while one was open for 0% of the time, Pallas kernels for 35%

profile of v4, /device:TPU:0, one launch (start us, length us, event | category | flops | bytes accessed | tf_op | source)
XLA Modules:
  0.0 94.7 jit_solution(258116551634365334)
XLA Ops:
  0.7 1.8 %pack.1.refs_0_ = f32[1,24,128]{2,1,0:T(8,128)} custom-call(f32[128,64]{1,0:T(8,128)} %bitcast.19, f32[1,64]{1,0:T(1,128)} %bitcast.20, f32[1,64]{1,0:T(1,128)} %bitcast.21, f32[1,64]{1,0:T(1,128)} %bitcast.22, f32[1,64]{1,0:T(1,128)} %bitcast.23, f32[1,8]{1,0:T(1,128)} %bitcast.24, f32[1,8]{1,0:T(1,128)} %bitcast.25, f32[1,128]{1,0:T(1,128)} %bitcast.26), custom_call_target="tpu_custom_call" | custom-call | flops 2300000000 | bytes 1000 | tf_op jit(solution)/shard_map/pack/pallas_call | solution.py:53
  2.5 4.1 %collective-permute-start = (f32[1,24,128]{2,1,0:T(8,128)}, f32[1,24,128]{2,1,0:T(8,128)S(1)}, u32[]{:S(2)}, u32[]{:S(2)}) collective-permute-start(f32[1,24,128]{2,1,0:T(8,128)} %pack.1.refs_0_), channel_id=1, source_target_pairs={{0,16},{4,20},{8,24},{12,28},{16,0},{20,4},{24,8},{28,12},{1,17},{... | collective-permute-start | bytes 36872 | tf_op jit(solution)/shard_map/ppermute | solution.py:766
  6.6 2.0 %layer_norm.1 = (f32[2,256,128]{2,1,0:T(8,128)S(1)}, f32[2,256,128]{2,1,0:T(8,128)S(1)}, f32[2,256,128]{2,1,0:T(8,128)S(1)}, f32[2,256,128]{2,1,0:T(8,128)S(1)}) custom-call(bf16[2,256,512]{2,1,0:T(8,128)(2,1)S(1)} %copy-done.2), custom_call_target="tpu_custom_call" | custom-call | flops 2300000000 | bytes 1000 | tf_op jit(solution)/shard_map/layer_norm/pallas_call | solution.py:53
  8.8 1.7 %collective-permute-start.1 = (f32[2,24,128]{2,1,0:T(8,128)S(1)}, f32[2,24,128]{2,1,0:T(8,128)S(1)}, u32[]{:S(2)}, u32[]{:S(2)}) collective-permute-start(f32[2,24,128]{2,1,0:T(8,128)S(1)} %pad_maximum_fusion.3), channel_id=1, source_target_pairs={{0,8},{4,12},{8,0},{12,4},{16,24},{20,28},{24,16},{28,20},{1,9},{5... | collective-permute-start | bytes 73736 | tf_op jit(solution)/shard_map/ppermute | solution.py:766
  10.5 2.6 %collective-permute-start.6 = (bf16[1,512,128]{2,1,0:T(8,128)(2,1)S(1)}, bf16[1,512,128]{2,1,0:T(8,128)(2,1)S(1)}, u32[]{:S(2)}, u32[]{:S(2)}) collective-permute-start(bf16[1,512,128]{2,1,0:T(8,128)(2,1)S(1)} %bitcast.17), channel_id=1, source_target_pairs={{0,16},{4,20},{8,24},{12,28},{16,0},{20,4},{24,8},{28,12},{1,17},{... | collective-permute-start | bytes 393224 | tf_op jit(solution)/shard_map/ppermute | solution.py:766
  13.1 1.5 %collective-permute-start.3 = (f32[2,256,128]{2,1,0:T(8,128)S(1)}, f32[2,256,128]{2,1,0:T(8,128)S(1)}, u32[]{:S(2)}, u32[]{:S(2)}) collective-permute-start(f32[2,256,128]{2,1,0:T(8,128)S(1)} %get-tuple-element.97), channel_id=1, source_target_pairs={{0,2},{1,3},{2,0},{3,1},{4,6},{5,7},{6,4},{7,5},{8,10},{9,11},{10,... | collective-permute-start | bytes 786440 | tf_op jit(solution)/shard_map/ppermute | solution.py:766
  14.6 1.6 %collective-permute-start.5 = (f32[4,24,128]{2,1,0:T(8,128)S(1)}, f32[4,24,128]{2,1,0:T(8,128)S(1)}, u32[]{:S(2)}, u32[]{:S(2)}) collective-permute-start(f32[4,24,128]{2,1,0:T(8,128)S(1)} %pad_maximum_fusion.2), channel_id=1, source_target_pairs={{0,4},{4,0},{8,12},{12,8},{16,20},{20,16},{24,28},{28,24},{1,5},{5... | collective-permute-start | bytes 147464 | tf_op jit(solution)/shard_map/ppermute | solution.py:766
  16.2 2.8 %collective-permute-done.5.refs_3_ = f32[4,24,128]{2,1,0:T(8,128)S(1)} collective-permute-done((f32[4,24,128]{2,1,0:T(8,128)S(1)}, f32[4,24,128]{2,1,0:T(8,128)S(1)}, u32[]{:S(2)}, u32[]{:S(2)}) %collective-permute-start.5) | collective-permute-done | bytes 49184 | tf_op jit(solution)/shard_map/ppermute | solution.py:766
  19.0 5.6 %lag_kernel.1 = (f32[4,512,128]{2,1,0:T(8,128)S(1)}, f32[8,128]{1,0:T(8,128)S(1)}, f32[128,128]{1,0:T(8,128)S(1)}, f32[13,64,128]{2,1,0:T(8,128)S(1)}, f32[26,64,128]{2,1,0:T(8,128)S(1)}) custom-call(f32[1,24,128]{2,1,0:T(8,128)S(1)} %copy-done.4, f32[1,24,128]{2,1,0:T(8,128)S(1)} %collective-permute-done.refs_1_, ...), custom_call_target="tpu_custom_call" | custom-call | bytes 1000 | tf_op jit(solution)/shard_map/lag_kernel/pallas_call | solution.py:53
  24.6 1.6 %collective-permute-start.8 = (bf16[2,512,128]{2,1,0:T(8,128)(2,1)S(1)}, bf16[2,512,128]{2,1,0:T(8,128)(2,1)S(1)}, u32[]{:S(2)}, u32[]{:S(2)}) collective-permute-start(bf16[2,512,128]{2,1,0:T(8,128)(2,1)S(1)} %pad_maximum_fusion.refs_1_), channel_id=1, source_target_pairs={{0,4},{4,0},{8,12},{12,8},{16,20},{20,16},{24,28},{28,24},{1,5},{5... | collective-permute-start | bytes 786440 | tf_op jit(solution)/shard_map/ppermute | solution.py:766
  26.2 0.4 collective-permute-start.7
  26.7 6.6 %doc_conv.1 = (bf16[2,256,128]{2,1,0:T(8,128)(2,1)S(1)}, bf16[2,256,128]{2,1,0:T(8,128)(2,1)S(1)}, bf16[2,256,128]{2,1,0:T(8,128)(2,1)S(1)}, bf16[2,256,128]{2,1...) custom-call(f32[2,256,128]{2,1,0:T(8,128)S(1)} %get-tuple-element.93.refs_0_, ...), custom_call_target="tpu_custom_call" | custom-call | flops 8049999872 | bytes 1000 | tf_op jit(solution)/shard_map/doc_conv/pallas_call | solution.py:53
  33.3 0.7 collective-permute-done.7.refs_2_
  33.9 0.5 collective-permute-start.12
  34.5 1.7 %collective-permute-start.10 = (bf16[2,256,128]{2,1,0:T(8,128)(2,1)S(1)}, bf16[2,256,128]{2,1,0:T(8,128)(2,1)S(1)}, u32[]{:S(2)}, u32[]{:S(2)}) collective-permute-start(bf16[2,256,128]{2,1,0:T(8,128)(2,1)S(1)} %get-tuple-element.114), channel_id=1, source_target_pairs={{0,2},{1,3},{2,0},{3,1},{4,6},{5,7},{6,4},{7,5},{8,10},{9,11},{10,... | collective-permute-start | bytes 393224 | tf_op jit(solution)/shard_map/ppermute | solution.py:766
  36.2 0.2 collective-permute-start.11
  36.4 0.5 state_powers.1.refs_14_.refs_17_.refs_11_.refs_5_.refs_3_
  36.9 3.9 %collective-permute-done.10.refs_2_ = bf16[2,256,128]{2,1,0:T(8,128)(2,1)S(1)} collective-permute-done((bf16[2,256,128]{2,1,0:T(8,128)(2,1)S(1)}, bf16[2,256,128]{2,1,0:T(8,128)(2,1)S(1)}, u32[]{:S(2)}, u32[]{:S(2)}) %collective-permute-start.10) | collective-permute-done | bytes 131104 | tf_op jit(solution)/shard_map/ppermute | solution.py:766
  40.8 0.7 collective-permute-done.12.refs_4_
  41.5 0.3 linear_rows.1
  41.8 0.9 collective-permute-done.11.refs_3_
  42.7 4.9 %gated_linear.1 = (bf16[2,256,512]{2,1,0:T(8,128)(2,1)}, f32[1,1024]{1,0:T(1,128)S(1)}, bf16[2,256,128]{2,1,0:T(8,128)(2,1)S(1)}, bf16[2,256,128]{2,1,0:T(8,128)...) custom-call(bf16[2,256,128]{2,1,0:T(8,128)(2,1)S(1)} %get-tuple-elem, ...), custom_call_target="tpu_custom_call" | custom-call | flops 5750000128 | bytes 1000 | tf_op jit(solution)/shard_map/gated_linear/pallas_call | solution.py:53
  47.6 0.4 collective-permute-start.15
  48.0 1.8 %collective-permute-start.14 = (bf16[2,256,128]{2,1,0:T(8,128)(2,1)S(1)}, bf16[2,256,128]{2,1,0:T(8,128)(2,1)S(1)}, u32[]{:S(2)}, u32[]{:S(2)}) collective-permute-start(bf16[2,256,128]{2,1,0:T(8,128)(2,1)S(1)} %get-tuple-element.128), channel_id=1, source_target_pairs={{0,2},{1,3},{2,0},{3,1},{4,6},{5,7},{6,4},{7,5},{8,10},{9,11},{10,... | collective-permute-start | bytes 393224 | tf_op jit(solution)/shard_map/ppermute | solution.py:766
  49.8 0.4 collective-permute-start.16
  50.3 1.8 %collective-permute-start.17 = (bf16[1,128,1024]{2,1,0:T(8,128)(2,1)S(1)}, bf16[1,128,1024]{2,1,0:T(8,128)(2,1)S(1)}, u32[]{:S(2)}, u32[]{:S(2)}) collective-permute-start(bf16[1,128,1024]{2,1,0:T(8,128)(2,1)S(1)} %get-tuple-element.131), channel_id=1, source_target_pairs={{0,2},{1,3},{2,0},{3,1},{4,6},{5,7},{6,4},{7,5},{8,10},{9,11},{10,... | collective-permute-start | bytes 786440 | tf_op jit(solution)/shard_map/ppermute | solution.py:766
  52.1 2.2 %collective-permute-done.14.refs_2_ = bf16[2,256,128]{2,1,0:T(8,128)(2,1)S(1)} collective-permute-done((bf16[2,256,128]{2,1,0:T(8,128)(2,1)S(1)}, bf16[2,256,128]{2,1,0:T(8,128)(2,1)S(1)}, u32[]{:S(2)}, u32[]{:S(2)}) %collective-permute-start.14) | collective-permute-done | bytes 131104 | tf_op jit(solution)/shard_map/ppermute | solution.py:766
  54.3 2.1 %collective-permute-done.16.refs_3_ = bf16[2,256,128]{2,1,0:T(8,128)(2,1)S(1)} collective-permute-done((bf16[2,256,128]{2,1,0:T(8,128)(2,1)S(1)}, bf16[2,256,128]{2,1,0:T(8,128)(2,1)S(1)}, u32[]{:S(2)}, u32[]{:S(2)}) %collective-permute-start.16) | collective-permute-done | bytes 131104 | tf_op jit(solution)/shard_map/ppermute | solution.py:766
  56.4 7.3 %doc_conv_grad.1 = (bf16[2,256,128]{2,1,0:T(8,128)(2,1)S(1)}, bf16[2,256,128]{2,1,0:T(8,128)(2,1)S(1)}, bf16[2,256,128]{2,1,0:T(8,128)(2,1)S(1)}, bf16[2,256,128...) custom-call(bf16[2,256,128]{2,1,0:T(8,128)(2,1)S(1)} %get-tuple-element.126.refs_0_, ...), custom_call_target="tpu_custom_call" | custom-call | flops 9200000000 | bytes 1000 | tf_op jit(solution)/shard_map/doc_conv_grad/pallas_call | solution.py:53
  63.7 0.2 weight_deal.1
  63.9 1.6 %collective-permute-start.21 = (f32[4,128,128]{2,1,0:T(8,128)S(1)}, f32[4,128,128]{2,1,0:T(8,128)S(1)}, u32[]{:S(2)}, u32[]{:S(2)}) collective-permute-start(f32[4,128,128]{2,1,0:T(8,128)S(1)} %get-tuple-element.136), channel_id=1, source_target_pairs={{0,4},{4,0},{8,12},{12,8},{16,20},{20,16},{24,28},{28,24},{1,5},{5... | collective-permute-start | bytes 786440 | tf_op jit(solution)/shard_map/ppermute | solution.py:766
  65.5 8.8 %state_grad.1 = f32[8,24,128]{2,1,0:T(8,128)} custom-call(f32[128,128]{1,0:T(8,128)S(1)} %get-tuple-element.103.refs_9_.refs_1_.refs_5_.refs_8_.refs_2_.refs_11_.refs_0_, f32[13,64,128]{2,1,0:T(8,128)S(1)} %get-tuple-element.104.refs_10_.refs_2_.refs_6_.refs_9_.refs_3_.refs_12_.refs_1_, ...), custom_call_target="tpu_custom_call" | custom-call | flops 11500000256 | bytes 1000 | tf_op jit(solution)/shard_map/state_grad/pallas_call | solution.py:53
  74.3 0.8 collective-permute-start.22
  75.1 3.4 %all-to-all-start = ((f32[8,24,128]{2,1,0:T(8,128)}), f32[8,24,128]{2,1,0:T(8,128)S(1)}, u32[]{:S(2)}, u32[]{:S(2)}) async-start(f32[8,24,128]{2,1,0:T(8,128)} %state_grad.1), calls=%async_computation | async-start | bytes 196608 | tf_op jit(solution)/shard_map/all_to_all | solution.py:935
  78.5 0.3 collective-permute-start.18
  78.8 1.2 %collective-permute-done.22.refs_1_ = f32[2,128,128]{2,1,0:T(8,128)S(1)} collective-permute-done((f32[2,128,128]{2,1,0:T(8,128)S(1)}, f32[2,128,128]{2,1,0:T(8,128)S(1)}, u32[]{:S(2)}, u32[]{:S(2)}) %collective-permute-start.22) | collective-permute-done | bytes 131104 | tf_op jit(solution)/shard_map/ppermute | solution.py:766
  80.1 1.4 %collective-permute-start.23 = (f32[1,128,128]{2,1,0:T(8,128)S(1)}, f32[1,128,128]{2,1,0:T(8,128)S(1)}, u32[]{:S(2)}, u32[]{:S(2)}) collective-permute-start(f32[1,128,128]{2,1,0:T(8,128)S(1)} %get-tuple-element.155), channel_id=1, source_target_pairs={{0,16},{4,20},{8,24},{12,28},{16,0},{20,4},{24,8},{28,12},{1,17},{... | collective-permute-start | bytes 196616 | tf_op jit(solution)/shard_map/ppermute | solution.py:766
  81.4 1.4 %collective-permute-start.19 = (bf16[2,256,128]{2,1,0:T(8,128)(2,1)S(1)}, bf16[2,256,128]{2,1,0:T(8,128)(2,1)S(1)}, u32[]{:S(2)}, u32[]{:S(2)}) collective-permute-start(bf16[2,256,128]{2,1,0:T(8,128)(2,1)S(1)} %get-tuple-element.146), channel_id=1, source_target_pairs={{0,2},{1,3},{2,0},{3,1},{4,6},{5,7},{6,4},{7,5},{8,10},{9,11},{10,... | collective-permute-start | bytes 393224 | tf_op jit(solution)/shard_map/ppermute | solution.py:766
  82.9 0.1 collective-permute-start.20
  83.0 3.6 %all-to-all-done.refs_0_ = f32[8,24,128]{2,1,0:T(8,128)S(1)} async-done(((f32[8,24,128]{2,1,0:T(8,128)}), f32[8,24,128]{2,1,0:T(8,128)S(1)}, u32[]{:S(2)}, u32[]{:S(2)}) %all-to-all-start) | async-done | bytes 98336 | tf_op jit(solution)/shard_map/all_to_all | solution.py:935
  86.6 0.9 collective-permute-done.23.refs_2_
  87.5 1.2 %collective-permute-start.26 = (f32[152,128]{1,0:T(8,128)S(1)}, f32[152,128]{1,0:T(8,128)S(1)}, u32[]{:S(2)}, u32[]{:S(2)}) collective-permute-start(f32[152,128]{1,0:T(8,128)S(1)} %last_sums.1.refs_0_), channel_id=1, source_target_pairs={{0,3},{1,2},{2,1},{3,0},{4,7},{5,6},{6,5},{7,4},{8,11},{9,10},{10,... | collective-permute-start | bytes 233480 | tf_op jit(solution)/shard_map/ppermute | solution.py:766
  88.7 0.5 collective-permute-start.25
  89.2 0.2 collective-permute-start.24
  89.4 1.8 %layer_norm_grad.1 = bf16[2,256,512]{2,1,0:T(8,128)(2,1)} custom-call(bf16[2,256,128]{2,1,0:T(8,128)(2,1)S(1)} %get-tuple-element.144.refs_0_, bf16[2,256,128]{2,1,0:T(8,128)(2,1)S(1)} %collective-permute-done.18.refs_1_, bf16[2,256,128]{2,1,0:T(8,128)(2,1)S(1)} %collective-permute-done.19.refs_2_, bf16[2,256,128]{2,1,0:T(8,128)(2,1)S(1)} %collective-permute-done.20.refs_3_, ...), custom_call_target="tpu_custom_call" | custom-call | bytes 1000 | tf_op jit(solution)/shard_map/layer_norm_grad/pallas_call | solution.py:53
  91.2 0.9 collective-permute-done.26.refs_3_
  92.1 1.8 %collective-permute-done.25.refs_2_ = f32[152,128]{1,0:T(8,128)S(1)} collective-permute-done((f32[152,128]{1,0:T(8,128)S(1)}, f32[152,128]{1,0:T(8,128)S(1)}, u32[]{:S(2)}, u32[]{:S(2)}) %collective-permute-start.25) | collective-permute-done | bytes 77856 | tf_op jit(solution)/shard_map/ppermute | solution.py:766
  93.9 0.8 last.1
  (42 shorter events, 0.5 us)
Async XLA Ops:
  0.6 6.0 %copy-start.2 = (bf16[2,256,512]{2,1,0:T(8,128)(2,1)S(1)}, bf16[2,256,512]{2,1,0:T(8,128)(2,1)}, u32[]{:S(2)}) copy-start(bf16[2,256,512]{2,1,0:T(8,128)(2,1)} %refs_4_.6) | copy-start | bytes 1572868
  2.5 6.3 %copy-start.4 = (f32[1,24,128]{2,1,0:T(8,128)S(1)}, f32[1,24,128]{2,1,0:T(8,128)}, u32[]{:S(2)}) copy-start(f32[1,24,128]{2,1,0:T(8,128)} %pack.1.refs_0_) | copy-start | bytes 36868
  2.5 8.0 %copy-start.6 = (bf16[512,128]{1,0:T(8,128)(2,1)S(1)}, bf16[512,128]{1,0:T(8,128)(2,1)}, u32[]{:S(2)}) copy-start(bf16[512,128]{1,0:T(8,128)(2,1)} %param.23) | copy-start | bytes 393220
  2.5 16.5 %copy-start = (bf16[256,1536]{1,0:T(8,128)(2,1)S(1)}, bf16[256,1536]{1,0:T(8,128)(2,1)}, u32[]{:S(2)}) copy-start(bf16[256,1536]{1,0:T(8,128)(2,1)} %constant.5.clone.refs_5_.refs_8_.refs_7_.refs_11_.refs_14_.refs_10_) | copy-start | bytes 2359300
  2.5 16.5 %copy-start.1 = (bf16[512,768]{1,0:T(8,128)(2,1)S(1)}, bf16[512,768]{1,0:T(8,128)(2,1)}, u32[]{:S(2)}) copy-start(bf16[512,768]{1,0:T(8,128)(2,1)} %constant.4.clone.refs_4_.refs_7_.refs_6_.refs_10_.refs_13_.refs_9_) | copy-start | bytes 2359300
  2.5 16.5 %copy-start.3 = (bf16[2,256,512]{2,1,0:T(8,128)(2,1)S(1)}, bf16[2,256,512]{2,1,0:T(8,128)(2,1)}, u32[]{:S(2)}) copy-start(bf16[2,256,512]{2,1,0:T(8,128)(2,1)} %refs_5_.6) | copy-start | bytes 1572868
  2.5 24.2 %copy-start.5 = (s32[2,4]{1,0:T(2,128)S(1)}, s32[2,4]{1,0:T(2,128)}, u32[]{:S(2)}) copy-start(s32[2,4]{1,0:T(2,128)} %refs_5_.5) | copy-start | bytes 100
  2.5 6.2 %collective-permute-start = (f32[1,24,128]{2,1,0:T(8,128)}, f32[1,24,128]{2,1,0:T(8,128)S(1)}, u32[]{:S(2)}, u32[]{:S(2)}) collective-permute-start(f32[1,24,128]{2,1,0:T(8,128)} %pack.1.refs_0_), channel_id=1, source_target_pairs={{0,16},{4,20},{8,24},{12,28},{16,0},{20,4},{24,8},{28,12},{1,17},{... | collective-permute-start | bytes 36872 | tf_op jit(solution)/shard_map/ppermute | solution.py:766
  8.7 5.9 %collective-permute-start.2 = (f32[2,256,128]{2,1,0:T(8,128)S(1)}, f32[2,256,128]{2,1,0:T(8,128)S(1)}, u32[]{:S(2)}, u32[]{:S(2)}) collective-permute-start(f32[2,256,128]{2,1,0:T(8,128)S(1)} %get-tuple-element.95), channel_id=1, source_target_pairs={{0,1},{1,0},{2,3},{3,2},{4,5},{5,4},{6,7},{7,6},{8,9},{9,8},{10,11... | collective-permute-start | bytes 786440 | tf_op jit(solution)/shard_map/ppermute | solution.py:766
  8.8 5.8 %collective-permute-start.1 = (f32[2,24,128]{2,1,0:T(8,128)S(1)}, f32[2,24,128]{2,1,0:T(8,128)S(1)}, u32[]{:S(2)}, u32[]{:S(2)}) collective-permute-start(f32[2,24,128]{2,1,0:T(8,128)S(1)} %pad_maximum_fusion.3), channel_id=1, source_target_pairs={{0,8},{4,12},{8,0},{12,4},{16,24},{20,28},{24,16},{28,20},{1,9},{5... | collective-permute-start | bytes 73736 | tf_op jit(solution)/shard_map/ppermute | solution.py:766
  10.5 14.1 %collective-permute-start.6 = (bf16[1,512,128]{2,1,0:T(8,128)(2,1)S(1)}, bf16[1,512,128]{2,1,0:T(8,128)(2,1)S(1)}, u32[]{:S(2)}, u32[]{:S(2)}) collective-permute-start(bf16[1,512,128]{2,1,0:T(8,128)(2,1)S(1)} %bitcast.17), channel_id=1, source_target_pairs={{0,16},{4,20},{8,24},{12,28},{16,0},{20,4},{24,8},{28,12},{1,17},{... | collective-permute-start | bytes 393224 | tf_op jit(solution)/shard_map/ppermute | solution.py:766
  13.1 13.6 %collective-permute-start.3 = (f32[2,256,128]{2,1,0:T(8,128)S(1)}, f32[2,256,128]{2,1,0:T(8,128)S(1)}, u32[]{:S(2)}, u32[]{:S(2)}) collective-permute-start(f32[2,256,128]{2,1,0:T(8,128)S(1)} %get-tuple-element.97), channel_id=1, source_target_pairs={{0,2},{1,3},{2,0},{3,1},{4,6},{5,7},{6,4},{7,5},{8,10},{9,11},{10,... | collective-permute-start | bytes 786440 | tf_op jit(solution)/shard_map/ppermute | solution.py:766
  14.6 12.1 %collective-permute-start.4 = (f32[2,256,128]{2,1,0:T(8,128)S(1)}, f32[2,256,128]{2,1,0:T(8,128)S(1)}, u32[]{:S(2)}, u32[]{:S(2)}) collective-permute-start(f32[2,256,128]{2,1,0:T(8,128)S(1)} %get-tuple-element.98), channel_id=1, source_target_pairs={{0,3},{1,2},{2,1},{3,0},{4,7},{5,6},{6,5},{7,4},{8,11},{9,10},{10,... | collective-permute-start | bytes 786440 | tf_op jit(solution)/shard_map/ppermute | solution.py:766
  14.6 4.4 %collective-permute-start.5 = (f32[4,24,128]{2,1,0:T(8,128)S(1)}, f32[4,24,128]{2,1,0:T(8,128)S(1)}, u32[]{:S(2)}, u32[]{:S(2)}) collective-permute-start(f32[4,24,128]{2,1,0:T(8,128)S(1)} %pad_maximum_fusion.2), channel_id=1, source_target_pairs={{0,4},{4,0},{8,12},{12,8},{16,20},{20,16},{24,28},{28,24},{1,5},{5... | collective-permute-start | bytes 147464 | tf_op jit(solution)/shard_map/ppermute | solution.py:766
  24.6 8.6 %collective-permute-start.8 = (bf16[2,512,128]{2,1,0:T(8,128)(2,1)S(1)}, bf16[2,512,128]{2,1,0:T(8,128)(2,1)S(1)}, u32[]{:S(2)}, u32[]{:S(2)}) collective-permute-start(bf16[2,512,128]{2,1,0:T(8,128)(2,1)S(1)} %pad_maximum_fusion.refs_1_), channel_id=1, source_target_pairs={{0,4},{4,0},{8,12},{12,8},{16,20},{20,16},{24,28},{28,24},{1,5},{5... | collective-permute-start | bytes 786440 | tf_op jit(solution)/shard_map/ppermute | solution.py:766
  26.2 7.7 %collective-permute-start.7 = (bf16[2,512,128]{2,1,0:T(8,128)(2,1)S(1)}, bf16[2,512,128]{2,1,0:T(8,128)(2,1)S(1)}, u32[]{:S(2)}, u32[]{:S(2)}) collective-permute-start(bf16[2,512,128]{2,1,0:T(8,128)(2,1)S(1)} %pad_maximum_fusion.refs_1_), channel_id=1, source_target_pairs={{0,8},{4,12},{8,0},{12,4},{16,24},{20,28},{24,16},{28,20},{1,9},{5... | collective-permute-start | bytes 786440 | tf_op jit(solution)/shard_map/ppermute | solution.py:766
  33.9 7.6 %collective-permute-start.12 = (bf16[2,512,128]{2,1,0:T(8,128)(2,1)S(1)}, bf16[2,512,128]{2,1,0:T(8,128)(2,1)S(1)}, u32[]{:S(2)}, u32[]{:S(2)}) collective-permute-start(bf16[2,512,128]{2,1,0:T(8,128)(2,1)S(1)} %collective-permute-done.7.refs_2_), channel_id=1, source_target_pairs={{0,4},{4,0},{8,12},{12,8},{16,20},{20,16},{24,28},{28,24},{1,5},{5... | collective-permute-start | bytes 786440 | tf_op jit(solution)/shard_map/ppermute | solution.py:766
  34.5 2.0 %collective-permute-start.9 = (bf16[2,256,128]{2,1,0:T(8,128)(2,1)S(1)}, bf16[2,256,128]{2,1,0:T(8,128)(2,1)S(1)}, u32[]{:S(2)}, u32[]{:S(2)}) collective-permute-start(bf16[2,256,128]{2,1,0:T(8,128)(2,1)S(1)} %get-tuple-element.112), channel_id=1, source_target_pairs={{0,1},{1,0},{2,3},{3,2},{4,5},{5,4},{6,7},{7,6},{8,9},{9,8},{10,11... | collective-permute-start | bytes 393224 | tf_op jit(solution)/shard_map/ppermute | solution.py:766
  34.5 6.3 %collective-permute-start.10 = (bf16[2,256,128]{2,1,0:T(8,128)(2,1)S(1)}, bf16[2,256,128]{2,1,0:T(8,128)(2,1)S(1)}, u32[]{:S(2)}, u32[]{:S(2)}) collective-permute-start(bf16[2,256,128]{2,1,0:T(8,128)(2,1)S(1)} %get-tuple-element.114), channel_id=1, source_target_pairs={{0,2},{1,3},{2,0},{3,1},{4,6},{5,7},{6,4},{7,5},{8,10},{9,11},{10,... | collective-permute-start | bytes 393224 | tf_op jit(solution)/shard_map/ppermute | solution.py:766
  36.2 6.5 %collective-permute-start.11 = (bf16[2,256,128]{2,1,0:T(8,128)(2,1)S(1)}, bf16[2,256,128]{2,1,0:T(8,128)(2,1)S(1)}, u32[]{:S(2)}, u32[]{:S(2)}) collective-permute-start(bf16[2,256,128]{2,1,0:T(8,128)(2,1)S(1)} %get-tuple-element.119), channel_id=1, source_target_pairs={{0,3},{1,2},{2,1},{3,0},{4,7},{5,6},{6,5},{7,4},{8,11},{9,10},{10,... | collective-permute-start | bytes 393224 | tf_op jit(solution)/shard_map/ppermute | solution.py:766
  47.6 2.5 %collective-permute-start.15 = (bf16[2,128,1024]{2,1,0:T(8,128)(2,1)S(1)}, bf16[2,128,1024]{2,1,0:T(8,128)(2,1)S(1)}, u32[]{:S(2)}, u32[]{:S(2)}) collective-permute-start(bf16[2,128,1024]{2,1,0:T(8,128)(2,1)S(1)} %get-tuple-element.130), channel_id=1, source_target_pairs={{0,1},{1,0},{2,3},{3,2},{4,5},{5,4},{6,7},{7,6},{8,9},{9,8},{10,11... | collective-permute-start | bytes 1572872 | tf_op jit(solution)/shard_map/ppermute | solution.py:766
  48.0 6.3 %collective-permute-start.14 = (bf16[2,256,128]{2,1,0:T(8,128)(2,1)S(1)}, bf16[2,256,128]{2,1,0:T(8,128)(2,1)S(1)}, u32[]{:S(2)}, u32[]{:S(2)}) collective-permute-start(bf16[2,256,128]{2,1,0:T(8,128)(2,1)S(1)} %get-tuple-element.128), channel_id=1, source_target_pairs={{0,2},{1,3},{2,0},{3,1},{4,6},{5,7},{6,4},{7,5},{8,10},{9,11},{10,... | collective-permute-start | bytes 393224 | tf_op jit(solution)/shard_map/ppermute | solution.py:766
  49.7 4.6 %collective-permute-start.13 = (bf16[2,256,128]{2,1,0:T(8,128)(2,1)S(1)}, bf16[2,256,128]{2,1,0:T(8,128)(2,1)S(1)}, u32[]{:S(2)}, u32[]{:S(2)}) collective-permute-start(bf16[2,256,128]{2,1,0:T(8,128)(2,1)S(1)} %get-tuple-element.127), channel_id=1, source_target_pairs={{0,1},{1,0},{2,3},{3,2},{4,5},{5,4},{6,7},{7,6},{8,9},{9,8},{10,11... | collective-permute-start | bytes 393224 | tf_op jit(solution)/shard_map/ppermute | solution.py:766
  49.8 6.7 %collective-permute-start.16 = (bf16[2,256,128]{2,1,0:T(8,128)(2,1)S(1)}, bf16[2,256,128]{2,1,0:T(8,128)(2,1)S(1)}, u32[]{:S(2)}, u32[]{:S(2)}) collective-permute-start(bf16[2,256,128]{2,1,0:T(8,128)(2,1)S(1)} %get-tuple-element.133), channel_id=1, source_target_pairs={{0,3},{1,2},{2,1},{3,0},{4,7},{5,6},{6,5},{7,4},{8,11},{9,10},{10,... | collective-permute-start | bytes 393224 | tf_op jit(solution)/shard_map/ppermute | solution.py:766
  50.3 13.5 %collective-permute-start.17 = (bf16[1,128,1024]{2,1,0:T(8,128)(2,1)S(1)}, bf16[1,128,1024]{2,1,0:T(8,128)(2,1)S(1)}, u32[]{:S(2)}, u32[]{:S(2)}) collective-permute-start(bf16[1,128,1024]{2,1,0:T(8,128)(2,1)S(1)} %get-tuple-element.131), channel_id=1, source_target_pairs={{0,2},{1,3},{2,0},{3,1},{4,6},{5,7},{6,4},{7,5},{8,10},{9,11},{10,... | collective-permute-start | bytes 786440 | tf_op jit(solution)/shard_map/ppermute | solution.py:766
  63.9 10.4 %collective-permute-start.21 = (f32[4,128,128]{2,1,0:T(8,128)S(1)}, f32[4,128,128]{2,1,0:T(8,128)S(1)}, u32[]{:S(2)}, u32[]{:S(2)}) collective-permute-start(f32[4,128,128]{2,1,0:T(8,128)S(1)} %get-tuple-element.136), channel_id=1, source_target_pairs={{0,4},{4,0},{8,12},{12,8},{16,20},{20,16},{24,28},{28,24},{1,5},{5... | collective-permute-start | bytes 786440 | tf_op jit(solution)/shard_map/ppermute | solution.py:766
  74.3 5.7 %collective-permute-start.22 = (f32[2,128,128]{2,1,0:T(8,128)S(1)}, f32[2,128,128]{2,1,0:T(8,128)S(1)}, u32[]{:S(2)}, u32[]{:S(2)}) collective-permute-start(f32[2,128,128]{2,1,0:T(8,128)S(1)} %get-tuple-element.153), channel_id=1, source_target_pairs={{0,8},{4,12},{8,0},{12,4},{16,24},{20,28},{24,16},{28,20},{1,9},{5... | collective-permute-start | bytes 393224 | tf_op jit(solution)/shard_map/ppermute | solution.py:766
  75.1 11.5 %all-to-all-start = ((f32[8,24,128]{2,1,0:T(8,128)}), f32[8,24,128]{2,1,0:T(8,128)S(1)}, u32[]{:S(2)}, u32[]{:S(2)}) async-start(f32[8,24,128]{2,1,0:T(8,128)} %state_grad.1), calls=%async_computation | async-start | bytes 196608 | tf_op jit(solution)/shard_map/all_to_all | solution.py:935
  78.5 10.7 %collective-permute-start.18 = (bf16[2,256,128]{2,1,0:T(8,128)(2,1)S(1)}, bf16[2,256,128]{2,1,0:T(8,128)(2,1)S(1)}, u32[]{:S(2)}, u32[]{:S(2)}) collective-permute-start(bf16[2,256,128]{2,1,0:T(8,128)(2,1)S(1)} %get-tuple-element.145), channel_id=1, source_target_pairs={{0,1},{1,0},{2,3},{3,2},{4,5},{5,4},{6,7},{7,6},{8,9},{9,8},{10,11... | collective-permute-start | bytes 393224 | tf_op jit(solution)/shard_map/ppermute | solution.py:766
  80.1 7.4 %collective-permute-start.23 = (f32[1,128,128]{2,1,0:T(8,128)S(1)}, f32[1,128,128]{2,1,0:T(8,128)S(1)}, u32[]{:S(2)}, u32[]{:S(2)}) collective-permute-start(f32[1,128,128]{2,1,0:T(8,128)S(1)} %get-tuple-element.155), channel_id=1, source_target_pairs={{0,16},{4,20},{8,24},{12,28},{16,0},{20,4},{24,8},{28,12},{1,17},{... | collective-permute-start | bytes 196616 | tf_op jit(solution)/shard_map/ppermute | solution.py:766
  81.4 8.0 %collective-permute-start.19 = (bf16[2,256,128]{2,1,0:T(8,128)(2,1)S(1)}, bf16[2,256,128]{2,1,0:T(8,128)(2,1)S(1)}, u32[]{:S(2)}, u32[]{:S(2)}) collective-permute-start(bf16[2,256,128]{2,1,0:T(8,128)(2,1)S(1)} %get-tuple-element.146), channel_id=1, source_target_pairs={{0,2},{1,3},{2,0},{3,1},{4,6},{5,7},{6,4},{7,5},{8,10},{9,11},{10,... | collective-permute-start | bytes 393224 | tf_op jit(solution)/shard_map/ppermute | solution.py:766
  82.9 6.5 %collective-permute-start.20 = (bf16[2,256,128]{2,1,0:T(8,128)(2,1)S(1)}, bf16[2,256,128]{2,1,0:T(8,128)(2,1)S(1)}, u32[]{:S(2)}, u32[]{:S(2)}) collective-permute-start(bf16[2,256,128]{2,1,0:T(8,128)(2,1)S(1)} %get-tuple-element.147), channel_id=1, source_target_pairs={{0,3},{1,2},{2,1},{3,0},{4,7},{5,6},{6,5},{7,4},{8,11},{9,10},{10,... | collective-permute-start | bytes 393224 | tf_op jit(solution)/shard_map/ppermute | solution.py:766
  87.5 4.6 %collective-permute-start.26 = (f32[152,128]{1,0:T(8,128)S(1)}, f32[152,128]{1,0:T(8,128)S(1)}, u32[]{:S(2)}, u32[]{:S(2)}) collective-permute-start(f32[152,128]{1,0:T(8,128)S(1)} %last_sums.1.refs_0_), channel_id=1, source_target_pairs={{0,3},{1,2},{2,1},{3,0},{4,7},{5,6},{6,5},{7,4},{8,11},{9,10},{10,... | collective-permute-start | bytes 233480 | tf_op jit(solution)/shard_map/ppermute | solution.py:766
  88.7 5.2 %collective-permute-start.25 = (f32[152,128]{1,0:T(8,128)S(1)}, f32[152,128]{1,0:T(8,128)S(1)}, u32[]{:S(2)}, u32[]{:S(2)}) collective-permute-start(f32[152,128]{1,0:T(8,128)S(1)} %last_sums.1.refs_0_), channel_id=1, source_target_pairs={{0,2},{1,3},{2,0},{3,1},{4,6},{5,7},{6,4},{7,5},{8,10},{9,11},{10,... | collective-permute-start | bytes 233480 | tf_op jit(solution)/shard_map/ppermute | solution.py:766
  89.2 4.7 %collective-permute-start.24 = (f32[152,128]{1,0:T(8,128)S(1)}, f32[152,128]{1,0:T(8,128)S(1)}, u32[]{:S(2)}, u32[]{:S(2)}) collective-permute-start(f32[152,128]{1,0:T(8,128)S(1)} %last_sums.1.refs_0_), channel_id=1, source_target_pairs={{0,1},{1,0},{2,3},{3,2},{4,5},{5,4},{6,7},{7,6},{8,9},{9,8},{10,11... | collective-permute-start | bytes 233480 | tf_op jit(solution)/shard_map/ppermute | solution.py:766

commit v5 on v4

--- a/solution.py
+++ b/solution.py
@@ -251,7 +251,19 @@
     return (iota((width, wide), 0) == (lane // sub) * own + c * sub + lane % sub).astype(f32).astype(bf16)
 
 
-def ln_kernel(own, sub, x_any, *refs):
+STAT_ROWS = 16
+
+
+def terms3(x):
+    hi, rest = x.astype(bf16), x
+    out = [hi]
+    for _ in range(2):
+        rest = rest - out[-1].astype(f32)
+        out.append(rest.astype(bf16))
+    return out
+
+
+def spread_kernel(own, sub, x_any, *refs):
     *o_refs, x_ref, sems = refs
     count, block, width = x_ref.shape
     wide = o_refs[0].shape[-1]
@@ -259,14 +271,37 @@
     for copy in copies:
         copy.start()
     places = [members(own, sub, lax.axis_index("seq") ^ d, width, wide) for d in range(len(o_refs))]
+    eye = (iota((block, block), 0) == iota((block, block), 1)).astype(f32).astype(bf16)
+    lane = iota((block, LANES), 1)
     for s in range(count):
         copies[s].wait()
+        for o_ref, cols in zip(o_refs, places):
+            o_ref[s, 0:block] = dot(x_ref[s], cols).astype(bf16)
         x = x_ref[s].astype(f32)
-        centre = x - jnp.mean(x, axis=-1, keepdims=True)
-        spread = jnp.mean(centre * centre, axis=-1, keepdims=True)
-        hi, lo = halves(centre * lax.rsqrt(spread + ln_eps))
-        for o_ref, cols in zip(o_refs, places):
-            o_ref[s] = dot(hi, cols) + dot(lo, cols)
+        mean = jnp.mean(x, axis=-1, keepdims=True)
+        centre = x - mean
+        inv = lax.rsqrt(jnp.mean(centre * centre, axis=-1, keepdims=True) + ln_eps)
+        table = jnp.zeros((block, LANES), f32)
+        for k, term in enumerate(terms3(mean) + terms3(inv)):
+            table = jnp.where(lane == k, term.astype(f32), table)
+        turned = dot(table.astype(bf16), eye, TN)
+        both = jnp.concatenate([turned[0:8, 0:LANES], turned[0:8, LANES:]], axis=0).astype(bf16)
+        for o_ref in o_refs:
+            o_ref[s, block:] = both
+
+
+def normal_inputs(piece_ref, s, block):
+    stats = piece_ref[s, block:]
+    spot, lane = iota((STAT_ROWS, 4 * LANES), 0), iota((STAT_ROWS, 4 * LANES), 1) // LANES
+    first = lane // 2 * 8 + lane % 2 * 3
+    pick = ((spot >= first) & (spot < first + 3)).astype(f32).astype(bf16)
+    cols = dot(stats, pick, TN)
+    parts = []
+    for half in (0, 1):
+        rows = piece_ref[s, half * LANES : (half + 1) * LANES].astype(f32)
+        at = 2 * half * LANES
+        parts.append((rows - cols[:, at : at + LANES]) * cols[:, at + LANES : at + 2 * LANES])
+    return jnp.concatenate(parts, axis=0)
 
 
 def ln_back_kernel(own, sub, g0, g1, g2, g3, x_ref, c_ref, o_ref):
@@ -355,13 +390,12 @@
 
 def conv_kernel(x0, x1, x2, x3, len_ref, vec_ref, kh_ref, f_ref, ft_ref,
                 o0, o1, o2, o3, s_scr, x_scr, len_scr, cut_ref, rhs_scr, acc_scr, y_scr, out_scr, sem):
-    count, block, lanes = x0.shape
-    parts = kh_ref.shape[0]
+    count, parts, block, lanes = x_scr.shape
     me = lax.axis_index("seq")
     lengths_in(len_ref, len_scr, sem)
     for d, x_ref in enumerate((x0, x1, x2, x3)):
         for s in range(count):
-            x_scr[s, me ^ d] = x_ref[s]
+            x_scr[s, me ^ d] = normal_inputs(x_ref, s, block)
     segments(len_scr, cut_ref, block, parts)
     gain, bias = vec_ref[2:3], vec_ref[3:4]
     items = cut_ref.shape[1] - 1
@@ -802,7 +836,7 @@
         row(lambda_log), row(lambda_imag), row(lin_bias)
     )
 
-    piece, piece32 = shape((count, block, wide), bf16), shape((count, block, wide))
+    piece = shape((count, block, wide), bf16)
     shared, shared_parts = packed, [packed]
     w_slots = [lin_weight[None]]
     f_table, ft_table = dft_tables(block)
@@ -810,16 +844,16 @@
     for number, step in enumerate(steps):
         more = swap(shared, "dp", step)
         if number == 0:
-            x_late, _ = tie(block_in, packed)
+            x_late, _ = tie(block_in, shared)
             hats = call(
-                partial(ln_kernel, own, sub), [piece32] * nseq, [AN],
-                scratch=[pltpu.VMEM((count, block, width), bf16), DMA((count,))], name="layer_norm", us=2,
+                partial(spread_kernel, own, sub), [shape((count, block + STAT_ROWS, wide), bf16)] * nseq, [AN],
+                scratch=[pltpu.VMEM((count, block, width), bf16), DMA((count,))], name="spread", us=2,
             )(x_late)
-            more, *hats = tie(more, *hats)
-        elif number == 1:
+            more, *_ = tie(more, *hats)
+        if number == 1:
             hats = trade(hats, "seq")
-            more, hats[1] = tie(more, hats[1])
-        elif number == 2:
+            more, _ = tie(more, hats[1])
+        if number == 2:
             w_more = swap(w_slots[0], "dp", steps[0])
         shared_parts.append(more)
         if number < len(steps) - 1:

time: 95 us -> 94.5 us (level)
  waiting for transfers between devices: 21.6 us -> 18.5 us
  starting transfers between devices: 31.3 us -> 34.4 us
    ppermute x27, waiting for transfers between devices: 18 us -> 15.2 us  [swap(): lax.ppermute(v, axis, [(i, i ^ by) for i in range(n)])]
    ppermute x27, starting transfers between devices: 27.9 us -> 29.6 us  [swap(): lax.ppermute(v, axis, [(i, i ^ by) for i in range(n)])]
    all_to_all x1, starting transfers between devices: 3.36 us -> 4.74 us  [on_device(): small = lax.all_to_all(small, 'dp', 0, 0, tiled=True)]
  transfers between devices with their start and end apart: 28 -> 28, of which waited for: 12 -> 11; matrix products, arithmetic and copies ran while one was open for 0% -> 0% of each run, Pallas kernels for 35% -> 35%
where the time goes in v5:
time: 94.5 us; the launch traced here: 94.2 us
  Pallas kernels  40.4 us (43%)
  starting transfers between devices  34.4 us (36%)
  waiting for transfers between devices  18.5 us (20%)
    pallas_call x16, Pallas kernels, call(): return lambda *args: kernel(*args, *keep)  40.4 us
    ppermute x27, starting transfers between devices, swap(): lax.ppermute(v, axis, [(i, i ^ by) for i in range(n)])  29.6 us
    ppermute x27, waiting for transfers between devices, swap(): lax.ppermute(v, axis, [(i, i ^ by) for i in range(n)])  15.2 us
    all_to_all x1, starting transfers between devices, on_device(): small = lax.all_to_all(small, 'dp', 0, 0, tiled=True)  4.74 us
    all_to_all x1, waiting for transfers between devices, on_device(): small = lax.all_to_all(small, 'dp', 0, 0, tiled=True)  3.28 us
  transfers between devices with their start and end apart: 28, of which 11 were waited for; matrix products, arithmetic and copies ran while one was open for 0% of the time, Pallas kernels for 35%

profile of v5, /device:TPU:0, one launch (start us, length us, event | category | flops | bytes accessed | tf_op | source)
XLA Modules:
  0.0 94.2 jit_solution(7663984234857016661)
XLA Ops:
  0.7 1.8 %pack.1.refs_0_ = f32[1,24,128]{2,1,0:T(8,128)} custom-call(f32[128,64]{1,0:T(8,128)} %bitcast.19, f32[1,64]{1,0:T(1,128)} %bitcast.20, f32[1,64]{1,0:T(1,128)} %bitcast.21, f32[1,64]{1,0:T(1,128)} %bitcast.22, f32[1,64]{1,0:T(1,128)} %bitcast.23, f32[1,8]{1,0:T(1,128)} %bitcast.24, f32[1,8]{1,0:T(1,128)} %bitcast.25, f32[1,128]{1,0:T(1,128)} %bitcast.26), custom_call_target="tpu_custom_call" | custom-call | flops 2300000000 | bytes 1000 | tf_op jit(solution)/shard_map/pack/pallas_call | solution.py:53
  2.5 0.0 copy-start.1
  2.5 4.1 %collective-permute-start.3 = (f32[1,24,128]{2,1,0:T(8,128)}, f32[1,24,128]{2,1,0:T(8,128)S(1)}, u32[]{:S(2)}, u32[]{:S(2)}) collective-permute-start(f32[1,24,128]{2,1,0:T(8,128)} %pack.1.refs_0_), channel_id=1, source_target_pairs={{0,16},{4,20},{8,24},{12,28},{16,0},{20,4},{24,8},{28,12},{1,17},{... | collective-permute-start | bytes 36872 | tf_op jit(solution)/shard_map/ppermute | solution.py:800
  6.6 1.2 %spread.1 = (bf16[2,272,128]{2,1,0:T(8,128)(2,1)S(1)}, bf16[2,272,128]{2,1,0:T(8,128)(2,1)S(1)}, bf16[2,272,128]{2,1,0:T(8,128)(2,1)S(1)}, bf16[2,272,128]{2,1,0:T(8,128)(2,1)S(1)}) custom-call(bf16[2,256,512]{2,1,0:T(8,128)(2,1)S(1)} %copy-done.2), custom_call_target="tpu_custom_call" | custom-call | flops 2300000000 | bytes 1000 | tf_op jit(solution)/shard_map/spread/pallas_call | solution.py:53
  7.9 0.1 collective-permute-start
  8.0 0.5 collective-permute-done.3.refs_1_
  8.5 1.9 %collective-permute-start.4 = (f32[2,24,128]{2,1,0:T(8,128)S(1)}, f32[2,24,128]{2,1,0:T(8,128)S(1)}, u32[]{:S(2)}, u32[]{:S(2)}) collective-permute-start(f32[2,24,128]{2,1,0:T(8,128)S(1)} %pad_maximum_fusion.3), channel_id=1, source_target_pairs={{0,8},{4,12},{8,0},{12,4},{16,24},{20,28},{24,16},{28,20},{1,9},{5... | collective-permute-start | bytes 73736 | tf_op jit(solution)/shard_map/ppermute | solution.py:800
  10.4 2.6 %collective-permute-start.6 = (bf16[1,512,128]{2,1,0:T(8,128)(2,1)S(1)}, bf16[1,512,128]{2,1,0:T(8,128)(2,1)S(1)}, u32[]{:S(2)}, u32[]{:S(2)}) collective-permute-start(bf16[1,512,128]{2,1,0:T(8,128)(2,1)S(1)} %bitcast.17), channel_id=1, source_target_pairs={{0,16},{4,20},{8,24},{12,28},{16,0},{20,4},{24,8},{28,12},{1,17},{... | collective-permute-start | bytes 393224 | tf_op jit(solution)/shard_map/ppermute | solution.py:800
  13.0 1.6 %collective-permute-start.5 = (f32[4,24,128]{2,1,0:T(8,128)S(1)}, f32[4,24,128]{2,1,0:T(8,128)S(1)}, u32[]{:S(2)}, u32[]{:S(2)}) collective-permute-start(f32[4,24,128]{2,1,0:T(8,128)S(1)} %pad_maximum_fusion.2), channel_id=1, source_target_pairs={{0,4},{4,0},{8,12},{12,8},{16,20},{20,16},{24,28},{28,24},{1,5},{5... | collective-permute-start | bytes 147464 | tf_op jit(solution)/shard_map/ppermute | solution.py:800
  14.6 1.5 %collective-permute-start.1 = (bf16[2,272,128]{2,1,0:T(8,128)(2,1)S(1)}, bf16[2,272,128]{2,1,0:T(8,128)(2,1)S(1)}, u32[]{:S(2)}, u32[]{:S(2)}) collective-permute-start(bf16[2,272,128]{2,1,0:T(8,128)(2,1)S(1)} %get-tuple-element.86), channel_id=1, source_target_pairs={{0,2},{1,3},{2,0},{3,1},{4,6},{5,7},{6,4},{7,5},{8,10},{9,11},{10,... | collective-permute-start | bytes 417800 | tf_op jit(solution)/shard_map/ppermute | solution.py:800
  16.1 1.1 %collective-permute-done.5.refs_3_ = f32[4,24,128]{2,1,0:T(8,128)S(1)} collective-permute-done((f32[4,24,128]{2,1,0:T(8,128)S(1)}, f32[4,24,128]{2,1,0:T(8,128)S(1)}, u32[]{:S(2)}, u32[]{:S(2)}) %collective-permute-start.5) | collective-permute-done | bytes 49184 | tf_op jit(solution)/shard_map/ppermute | solution.py:800
  17.2 5.6 %lag_kernel.1 = (f32[4,512,128]{2,1,0:T(8,128)S(1)}, f32[8,128]{1,0:T(8,128)S(1)}, f32[128,128]{1,0:T(8,128)S(1)}, f32[13,64,128]{2,1,0:T(8,128)S(1)}, f32[26,64,128]{2,1,0:T(8,128)S(1)}) custom-call(f32[1,24,128]{2,1,0:T(8,128)S(1)} %copy-done.4, f32[1,24,128]{2,1,0:T(8,128)S(1)} %collective-permute-done.3.refs_1_, ...), custom_call_target="tpu_custom_call" | custom-call | bytes 1000 | tf_op jit(solution)/shard_map/lag_kernel/pallas_call | solution.py:53
  22.9 1.6 %collective-permute-start.8 = (bf16[2,512,128]{2,1,0:T(8,128)(2,1)S(1)}, bf16[2,512,128]{2,1,0:T(8,128)(2,1)S(1)}, u32[]{:S(2)}, u32[]{:S(2)}) collective-permute-start(bf16[2,512,128]{2,1,0:T(8,128)(2,1)S(1)} %pad_maximum_fusion.refs_1_), channel_id=1, source_target_pairs={{0,4},{4,0},{8,12},{12,8},{16,20},{20,16},{24,28},{28,24},{1,5},{5... | collective-permute-start | bytes 786440 | tf_op jit(solution)/shard_map/ppermute | solution.py:800
  24.5 1.4 %collective-permute-start.7 = (bf16[2,512,128]{2,1,0:T(8,128)(2,1)S(1)}, bf16[2,512,128]{2,1,0:T(8,128)(2,1)S(1)}, u32[]{:S(2)}, u32[]{:S(2)}) collective-permute-start(bf16[2,512,128]{2,1,0:T(8,128)(2,1)S(1)} %pad_maximum_fusion.refs_1_), channel_id=1, source_target_pairs={{0,8},{4,12},{8,0},{12,4},{16,24},{20,28},{24,16},{28,20},{1,9},{5... | collective-permute-start | bytes 786440 | tf_op jit(solution)/shard_map/ppermute | solution.py:800
  25.9 6.9 %doc_conv.1 = (bf16[2,256,128]{2,1,0:T(8,128)(2,1)S(1)}, bf16[2,256,128]{2,1,0:T(8,128)(2,1)S(1)}, bf16[2,256,128]{2,1,0:T(8,128)(2,1)S(1)}, bf16[2,256,128]{2,1...) custom-call(bf16[2,272,128]{2,1,0:T(8,128)(2,1)S(1)} %get-tuple-element.84.refs_0_, ...), custom_call_target="tpu_custom_call" | custom-call | flops 8049999872 | bytes 1000 | tf_op jit(solution)/shard_map/doc_conv/pallas_call | solution.py:53
  32.9 0.6 collective-permute-start.12
  33.5 1.5 %collective-permute-start.10 = (bf16[2,256,128]{2,1,0:T(8,128)(2,1)S(1)}, bf16[2,256,128]{2,1,0:T(8,128)(2,1)S(1)}, u32[]{:S(2)}, u32[]{:S(2)}) collective-permute-start(bf16[2,256,128]{2,1,0:T(8,128)(2,1)S(1)} %get-tuple-element.104), channel_id=1, source_target_pairs={{0,2},{1,3},{2,0},{3,1},{4,6},{5,7},{6,4},{7,5},{8,10},{9,11},{10,... | collective-permute-start | bytes 393224 | tf_op jit(solution)/shard_map/ppermute | solution.py:800
  34.9 0.4 collective-permute-start.11
  35.4 0.5 state_powers.1.refs_14_.refs_17_.refs_11_.refs_5_.refs_3_
  35.9 3.9 %collective-permute-done.10.refs_2_ = bf16[2,256,128]{2,1,0:T(8,128)(2,1)S(1)} collective-permute-done((bf16[2,256,128]{2,1,0:T(8,128)(2,1)S(1)}, bf16[2,256,128]{2,1,0:T(8,128)(2,1)S(1)}, u32[]{:S(2)}, u32[]{:S(2)}) %collective-permute-start.10) | collective-permute-done | bytes 131104 | tf_op jit(solution)/shard_map/ppermute | solution.py:800
  39.7 0.3 linear_rows.1
  40.1 1.7 %collective-permute-done.11.refs_3_ = bf16[2,256,128]{2,1,0:T(8,128)(2,1)S(1)} collective-permute-done((bf16[2,256,128]{2,1,0:T(8,128)(2,1)S(1)}, bf16[2,256,128]{2,1,0:T(8,128)(2,1)S(1)}, u32[]{:S(2)}, u32[]{:S(2)}) %collective-permute-start.11) | collective-permute-done | bytes 131104 | tf_op jit(solution)/shard_map/ppermute | solution.py:800
  41.8 4.9 %gated_linear.1 = (bf16[2,256,512]{2,1,0:T(8,128)(2,1)}, f32[1,1024]{1,0:T(1,128)S(1)}, bf16[2,256,128]{2,1,0:T(8,128)(2,1)S(1)}, bf16[2,256,128]{2,1,0:T(8,128)...) custom-call(bf16[2,256,128]{2,1,0:T(8,128)(2,1)S(1)} %get-tuple-elem, ...), custom_call_target="tpu_custom_call" | custom-call | flops 5750000128 | bytes 1000 | tf_op jit(solution)/shard_map/gated_linear/pallas_call | solution.py:53
  46.7 0.3 collective-permute-start.15
  47.0 1.5 %collective-permute-start.14 = (bf16[2,256,128]{2,1,0:T(8,128)(2,1)S(1)}, bf16[2,256,128]{2,1,0:T(8,128)(2,1)S(1)}, u32[]{:S(2)}, u32[]{:S(2)}) collective-permute-start(bf16[2,256,128]{2,1,0:T(8,128)(2,1)S(1)} %get-tuple-element.118), channel_id=1, source_target_pairs={{0,2},{1,3},{2,0},{3,1},{4,6},{5,7},{6,4},{7,5},{8,10},{9,11},{10,... | collective-permute-start | bytes 393224 | tf_op jit(solution)/shard_map/ppermute | solution.py:800
  48.5 0.6 collective-permute-start.16
  49.1 0.1 weight_half.3
  49.2 1.6 %collective-permute-start.17 = (bf16[1,128,1024]{2,1,0:T(8,128)(2,1)S(1)}, bf16[1,128,1024]{2,1,0:T(8,128)(2,1)S(1)}, u32[]{:S(2)}, u32[]{:S(2)}) collective-permute-start(bf16[1,128,1024]{2,1,0:T(8,128)(2,1)S(1)} %get-tuple-element.121), channel_id=1, source_target_pairs={{0,2},{1,3},{2,0},{3,1},{4,6},{5,7},{6,4},{7,5},{8,10},{9,11},{10,... | collective-permute-start | bytes 786440 | tf_op jit(solution)/shard_map/ppermute | solution.py:800
  50.8 2.5 %collective-permute-done.14.refs_2_ = bf16[2,256,128]{2,1,0:T(8,128)(2,1)S(1)} collective-permute-done((bf16[2,256,128]{2,1,0:T(8,128)(2,1)S(1)}, bf16[2,256,128]{2,1,0:T(8,128)(2,1)S(1)}, u32[]{:S(2)}, u32[]{:S(2)}) %collective-permute-start.14) | collective-permute-done | bytes 131104 | tf_op jit(solution)/shard_map/ppermute | solution.py:800
  53.3 1.8 %collective-permute-done.16.refs_3_ = bf16[2,256,128]{2,1,0:T(8,128)(2,1)S(1)} collective-permute-done((bf16[2,256,128]{2,1,0:T(8,128)(2,1)S(1)}, bf16[2,256,128]{2,1,0:T(8,128)(2,1)S(1)}, u32[]{:S(2)}, u32[]{:S(2)}) %collective-permute-start.16) | collective-permute-done | bytes 131104 | tf_op jit(solution)/shard_map/ppermute | solution.py:800
  55.1 7.3 %doc_conv_grad.1 = (bf16[2,256,128]{2,1,0:T(8,128)(2,1)S(1)}, bf16[2,256,128]{2,1,0:T(8,128)(2,1)S(1)}, bf16[2,256,128]{2,1,0:T(8,128)(2,1)S(1)}, bf16[2,256,128...) custom-call(bf16[2,256,128]{2,1,0:T(8,128)(2,1)S(1)} %get-tuple-element.116.refs_0_, ...), custom_call_target="tpu_custom_call" | custom-call | flops 9200000000 | bytes 1000 | tf_op jit(solution)/shard_map/doc_conv_grad/pallas_call | solution.py:53
  62.5 0.2 weight_deal.1
  62.6 1.6 %collective-permute-start.21 = (f32[4,128,128]{2,1,0:T(8,128)S(1)}, f32[4,128,128]{2,1,0:T(8,128)S(1)}, u32[]{:S(2)}, u32[]{:S(2)}) collective-permute-start(f32[4,128,128]{2,1,0:T(8,128)S(1)} %get-tuple-element.126), channel_id=1, source_target_pairs={{0,4},{4,0},{8,12},{12,8},{16,20},{20,16},{24,28},{28,24},{1,5},{5... | collective-permute-start | bytes 786440 | tf_op jit(solution)/shard_map/ppermute | solution.py:800
  64.2 8.8 %state_grad.1 = f32[8,24,128]{2,1,0:T(8,128)} custom-call(f32[128,128]{1,0:T(8,128)S(1)} %get-tuple-element.93.refs_9_.refs_1_.refs_5_.refs_8_.refs_2_.refs_11_.refs_0_, f32[13,64,128]{2,1,0:T(8,128)S(1)} %get-tuple-element.94.refs_10_.refs_2_.refs_6_.refs_9_.refs_3_.refs_12_.refs_1_, ...), custom_call_target="tpu_custom_call" | custom-call | flops 11500000256 | bytes 1000 | tf_op jit(solution)/shard_map/state_grad/pallas_call | solution.py:53
  73.1 0.6 collective-permute-start.22
  73.7 4.7 %all-to-all-start = ((f32[8,24,128]{2,1,0:T(8,128)}), f32[8,24,128]{2,1,0:T(8,128)S(1)}, u32[]{:S(2)}, u32[]{:S(2)}) async-start(f32[8,24,128]{2,1,0:T(8,128)} %state_grad.1), calls=%async_computation | async-start | bytes 196608 | tf_op jit(solution)/shard_map/all_to_all | solution.py:969
  78.5 0.6 collective-permute-done.22.refs_1_
  79.1 2.7 %collective-permute-start.23 = (f32[1,128,128]{2,1,0:T(8,128)S(1)}, f32[1,128,128]{2,1,0:T(8,128)S(1)}, u32[]{:S(2)}, u32[]{:S(2)}) collective-permute-start(f32[1,128,128]{2,1,0:T(8,128)S(1)} %get-tuple-element.145), channel_id=1, source_target_pairs={{0,16},{4,20},{8,24},{12,28},{16,0},{20,4},{24,8},{28,12},{1,17},{... | collective-permute-start | bytes 196616 | tf_op jit(solution)/shard_map/ppermute | solution.py:800
  81.7 1.5 %collective-permute-start.19 = (bf16[2,256,128]{2,1,0:T(8,128)(2,1)S(1)}, bf16[2,256,128]{2,1,0:T(8,128)(2,1)S(1)}, u32[]{:S(2)}, u32[]{:S(2)}) collective-permute-start(bf16[2,256,128]{2,1,0:T(8,128)(2,1)S(1)} %get-tuple-element.136), channel_id=1, source_target_pairs={{0,2},{1,3},{2,0},{3,1},{4,6},{5,7},{6,4},{7,5},{8,10},{9,11},{10,... | collective-permute-start | bytes 393224 | tf_op jit(solution)/shard_map/ppermute | solution.py:800
  83.2 3.3 %all-to-all-done.refs_0_ = f32[8,24,128]{2,1,0:T(8,128)S(1)} async-done(((f32[8,24,128]{2,1,0:T(8,128)}), f32[8,24,128]{2,1,0:T(8,128)S(1)}, u32[]{:S(2)}, u32[]{:S(2)}) %all-to-all-start) | async-done | bytes 98336 | tf_op jit(solution)/shard_map/all_to_all | solution.py:969
  86.5 0.7 collective-permute-done.23.refs_2_
  87.2 0.4 collective-permute-start.26
  87.6 1.1 %collective-permute-start.25 = (f32[152,128]{1,0:T(8,128)S(1)}, f32[152,128]{1,0:T(8,128)S(1)}, u32[]{:S(2)}, u32[]{:S(2)}) collective-permute-start(f32[152,128]{1,0:T(8,128)S(1)} %last_sums.1.refs_0_), channel_id=1, source_target_pairs={{0,2},{1,3},{2,0},{3,1},{4,6},{5,7},{6,4},{7,5},{8,10},{9,11},{10,... | collective-permute-start | bytes 233480 | tf_op jit(solution)/shard_map/ppermute | solution.py:800
  88.7 0.5 collective-permute-start.24
  89.2 1.8 %layer_norm_grad.1 = bf16[2,256,512]{2,1,0:T(8,128)(2,1)} custom-call(bf16[2,256,128]{2,1,0:T(8,128)(2,1)S(1)} %get-tuple-element.134.refs_0_, bf16[2,256,128]{2,1,0:T(8,128)(2,1)S(1)} %collective-permute-done.18.refs_1_, bf16[2,256,128]{2,1,0:T(8,128)(2,1)S(1)} %collective-permute-done.19.refs_2_, bf16[2,256,128]{2,1,0:T(8,128)(2,1)S(1)} %collective-permute-done.20.refs_3_, ...), custom_call_target="tpu_custom_call" | custom-call | bytes 1000 | tf_op jit(solution)/shard_map/layer_norm_grad/pallas_call | solution.py:53
  91.0 1.0 %collective-permute-done.26.refs_3_ = f32[152,128]{1,0:T(8,128)S(1)} collective-permute-done((f32[152,128]{1,0:T(8,128)S(1)}, f32[152,128]{1,0:T(8,128)S(1)}, u32[]{:S(2)}, u32[]{:S(2)}) %collective-permute-start.26) | collective-permute-done | bytes 77856 | tf_op jit(solution)/shard_map/ppermute | solution.py:800
  92.0 1.4 %collective-permute-done.25.refs_2_ = f32[152,128]{1,0:T(8,128)S(1)} collective-permute-done((f32[152,128]{1,0:T(8,128)S(1)}, f32[152,128]{1,0:T(8,128)S(1)}, u32[]{:S(2)}, u32[]{:S(2)}) %collective-permute-start.25) | collective-permute-done | bytes 77856 | tf_op jit(solution)/shard_map/ppermute | solution.py:800
  93.4 0.8 last.1
  (42 shorter events, 0.2 us)
Async XLA Ops:
  0.6 6.0 %copy-start.2 = (bf16[2,256,512]{2,1,0:T(8,128)(2,1)S(1)}, bf16[2,256,512]{2,1,0:T(8,128)(2,1)}, u32[]{:S(2)}) copy-start(bf16[2,256,512]{2,1,0:T(8,128)(2,1)} %refs_4_.6) | copy-start | bytes 1572868
  2.5 6.0 %copy-start.4 = (f32[1,24,128]{2,1,0:T(8,128)S(1)}, f32[1,24,128]{2,1,0:T(8,128)}, u32[]{:S(2)}) copy-start(f32[1,24,128]{2,1,0:T(8,128)} %pack.1.refs_0_) | copy-start | bytes 36868
  2.5 7.9 %copy-start.6 = (bf16[512,128]{1,0:T(8,128)(2,1)S(1)}, bf16[512,128]{1,0:T(8,128)(2,1)}, u32[]{:S(2)}) copy-start(bf16[512,128]{1,0:T(8,128)(2,1)} %param.23) | copy-start | bytes 393220
  2.5 14.7 %copy-start = (bf16[256,1536]{1,0:T(8,128)(2,1)S(1)}, bf16[256,1536]{1,0:T(8,128)(2,1)}, u32[]{:S(2)}) copy-start(bf16[256,1536]{1,0:T(8,128)(2,1)} %constant.5.clone.refs_5_.refs_8_.refs_7_.refs_11_.refs_14_.refs_10_) | copy-start | bytes 2359300
  2.5 14.7 %copy-start.1 = (bf16[512,768]{1,0:T(8,128)(2,1)S(1)}, bf16[512,768]{1,0:T(8,128)(2,1)}, u32[]{:S(2)}) copy-start(bf16[512,768]{1,0:T(8,128)(2,1)} %constant.4.clone.refs_4_.refs_7_.refs_6_.refs_10_.refs_13_.refs_9_) | copy-start | bytes 2359300
  2.5 14.7 %copy-start.3 = (bf16[2,256,512]{2,1,0:T(8,128)(2,1)S(1)}, bf16[2,256,512]{2,1,0:T(8,128)(2,1)}, u32[]{:S(2)}) copy-start(bf16[2,256,512]{2,1,0:T(8,128)(2,1)} %refs_5_.6) | copy-start | bytes 1572868
  2.5 23.4 %copy-start.5 = (s32[2,4]{1,0:T(2,128)S(1)}, s32[2,4]{1,0:T(2,128)}, u32[]{:S(2)}) copy-start(s32[2,4]{1,0:T(2,128)} %refs_5_.5) | copy-start | bytes 100
  2.5 6.0 %collective-permute-start.3 = (f32[1,24,128]{2,1,0:T(8,128)}, f32[1,24,128]{2,1,0:T(8,128)S(1)}, u32[]{:S(2)}, u32[]{:S(2)}) collective-permute-start(f32[1,24,128]{2,1,0:T(8,128)} %pack.1.refs_0_), channel_id=1, source_target_pairs={{0,16},{4,20},{8,24},{12,28},{16,0},{20,4},{24,8},{28,12},{1,17},{... | collective-permute-start | bytes 36872 | tf_op jit(solution)/shard_map/ppermute | solution.py:800
  7.9 5.2 %collective-permute-start = (bf16[2,272,128]{2,1,0:T(8,128)(2,1)S(1)}, bf16[2,272,128]{2,1,0:T(8,128)(2,1)S(1)}, u32[]{:S(2)}, u32[]{:S(2)}) collective-permute-start(bf16[2,272,128]{2,1,0:T(8,128)(2,1)S(1)} %get-tuple-element.85), channel_id=1, source_target_pairs={{0,1},{1,0},{2,3},{3,2},{4,5},{5,4},{6,7},{7,6},{8,9},{9,8},{10,11... | collective-permute-start | bytes 417800 | tf_op jit(solution)/shard_map/ppermute | solution.py:800
  8.5 4.5 %collective-permute-start.4 = (f32[2,24,128]{2,1,0:T(8,128)S(1)}, f32[2,24,128]{2,1,0:T(8,128)S(1)}, u32[]{:S(2)}, u32[]{:S(2)}) collective-permute-start(f32[2,24,128]{2,1,0:T(8,128)S(1)} %pad_maximum_fusion.3), channel_id=1, source_target_pairs={{0,8},{4,12},{8,0},{12,4},{16,24},{20,28},{24,16},{28,20},{1,9},{5... | collective-permute-start | bytes 73736 | tf_op jit(solution)/shard_map/ppermute | solution.py:800
  10.4 12.4 %collective-permute-start.6 = (bf16[1,512,128]{2,1,0:T(8,128)(2,1)S(1)}, bf16[1,512,128]{2,1,0:T(8,128)(2,1)S(1)}, u32[]{:S(2)}, u32[]{:S(2)}) collective-permute-start(bf16[1,512,128]{2,1,0:T(8,128)(2,1)S(1)} %bitcast.17), channel_id=1, source_target_pairs={{0,16},{4,20},{8,24},{12,28},{16,0},{20,4},{24,8},{28,12},{1,17},{... | collective-permute-start | bytes 393224 | tf_op jit(solution)/shard_map/ppermute | solution.py:800
  13.0 4.2 %collective-permute-start.5 = (f32[4,24,128]{2,1,0:T(8,128)S(1)}, f32[4,24,128]{2,1,0:T(8,128)S(1)}, u32[]{:S(2)}, u32[]{:S(2)}) collective-permute-start(f32[4,24,128]{2,1,0:T(8,128)S(1)} %pad_maximum_fusion.2), channel_id=1, source_target_pairs={{0,4},{4,0},{8,12},{12,8},{16,20},{20,16},{24,28},{28,24},{1,5},{5... | collective-permute-start | bytes 147464 | tf_op jit(solution)/shard_map/ppermute | solution.py:800
  14.6 11.3 %collective-permute-start.1 = (bf16[2,272,128]{2,1,0:T(8,128)(2,1)S(1)}, bf16[2,272,128]{2,1,0:T(8,128)(2,1)S(1)}, u32[]{:S(2)}, u32[]{:S(2)}) collective-permute-start(bf16[2,272,128]{2,1,0:T(8,128)(2,1)S(1)} %get-tuple-element.86), channel_id=1, source_target_pairs={{0,2},{1,3},{2,0},{3,1},{4,6},{5,7},{6,4},{7,5},{8,10},{9,11},{10,... | collective-permute-start | bytes 417800 | tf_op jit(solution)/shard_map/ppermute | solution.py:800
  16.1 9.8 %collective-permute-start.2 = (bf16[2,272,128]{2,1,0:T(8,128)(2,1)S(1)}, bf16[2,272,128]{2,1,0:T(8,128)(2,1)S(1)}, u32[]{:S(2)}, u32[]{:S(2)}) collective-permute-start(bf16[2,272,128]{2,1,0:T(8,128)(2,1)S(1)} %get-tuple-element.87), channel_id=1, source_target_pairs={{0,3},{1,2},{2,1},{3,0},{4,7},{5,6},{6,5},{7,4},{8,11},{9,10},{10,... | collective-permute-start | bytes 417800 | tf_op jit(solution)/shard_map/ppermute | solution.py:800
  22.9 10.0 %collective-permute-start.8 = (bf16[2,512,128]{2,1,0:T(8,128)(2,1)S(1)}, bf16[2,512,128]{2,1,0:T(8,128)(2,1)S(1)}, u32[]{:S(2)}, u32[]{:S(2)}) collective-permute-start(bf16[2,512,128]{2,1,0:T(8,128)(2,1)S(1)} %pad_maximum_fusion.refs_1_), channel_id=1, source_target_pairs={{0,4},{4,0},{8,12},{12,8},{16,20},{20,16},{24,28},{28,24},{1,5},{5... | collective-permute-start | bytes 786440 | tf_op jit(solution)/shard_map/ppermute | solution.py:800
  24.5 8.4 %collective-permute-start.7 = (bf16[2,512,128]{2,1,0:T(8,128)(2,1)S(1)}, bf16[2,512,128]{2,1,0:T(8,128)(2,1)S(1)}, u32[]{:S(2)}, u32[]{:S(2)}) collective-permute-start(bf16[2,512,128]{2,1,0:T(8,128)(2,1)S(1)} %pad_maximum_fusion.refs_1_), channel_id=1, source_target_pairs={{0,8},{4,12},{8,0},{12,4},{16,24},{20,28},{24,16},{28,20},{1,9},{5... | collective-permute-start | bytes 786440 | tf_op jit(solution)/shard_map/ppermute | solution.py:800
  32.9 6.9 %collective-permute-start.12 = (bf16[2,512,128]{2,1,0:T(8,128)(2,1)S(1)}, bf16[2,512,128]{2,1,0:T(8,128)(2,1)S(1)}, u32[]{:S(2)}, u32[]{:S(2)}) collective-permute-start(bf16[2,512,128]{2,1,0:T(8,128)(2,1)S(1)} %collective-permute-done.7.refs_2_), channel_id=1, source_target_pairs={{0,4},{4,0},{8,12},{12,8},{16,20},{20,16},{24,28},{28,24},{1,5},{5... | collective-permute-start | bytes 786440 | tf_op jit(solution)/shard_map/ppermute | solution.py:800
  33.4 1.9 %collective-permute-start.9 = (bf16[2,256,128]{2,1,0:T(8,128)(2,1)S(1)}, bf16[2,256,128]{2,1,0:T(8,128)(2,1)S(1)}, u32[]{:S(2)}, u32[]{:S(2)}) collective-permute-start(bf16[2,256,128]{2,1,0:T(8,128)(2,1)S(1)} %get-tuple-element.102), channel_id=1, source_target_pairs={{0,1},{1,0},{2,3},{3,2},{4,5},{5,4},{6,7},{7,6},{8,9},{9,8},{10,11... | collective-permute-start | bytes 393224 | tf_op jit(solution)/shard_map/ppermute | solution.py:800
  33.5 6.3 %collective-permute-start.10 = (bf16[2,256,128]{2,1,0:T(8,128)(2,1)S(1)}, bf16[2,256,128]{2,1,0:T(8,128)(2,1)S(1)}, u32[]{:S(2)}, u32[]{:S(2)}) collective-permute-start(bf16[2,256,128]{2,1,0:T(8,128)(2,1)S(1)} %get-tuple-element.104), channel_id=1, source_target_pairs={{0,2},{1,3},{2,0},{3,1},{4,6},{5,7},{6,4},{7,5},{8,10},{9,11},{10,... | collective-permute-start | bytes 393224 | tf_op jit(solution)/shard_map/ppermute | solution.py:800
  34.9 6.8 %collective-permute-start.11 = (bf16[2,256,128]{2,1,0:T(8,128)(2,1)S(1)}, bf16[2,256,128]{2,1,0:T(8,128)(2,1)S(1)}, u32[]{:S(2)}, u32[]{:S(2)}) collective-permute-start(bf16[2,256,128]{2,1,0:T(8,128)(2,1)S(1)} %get-tuple-element.109), channel_id=1, source_target_pairs={{0,3},{1,2},{2,1},{3,0},{4,7},{5,6},{6,5},{7,4},{8,11},{9,10},{10,... | collective-permute-start | bytes 393224 | tf_op jit(solution)/shard_map/ppermute | solution.py:800
  46.7 2.4 %collective-permute-start.15 = (bf16[2,128,1024]{2,1,0:T(8,128)(2,1)S(1)}, bf16[2,128,1024]{2,1,0:T(8,128)(2,1)S(1)}, u32[]{:S(2)}, u32[]{:S(2)}) collective-permute-start(bf16[2,128,1024]{2,1,0:T(8,128)(2,1)S(1)} %get-tuple-element.120), channel_id=1, source_target_pairs={{0,1},{1,0},{2,3},{3,2},{4,5},{5,4},{6,7},{7,6},{8,9},{9,8},{10,11... | collective-permute-start | bytes 1572872 | tf_op jit(solution)/shard_map/ppermute | solution.py:800
  47.0 6.3 %collective-permute-start.14 = (bf16[2,256,128]{2,1,0:T(8,128)(2,1)S(1)}, bf16[2,256,128]{2,1,0:T(8,128)(2,1)S(1)}, u32[]{:S(2)}, u32[]{:S(2)}) collective-permute-start(bf16[2,256,128]{2,1,0:T(8,128)(2,1)S(1)} %get-tuple-element.118), channel_id=1, source_target_pairs={{0,2},{1,3},{2,0},{3,1},{4,6},{5,7},{6,4},{7,5},{8,10},{9,11},{10,... | collective-permute-start | bytes 393224 | tf_op jit(solution)/shard_map/ppermute | solution.py:800
  48.5 4.8 %collective-permute-start.13 = (bf16[2,256,128]{2,1,0:T(8,128)(2,1)S(1)}, bf16[2,256,128]{2,1,0:T(8,128)(2,1)S(1)}, u32[]{:S(2)}, u32[]{:S(2)}) collective-permute-start(bf16[2,256,128]{2,1,0:T(8,128)(2,1)S(1)} %get-tuple-element.117), channel_id=1, source_target_pairs={{0,1},{1,0},{2,3},{3,2},{4,5},{5,4},{6,7},{7,6},{8,9},{9,8},{10,11... | collective-permute-start | bytes 393224 | tf_op jit(solution)/shard_map/ppermute | solution.py:800
  48.5 6.7 %collective-permute-start.16 = (bf16[2,256,128]{2,1,0:T(8,128)(2,1)S(1)}, bf16[2,256,128]{2,1,0:T(8,128)(2,1)S(1)}, u32[]{:S(2)}, u32[]{:S(2)}) collective-permute-start(bf16[2,256,128]{2,1,0:T(8,128)(2,1)S(1)} %get-tuple-element.123), channel_id=1, source_target_pairs={{0,3},{1,2},{2,1},{3,0},{4,7},{5,6},{6,5},{7,4},{8,11},{9,10},{10,... | collective-permute-start | bytes 393224 | tf_op jit(solution)/shard_map/ppermute | solution.py:800
  49.2 13.2 %collective-permute-start.17 = (bf16[1,128,1024]{2,1,0:T(8,128)(2,1)S(1)}, bf16[1,128,1024]{2,1,0:T(8,128)(2,1)S(1)}, u32[]{:S(2)}, u32[]{:S(2)}) collective-permute-start(bf16[1,128,1024]{2,1,0:T(8,128)(2,1)S(1)} %get-tuple-element.121), channel_id=1, source_target_pairs={{0,2},{1,3},{2,0},{3,1},{4,6},{5,7},{6,4},{7,5},{8,10},{9,11},{10,... | collective-permute-start | bytes 786440 | tf_op jit(solution)/shard_map/ppermute | solution.py:800
  62.6 10.4 %collective-permute-start.21 = (f32[4,128,128]{2,1,0:T(8,128)S(1)}, f32[4,128,128]{2,1,0:T(8,128)S(1)}, u32[]{:S(2)}, u32[]{:S(2)}) collective-permute-start(f32[4,128,128]{2,1,0:T(8,128)S(1)} %get-tuple-element.126), channel_id=1, source_target_pairs={{0,4},{4,0},{8,12},{12,8},{16,20},{20,16},{24,28},{28,24},{1,5},{5... | collective-permute-start | bytes 786440 | tf_op jit(solution)/shard_map/ppermute | solution.py:800
  73.1 6.0 %collective-permute-start.22 = (f32[2,128,128]{2,1,0:T(8,128)S(1)}, f32[2,128,128]{2,1,0:T(8,128)S(1)}, u32[]{:S(2)}, u32[]{:S(2)}) collective-permute-start(f32[2,128,128]{2,1,0:T(8,128)S(1)} %get-tuple-element.143), channel_id=1, source_target_pairs={{0,8},{4,12},{8,0},{12,4},{16,24},{20,28},{24,16},{28,20},{1,9},{5... | collective-permute-start | bytes 393224 | tf_op jit(solution)/shard_map/ppermute | solution.py:800
  73.7 12.8 %all-to-all-start = ((f32[8,24,128]{2,1,0:T(8,128)}), f32[8,24,128]{2,1,0:T(8,128)S(1)}, u32[]{:S(2)}, u32[]{:S(2)}) async-start(f32[8,24,128]{2,1,0:T(8,128)} %state_grad.1), calls=%async_computation | async-start | bytes 196608 | tf_op jit(solution)/shard_map/all_to_all | solution.py:969
  78.5 10.2 %collective-permute-start.18 = (bf16[2,256,128]{2,1,0:T(8,128)(2,1)S(1)}, bf16[2,256,128]{2,1,0:T(8,128)(2,1)S(1)}, u32[]{:S(2)}, u32[]{:S(2)}) collective-permute-start(bf16[2,256,128]{2,1,0:T(8,128)(2,1)S(1)} %get-tuple-element.135), channel_id=1, source_target_pairs={{0,1},{1,0},{2,3},{3,2},{4,5},{5,4},{6,7},{7,6},{8,9},{9,8},{10,11... | collective-permute-start | bytes 393224 | tf_op jit(solution)/shard_map/ppermute | solution.py:800
  79.1 8.2 %collective-permute-start.23 = (f32[1,128,128]{2,1,0:T(8,128)S(1)}, f32[1,128,128]{2,1,0:T(8,128)S(1)}, u32[]{:S(2)}, u32[]{:S(2)}) collective-permute-start(f32[1,128,128]{2,1,0:T(8,128)S(1)} %get-tuple-element.145), channel_id=1, source_target_pairs={{0,16},{4,20},{8,24},{12,28},{16,0},{20,4},{24,8},{28,12},{1,17},{... | collective-permute-start | bytes 196616 | tf_op jit(solution)/shard_map/ppermute | solution.py:800
  81.7 7.4 %collective-permute-start.19 = (bf16[2,256,128]{2,1,0:T(8,128)(2,1)S(1)}, bf16[2,256,128]{2,1,0:T(8,128)(2,1)S(1)}, u32[]{:S(2)}, u32[]{:S(2)}) collective-permute-start(bf16[2,256,128]{2,1,0:T(8,128)(2,1)S(1)} %get-tuple-element.136), channel_id=1, source_target_pairs={{0,2},{1,3},{2,0},{3,1},{4,6},{5,7},{6,4},{7,5},{8,10},{9,11},{10,... | collective-permute-start | bytes 393224 | tf_op jit(solution)/shard_map/ppermute | solution.py:800
  83.2 5.9 %collective-permute-start.20 = (bf16[2,256,128]{2,1,0:T(8,128)(2,1)S(1)}, bf16[2,256,128]{2,1,0:T(8,128)(2,1)S(1)}, u32[]{:S(2)}, u32[]{:S(2)}) collective-permute-start(bf16[2,256,128]{2,1,0:T(8,128)(2,1)S(1)} %get-tuple-element.137), channel_id=1, source_target_pairs={{0,3},{1,2},{2,1},{3,0},{4,7},{5,6},{6,5},{7,4},{8,11},{9,10},{10,... | collective-permute-start | bytes 393224 | tf_op jit(solution)/shard_map/ppermute | solution.py:800
  87.2 4.7 %collective-permute-start.26 = (f32[152,128]{1,0:T(8,128)S(1)}, f32[152,128]{1,0:T(8,128)S(1)}, u32[]{:S(2)}, u32[]{:S(2)}) collective-permute-start(f32[152,128]{1,0:T(8,128)S(1)} %last_sums.1.refs_0_), channel_id=1, source_target_pairs={{0,3},{1,2},{2,1},{3,0},{4,7},{5,6},{6,5},{7,4},{8,11},{9,10},{10,... | collective-permute-start | bytes 233480 | tf_op jit(solution)/shard_map/ppermute | solution.py:800
  87.6 5.7 %collective-permute-start.25 = (f32[152,128]{1,0:T(8,128)S(1)}, f32[152,128]{1,0:T(8,128)S(1)}, u32[]{:S(2)}, u32[]{:S(2)}) collective-permute-start(f32[152,128]{1,0:T(8,128)S(1)} %last_sums.1.refs_0_), channel_id=1, source_target_pairs={{0,2},{1,3},{2,0},{3,1},{4,6},{5,7},{6,4},{7,5},{8,10},{9,11},{10,... | collective-permute-start | bytes 233480 | tf_op jit(solution)/shard_map/ppermute | solution.py:800
  88.7 4.7 %collective-permute-start.24 = (f32[152,128]{1,0:T(8,128)S(1)}, f32[152,128]{1,0:T(8,128)S(1)}, u32[]{:S(2)}, u32[]{:S(2)}) collective-permute-start(f32[152,128]{1,0:T(8,128)S(1)} %last_sums.1.refs_0_), channel_id=1, source_target_pairs={{0,1},{1,0},{2,3},{3,2},{4,5},{5,4},{6,7},{7,6},{8,9},{9,8},{10,11... | collective-permute-start | bytes 233480 | tf_op jit(solution)/shard_map/ppermute | solution.py:800

commit v6 on v5

--- a/solution.py
+++ b/solution.py
@@ -378,7 +378,7 @@
 
 def split_rows(y_scr, rows, cols, value, block, half):
     hi, lo = halves(value)
-    for third, part in enumerate((hi, lo, hi)):
+    for third, part in enumerate((hi, lo, hi)[: y_scr.shape[0] // (2 * block)]):
         at = (2 * third + half) * block
         y_scr[at + rows.start : at + rows.stop, cols] = part
 
@@ -436,7 +436,7 @@
         return 0
 
     lax.fori_loop(0, items, own, 0)
-    acc_scr[0:block] = dot(ft_ref[...], y_scr[...])
+    acc_scr[0:block] = dot(ft_ref[:, 0 : y_scr.shape[0]], y_scr[...])
     for j in range(items):
         for s in range(count):
             b, keep = within(cut_ref, s, j, block, lanes)
@@ -465,10 +465,9 @@
             b, keep = within(cut_ref, s, j, block, lanes)
             v = jnp.where(keep, v_scr[s, b].astype(f32), 0.0).astype(bf16)
             cols = slice((j * count + s) * lanes, (j * count + s + 1) * lanes)
-            rhs_scr[0:block, cols] = v
-            rhs_scr[block:, cols] = v
+            rhs_scr[:, cols] = v
         tile = slice(j * count * lanes, (j + 1) * count * lanes)
-        sv_scr[:, tile] = dot(f_ref[:, block:], rhs_scr[:, tile])
+        sv_scr[:, tile] = dot(f_ref[:, 0:block], rhs_scr[:, tile])
 
     def own(j, _):
         for s in range(count):
@@ -505,7 +504,7 @@
         return 0
 
     lax.fori_loop(0, items, own, 0)
-    acc_scr[0:block] = dot(ft_ref[...], y_scr[...])
+    acc_scr[0:block] = dot(ft_ref[:, 0 : y_scr.shape[0]], y_scr[...])
     for j in range(items):
         for s in range(count):
             b, keep = within(cut_ref, s, j, block, lanes)
@@ -944,9 +943,9 @@
     out = call(
         back_kernel, [piece] * nseq + [shape(spec), shape((3, wide))],
         [VM] * (nseq + 1) + [AN] + [VM] * 5,
-        scratch=[lens, cuts, pltpu.VMEM(blocks4, bf16), pltpu.VMEM((2 * block, across), bf16),
+        scratch=[lens, cuts, pltpu.VMEM(blocks4, bf16), pltpu.VMEM((block, across), bf16),
                  pltpu.VMEM((2 * block, across), f32), pltpu.VMEM((2 * block, across), f32),
-                 pltpu.VMEM((6 * block, across), bf16), pltpu.VMEM(blocks4, f32), DMA],
+                 pltpu.VMEM((4 * block, across), bf16), pltpu.VMEM(blocks4, f32), DMA],
         name="doc_conv_grad", mib=24, us=8, keep=[w_all, terms, pows, far],
     )(*d_convs, x_blocks, doc_lengths, spectra_u, vec, kh, f_table, ft_table)
     g_own, dkh, d_norm = out[:nseq], out[nseq], out[nseq + 1]

time: 94.5 us -> 93.3 us (0.987)
  Pallas kernels: 40.4 us -> 39.2 us
    pallas_call x16, Pallas kernels: 40.4 us -> 39.2 us  [call(): return lambda *args: kernel(*args, *keep)]
  transfers between devices with their start and end apart: 28 -> 28, of which waited for: 11 -> 11; matrix products, arithmetic and copies ran while one was open for 0% -> 0% of each run, Pallas kernels for 35% -> 34%
where the time goes in v6:
time: 93.3 us; the launch traced here: 93 us
  Pallas kernels  39.2 us (42%)
  starting transfers between devices  34.4 us (37%)
  waiting for transfers between devices  18.5 us (20%)
    pallas_call x16, Pallas kernels, call(): return lambda *args: kernel(*args, *keep)  39.2 us
    ppermute x27, starting transfers between devices, swap(): lax.ppermute(v, axis, [(i, i ^ by) for i in range(n)])  29.6 us
    ppermute x27, waiting for transfers between devices, swap(): lax.ppermute(v, axis, [(i, i ^ by) for i in range(n)])  15.2 us
    all_to_all x1, starting transfers between devices, on_device(): small = lax.all_to_all(small, 'dp', 0, 0, tiled=True)  4.75 us
    all_to_all x1, waiting for transfers between devices, on_device(): small = lax.all_to_all(small, 'dp', 0, 0, tiled=True)  3.28 us
  transfers between devices with their start and end apart: 28, of which 11 were waited for; matrix products, arithmetic and copies ran while one was open for 0% of the time, Pallas kernels for 34%

profile of v6, /device:TPU:0, one launch (start us, length us, event | category | flops | bytes accessed | tf_op | source)
XLA Modules:
  0.0 93.0 jit_solution(3190208841174854156)
XLA Ops:
  0.7 1.8 %pack.1.refs_0_ = f32[1,24,128]{2,1,0:T(8,128)} custom-call(f32[128,64]{1,0:T(8,128)} %bitcast.19, f32[1,64]{1,0:T(1,128)} %bitcast.20, f32[1,64]{1,0:T(1,128)} %bitcast.21, f32[1,64]{1,0:T(1,128)} %bitcast.22, f32[1,64]{1,0:T(1,128)} %bitcast.23, f32[1,8]{1,0:T(1,128)} %bitcast.24, f32[1,8]{1,0:T(1,128)} %bitcast.25, f32[1,128]{1,0:T(1,128)} %bitcast.26), custom_call_target="tpu_custom_call" | custom-call | flops 2300000000 | bytes 1000 | tf_op jit(solution)/shard_map/pack/pallas_call | solution.py:53
  2.5 4.1 %collective-permute-start.3 = (f32[1,24,128]{2,1,0:T(8,128)}, f32[1,24,128]{2,1,0:T(8,128)S(1)}, u32[]{:S(2)}, u32[]{:S(2)}) collective-permute-start(f32[1,24,128]{2,1,0:T(8,128)} %pack.1.refs_0_), channel_id=1, source_target_pairs={{0,16},{4,20},{8,24},{12,28},{16,0},{20,4},{24,8},{28,12},{1,17},{... | collective-permute-start | bytes 36872 | tf_op jit(solution)/shard_map/ppermute | solution.py:799
  6.6 1.2 %spread.1 = (bf16[2,272,128]{2,1,0:T(8,128)(2,1)S(1)}, bf16[2,272,128]{2,1,0:T(8,128)(2,1)S(1)}, bf16[2,272,128]{2,1,0:T(8,128)(2,1)S(1)}, bf16[2,272,128]{2,1,0:T(8,128)(2,1)S(1)}) custom-call(bf16[2,256,512]{2,1,0:T(8,128)(2,1)S(1)} %copy-done.2), custom_call_target="tpu_custom_call" | custom-call | flops 2300000000 | bytes 1000 | tf_op jit(solution)/shard_map/spread/pallas_call | solution.py:53
  7.9 0.1 collective-permute-start
  8.0 0.5 collective-permute-done.3.refs_1_
  8.5 1.9 %collective-permute-start.4 = (f32[2,24,128]{2,1,0:T(8,128)S(1)}, f32[2,24,128]{2,1,0:T(8,128)S(1)}, u32[]{:S(2)}, u32[]{:S(2)}) collective-permute-start(f32[2,24,128]{2,1,0:T(8,128)S(1)} %pad_maximum_fusion.3), channel_id=1, source_target_pairs={{0,8},{4,12},{8,0},{12,4},{16,24},{20,28},{24,16},{28,20},{1,9},{5... | collective-permute-start | bytes 73736 | tf_op jit(solution)/shard_map/ppermute | solution.py:799
  10.4 2.6 %collective-permute-start.6 = (bf16[1,512,128]{2,1,0:T(8,128)(2,1)S(1)}, bf16[1,512,128]{2,1,0:T(8,128)(2,1)S(1)}, u32[]{:S(2)}, u32[]{:S(2)}) collective-permute-start(bf16[1,512,128]{2,1,0:T(8,128)(2,1)S(1)} %bitcast.17), channel_id=1, source_target_pairs={{0,16},{4,20},{8,24},{12,28},{16,0},{20,4},{24,8},{28,12},{1,17},{... | collective-permute-start | bytes 393224 | tf_op jit(solution)/shard_map/ppermute | solution.py:799
  13.0 1.6 %collective-permute-start.5 = (f32[4,24,128]{2,1,0:T(8,128)S(1)}, f32[4,24,128]{2,1,0:T(8,128)S(1)}, u32[]{:S(2)}, u32[]{:S(2)}) collective-permute-start(f32[4,24,128]{2,1,0:T(8,128)S(1)} %pad_maximum_fusion.2), channel_id=1, source_target_pairs={{0,4},{4,0},{8,12},{12,8},{16,20},{20,16},{24,28},{28,24},{1,5},{5... | collective-permute-start | bytes 147464 | tf_op jit(solution)/shard_map/ppermute | solution.py:799
  14.6 1.5 %collective-permute-start.1 = (bf16[2,272,128]{2,1,0:T(8,128)(2,1)S(1)}, bf16[2,272,128]{2,1,0:T(8,128)(2,1)S(1)}, u32[]{:S(2)}, u32[]{:S(2)}) collective-permute-start(bf16[2,272,128]{2,1,0:T(8,128)(2,1)S(1)} %get-tuple-element.86), channel_id=1, source_target_pairs={{0,2},{1,3},{2,0},{3,1},{4,6},{5,7},{6,4},{7,5},{8,10},{9,11},{10,... | collective-permute-start | bytes 417800 | tf_op jit(solution)/shard_map/ppermute | solution.py:799
  16.1 1.1 %collective-permute-done.5.refs_3_ = f32[4,24,128]{2,1,0:T(8,128)S(1)} collective-permute-done((f32[4,24,128]{2,1,0:T(8,128)S(1)}, f32[4,24,128]{2,1,0:T(8,128)S(1)}, u32[]{:S(2)}, u32[]{:S(2)}) %collective-permute-start.5) | collective-permute-done | bytes 49184 | tf_op jit(solution)/shard_map/ppermute | solution.py:799
  17.2 5.6 %lag_kernel.1 = (f32[4,512,128]{2,1,0:T(8,128)S(1)}, f32[8,128]{1,0:T(8,128)S(1)}, f32[128,128]{1,0:T(8,128)S(1)}, f32[13,64,128]{2,1,0:T(8,128)S(1)}, f32[26,64,128]{2,1,0:T(8,128)S(1)}) custom-call(f32[1,24,128]{2,1,0:T(8,128)S(1)} %copy-done.4, f32[1,24,128]{2,1,0:T(8,128)S(1)} %collective-permute-done.3.refs_1_, ...), custom_call_target="tpu_custom_call" | custom-call | bytes 1000 | tf_op jit(solution)/shard_map/lag_kernel/pallas_call | solution.py:53
  22.9 1.6 %collective-permute-start.8 = (bf16[2,512,128]{2,1,0:T(8,128)(2,1)S(1)}, bf16[2,512,128]{2,1,0:T(8,128)(2,1)S(1)}, u32[]{:S(2)}, u32[]{:S(2)}) collective-permute-start(bf16[2,512,128]{2,1,0:T(8,128)(2,1)S(1)} %pad_maximum_fusion.refs_1_), channel_id=1, source_target_pairs={{0,4},{4,0},{8,12},{12,8},{16,20},{20,16},{24,28},{28,24},{1,5},{5... | collective-permute-start | bytes 786440 | tf_op jit(solution)/shard_map/ppermute | solution.py:799
  24.5 1.4 %collective-permute-start.7 = (bf16[2,512,128]{2,1,0:T(8,128)(2,1)S(1)}, bf16[2,512,128]{2,1,0:T(8,128)(2,1)S(1)}, u32[]{:S(2)}, u32[]{:S(2)}) collective-permute-start(bf16[2,512,128]{2,1,0:T(8,128)(2,1)S(1)} %pad_maximum_fusion.refs_1_), channel_id=1, source_target_pairs={{0,8},{4,12},{8,0},{12,4},{16,24},{20,28},{24,16},{28,20},{1,9},{5... | collective-permute-start | bytes 786440 | tf_op jit(solution)/shard_map/ppermute | solution.py:799
  25.9 7.0 %doc_conv.1 = (bf16[2,256,128]{2,1,0:T(8,128)(2,1)S(1)}, bf16[2,256,128]{2,1,0:T(8,128)(2,1)S(1)}, bf16[2,256,128]{2,1,0:T(8,128)(2,1)S(1)}, bf16[2,256,128]{2,1...) custom-call(bf16[2,272,128]{2,1,0:T(8,128)(2,1)S(1)} %get-tuple-element.84.refs_0_, ...), custom_call_target="tpu_custom_call" | custom-call | flops 8049999872 | bytes 1000 | tf_op jit(solution)/shard_map/doc_conv/pallas_call | solution.py:53
  32.9 0.6 collective-permute-start.12
  33.4 1.5 %collective-permute-start.10 = (bf16[2,256,128]{2,1,0:T(8,128)(2,1)S(1)}, bf16[2,256,128]{2,1,0:T(8,128)(2,1)S(1)}, u32[]{:S(2)}, u32[]{:S(2)}) collective-permute-start(bf16[2,256,128]{2,1,0:T(8,128)(2,1)S(1)} %get-tuple-element.104), channel_id=1, source_target_pairs={{0,2},{1,3},{2,0},{3,1},{4,6},{5,7},{6,4},{7,5},{8,10},{9,11},{10,... | collective-permute-start | bytes 393224 | tf_op jit(solution)/shard_map/ppermute | solution.py:799
  34.9 0.4 collective-permute-start.11
  35.4 0.5 state_powers.1.refs_14_.refs_17_.refs_11_.refs_5_.refs_3_
  35.9 3.9 %collective-permute-done.10.refs_2_ = bf16[2,256,128]{2,1,0:T(8,128)(2,1)S(1)} collective-permute-done((bf16[2,256,128]{2,1,0:T(8,128)(2,1)S(1)}, bf16[2,256,128]{2,1,0:T(8,128)(2,1)S(1)}, u32[]{:S(2)}, u32[]{:S(2)}) %collective-permute-start.10) | collective-permute-done | bytes 131104 | tf_op jit(solution)/shard_map/ppermute | solution.py:799
  39.7 0.3 linear_rows.1
  40.1 1.7 %collective-permute-done.11.refs_3_ = bf16[2,256,128]{2,1,0:T(8,128)(2,1)S(1)} collective-permute-done((bf16[2,256,128]{2,1,0:T(8,128)(2,1)S(1)}, bf16[2,256,128]{2,1,0:T(8,128)(2,1)S(1)}, u32[]{:S(2)}, u32[]{:S(2)}) %collective-permute-start.11) | collective-permute-done | bytes 131104 | tf_op jit(solution)/shard_map/ppermute | solution.py:799
  41.8 4.9 %gated_linear.1 = (bf16[2,256,512]{2,1,0:T(8,128)(2,1)}, f32[1,1024]{1,0:T(1,128)S(1)}, bf16[2,256,128]{2,1,0:T(8,128)(2,1)S(1)}, bf16[2,256,128]{2,1,0:T(8,128)...) custom-call(bf16[2,256,128]{2,1,0:T(8,128)(2,1)S(1)} %get-tuple-elem, ...), custom_call_target="tpu_custom_call" | custom-call | flops 5750000128 | bytes 1000 | tf_op jit(solution)/shard_map/gated_linear/pallas_call | solution.py:53
  46.7 0.3 collective-permute-start.15
  47.0 1.5 %collective-permute-start.14 = (bf16[2,256,128]{2,1,0:T(8,128)(2,1)S(1)}, bf16[2,256,128]{2,1,0:T(8,128)(2,1)S(1)}, u32[]{:S(2)}, u32[]{:S(2)}) collective-permute-start(bf16[2,256,128]{2,1,0:T(8,128)(2,1)S(1)} %get-tuple-element.118), channel_id=1, source_target_pairs={{0,2},{1,3},{2,0},{3,1},{4,6},{5,7},{6,4},{7,5},{8,10},{9,11},{10,... | collective-permute-start | bytes 393224 | tf_op jit(solution)/shard_map/ppermute | solution.py:799
  48.5 0.0 collective-permute-start.13
  48.5 0.6 collective-permute-start.16
  49.1 0.1 weight_half.3
  49.2 1.6 %collective-permute-start.17 = (bf16[1,128,1024]{2,1,0:T(8,128)(2,1)S(1)}, bf16[1,128,1024]{2,1,0:T(8,128)(2,1)S(1)}, u32[]{:S(2)}, u32[]{:S(2)}) collective-permute-start(bf16[1,128,1024]{2,1,0:T(8,128)(2,1)S(1)} %get-tuple-element.121), channel_id=1, source_target_pairs={{0,2},{1,3},{2,0},{3,1},{4,6},{5,7},{6,4},{7,5},{8,10},{9,11},{10,... | collective-permute-start | bytes 786440 | tf_op jit(solution)/shard_map/ppermute | solution.py:799
  50.8 2.5 %collective-permute-done.14.refs_2_ = bf16[2,256,128]{2,1,0:T(8,128)(2,1)S(1)} collective-permute-done((bf16[2,256,128]{2,1,0:T(8,128)(2,1)S(1)}, bf16[2,256,128]{2,1,0:T(8,128)(2,1)S(1)}, u32[]{:S(2)}, u32[]{:S(2)}) %collective-permute-start.14) | collective-permute-done | bytes 131104 | tf_op jit(solution)/shard_map/ppermute | solution.py:799
  53.3 1.8 %collective-permute-done.16.refs_3_ = bf16[2,256,128]{2,1,0:T(8,128)(2,1)S(1)} collective-permute-done((bf16[2,256,128]{2,1,0:T(8,128)(2,1)S(1)}, bf16[2,256,128]{2,1,0:T(8,128)(2,1)S(1)}, u32[]{:S(2)}, u32[]{:S(2)}) %collective-permute-start.16) | collective-permute-done | bytes 131104 | tf_op jit(solution)/shard_map/ppermute | solution.py:799
  55.1 6.1 %doc_conv_grad.1 = (bf16[2,256,128]{2,1,0:T(8,128)(2,1)S(1)}, bf16[2,256,128]{2,1,0:T(8,128)(2,1)S(1)}, bf16[2,256,128]{2,1,0:T(8,128)(2,1)S(1)}, bf16[2,256,128...) custom-call(bf16[2,256,128]{2,1,0:T(8,128)(2,1)S(1)} %get-tuple-element.116.refs_0_, ...), custom_call_target="tpu_custom_call" | custom-call | flops 9200000000 | bytes 1000 | tf_op jit(solution)/shard_map/doc_conv_grad/pallas_call | solution.py:53
  61.3 0.2 weight_deal.1
  61.4 1.6 %collective-permute-start.21 = (f32[4,128,128]{2,1,0:T(8,128)S(1)}, f32[4,128,128]{2,1,0:T(8,128)S(1)}, u32[]{:S(2)}, u32[]{:S(2)}) collective-permute-start(f32[4,128,128]{2,1,0:T(8,128)S(1)} %get-tuple-element.126), channel_id=1, source_target_pairs={{0,4},{4,0},{8,12},{12,8},{16,20},{20,16},{24,28},{28,24},{1,5},{5... | collective-permute-start | bytes 786440 | tf_op jit(solution)/shard_map/ppermute | solution.py:799
  63.0 8.8 %state_grad.1 = f32[8,24,128]{2,1,0:T(8,128)} custom-call(f32[128,128]{1,0:T(8,128)S(1)} %get-tuple-element.93.refs_9_.refs_1_.refs_5_.refs_8_.refs_2_.refs_11_.refs_0_, f32[13,64,128]{2,1,0:T(8,128)S(1)} %get-tuple-element.94.refs_10_.refs_2_.refs_6_.refs_9_.refs_3_.refs_12_.refs_1_, ...), custom_call_target="tpu_custom_call" | custom-call | flops 11500000256 | bytes 1000 | tf_op jit(solution)/shard_map/state_grad/pallas_call | solution.py:53
  71.9 0.7 collective-permute-start.22
  72.5 4.8 %all-to-all-start = ((f32[8,24,128]{2,1,0:T(8,128)}), f32[8,24,128]{2,1,0:T(8,128)S(1)}, u32[]{:S(2)}, u32[]{:S(2)}) async-start(f32[8,24,128]{2,1,0:T(8,128)} %state_grad.1), calls=%async_computation | async-start | bytes 196608 | tf_op jit(solution)/shard_map/all_to_all | solution.py:968
  77.3 0.6 collective-permute-done.22.refs_1_
  77.9 2.7 %collective-permute-start.23 = (f32[1,128,128]{2,1,0:T(8,128)S(1)}, f32[1,128,128]{2,1,0:T(8,128)S(1)}, u32[]{:S(2)}, u32[]{:S(2)}) collective-permute-start(f32[1,128,128]{2,1,0:T(8,128)S(1)} %get-tuple-element.145), channel_id=1, source_target_pairs={{0,16},{4,20},{8,24},{12,28},{16,0},{20,4},{24,8},{28,12},{1,17},{... | collective-permute-start | bytes 196616 | tf_op jit(solution)/shard_map/ppermute | solution.py:799
  80.6 1.5 %collective-permute-start.19 = (bf16[2,256,128]{2,1,0:T(8,128)(2,1)S(1)}, bf16[2,256,128]{2,1,0:T(8,128)(2,1)S(1)}, u32[]{:S(2)}, u32[]{:S(2)}) collective-permute-start(bf16[2,256,128]{2,1,0:T(8,128)(2,1)S(1)} %get-tuple-element.136), channel_id=1, source_target_pairs={{0,2},{1,3},{2,0},{3,1},{4,6},{5,7},{6,4},{7,5},{8,10},{9,11},{10,... | collective-permute-start | bytes 393224 | tf_op jit(solution)/shard_map/ppermute | solution.py:799
  82.1 3.3 %all-to-all-done.refs_0_ = f32[8,24,128]{2,1,0:T(8,128)S(1)} async-done(((f32[8,24,128]{2,1,0:T(8,128)}), f32[8,24,128]{2,1,0:T(8,128)S(1)}, u32[]{:S(2)}, u32[]{:S(2)}) %all-to-all-start) | async-done | bytes 98336 | tf_op jit(solution)/shard_map/all_to_all | solution.py:968
  85.3 0.7 collective-permute-done.23.refs_2_
  86.1 0.3 collective-permute-start.26
  86.4 1.1 %collective-permute-start.25 = (f32[152,128]{1,0:T(8,128)S(1)}, f32[152,128]{1,0:T(8,128)S(1)}, u32[]{:S(2)}, u32[]{:S(2)}) collective-permute-start(f32[152,128]{1,0:T(8,128)S(1)} %last_sums.1.refs_0_), channel_id=1, source_target_pairs={{0,2},{1,3},{2,0},{3,1},{4,6},{5,7},{6,4},{7,5},{8,10},{9,11},{10,... | collective-permute-start | bytes 233480 | tf_op jit(solution)/shard_map/ppermute | solution.py:799
  87.5 0.5 collective-permute-start.24
  88.0 1.8 %layer_norm_grad.1 = bf16[2,256,512]{2,1,0:T(8,128)(2,1)} custom-call(bf16[2,256,128]{2,1,0:T(8,128)(2,1)S(1)} %get-tuple-element.134.refs_0_, bf16[2,256,128]{2,1,0:T(8,128)(2,1)S(1)} %collective-permute-done.18.refs_1_, bf16[2,256,128]{2,1,0:T(8,128)(2,1)S(1)} %collective-permute-done.19.refs_2_, bf16[2,256,128]{2,1,0:T(8,128)(2,1)S(1)} %collective-permute-done.20.refs_3_, ...), custom_call_target="tpu_custom_call" | custom-call | bytes 1000 | tf_op jit(solution)/shard_map/layer_norm_grad/pallas_call | solution.py:53
  89.8 1.0 %collective-permute-done.26.refs_3_ = f32[152,128]{1,0:T(8,128)S(1)} collective-permute-done((f32[152,128]{1,0:T(8,128)S(1)}, f32[152,128]{1,0:T(8,128)S(1)}, u32[]{:S(2)}, u32[]{:S(2)}) %collective-permute-start.26) | collective-permute-done | bytes 77856 | tf_op jit(solution)/shard_map/ppermute | solution.py:799
  90.8 1.4 %collective-permute-done.25.refs_2_ = f32[152,128]{1,0:T(8,128)S(1)} collective-permute-done((f32[152,128]{1,0:T(8,128)S(1)}, f32[152,128]{1,0:T(8,128)S(1)}, u32[]{:S(2)}, u32[]{:S(2)}) %collective-permute-start.25) | collective-permute-done | bytes 77856 | tf_op jit(solution)/shard_map/ppermute | solution.py:799
  92.2 0.8 last.1
  (42 shorter events, 0.2 us)
Async XLA Ops:
  0.6 6.0 %copy-start.2 = (bf16[2,256,512]{2,1,0:T(8,128)(2,1)S(1)}, bf16[2,256,512]{2,1,0:T(8,128)(2,1)}, u32[]{:S(2)}) copy-start(bf16[2,256,512]{2,1,0:T(8,128)(2,1)} %refs_4_.6) | copy-start | bytes 1572868
  2.5 6.0 %copy-start.4 = (f32[1,24,128]{2,1,0:T(8,128)S(1)}, f32[1,24,128]{2,1,0:T(8,128)}, u32[]{:S(2)}) copy-start(f32[1,24,128]{2,1,0:T(8,128)} %pack.1.refs_0_) | copy-start | bytes 36868
  2.5 7.9 %copy-start.6 = (bf16[512,128]{1,0:T(8,128)(2,1)S(1)}, bf16[512,128]{1,0:T(8,128)(2,1)}, u32[]{:S(2)}) copy-start(bf16[512,128]{1,0:T(8,128)(2,1)} %param.23) | copy-start | bytes 393220
  2.5 14.7 %copy-start = (bf16[256,1536]{1,0:T(8,128)(2,1)S(1)}, bf16[256,1536]{1,0:T(8,128)(2,1)}, u32[]{:S(2)}) copy-start(bf16[256,1536]{1,0:T(8,128)(2,1)} %constant.5.clone.refs_5_.refs_8_.refs_7_.refs_11_.refs_14_.refs_10_) | copy-start | bytes 2359300
  2.5 14.7 %copy-start.1 = (bf16[512,768]{1,0:T(8,128)(2,1)S(1)}, bf16[512,768]{1,0:T(8,128)(2,1)}, u32[]{:S(2)}) copy-start(bf16[512,768]{1,0:T(8,128)(2,1)} %constant.4.clone.refs_4_.refs_7_.refs_6_.refs_10_.refs_13_.refs_9_) | copy-start | bytes 2359300
  2.5 14.7 %copy-start.3 = (bf16[2,256,512]{2,1,0:T(8,128)(2,1)S(1)}, bf16[2,256,512]{2,1,0:T(8,128)(2,1)}, u32[]{:S(2)}) copy-start(bf16[2,256,512]{2,1,0:T(8,128)(2,1)} %refs_5_.6) | copy-start | bytes 1572868
  2.5 23.4 %copy-start.5 = (s32[2,4]{1,0:T(2,128)S(1)}, s32[2,4]{1,0:T(2,128)}, u32[]{:S(2)}) copy-start(s32[2,4]{1,0:T(2,128)} %refs_5_.5) | copy-start | bytes 100
  2.5 6.0 %collective-permute-start.3 = (f32[1,24,128]{2,1,0:T(8,128)}, f32[1,24,128]{2,1,0:T(8,128)S(1)}, u32[]{:S(2)}, u32[]{:S(2)}) collective-permute-start(f32[1,24,128]{2,1,0:T(8,128)} %pack.1.refs_0_), channel_id=1, source_target_pairs={{0,16},{4,20},{8,24},{12,28},{16,0},{20,4},{24,8},{28,12},{1,17},{... | collective-permute-start | bytes 36872 | tf_op jit(solution)/shard_map/ppermute | solution.py:799
  7.9 5.2 %collective-permute-start = (bf16[2,272,128]{2,1,0:T(8,128)(2,1)S(1)}, bf16[2,272,128]{2,1,0:T(8,128)(2,1)S(1)}, u32[]{:S(2)}, u32[]{:S(2)}) collective-permute-start(bf16[2,272,128]{2,1,0:T(8,128)(2,1)S(1)} %get-tuple-element.85), channel_id=1, source_target_pairs={{0,1},{1,0},{2,3},{3,2},{4,5},{5,4},{6,7},{7,6},{8,9},{9,8},{10,11... | collective-permute-start | bytes 417800 | tf_op jit(solution)/shard_map/ppermute | solution.py:799
  8.5 4.5 %collective-permute-start.4 = (f32[2,24,128]{2,1,0:T(8,128)S(1)}, f32[2,24,128]{2,1,0:T(8,128)S(1)}, u32[]{:S(2)}, u32[]{:S(2)}) collective-permute-start(f32[2,24,128]{2,1,0:T(8,128)S(1)} %pad_maximum_fusion.3), channel_id=1, source_target_pairs={{0,8},{4,12},{8,0},{12,4},{16,24},{20,28},{24,16},{28,20},{1,9},{5... | collective-permute-start | bytes 73736 | tf_op jit(solution)/shard_map/ppermute | solution.py:799
  10.4 12.4 %collective-permute-start.6 = (bf16[1,512,128]{2,1,0:T(8,128)(2,1)S(1)}, bf16[1,512,128]{2,1,0:T(8,128)(2,1)S(1)}, u32[]{:S(2)}, u32[]{:S(2)}) collective-permute-start(bf16[1,512,128]{2,1,0:T(8,128)(2,1)S(1)} %bitcast.17), channel_id=1, source_target_pairs={{0,16},{4,20},{8,24},{12,28},{16,0},{20,4},{24,8},{28,12},{1,17},{... | collective-permute-start | bytes 393224 | tf_op jit(solution)/shard_map/ppermute | solution.py:799
  13.0 4.2 %collective-permute-start.5 = (f32[4,24,128]{2,1,0:T(8,128)S(1)}, f32[4,24,128]{2,1,0:T(8,128)S(1)}, u32[]{:S(2)}, u32[]{:S(2)}) collective-permute-start(f32[4,24,128]{2,1,0:T(8,128)S(1)} %pad_maximum_fusion.2), channel_id=1, source_target_pairs={{0,4},{4,0},{8,12},{12,8},{16,20},{20,16},{24,28},{28,24},{1,5},{5... | collective-permute-start | bytes 147464 | tf_op jit(solution)/shard_map/ppermute | solution.py:799
  14.6 11.3 %collective-permute-start.1 = (bf16[2,272,128]{2,1,0:T(8,128)(2,1)S(1)}, bf16[2,272,128]{2,1,0:T(8,128)(2,1)S(1)}, u32[]{:S(2)}, u32[]{:S(2)}) collective-permute-start(bf16[2,272,128]{2,1,0:T(8,128)(2,1)S(1)} %get-tuple-element.86), channel_id=1, source_target_pairs={{0,2},{1,3},{2,0},{3,1},{4,6},{5,7},{6,4},{7,5},{8,10},{9,11},{10,... | collective-permute-start | bytes 417800 | tf_op jit(solution)/shard_map/ppermute | solution.py:799
  16.1 9.8 %collective-permute-start.2 = (bf16[2,272,128]{2,1,0:T(8,128)(2,1)S(1)}, bf16[2,272,128]{2,1,0:T(8,128)(2,1)S(1)}, u32[]{:S(2)}, u32[]{:S(2)}) collective-permute-start(bf16[2,272,128]{2,1,0:T(8,128)(2,1)S(1)} %get-tuple-element.87), channel_id=1, source_target_pairs={{0,3},{1,2},{2,1},{3,0},{4,7},{5,6},{6,5},{7,4},{8,11},{9,10},{10,... | collective-permute-start | bytes 417800 | tf_op jit(solution)/shard_map/ppermute | solution.py:799
  22.9 10.0 %collective-permute-start.8 = (bf16[2,512,128]{2,1,0:T(8,128)(2,1)S(1)}, bf16[2,512,128]{2,1,0:T(8,128)(2,1)S(1)}, u32[]{:S(2)}, u32[]{:S(2)}) collective-permute-start(bf16[2,512,128]{2,1,0:T(8,128)(2,1)S(1)} %pad_maximum_fusion.refs_1_), channel_id=1, source_target_pairs={{0,4},{4,0},{8,12},{12,8},{16,20},{20,16},{24,28},{28,24},{1,5},{5... | collective-permute-start | bytes 786440 | tf_op jit(solution)/shard_map/ppermute | solution.py:799
  24.5 8.4 %collective-permute-start.7 = (bf16[2,512,128]{2,1,0:T(8,128)(2,1)S(1)}, bf16[2,512,128]{2,1,0:T(8,128)(2,1)S(1)}, u32[]{:S(2)}, u32[]{:S(2)}) collective-permute-start(bf16[2,512,128]{2,1,0:T(8,128)(2,1)S(1)} %pad_maximum_fusion.refs_1_), channel_id=1, source_target_pairs={{0,8},{4,12},{8,0},{12,4},{16,24},{20,28},{24,16},{28,20},{1,9},{5... | collective-permute-start | bytes 786440 | tf_op jit(solution)/shard_map/ppermute | solution.py:799
  32.9 6.9 %collective-permute-start.12 = (bf16[2,512,128]{2,1,0:T(8,128)(2,1)S(1)}, bf16[2,512,128]{2,1,0:T(8,128)(2,1)S(1)}, u32[]{:S(2)}, u32[]{:S(2)}) collective-permute-start(bf16[2,512,128]{2,1,0:T(8,128)(2,1)S(1)} %collective-permute-done.7.refs_2_), channel_id=1, source_target_pairs={{0,4},{4,0},{8,12},{12,8},{16,20},{20,16},{24,28},{28,24},{1,5},{5... | collective-permute-start | bytes 786440 | tf_op jit(solution)/shard_map/ppermute | solution.py:799
  33.4 1.9 %collective-permute-start.9 = (bf16[2,256,128]{2,1,0:T(8,128)(2,1)S(1)}, bf16[2,256,128]{2,1,0:T(8,128)(2,1)S(1)}, u32[]{:S(2)}, u32[]{:S(2)}) collective-permute-start(bf16[2,256,128]{2,1,0:T(8,128)(2,1)S(1)} %get-tuple-element.102), channel_id=1, source_target_pairs={{0,1},{1,0},{2,3},{3,2},{4,5},{5,4},{6,7},{7,6},{8,9},{9,8},{10,11... | collective-permute-start | bytes 393224 | tf_op jit(solution)/shard_map/ppermute | solution.py:799
  33.4 6.3 %collective-permute-start.10 = (bf16[2,256,128]{2,1,0:T(8,128)(2,1)S(1)}, bf16[2,256,128]{2,1,0:T(8,128)(2,1)S(1)}, u32[]{:S(2)}, u32[]{:S(2)}) collective-permute-start(bf16[2,256,128]{2,1,0:T(8,128)(2,1)S(1)} %get-tuple-element.104), channel_id=1, source_target_pairs={{0,2},{1,3},{2,0},{3,1},{4,6},{5,7},{6,4},{7,5},{8,10},{9,11},{10,... | collective-permute-start | bytes 393224 | tf_op jit(solution)/shard_map/ppermute | solution.py:799
  34.9 6.8 %collective-permute-start.11 = (bf16[2,256,128]{2,1,0:T(8,128)(2,1)S(1)}, bf16[2,256,128]{2,1,0:T(8,128)(2,1)S(1)}, u32[]{:S(2)}, u32[]{:S(2)}) collective-permute-start(bf16[2,256,128]{2,1,0:T(8,128)(2,1)S(1)} %get-tuple-element.109), channel_id=1, source_target_pairs={{0,3},{1,2},{2,1},{3,0},{4,7},{5,6},{6,5},{7,4},{8,11},{9,10},{10,... | collective-permute-start | bytes 393224 | tf_op jit(solution)/shard_map/ppermute | solution.py:799
  46.7 2.5 %collective-permute-start.15 = (bf16[2,128,1024]{2,1,0:T(8,128)(2,1)S(1)}, bf16[2,128,1024]{2,1,0:T(8,128)(2,1)S(1)}, u32[]{:S(2)}, u32[]{:S(2)}) collective-permute-start(bf16[2,128,1024]{2,1,0:T(8,128)(2,1)S(1)} %get-tuple-element.120), channel_id=1, source_target_pairs={{0,1},{1,0},{2,3},{3,2},{4,5},{5,4},{6,7},{7,6},{8,9},{9,8},{10,11... | collective-permute-start | bytes 1572872 | tf_op jit(solution)/shard_map/ppermute | solution.py:799
  47.0 6.3 %collective-permute-start.14 = (bf16[2,256,128]{2,1,0:T(8,128)(2,1)S(1)}, bf16[2,256,128]{2,1,0:T(8,128)(2,1)S(1)}, u32[]{:S(2)}, u32[]{:S(2)}) collective-permute-start(bf16[2,256,128]{2,1,0:T(8,128)(2,1)S(1)} %get-tuple-element.118), channel_id=1, source_target_pairs={{0,2},{1,3},{2,0},{3,1},{4,6},{5,7},{6,4},{7,5},{8,10},{9,11},{10,... | collective-permute-start | bytes 393224 | tf_op jit(solution)/shard_map/ppermute | solution.py:799
  48.5 4.8 %collective-permute-start.13 = (bf16[2,256,128]{2,1,0:T(8,128)(2,1)S(1)}, bf16[2,256,128]{2,1,0:T(8,128)(2,1)S(1)}, u32[]{:S(2)}, u32[]{:S(2)}) collective-permute-start(bf16[2,256,128]{2,1,0:T(8,128)(2,1)S(1)} %get-tuple-element.117), channel_id=1, source_target_pairs={{0,1},{1,0},{2,3},{3,2},{4,5},{5,4},{6,7},{7,6},{8,9},{9,8},{10,11... | collective-permute-start | bytes 393224 | tf_op jit(solution)/shard_map/ppermute | solution.py:799
  48.5 6.6 %collective-permute-start.16 = (bf16[2,256,128]{2,1,0:T(8,128)(2,1)S(1)}, bf16[2,256,128]{2,1,0:T(8,128)(2,1)S(1)}, u32[]{:S(2)}, u32[]{:S(2)}) collective-permute-start(bf16[2,256,128]{2,1,0:T(8,128)(2,1)S(1)} %get-tuple-element.123), channel_id=1, source_target_pairs={{0,3},{1,2},{2,1},{3,0},{4,7},{5,6},{6,5},{7,4},{8,11},{9,10},{10,... | collective-permute-start | bytes 393224 | tf_op jit(solution)/shard_map/ppermute | solution.py:799
  49.2 12.0 %collective-permute-start.17 = (bf16[1,128,1024]{2,1,0:T(8,128)(2,1)S(1)}, bf16[1,128,1024]{2,1,0:T(8,128)(2,1)S(1)}, u32[]{:S(2)}, u32[]{:S(2)}) collective-permute-start(bf16[1,128,1024]{2,1,0:T(8,128)(2,1)S(1)} %get-tuple-element.121), channel_id=1, source_target_pairs={{0,2},{1,3},{2,0},{3,1},{4,6},{5,7},{6,4},{7,5},{8,10},{9,11},{10,... | collective-permute-start | bytes 786440 | tf_op jit(solution)/shard_map/ppermute | solution.py:799
  61.4 10.4 %collective-permute-start.21 = (f32[4,128,128]{2,1,0:T(8,128)S(1)}, f32[4,128,128]{2,1,0:T(8,128)S(1)}, u32[]{:S(2)}, u32[]{:S(2)}) collective-permute-start(f32[4,128,128]{2,1,0:T(8,128)S(1)} %get-tuple-element.126), channel_id=1, source_target_pairs={{0,4},{4,0},{8,12},{12,8},{16,20},{20,16},{24,28},{28,24},{1,5},{5... | collective-permute-start | bytes 786440 | tf_op jit(solution)/shard_map/ppermute | solution.py:799
  71.9 6.0 %collective-permute-start.22 = (f32[2,128,128]{2,1,0:T(8,128)S(1)}, f32[2,128,128]{2,1,0:T(8,128)S(1)}, u32[]{:S(2)}, u32[]{:S(2)}) collective-permute-start(f32[2,128,128]{2,1,0:T(8,128)S(1)} %get-tuple-element.143), channel_id=1, source_target_pairs={{0,8},{4,12},{8,0},{12,4},{16,24},{20,28},{24,16},{28,20},{1,9},{5... | collective-permute-start | bytes 393224 | tf_op jit(solution)/shard_map/ppermute | solution.py:799
  72.5 12.8 %all-to-all-start = ((f32[8,24,128]{2,1,0:T(8,128)}), f32[8,24,128]{2,1,0:T(8,128)S(1)}, u32[]{:S(2)}, u32[]{:S(2)}) async-start(f32[8,24,128]{2,1,0:T(8,128)} %state_grad.1), calls=%async_computation | async-start | bytes 196608 | tf_op jit(solution)/shard_map/all_to_all | solution.py:968
  77.3 10.2 %collective-permute-start.18 = (bf16[2,256,128]{2,1,0:T(8,128)(2,1)S(1)}, bf16[2,256,128]{2,1,0:T(8,128)(2,1)S(1)}, u32[]{:S(2)}, u32[]{:S(2)}) collective-permute-start(bf16[2,256,128]{2,1,0:T(8,128)(2,1)S(1)} %get-tuple-element.135), channel_id=1, source_target_pairs={{0,1},{1,0},{2,3},{3,2},{4,5},{5,4},{6,7},{7,6},{8,9},{9,8},{10,11... | collective-permute-start | bytes 393224 | tf_op jit(solution)/shard_map/ppermute | solution.py:799
  77.9 8.2 %collective-permute-start.23 = (f32[1,128,128]{2,1,0:T(8,128)S(1)}, f32[1,128,128]{2,1,0:T(8,128)S(1)}, u32[]{:S(2)}, u32[]{:S(2)}) collective-permute-start(f32[1,128,128]{2,1,0:T(8,128)S(1)} %get-tuple-element.145), channel_id=1, source_target_pairs={{0,16},{4,20},{8,24},{12,28},{16,0},{20,4},{24,8},{28,12},{1,17},{... | collective-permute-start | bytes 196616 | tf_op jit(solution)/shard_map/ppermute | solution.py:799
  80.6 7.4 %collective-permute-start.19 = (bf16[2,256,128]{2,1,0:T(8,128)(2,1)S(1)}, bf16[2,256,128]{2,1,0:T(8,128)(2,1)S(1)}, u32[]{:S(2)}, u32[]{:S(2)}) collective-permute-start(bf16[2,256,128]{2,1,0:T(8,128)(2,1)S(1)} %get-tuple-element.136), channel_id=1, source_target_pairs={{0,2},{1,3},{2,0},{3,1},{4,6},{5,7},{6,4},{7,5},{8,10},{9,11},{10,... | collective-permute-start | bytes 393224 | tf_op jit(solution)/shard_map/ppermute | solution.py:799
  82.1 5.9 %collective-permute-start.20 = (bf16[2,256,128]{2,1,0:T(8,128)(2,1)S(1)}, bf16[2,256,128]{2,1,0:T(8,128)(2,1)S(1)}, u32[]{:S(2)}, u32[]{:S(2)}) collective-permute-start(bf16[2,256,128]{2,1,0:T(8,128)(2,1)S(1)} %get-tuple-element.137), channel_id=1, source_target_pairs={{0,3},{1,2},{2,1},{3,0},{4,7},{5,6},{6,5},{7,4},{8,11},{9,10},{10,... | collective-permute-start | bytes 393224 | tf_op jit(solution)/shard_map/ppermute | solution.py:799
  86.1 4.7 %collective-permute-start.26 = (f32[152,128]{1,0:T(8,128)S(1)}, f32[152,128]{1,0:T(8,128)S(1)}, u32[]{:S(2)}, u32[]{:S(2)}) collective-permute-start(f32[152,128]{1,0:T(8,128)S(1)} %last_sums.1.refs_0_), channel_id=1, source_target_pairs={{0,3},{1,2},{2,1},{3,0},{4,7},{5,6},{6,5},{7,4},{8,11},{9,10},{10,... | collective-permute-start | bytes 233480 | tf_op jit(solution)/shard_map/ppermute | solution.py:799
  86.4 5.8 %collective-permute-start.25 = (f32[152,128]{1,0:T(8,128)S(1)}, f32[152,128]{1,0:T(8,128)S(1)}, u32[]{:S(2)}, u32[]{:S(2)}) collective-permute-start(f32[152,128]{1,0:T(8,128)S(1)} %last_sums.1.refs_0_), channel_id=1, source_target_pairs={{0,2},{1,3},{2,0},{3,1},{4,6},{5,7},{6,4},{7,5},{8,10},{9,11},{10,... | collective-permute-start | bytes 233480 | tf_op jit(solution)/shard_map/ppermute | solution.py:799
  87.5 4.7 %collective-permute-start.24 = (f32[152,128]{1,0:T(8,128)S(1)}, f32[152,128]{1,0:T(8,128)S(1)}, u32[]{:S(2)}, u32[]{:S(2)}) collective-permute-start(f32[152,128]{1,0:T(8,128)S(1)} %last_sums.1.refs_0_), channel_id=1, source_target_pairs={{0,1},{1,0},{2,3},{3,2},{4,5},{5,4},{6,7},{7,6},{8,9},{9,8},{10,11... | collective-permute-start | bytes 233480 | tf_op jit(solution)/shard_map/ppermute | solution.py:799

commit v7 on v6

--- a/solution.py
+++ b/solution.py
@@ -625,12 +625,14 @@
 
 
 def merge_kernel(x_ref, mine_ref, other_ref, o_ref):
-    rows = x_ref.shape[1]
+    span = -(-x_ref.shape[1] // 32) * 32
     total = x_ref[0]
     for i in range(1, x_ref.shape[0]):
         total = total + x_ref[i]
-    o_ref[0:rows] = total
-    o_ref[rows:] = mine_ref[0] + other_ref[0]
+    total = jnp.concatenate([total, jnp.zeros((span - total.shape[0], LANES), f32)], axis=0)
+    for k, term in enumerate(terms3(total)):
+        o_ref[k * span : (k + 1) * span] = term
+    o_ref[3 * span :] = (mine_ref[0] + other_ref[0]).astype(bf16)
 
 
 PAIR = 2 * FINE
@@ -773,7 +775,12 @@
     per, cols = lam_ref.shape[1], lb_ref.shape[1]
     group = iota((1, LANES), 1) // sub
     me = lax.axis_index("seq")
-    small = [part[0:rows] for part in parts]
+    merged = not dws
+    if merged:
+        span = -(-rows // 32) * 32
+        small = [sum(part[k * span : k * span + rows].astype(f32) for k in range(3)) for part in parts]
+    else:
+        small = [part[0:rows] for part in parts]
     for u in range(groups):
         acc = jnp.zeros((rows, LANES), f32)
         for d, value in enumerate(small):
@@ -787,11 +794,11 @@
     imag_ref[...] = pltpu.roll(total, LANES - per, 1)[height + 1 : height + 2, 0:per]
     lb_ref[...] = total[height + 2 : height + 3, 0:cols]
     for d in range(nseq):
-        part_ref, first = (dws[d], 0) if dws else (parts[d], rows)
+        part_ref, first = (parts[d], 3 * span) if merged else (dws[d], 0)
         c = me ^ d
         for i in range((part_ref.shape[0] - first) // sub):
             at = pl.multiple_of((i * nseq + c) * sub, sub)
-            dw_ref[pl.ds(at, sub)] = part_ref[first + i * sub : first + (i + 1) * sub]
+            dw_ref[pl.ds(at, sub)] = part_ref[first + i * sub : first + (i + 1) * sub].astype(f32)
 
 
 def swap(x, axis, by):
@@ -980,7 +987,7 @@
         name="layer_norm_grad", mib=12,
     )(*gs, block_in, cotangent)
     if staged:
-        merged = call(merge_kernel, shape((rows + wide, cols)), [VM] * 3, name="last_sums", us=0.5)(small, stay, dw_other)
+        merged = call(merge_kernel, shape((-(-rows // 32) * 96 + wide, cols), bf16), [VM] * 3, name="last_sums", us=0.5)(small, stay, dw_other)
         merged = trade([merged] * nseq, "seq")
         smalls, dws = merged, []
     else:

time: 93.3 us -> 92.4 us (level)
  no operation moved by 1% of the time
where the time goes in v7:
time: 92.4 us; the launch traced here: 92.1 us
  Pallas kernels  39.2 us (42%)
  starting transfers between devices  34.4 us (37%)
  waiting for transfers between devices  17.6 us (19%)
    pallas_call x16, Pallas kernels, call(): return lambda *args: kernel(*args, *keep)  39.2 us
    ppermute x27, starting transfers between devices, swap(): lax.ppermute(v, axis, [(i, i ^ by) for i in range(n)])  29.7 us
    ppermute x27, waiting for transfers between devices, swap(): lax.ppermute(v, axis, [(i, i ^ by) for i in range(n)])  14.3 us
    all_to_all x1, starting transfers between devices, on_device(): small = lax.all_to_all(small, 'dp', 0, 0, tiled=True)  4.72 us
    all_to_all x1, waiting for transfers between devices, on_device(): small = lax.all_to_all(small, 'dp', 0, 0, tiled=True)  3.29 us
  transfers between devices with their start and end apart: 28, of which 11 were waited for; matrix products, arithmetic and copies ran while one was open for 0% of the time, Pallas kernels for 34%

profile of v7, /device:TPU:0, one launch (start us, length us, event | category | flops | bytes accessed | tf_op | source)
XLA Modules:
  0.0 92.1 jit_solution(259169720277617465)
XLA Ops:
  0.7 1.8 %pack.1.refs_0_ = f32[1,24,128]{2,1,0:T(8,128)} custom-call(f32[128,64]{1,0:T(8,128)} %bitcast.19, f32[1,64]{1,0:T(1,128)} %bitcast.20, f32[1,64]{1,0:T(1,128)} %bitcast.21, f32[1,64]{1,0:T(1,128)} %bitcast.22, f32[1,64]{1,0:T(1,128)} %bitcast.23, f32[1,8]{1,0:T(1,128)} %bitcast.24, f32[1,8]{1,0:T(1,128)} %bitcast.25, f32[1,128]{1,0:T(1,128)} %bitcast.26), custom_call_target="tpu_custom_call" | custom-call | flops 2300000000 | bytes 1000 | tf_op jit(solution)/shard_map/pack/pallas_call | solution.py:53
  2.5 0.0 copy-start.1
  2.5 4.1 %collective-permute-start.3 = (f32[1,24,128]{2,1,0:T(8,128)}, f32[1,24,128]{2,1,0:T(8,128)S(1)}, u32[]{:S(2)}, u32[]{:S(2)}) collective-permute-start(f32[1,24,128]{2,1,0:T(8,128)} %pack.1.refs_0_), channel_id=1, source_target_pairs={{0,16},{4,20},{8,24},{12,28},{16,0},{20,4},{24,8},{28,12},{1,17},{... | collective-permute-start | bytes 36872 | tf_op jit(solution)/shard_map/ppermute | solution.py:806
  6.6 1.2 %spread.1 = (bf16[2,272,128]{2,1,0:T(8,128)(2,1)S(1)}, bf16[2,272,128]{2,1,0:T(8,128)(2,1)S(1)}, bf16[2,272,128]{2,1,0:T(8,128)(2,1)S(1)}, bf16[2,272,128]{2,1,0:T(8,128)(2,1)S(1)}) custom-call(bf16[2,256,512]{2,1,0:T(8,128)(2,1)S(1)} %copy-done.2), custom_call_target="tpu_custom_call" | custom-call | flops 2300000000 | bytes 1000 | tf_op jit(solution)/shard_map/spread/pallas_call | solution.py:53
  7.9 0.1 collective-permute-start
  8.0 0.5 collective-permute-done.3.refs_1_
  8.5 1.9 %collective-permute-start.4 = (f32[2,24,128]{2,1,0:T(8,128)S(1)}, f32[2,24,128]{2,1,0:T(8,128)S(1)}, u32[]{:S(2)}, u32[]{:S(2)}) collective-permute-start(f32[2,24,128]{2,1,0:T(8,128)S(1)} %pad_maximum_fusion.3), channel_id=1, source_target_pairs={{0,8},{4,12},{8,0},{12,4},{16,24},{20,28},{24,16},{28,20},{1,9},{5... | collective-permute-start | bytes 73736 | tf_op jit(solution)/shard_map/ppermute | solution.py:806
  10.4 2.6 %collective-permute-start.6 = (bf16[1,512,128]{2,1,0:T(8,128)(2,1)S(1)}, bf16[1,512,128]{2,1,0:T(8,128)(2,1)S(1)}, u32[]{:S(2)}, u32[]{:S(2)}) collective-permute-start(bf16[1,512,128]{2,1,0:T(8,128)(2,1)S(1)} %bitcast.17), channel_id=1, source_target_pairs={{0,16},{4,20},{8,24},{12,28},{16,0},{20,4},{24,8},{28,12},{1,17},{... | collective-permute-start | bytes 393224 | tf_op jit(solution)/shard_map/ppermute | solution.py:806
  13.0 1.6 %collective-permute-start.5 = (f32[4,24,128]{2,1,0:T(8,128)S(1)}, f32[4,24,128]{2,1,0:T(8,128)S(1)}, u32[]{:S(2)}, u32[]{:S(2)}) collective-permute-start(f32[4,24,128]{2,1,0:T(8,128)S(1)} %pad_maximum_fusion.2), channel_id=1, source_target_pairs={{0,4},{4,0},{8,12},{12,8},{16,20},{20,16},{24,28},{28,24},{1,5},{5... | collective-permute-start | bytes 147464 | tf_op jit(solution)/shard_map/ppermute | solution.py:806
  14.6 1.5 %collective-permute-start.1 = (bf16[2,272,128]{2,1,0:T(8,128)(2,1)S(1)}, bf16[2,272,128]{2,1,0:T(8,128)(2,1)S(1)}, u32[]{:S(2)}, u32[]{:S(2)}) collective-permute-start(bf16[2,272,128]{2,1,0:T(8,128)(2,1)S(1)} %get-tuple-element.86), channel_id=1, source_target_pairs={{0,2},{1,3},{2,0},{3,1},{4,6},{5,7},{6,4},{7,5},{8,10},{9,11},{10,... | collective-permute-start | bytes 417800 | tf_op jit(solution)/shard_map/ppermute | solution.py:806
  16.1 1.1 %collective-permute-done.5.refs_3_ = f32[4,24,128]{2,1,0:T(8,128)S(1)} collective-permute-done((f32[4,24,128]{2,1,0:T(8,128)S(1)}, f32[4,24,128]{2,1,0:T(8,128)S(1)}, u32[]{:S(2)}, u32[]{:S(2)}) %collective-permute-start.5) | collective-permute-done | bytes 49184 | tf_op jit(solution)/shard_map/ppermute | solution.py:806
  17.2 5.6 %lag_kernel.1 = (f32[4,512,128]{2,1,0:T(8,128)S(1)}, f32[8,128]{1,0:T(8,128)S(1)}, f32[128,128]{1,0:T(8,128)S(1)}, f32[13,64,128]{2,1,0:T(8,128)S(1)}, f32[26,64,128]{2,1,0:T(8,128)S(1)}) custom-call(f32[1,24,128]{2,1,0:T(8,128)S(1)} %copy-done.4, f32[1,24,128]{2,1,0:T(8,128)S(1)} %collective-permute-done.3.refs_1_, ...), custom_call_target="tpu_custom_call" | custom-call | bytes 1000 | tf_op jit(solution)/shard_map/lag_kernel/pallas_call | solution.py:53
  22.9 1.6 %collective-permute-start.8 = (bf16[2,512,128]{2,1,0:T(8,128)(2,1)S(1)}, bf16[2,512,128]{2,1,0:T(8,128)(2,1)S(1)}, u32[]{:S(2)}, u32[]{:S(2)}) collective-permute-start(bf16[2,512,128]{2,1,0:T(8,128)(2,1)S(1)} %pad_maximum_fusion.refs_1_), channel_id=1, source_target_pairs={{0,4},{4,0},{8,12},{12,8},{16,20},{20,16},{24,28},{28,24},{1,5},{5... | collective-permute-start | bytes 786440 | tf_op jit(solution)/shard_map/ppermute | solution.py:806
  24.5 1.4 %collective-permute-start.7 = (bf16[2,512,128]{2,1,0:T(8,128)(2,1)S(1)}, bf16[2,512,128]{2,1,0:T(8,128)(2,1)S(1)}, u32[]{:S(2)}, u32[]{:S(2)}) collective-permute-start(bf16[2,512,128]{2,1,0:T(8,128)(2,1)S(1)} %pad_maximum_fusion.refs_1_), channel_id=1, source_target_pairs={{0,8},{4,12},{8,0},{12,4},{16,24},{20,28},{24,16},{28,20},{1,9},{5... | collective-permute-start | bytes 786440 | tf_op jit(solution)/shard_map/ppermute | solution.py:806
  25.9 6.9 %doc_conv.1 = (bf16[2,256,128]{2,1,0:T(8,128)(2,1)S(1)}, bf16[2,256,128]{2,1,0:T(8,128)(2,1)S(1)}, bf16[2,256,128]{2,1,0:T(8,128)(2,1)S(1)}, bf16[2,256,128]{2,1...) custom-call(bf16[2,272,128]{2,1,0:T(8,128)(2,1)S(1)} %get-tuple-element.84.refs_0_, ...), custom_call_target="tpu_custom_call" | custom-call | flops 8049999872 | bytes 1000 | tf_op jit(solution)/shard_map/doc_conv/pallas_call | solution.py:53
  32.9 0.6 collective-permute-start.12
  33.5 1.5 %collective-permute-start.10 = (bf16[2,256,128]{2,1,0:T(8,128)(2,1)S(1)}, bf16[2,256,128]{2,1,0:T(8,128)(2,1)S(1)}, u32[]{:S(2)}, u32[]{:S(2)}) collective-permute-start(bf16[2,256,128]{2,1,0:T(8,128)(2,1)S(1)} %get-tuple-element.104), channel_id=1, source_target_pairs={{0,2},{1,3},{2,0},{3,1},{4,6},{5,7},{6,4},{7,5},{8,10},{9,11},{10,... | collective-permute-start | bytes 393224 | tf_op jit(solution)/shard_map/ppermute | solution.py:806
  34.9 0.4 collective-permute-start.11
  35.4 0.5 state_powers.1.refs_14_.refs_17_.refs_11_.refs_5_.refs_3_
  35.9 3.9 %collective-permute-done.10.refs_2_ = bf16[2,256,128]{2,1,0:T(8,128)(2,1)S(1)} collective-permute-done((bf16[2,256,128]{2,1,0:T(8,128)(2,1)S(1)}, bf16[2,256,128]{2,1,0:T(8,128)(2,1)S(1)}, u32[]{:S(2)}, u32[]{:S(2)}) %collective-permute-start.10) | collective-permute-done | bytes 131104 | tf_op jit(solution)/shard_map/ppermute | solution.py:806
  39.7 0.3 linear_rows.1
  40.1 1.7 %collective-permute-done.11.refs_3_ = bf16[2,256,128]{2,1,0:T(8,128)(2,1)S(1)} collective-permute-done((bf16[2,256,128]{2,1,0:T(8,128)(2,1)S(1)}, bf16[2,256,128]{2,1,0:T(8,128)(2,1)S(1)}, u32[]{:S(2)}, u32[]{:S(2)}) %collective-permute-start.11) | collective-permute-done | bytes 131104 | tf_op jit(solution)/shard_map/ppermute | solution.py:806
  41.8 4.9 %gated_linear.1 = (bf16[2,256,512]{2,1,0:T(8,128)(2,1)}, f32[1,1024]{1,0:T(1,128)S(1)}, bf16[2,256,128]{2,1,0:T(8,128)(2,1)S(1)}, bf16[2,256,128]{2,1,0:T(8,128)...) custom-call(bf16[2,256,128]{2,1,0:T(8,128)(2,1)S(1)} %get-tuple-elem, ...), custom_call_target="tpu_custom_call" | custom-call | flops 5750000128 | bytes 1000 | tf_op jit(solution)/shard_map/gated_linear/pallas_call | solution.py:53
  46.7 0.3 collective-permute-start.15
  47.0 1.5 %collective-permute-start.14 = (bf16[2,256,128]{2,1,0:T(8,128)(2,1)S(1)}, bf16[2,256,128]{2,1,0:T(8,128)(2,1)S(1)}, u32[]{:S(2)}, u32[]{:S(2)}) collective-permute-start(bf16[2,256,128]{2,1,0:T(8,128)(2,1)S(1)} %get-tuple-element.118), channel_id=1, source_target_pairs={{0,2},{1,3},{2,0},{3,1},{4,6},{5,7},{6,4},{7,5},{8,10},{9,11},{10,... | collective-permute-start | bytes 393224 | tf_op jit(solution)/shard_map/ppermute | solution.py:806
  48.5 0.6 collective-permute-start.16
  49.1 0.1 weight_half.3
  49.2 1.6 %collective-permute-start.17 = (bf16[1,128,1024]{2,1,0:T(8,128)(2,1)S(1)}, bf16[1,128,1024]{2,1,0:T(8,128)(2,1)S(1)}, u32[]{:S(2)}, u32[]{:S(2)}) collective-permute-start(bf16[1,128,1024]{2,1,0:T(8,128)(2,1)S(1)} %get-tuple-element.121), channel_id=1, source_target_pairs={{0,2},{1,3},{2,0},{3,1},{4,6},{5,7},{6,4},{7,5},{8,10},{9,11},{10,... | collective-permute-start | bytes 786440 | tf_op jit(solution)/shard_map/ppermute | solution.py:806
  50.8 2.5 %collective-permute-done.14.refs_2_ = bf16[2,256,128]{2,1,0:T(8,128)(2,1)S(1)} collective-permute-done((bf16[2,256,128]{2,1,0:T(8,128)(2,1)S(1)}, bf16[2,256,128]{2,1,0:T(8,128)(2,1)S(1)}, u32[]{:S(2)}, u32[]{:S(2)}) %collective-permute-start.14) | collective-permute-done | bytes 131104 | tf_op jit(solution)/shard_map/ppermute | solution.py:806
  53.3 1.8 %collective-permute-done.16.refs_3_ = bf16[2,256,128]{2,1,0:T(8,128)(2,1)S(1)} collective-permute-done((bf16[2,256,128]{2,1,0:T(8,128)(2,1)S(1)}, bf16[2,256,128]{2,1,0:T(8,128)(2,1)S(1)}, u32[]{:S(2)}, u32[]{:S(2)}) %collective-permute-start.16) | collective-permute-done | bytes 131104 | tf_op jit(solution)/shard_map/ppermute | solution.py:806
  55.1 6.1 %doc_conv_grad.1 = (bf16[2,256,128]{2,1,0:T(8,128)(2,1)S(1)}, bf16[2,256,128]{2,1,0:T(8,128)(2,1)S(1)}, bf16[2,256,128]{2,1,0:T(8,128)(2,1)S(1)}, bf16[2,256,128...) custom-call(bf16[2,256,128]{2,1,0:T(8,128)(2,1)S(1)} %get-tuple-element.116.refs_0_, ...), custom_call_target="tpu_custom_call" | custom-call | flops 9200000000 | bytes 1000 | tf_op jit(solution)/shard_map/doc_conv_grad/pallas_call | solution.py:53
  61.3 0.2 weight_deal.1
  61.4 1.6 %collective-permute-start.21 = (f32[4,128,128]{2,1,0:T(8,128)S(1)}, f32[4,128,128]{2,1,0:T(8,128)S(1)}, u32[]{:S(2)}, u32[]{:S(2)}) collective-permute-start(f32[4,128,128]{2,1,0:T(8,128)S(1)} %get-tuple-element.126), channel_id=1, source_target_pairs={{0,4},{4,0},{8,12},{12,8},{16,20},{20,16},{24,28},{28,24},{1,5},{5... | collective-permute-start | bytes 786440 | tf_op jit(solution)/shard_map/ppermute | solution.py:806
  63.0 8.8 %state_grad.1 = f32[8,24,128]{2,1,0:T(8,128)} custom-call(f32[128,128]{1,0:T(8,128)S(1)} %get-tuple-element.93.refs_9_.refs_1_.refs_5_.refs_8_.refs_2_.refs_11_.refs_0_, f32[13,64,128]{2,1,0:T(8,128)S(1)} %get-tuple-element.94.refs_10_.refs_2_.refs_6_.refs_9_.refs_3_.refs_12_.refs_1_, ...), custom_call_target="tpu_custom_call" | custom-call | flops 11500000256 | bytes 1000 | tf_op jit(solution)/shard_map/state_grad/pallas_call | solution.py:53
  71.9 0.7 collective-permute-start.22
  72.6 4.7 %all-to-all-start = ((f32[8,24,128]{2,1,0:T(8,128)}), f32[8,24,128]{2,1,0:T(8,128)S(1)}, u32[]{:S(2)}, u32[]{:S(2)}) async-start(f32[8,24,128]{2,1,0:T(8,128)} %state_grad.1), calls=%async_computation | async-start | bytes 196608 | tf_op jit(solution)/shard_map/all_to_all | solution.py:975
  77.3 0.6 collective-permute-done.22.refs_1_
  77.9 2.7 %collective-permute-start.23 = (f32[1,128,128]{2,1,0:T(8,128)S(1)}, f32[1,128,128]{2,1,0:T(8,128)S(1)}, u32[]{:S(2)}, u32[]{:S(2)}) collective-permute-start(f32[1,128,128]{2,1,0:T(8,128)S(1)} %get-tuple-element.145), channel_id=1, source_target_pairs={{0,16},{4,20},{8,24},{12,28},{16,0},{20,4},{24,8},{28,12},{1,17},{... | collective-permute-start | bytes 196616 | tf_op jit(solution)/shard_map/ppermute | solution.py:806
  80.5 1.5 %collective-permute-start.19 = (bf16[2,256,128]{2,1,0:T(8,128)(2,1)S(1)}, bf16[2,256,128]{2,1,0:T(8,128)(2,1)S(1)}, u32[]{:S(2)}, u32[]{:S(2)}) collective-permute-start(bf16[2,256,128]{2,1,0:T(8,128)(2,1)S(1)} %get-tuple-element.136), channel_id=1, source_target_pairs={{0,2},{1,3},{2,0},{3,1},{4,6},{5,7},{6,4},{7,5},{8,10},{9,11},{10,... | collective-permute-start | bytes 393224 | tf_op jit(solution)/shard_map/ppermute | solution.py:806
  82.1 3.3 %all-to-all-done.refs_0_ = f32[8,24,128]{2,1,0:T(8,128)S(1)} async-done(((f32[8,24,128]{2,1,0:T(8,128)}), f32[8,24,128]{2,1,0:T(8,128)S(1)}, u32[]{:S(2)}, u32[]{:S(2)}) %all-to-all-start) | async-done | bytes 98336 | tf_op jit(solution)/shard_map/all_to_all | solution.py:975
  85.3 0.7 collective-permute-done.23.refs_2_
  86.1 0.3 collective-permute-start.26
  86.4 1.1 %collective-permute-start.25 = (bf16[224,128]{1,0:T(8,128)(2,1)S(1)}, bf16[224,128]{1,0:T(8,128)(2,1)S(1)}, u32[]{:S(2)}, u32[]{:S(2)}) collective-permute-start(bf16[224,128]{1,0:T(8,128)(2,1)S(1)} %last_sums.1.refs_0_), channel_id=1, source_target_pairs={{0,2},{1,3},{2,0},{3,1},{4,6},{5,7},{6,4},{7,5},{8,10},{9,11},{10,... | collective-permute-start | bytes 172040 | tf_op jit(solution)/shard_map/ppermute | solution.py:806
  87.5 0.5 collective-permute-start.24
  88.0 1.8 %layer_norm_grad.1 = bf16[2,256,512]{2,1,0:T(8,128)(2,1)} custom-call(bf16[2,256,128]{2,1,0:T(8,128)(2,1)S(1)} %get-tuple-element.134.refs_0_, bf16[2,256,128]{2,1,0:T(8,128)(2,1)S(1)} %collective-permute-done.18.refs_1_, bf16[2,256,128]{2,1,0:T(8,128)(2,1)S(1)} %collective-permute-done.19.refs_2_, bf16[2,256,128]{2,1,0:T(8,128)(2,1)S(1)} %collective-permute-done.20.refs_3_, ...), custom_call_target="tpu_custom_call" | custom-call | bytes 1000 | tf_op jit(solution)/shard_map/layer_norm_grad/pallas_call | solution.py:53
  89.8 0.5 collective-permute-done.26.refs_3_
  90.3 1.0 %collective-permute-done.25.refs_2_ = bf16[224,128]{1,0:T(8,128)(2,1)S(1)} collective-permute-done((bf16[224,128]{1,0:T(8,128)(2,1)S(1)}, bf16[224,128]{1,0:T(8,128)(2,1)S(1)}, u32[]{:S(2)}, u32[]{:S(2)}) %collective-permute-start.25) | collective-permute-done | bytes 57376 | tf_op jit(solution)/shard_map/ppermute | solution.py:806
  91.3 0.8 last.1
  (42 shorter events, 0.2 us)
Async XLA Ops:
  0.6 6.0 %copy-start.2 = (bf16[2,256,512]{2,1,0:T(8,128)(2,1)S(1)}, bf16[2,256,512]{2,1,0:T(8,128)(2,1)}, u32[]{:S(2)}) copy-start(bf16[2,256,512]{2,1,0:T(8,128)(2,1)} %refs_4_.6) | copy-start | bytes 1572868
  2.5 6.0 %copy-start.4 = (f32[1,24,128]{2,1,0:T(8,128)S(1)}, f32[1,24,128]{2,1,0:T(8,128)}, u32[]{:S(2)}) copy-start(f32[1,24,128]{2,1,0:T(8,128)} %pack.1.refs_0_) | copy-start | bytes 36868
  2.5 7.9 %copy-start.6 = (bf16[512,128]{1,0:T(8,128)(2,1)S(1)}, bf16[512,128]{1,0:T(8,128)(2,1)}, u32[]{:S(2)}) copy-start(bf16[512,128]{1,0:T(8,128)(2,1)} %param.23) | copy-start | bytes 393220
  2.5 14.7 %copy-start = (bf16[256,1536]{1,0:T(8,128)(2,1)S(1)}, bf16[256,1536]{1,0:T(8,128)(2,1)}, u32[]{:S(2)}) copy-start(bf16[256,1536]{1,0:T(8,128)(2,1)} %constant.5.clone.refs_5_.refs_8_.refs_7_.refs_11_.refs_14_.refs_10_) | copy-start | bytes 2359300
  2.5 14.7 %copy-start.1 = (bf16[512,768]{1,0:T(8,128)(2,1)S(1)}, bf16[512,768]{1,0:T(8,128)(2,1)}, u32[]{:S(2)}) copy-start(bf16[512,768]{1,0:T(8,128)(2,1)} %constant.4.clone.refs_4_.refs_7_.refs_6_.refs_10_.refs_13_.refs_9_) | copy-start | bytes 2359300
  2.5 14.7 %copy-start.3 = (bf16[2,256,512]{2,1,0:T(8,128)(2,1)S(1)}, bf16[2,256,512]{2,1,0:T(8,128)(2,1)}, u32[]{:S(2)}) copy-start(bf16[2,256,512]{2,1,0:T(8,128)(2,1)} %refs_5_.6) | copy-start | bytes 1572868
  2.5 23.4 %copy-start.5 = (s32[2,4]{1,0:T(2,128)S(1)}, s32[2,4]{1,0:T(2,128)}, u32[]{:S(2)}) copy-start(s32[2,4]{1,0:T(2,128)} %refs_5_.5) | copy-start | bytes 100
  2.5 6.0 %collective-permute-start.3 = (f32[1,24,128]{2,1,0:T(8,128)}, f32[1,24,128]{2,1,0:T(8,128)S(1)}, u32[]{:S(2)}, u32[]{:S(2)}) collective-permute-start(f32[1,24,128]{2,1,0:T(8,128)} %pack.1.refs_0_), channel_id=1, source_target_pairs={{0,16},{4,20},{8,24},{12,28},{16,0},{20,4},{24,8},{28,12},{1,17},{... | collective-permute-start | bytes 36872 | tf_op jit(solution)/shard_map/ppermute | solution.py:806
  7.9 5.2 %collective-permute-start = (bf16[2,272,128]{2,1,0:T(8,128)(2,1)S(1)}, bf16[2,272,128]{2,1,0:T(8,128)(2,1)S(1)}, u32[]{:S(2)}, u32[]{:S(2)}) collective-permute-start(bf16[2,272,128]{2,1,0:T(8,128)(2,1)S(1)} %get-tuple-element.85), channel_id=1, source_target_pairs={{0,1},{1,0},{2,3},{3,2},{4,5},{5,4},{6,7},{7,6},{8,9},{9,8},{10,11... | collective-permute-start | bytes 417800 | tf_op jit(solution)/shard_map/ppermute | solution.py:806
  8.5 4.5 %collective-permute-start.4 = (f32[2,24,128]{2,1,0:T(8,128)S(1)}, f32[2,24,128]{2,1,0:T(8,128)S(1)}, u32[]{:S(2)}, u32[]{:S(2)}) collective-permute-start(f32[2,24,128]{2,1,0:T(8,128)S(1)} %pad_maximum_fusion.3), channel_id=1, source_target_pairs={{0,8},{4,12},{8,0},{12,4},{16,24},{20,28},{24,16},{28,20},{1,9},{5... | collective-permute-start | bytes 73736 | tf_op jit(solution)/shard_map/ppermute | solution.py:806
  10.4 12.4 %collective-permute-start.6 = (bf16[1,512,128]{2,1,0:T(8,128)(2,1)S(1)}, bf16[1,512,128]{2,1,0:T(8,128)(2,1)S(1)}, u32[]{:S(2)}, u32[]{:S(2)}) collective-permute-start(bf16[1,512,128]{2,1,0:T(8,128)(2,1)S(1)} %bitcast.17), channel_id=1, source_target_pairs={{0,16},{4,20},{8,24},{12,28},{16,0},{20,4},{24,8},{28,12},{1,17},{... | collective-permute-start | bytes 393224 | tf_op jit(solution)/shard_map/ppermute | solution.py:806
  13.0 4.2 %collective-permute-start.5 = (f32[4,24,128]{2,1,0:T(8,128)S(1)}, f32[4,24,128]{2,1,0:T(8,128)S(1)}, u32[]{:S(2)}, u32[]{:S(2)}) collective-permute-start(f32[4,24,128]{2,1,0:T(8,128)S(1)} %pad_maximum_fusion.2), channel_id=1, source_target_pairs={{0,4},{4,0},{8,12},{12,8},{16,20},{20,16},{24,28},{28,24},{1,5},{5... | collective-permute-start | bytes 147464 | tf_op jit(solution)/shard_map/ppermute | solution.py:806
  14.6 11.3 %collective-permute-start.1 = (bf16[2,272,128]{2,1,0:T(8,128)(2,1)S(1)}, bf16[2,272,128]{2,1,0:T(8,128)(2,1)S(1)}, u32[]{:S(2)}, u32[]{:S(2)}) collective-permute-start(bf16[2,272,128]{2,1,0:T(8,128)(2,1)S(1)} %get-tuple-element.86), channel_id=1, source_target_pairs={{0,2},{1,3},{2,0},{3,1},{4,6},{5,7},{6,4},{7,5},{8,10},{9,11},{10,... | collective-permute-start | bytes 417800 | tf_op jit(solution)/shard_map/ppermute | solution.py:806
  16.1 9.8 %collective-permute-start.2 = (bf16[2,272,128]{2,1,0:T(8,128)(2,1)S(1)}, bf16[2,272,128]{2,1,0:T(8,128)(2,1)S(1)}, u32[]{:S(2)}, u32[]{:S(2)}) collective-permute-start(bf16[2,272,128]{2,1,0:T(8,128)(2,1)S(1)} %get-tuple-element.87), channel_id=1, source_target_pairs={{0,3},{1,2},{2,1},{3,0},{4,7},{5,6},{6,5},{7,4},{8,11},{9,10},{10,... | collective-permute-start | bytes 417800 | tf_op jit(solution)/shard_map/ppermute | solution.py:806
  22.9 10.0 %collective-permute-start.8 = (bf16[2,512,128]{2,1,0:T(8,128)(2,1)S(1)}, bf16[2,512,128]{2,1,0:T(8,128)(2,1)S(1)}, u32[]{:S(2)}, u32[]{:S(2)}) collective-permute-start(bf16[2,512,128]{2,1,0:T(8,128)(2,1)S(1)} %pad_maximum_fusion.refs_1_), channel_id=1, source_target_pairs={{0,4},{4,0},{8,12},{12,8},{16,20},{20,16},{24,28},{28,24},{1,5},{5... | collective-permute-start | bytes 786440 | tf_op jit(solution)/shard_map/ppermute | solution.py:806
  24.5 8.4 %collective-permute-start.7 = (bf16[2,512,128]{2,1,0:T(8,128)(2,1)S(1)}, bf16[2,512,128]{2,1,0:T(8,128)(2,1)S(1)}, u32[]{:S(2)}, u32[]{:S(2)}) collective-permute-start(bf16[2,512,128]{2,1,0:T(8,128)(2,1)S(1)} %pad_maximum_fusion.refs_1_), channel_id=1, source_target_pairs={{0,8},{4,12},{8,0},{12,4},{16,24},{20,28},{24,16},{28,20},{1,9},{5... | collective-permute-start | bytes 786440 | tf_op jit(solution)/shard_map/ppermute | solution.py:806
  32.9 6.9 %collective-permute-start.12 = (bf16[2,512,128]{2,1,0:T(8,128)(2,1)S(1)}, bf16[2,512,128]{2,1,0:T(8,128)(2,1)S(1)}, u32[]{:S(2)}, u32[]{:S(2)}) collective-permute-start(bf16[2,512,128]{2,1,0:T(8,128)(2,1)S(1)} %collective-permute-done.7.refs_2_), channel_id=1, source_target_pairs={{0,4},{4,0},{8,12},{12,8},{16,20},{20,16},{24,28},{28,24},{1,5},{5... | collective-permute-start | bytes 786440 | tf_op jit(solution)/shard_map/ppermute | solution.py:806
  33.4 1.9 %collective-permute-start.9 = (bf16[2,256,128]{2,1,0:T(8,128)(2,1)S(1)}, bf16[2,256,128]{2,1,0:T(8,128)(2,1)S(1)}, u32[]{:S(2)}, u32[]{:S(2)}) collective-permute-start(bf16[2,256,128]{2,1,0:T(8,128)(2,1)S(1)} %get-tuple-element.102), channel_id=1, source_target_pairs={{0,1},{1,0},{2,3},{3,2},{4,5},{5,4},{6,7},{7,6},{8,9},{9,8},{10,11... | collective-permute-start | bytes 393224 | tf_op jit(solution)/shard_map/ppermute | solution.py:806
  33.5 6.3 %collective-permute-start.10 = (bf16[2,256,128]{2,1,0:T(8,128)(2,1)S(1)}, bf16[2,256,128]{2,1,0:T(8,128)(2,1)S(1)}, u32[]{:S(2)}, u32[]{:S(2)}) collective-permute-start(bf16[2,256,128]{2,1,0:T(8,128)(2,1)S(1)} %get-tuple-element.104), channel_id=1, source_target_pairs={{0,2},{1,3},{2,0},{3,1},{4,6},{5,7},{6,4},{7,5},{8,10},{9,11},{10,... | collective-permute-start | bytes 393224 | tf_op jit(solution)/shard_map/ppermute | solution.py:806
  34.9 6.8 %collective-permute-start.11 = (bf16[2,256,128]{2,1,0:T(8,128)(2,1)S(1)}, bf16[2,256,128]{2,1,0:T(8,128)(2,1)S(1)}, u32[]{:S(2)}, u32[]{:S(2)}) collective-permute-start(bf16[2,256,128]{2,1,0:T(8,128)(2,1)S(1)} %get-tuple-element.109), channel_id=1, source_target_pairs={{0,3},{1,2},{2,1},{3,0},{4,7},{5,6},{6,5},{7,4},{8,11},{9,10},{10,... | collective-permute-start | bytes 393224 | tf_op jit(solution)/shard_map/ppermute | solution.py:806
  46.7 2.4 %collective-permute-start.15 = (bf16[2,128,1024]{2,1,0:T(8,128)(2,1)S(1)}, bf16[2,128,1024]{2,1,0:T(8,128)(2,1)S(1)}, u32[]{:S(2)}, u32[]{:S(2)}) collective-permute-start(bf16[2,128,1024]{2,1,0:T(8,128)(2,1)S(1)} %get-tuple-element.120), channel_id=1, source_target_pairs={{0,1},{1,0},{2,3},{3,2},{4,5},{5,4},{6,7},{7,6},{8,9},{9,8},{10,11... | collective-permute-start | bytes 1572872 | tf_op jit(solution)/shard_map/ppermute | solution.py:806
  47.0 6.3 %collective-permute-start.14 = (bf16[2,256,128]{2,1,0:T(8,128)(2,1)S(1)}, bf16[2,256,128]{2,1,0:T(8,128)(2,1)S(1)}, u32[]{:S(2)}, u32[]{:S(2)}) collective-permute-start(bf16[2,256,128]{2,1,0:T(8,128)(2,1)S(1)} %get-tuple-element.118), channel_id=1, source_target_pairs={{0,2},{1,3},{2,0},{3,1},{4,6},{5,7},{6,4},{7,5},{8,10},{9,11},{10,... | collective-permute-start | bytes 393224 | tf_op jit(solution)/shard_map/ppermute | solution.py:806
  48.5 4.8 %collective-permute-start.13 = (bf16[2,256,128]{2,1,0:T(8,128)(2,1)S(1)}, bf16[2,256,128]{2,1,0:T(8,128)(2,1)S(1)}, u32[]{:S(2)}, u32[]{:S(2)}) collective-permute-start(bf16[2,256,128]{2,1,0:T(8,128)(2,1)S(1)} %get-tuple-element.117), channel_id=1, source_target_pairs={{0,1},{1,0},{2,3},{3,2},{4,5},{5,4},{6,7},{7,6},{8,9},{9,8},{10,11... | collective-permute-start | bytes 393224 | tf_op jit(solution)/shard_map/ppermute | solution.py:806
  48.5 6.7 %collective-permute-start.16 = (bf16[2,256,128]{2,1,0:T(8,128)(2,1)S(1)}, bf16[2,256,128]{2,1,0:T(8,128)(2,1)S(1)}, u32[]{:S(2)}, u32[]{:S(2)}) collective-permute-start(bf16[2,256,128]{2,1,0:T(8,128)(2,1)S(1)} %get-tuple-element.123), channel_id=1, source_target_pairs={{0,3},{1,2},{2,1},{3,0},{4,7},{5,6},{6,5},{7,4},{8,11},{9,10},{10,... | collective-permute-start | bytes 393224 | tf_op jit(solution)/shard_map/ppermute | solution.py:806
  49.2 12.1 %collective-permute-start.17 = (bf16[1,128,1024]{2,1,0:T(8,128)(2,1)S(1)}, bf16[1,128,1024]{2,1,0:T(8,128)(2,1)S(1)}, u32[]{:S(2)}, u32[]{:S(2)}) collective-permute-start(bf16[1,128,1024]{2,1,0:T(8,128)(2,1)S(1)} %get-tuple-element.121), channel_id=1, source_target_pairs={{0,2},{1,3},{2,0},{3,1},{4,6},{5,7},{6,4},{7,5},{8,10},{9,11},{10,... | collective-permute-start | bytes 786440 | tf_op jit(solution)/shard_map/ppermute | solution.py:806
  61.4 10.4 %collective-permute-start.21 = (f32[4,128,128]{2,1,0:T(8,128)S(1)}, f32[4,128,128]{2,1,0:T(8,128)S(1)}, u32[]{:S(2)}, u32[]{:S(2)}) collective-permute-start(f32[4,128,128]{2,1,0:T(8,128)S(1)} %get-tuple-element.126), channel_id=1, source_target_pairs={{0,4},{4,0},{8,12},{12,8},{16,20},{20,16},{24,28},{28,24},{1,5},{5... | collective-permute-start | bytes 786440 | tf_op jit(solution)/shard_map/ppermute | solution.py:806
  71.9 6.0 %collective-permute-start.22 = (f32[2,128,128]{2,1,0:T(8,128)S(1)}, f32[2,128,128]{2,1,0:T(8,128)S(1)}, u32[]{:S(2)}, u32[]{:S(2)}) collective-permute-start(f32[2,128,128]{2,1,0:T(8,128)S(1)} %get-tuple-element.143), channel_id=1, source_target_pairs={{0,8},{4,12},{8,0},{12,4},{16,24},{20,28},{24,16},{28,20},{1,9},{5... | collective-permute-start | bytes 393224 | tf_op jit(solution)/shard_map/ppermute | solution.py:806
  72.6 12.8 %all-to-all-start = ((f32[8,24,128]{2,1,0:T(8,128)}), f32[8,24,128]{2,1,0:T(8,128)S(1)}, u32[]{:S(2)}, u32[]{:S(2)}) async-start(f32[8,24,128]{2,1,0:T(8,128)} %state_grad.1), calls=%async_computation | async-start | bytes 196608 | tf_op jit(solution)/shard_map/all_to_all | solution.py:975
  77.3 10.2 %collective-permute-start.18 = (bf16[2,256,128]{2,1,0:T(8,128)(2,1)S(1)}, bf16[2,256,128]{2,1,0:T(8,128)(2,1)S(1)}, u32[]{:S(2)}, u32[]{:S(2)}) collective-permute-start(bf16[2,256,128]{2,1,0:T(8,128)(2,1)S(1)} %get-tuple-element.135), channel_id=1, source_target_pairs={{0,1},{1,0},{2,3},{3,2},{4,5},{5,4},{6,7},{7,6},{8,9},{9,8},{10,11... | collective-permute-start | bytes 393224 | tf_op jit(solution)/shard_map/ppermute | solution.py:806
  77.9 8.2 %collective-permute-start.23 = (f32[1,128,128]{2,1,0:T(8,128)S(1)}, f32[1,128,128]{2,1,0:T(8,128)S(1)}, u32[]{:S(2)}, u32[]{:S(2)}) collective-permute-start(f32[1,128,128]{2,1,0:T(8,128)S(1)} %get-tuple-element.145), channel_id=1, source_target_pairs={{0,16},{4,20},{8,24},{12,28},{16,0},{20,4},{24,8},{28,12},{1,17},{... | collective-permute-start | bytes 196616 | tf_op jit(solution)/shard_map/ppermute | solution.py:806
  80.5 7.5 %collective-permute-start.19 = (bf16[2,256,128]{2,1,0:T(8,128)(2,1)S(1)}, bf16[2,256,128]{2,1,0:T(8,128)(2,1)S(1)}, u32[]{:S(2)}, u32[]{:S(2)}) collective-permute-start(bf16[2,256,128]{2,1,0:T(8,128)(2,1)S(1)} %get-tuple-element.136), channel_id=1, source_target_pairs={{0,2},{1,3},{2,0},{3,1},{4,6},{5,7},{6,4},{7,5},{8,10},{9,11},{10,... | collective-permute-start | bytes 393224 | tf_op jit(solution)/shard_map/ppermute | solution.py:806
  82.0 6.0 %collective-permute-start.20 = (bf16[2,256,128]{2,1,0:T(8,128)(2,1)S(1)}, bf16[2,256,128]{2,1,0:T(8,128)(2,1)S(1)}, u32[]{:S(2)}, u32[]{:S(2)}) collective-permute-start(bf16[2,256,128]{2,1,0:T(8,128)(2,1)S(1)} %get-tuple-element.137), channel_id=1, source_target_pairs={{0,3},{1,2},{2,1},{3,0},{4,7},{5,6},{6,5},{7,4},{8,11},{9,10},{10,... | collective-permute-start | bytes 393224 | tf_op jit(solution)/shard_map/ppermute | solution.py:806
  86.1 4.3 %collective-permute-start.26 = (bf16[224,128]{1,0:T(8,128)(2,1)S(1)}, bf16[224,128]{1,0:T(8,128)(2,1)S(1)}, u32[]{:S(2)}, u32[]{:S(2)}) collective-permute-start(bf16[224,128]{1,0:T(8,128)(2,1)S(1)} %last_sums.1.refs_0_), channel_id=1, source_target_pairs={{0,3},{1,2},{2,1},{3,0},{4,7},{5,6},{6,5},{7,4},{8,11},{9,10},{10,... | collective-permute-start | bytes 172040 | tf_op jit(solution)/shard_map/ppermute | solution.py:806
  86.4 4.9 %collective-permute-start.25 = (bf16[224,128]{1,0:T(8,128)(2,1)S(1)}, bf16[224,128]{1,0:T(8,128)(2,1)S(1)}, u32[]{:S(2)}, u32[]{:S(2)}) collective-permute-start(bf16[224,128]{1,0:T(8,128)(2,1)S(1)} %last_sums.1.refs_0_), channel_id=1, source_target_pairs={{0,2},{1,3},{2,0},{3,1},{4,6},{5,7},{6,4},{7,5},{8,10},{9,11},{10,... | collective-permute-start | bytes 172040 | tf_op jit(solution)/shard_map/ppermute | solution.py:806
  87.5 3.8 %collective-permute-start.24 = (bf16[224,128]{1,0:T(8,128)(2,1)S(1)}, bf16[224,128]{1,0:T(8,128)(2,1)S(1)}, u32[]{:S(2)}, u32[]{:S(2)}) collective-permute-start(bf16[224,128]{1,0:T(8,128)(2,1)S(1)} %last_sums.1.refs_0_), channel_id=1, source_target_pairs={{0,1},{1,0},{2,3},{3,2},{4,5},{5,4},{6,7},{7,6},{8,9},{9,8},{10,11... | collective-permute-start | bytes 172040 | tf_op jit(solution)/shard_map/ppermute | solution.py:806

commit v8 on v7

--- a/solution.py
+++ b/solution.py
@@ -72,8 +72,8 @@
     step = jnp.exp(step_log)
     a = -jnp.exp(rate_log) * step
     b = freq * step
-    half = jnp.sin(0.5 * b)
-    cos_b, sin_b, mag = jnp.cos(b), jnp.sin(b), jnp.exp(a)
+    half, other = jnp.sin(0.5 * b), jnp.cos(0.5 * b)
+    cos_b, sin_b, mag = 1.0 - 2.0 * half * half, 2.0 * half * other, jnp.exp(a)
     one_re = 2.0 * half * half - small_expm1(a) * cos_b
     one_im = -mag * sin_b
     far = jnp.exp(length * a)
@@ -229,7 +229,7 @@
                 one[0] = cmul(*one[0], *one[1][COARSE])
         return 0
 
-    lax.fori_loop(0, nstate // 2, pair, 0)
+    lax.fori_loop(0, nstate // 2, pair, 0, unroll=2)
     k_scr[0:1] += vec_ref[1:2]
     parts = length // block
     for p in range(parts):
@@ -967,7 +967,7 @@
         partial(state_grad_kernel, sub, length), shape((ndp, rows, LANES)), [VM] * 8,
         scratch=[pltpu.VMEM((length, wide), f32), pltpu.VMEM((4, nstate, wide), f32), pltpu.VMEM((n_w, wide), f32),
                  pltpu.VMEM((6 * block, nseq * wide), bf16)],
-        name="state_grad", mib=10, us=10,
+        name="state_grad", mib=10, us=5,
     )(w_all, terms, pows, far, dkh, d_norm, d_lin_bias, ft_table)
     small, *g_own = tie(small, *g_own)
     if staged:

time: 92.4 us -> 92.3 us (level)
  no operation moved by 1% of the time
where the time goes in v8:
time: 92.3 us; the launch traced here: 92 us
  Pallas kernels  39.1 us (42%)
  starting transfers between devices  34.4 us (37%)
  waiting for transfers between devices  17.6 us (19%)
    pallas_call x16, Pallas kernels, call(): return lambda *args: kernel(*args, *keep)  39.1 us
    ppermute x27, starting transfers between devices, swap(): lax.ppermute(v, axis, [(i, i ^ by) for i in range(n)])  29.6 us
    ppermute x27, waiting for transfers between devices, swap(): lax.ppermute(v, axis, [(i, i ^ by) for i in range(n)])  14.3 us
    all_to_all x1, starting transfers between devices, on_device(): small = lax.all_to_all(small, 'dp', 0, 0, tiled=True)  4.73 us
    all_to_all x1, waiting for transfers between devices, on_device(): small = lax.all_to_all(small, 'dp', 0, 0, tiled=True)  3.28 us
  transfers between devices with their start and end apart: 28, of which 11 were waited for; matrix products, arithmetic and copies ran while one was open for 0% of the time, Pallas kernels for 34%

profile of v8, /device:TPU:0, one launch (start us, length us, event | category | flops | bytes accessed | tf_op | source)
XLA Modules:
  0.0 92.0 jit_solution(7154369551039777293)
XLA Ops:
  0.7 1.8 %pack.1.refs_0_ = f32[1,24,128]{2,1,0:T(8,128)} custom-call(f32[128,64]{1,0:T(8,128)} %bitcast.19, f32[1,64]{1,0:T(1,128)} %bitcast.20, f32[1,64]{1,0:T(1,128)} %bitcast.21, f32[1,64]{1,0:T(1,128)} %bitcast.22, f32[1,64]{1,0:T(1,128)} %bitcast.23, f32[1,8]{1,0:T(1,128)} %bitcast.24, f32[1,8]{1,0:T(1,128)} %bitcast.25, f32[1,128]{1,0:T(1,128)} %bitcast.26), custom_call_target="tpu_custom_call" | custom-call | flops 2300000000 | bytes 1000 | tf_op jit(solution)/shard_map/pack/pallas_call | solution.py:53
  2.5 0.0 copy-start.1
  2.5 4.1 %collective-permute-start.3 = (f32[1,24,128]{2,1,0:T(8,128)}, f32[1,24,128]{2,1,0:T(8,128)S(1)}, u32[]{:S(2)}, u32[]{:S(2)}) collective-permute-start(f32[1,24,128]{2,1,0:T(8,128)} %pack.1.refs_0_), channel_id=1, source_target_pairs={{0,16},{4,20},{8,24},{12,28},{16,0},{20,4},{24,8},{28,12},{1,17},{... | collective-permute-start | bytes 36872 | tf_op jit(solution)/shard_map/ppermute | solution.py:806
  6.6 1.2 %spread.1 = (bf16[2,272,128]{2,1,0:T(8,128)(2,1)S(1)}, bf16[2,272,128]{2,1,0:T(8,128)(2,1)S(1)}, bf16[2,272,128]{2,1,0:T(8,128)(2,1)S(1)}, bf16[2,272,128]{2,1,0:T(8,128)(2,1)S(1)}) custom-call(bf16[2,256,512]{2,1,0:T(8,128)(2,1)S(1)} %copy-done.2), custom_call_target="tpu_custom_call" | custom-call | flops 2300000000 | bytes 1000 | tf_op jit(solution)/shard_map/spread/pallas_call | solution.py:53
  7.9 0.1 collective-permute-start
  8.0 0.5 collective-permute-done.3.refs_1_
  8.5 1.9 %collective-permute-start.4 = (f32[2,24,128]{2,1,0:T(8,128)S(1)}, f32[2,24,128]{2,1,0:T(8,128)S(1)}, u32[]{:S(2)}, u32[]{:S(2)}) collective-permute-start(f32[2,24,128]{2,1,0:T(8,128)S(1)} %pad_maximum_fusion.3), channel_id=1, source_target_pairs={{0,8},{4,12},{8,0},{12,4},{16,24},{20,28},{24,16},{28,20},{1,9},{5... | collective-permute-start | bytes 73736 | tf_op jit(solution)/shard_map/ppermute | solution.py:806
  10.4 2.6 %collective-permute-start.6 = (bf16[1,512,128]{2,1,0:T(8,128)(2,1)S(1)}, bf16[1,512,128]{2,1,0:T(8,128)(2,1)S(1)}, u32[]{:S(2)}, u32[]{:S(2)}) collective-permute-start(bf16[1,512,128]{2,1,0:T(8,128)(2,1)S(1)} %bitcast.17), channel_id=1, source_target_pairs={{0,16},{4,20},{8,24},{12,28},{16,0},{20,4},{24,8},{28,12},{1,17},{... | collective-permute-start | bytes 393224 | tf_op jit(solution)/shard_map/ppermute | solution.py:806
  13.0 1.6 %collective-permute-start.5 = (f32[4,24,128]{2,1,0:T(8,128)S(1)}, f32[4,24,128]{2,1,0:T(8,128)S(1)}, u32[]{:S(2)}, u32[]{:S(2)}) collective-permute-start(f32[4,24,128]{2,1,0:T(8,128)S(1)} %pad_maximum_fusion.2), channel_id=1, source_target_pairs={{0,4},{4,0},{8,12},{12,8},{16,20},{20,16},{24,28},{28,24},{1,5},{5... | collective-permute-start | bytes 147464 | tf_op jit(solution)/shard_map/ppermute | solution.py:806
  14.6 1.5 %collective-permute-start.1 = (bf16[2,272,128]{2,1,0:T(8,128)(2,1)S(1)}, bf16[2,272,128]{2,1,0:T(8,128)(2,1)S(1)}, u32[]{:S(2)}, u32[]{:S(2)}) collective-permute-start(bf16[2,272,128]{2,1,0:T(8,128)(2,1)S(1)} %get-tuple-element.86), channel_id=1, source_target_pairs={{0,2},{1,3},{2,0},{3,1},{4,6},{5,7},{6,4},{7,5},{8,10},{9,11},{10,... | collective-permute-start | bytes 417800 | tf_op jit(solution)/shard_map/ppermute | solution.py:806
  16.1 1.1 %collective-permute-done.5.refs_3_ = f32[4,24,128]{2,1,0:T(8,128)S(1)} collective-permute-done((f32[4,24,128]{2,1,0:T(8,128)S(1)}, f32[4,24,128]{2,1,0:T(8,128)S(1)}, u32[]{:S(2)}, u32[]{:S(2)}) %collective-permute-start.5) | collective-permute-done | bytes 49184 | tf_op jit(solution)/shard_map/ppermute | solution.py:806
  17.2 5.5 %lag_kernel.1 = (f32[4,512,128]{2,1,0:T(8,128)S(1)}, f32[8,128]{1,0:T(8,128)S(1)}, f32[128,128]{1,0:T(8,128)S(1)}, f32[13,64,128]{2,1,0:T(8,128)S(1)}, f32[26,64,128]{2,1,0:T(8,128)S(1)}) custom-call(f32[1,24,128]{2,1,0:T(8,128)S(1)} %copy-done.4, f32[1,24,128]{2,1,0:T(8,128)S(1)} %collective-permute-done.3.refs_1_, ...), custom_call_target="tpu_custom_call" | custom-call | bytes 1000 | tf_op jit(solution)/shard_map/lag_kernel/pallas_call | solution.py:53
  22.7 1.6 %collective-permute-start.8 = (bf16[2,512,128]{2,1,0:T(8,128)(2,1)S(1)}, bf16[2,512,128]{2,1,0:T(8,128)(2,1)S(1)}, u32[]{:S(2)}, u32[]{:S(2)}) collective-permute-start(bf16[2,512,128]{2,1,0:T(8,128)(2,1)S(1)} %pad_maximum_fusion.refs_1_), channel_id=1, source_target_pairs={{0,4},{4,0},{8,12},{12,8},{16,20},{20,16},{24,28},{28,24},{1,5},{5... | collective-permute-start | bytes 786440 | tf_op jit(solution)/shard_map/ppermute | solution.py:806
  24.3 1.4 %collective-permute-start.7 = (bf16[2,512,128]{2,1,0:T(8,128)(2,1)S(1)}, bf16[2,512,128]{2,1,0:T(8,128)(2,1)S(1)}, u32[]{:S(2)}, u32[]{:S(2)}) collective-permute-start(bf16[2,512,128]{2,1,0:T(8,128)(2,1)S(1)} %pad_maximum_fusion.refs_1_), channel_id=1, source_target_pairs={{0,8},{4,12},{8,0},{12,4},{16,24},{20,28},{24,16},{28,20},{1,9},{5... | collective-permute-start | bytes 786440 | tf_op jit(solution)/shard_map/ppermute | solution.py:806
  25.8 6.9 %doc_conv.1 = (bf16[2,256,128]{2,1,0:T(8,128)(2,1)S(1)}, bf16[2,256,128]{2,1,0:T(8,128)(2,1)S(1)}, bf16[2,256,128]{2,1,0:T(8,128)(2,1)S(1)}, bf16[2,256,128]{2,1...) custom-call(bf16[2,272,128]{2,1,0:T(8,128)(2,1)S(1)} %get-tuple-element.84.refs_0_, ...), custom_call_target="tpu_custom_call" | custom-call | flops 8049999872 | bytes 1000 | tf_op jit(solution)/shard_map/doc_conv/pallas_call | solution.py:53
  32.7 0.6 collective-permute-start.12
  33.3 1.5 %collective-permute-start.10 = (bf16[2,256,128]{2,1,0:T(8,128)(2,1)S(1)}, bf16[2,256,128]{2,1,0:T(8,128)(2,1)S(1)}, u32[]{:S(2)}, u32[]{:S(2)}) collective-permute-start(bf16[2,256,128]{2,1,0:T(8,128)(2,1)S(1)} %get-tuple-element.104), channel_id=1, source_target_pairs={{0,2},{1,3},{2,0},{3,1},{4,6},{5,7},{6,4},{7,5},{8,10},{9,11},{10,... | collective-permute-start | bytes 393224 | tf_op jit(solution)/shard_map/ppermute | solution.py:806
  34.8 0.4 collective-permute-start.11
  35.2 0.5 state_powers.1.refs_14_.refs_17_.refs_11_.refs_5_.refs_3_
  35.7 3.9 %collective-permute-done.10.refs_2_ = bf16[2,256,128]{2,1,0:T(8,128)(2,1)S(1)} collective-permute-done((bf16[2,256,128]{2,1,0:T(8,128)(2,1)S(1)}, bf16[2,256,128]{2,1,0:T(8,128)(2,1)S(1)}, u32[]{:S(2)}, u32[]{:S(2)}) %collective-permute-start.10) | collective-permute-done | bytes 131104 | tf_op jit(solution)/shard_map/ppermute | solution.py:806
  39.6 0.3 linear_rows.1
  39.9 1.7 %collective-permute-done.11.refs_3_ = bf16[2,256,128]{2,1,0:T(8,128)(2,1)S(1)} collective-permute-done((bf16[2,256,128]{2,1,0:T(8,128)(2,1)S(1)}, bf16[2,256,128]{2,1,0:T(8,128)(2,1)S(1)}, u32[]{:S(2)}, u32[]{:S(2)}) %collective-permute-start.11) | collective-permute-done | bytes 131104 | tf_op jit(solution)/shard_map/ppermute | solution.py:806
  41.6 4.9 %gated_linear.1 = (bf16[2,256,512]{2,1,0:T(8,128)(2,1)}, f32[1,1024]{1,0:T(1,128)S(1)}, bf16[2,256,128]{2,1,0:T(8,128)(2,1)S(1)}, bf16[2,256,128]{2,1,0:T(8,128)...) custom-call(bf16[2,256,128]{2,1,0:T(8,128)(2,1)S(1)} %get-tuple-elem, ...), custom_call_target="tpu_custom_call" | custom-call | flops 5750000128 | bytes 1000 | tf_op jit(solution)/shard_map/gated_linear/pallas_call | solution.py:53
  46.5 0.3 collective-permute-start.15
  46.8 1.5 %collective-permute-start.14 = (bf16[2,256,128]{2,1,0:T(8,128)(2,1)S(1)}, bf16[2,256,128]{2,1,0:T(8,128)(2,1)S(1)}, u32[]{:S(2)}, u32[]{:S(2)}) collective-permute-start(bf16[2,256,128]{2,1,0:T(8,128)(2,1)S(1)} %get-tuple-element.118), channel_id=1, source_target_pairs={{0,2},{1,3},{2,0},{3,1},{4,6},{5,7},{6,4},{7,5},{8,10},{9,11},{10,... | collective-permute-start | bytes 393224 | tf_op jit(solution)/shard_map/ppermute | solution.py:806
  48.3 0.6 collective-permute-start.16
  49.0 0.1 weight_half.3
  49.1 1.6 %collective-permute-start.17 = (bf16[1,128,1024]{2,1,0:T(8,128)(2,1)S(1)}, bf16[1,128,1024]{2,1,0:T(8,128)(2,1)S(1)}, u32[]{:S(2)}, u32[]{:S(2)}) collective-permute-start(bf16[1,128,1024]{2,1,0:T(8,128)(2,1)S(1)} %get-tuple-element.121), channel_id=1, source_target_pairs={{0,2},{1,3},{2,0},{3,1},{4,6},{5,7},{6,4},{7,5},{8,10},{9,11},{10,... | collective-permute-start | bytes 786440 | tf_op jit(solution)/shard_map/ppermute | solution.py:806
  50.7 2.5 %collective-permute-done.14.refs_2_ = bf16[2,256,128]{2,1,0:T(8,128)(2,1)S(1)} collective-permute-done((bf16[2,256,128]{2,1,0:T(8,128)(2,1)S(1)}, bf16[2,256,128]{2,1,0:T(8,128)(2,1)S(1)}, u32[]{:S(2)}, u32[]{:S(2)}) %collective-permute-start.14) | collective-permute-done | bytes 131104 | tf_op jit(solution)/shard_map/ppermute | solution.py:806
  53.1 1.8 %collective-permute-done.16.refs_3_ = bf16[2,256,128]{2,1,0:T(8,128)(2,1)S(1)} collective-permute-done((bf16[2,256,128]{2,1,0:T(8,128)(2,1)S(1)}, bf16[2,256,128]{2,1,0:T(8,128)(2,1)S(1)}, u32[]{:S(2)}, u32[]{:S(2)}) %collective-permute-start.16) | collective-permute-done | bytes 131104 | tf_op jit(solution)/shard_map/ppermute | solution.py:806
  55.0 6.1 %doc_conv_grad.1 = (bf16[2,256,128]{2,1,0:T(8,128)(2,1)S(1)}, bf16[2,256,128]{2,1,0:T(8,128)(2,1)S(1)}, bf16[2,256,128]{2,1,0:T(8,128)(2,1)S(1)}, bf16[2,256,128...) custom-call(bf16[2,256,128]{2,1,0:T(8,128)(2,1)S(1)} %get-tuple-element.116.refs_0_, ...), custom_call_target="tpu_custom_call" | custom-call | flops 9200000000 | bytes 1000 | tf_op jit(solution)/shard_map/doc_conv_grad/pallas_call | solution.py:53
  61.1 0.2 weight_deal.1
  61.3 1.6 %collective-permute-start.21 = (f32[4,128,128]{2,1,0:T(8,128)S(1)}, f32[4,128,128]{2,1,0:T(8,128)S(1)}, u32[]{:S(2)}, u32[]{:S(2)}) collective-permute-start(f32[4,128,128]{2,1,0:T(8,128)S(1)} %get-tuple-element.126), channel_id=1, source_target_pairs={{0,4},{4,0},{8,12},{12,8},{16,20},{20,16},{24,28},{28,24},{1,5},{5... | collective-permute-start | bytes 786440 | tf_op jit(solution)/shard_map/ppermute | solution.py:806
  62.9 8.8 %state_grad.1 = f32[8,24,128]{2,1,0:T(8,128)} custom-call(f32[128,128]{1,0:T(8,128)S(1)} %get-tuple-element.93.refs_9_.refs_1_.refs_5_.refs_8_.refs_2_.refs_11_.refs_0_, f32[13,64,128]{2,1,0:T(8,128)S(1)} %get-tuple-element.94.refs_10_.refs_2_.refs_6_.refs_9_.refs_3_.refs_12_.refs_1_, ...), custom_call_target="tpu_custom_call" | custom-call | flops 5750000128 | bytes 1000 | tf_op jit(solution)/shard_map/state_grad/pallas_call | solution.py:53
  71.7 0.7 collective-permute-start.22
  72.4 4.7 %all-to-all-start = ((f32[8,24,128]{2,1,0:T(8,128)}), f32[8,24,128]{2,1,0:T(8,128)S(1)}, u32[]{:S(2)}, u32[]{:S(2)}) async-start(f32[8,24,128]{2,1,0:T(8,128)} %state_grad.1), calls=%async_computation | async-start | bytes 196608 | tf_op jit(solution)/shard_map/all_to_all | solution.py:975
  77.1 0.6 collective-permute-done.22.refs_1_
  77.7 2.7 %collective-permute-start.23 = (f32[1,128,128]{2,1,0:T(8,128)S(1)}, f32[1,128,128]{2,1,0:T(8,128)S(1)}, u32[]{:S(2)}, u32[]{:S(2)}) collective-permute-start(f32[1,128,128]{2,1,0:T(8,128)S(1)} %get-tuple-element.145), channel_id=1, source_target_pairs={{0,16},{4,20},{8,24},{12,28},{16,0},{20,4},{24,8},{28,12},{1,17},{... | collective-permute-start | bytes 196616 | tf_op jit(solution)/shard_map/ppermute | solution.py:806
  80.4 1.5 %collective-permute-start.19 = (bf16[2,256,128]{2,1,0:T(8,128)(2,1)S(1)}, bf16[2,256,128]{2,1,0:T(8,128)(2,1)S(1)}, u32[]{:S(2)}, u32[]{:S(2)}) collective-permute-start(bf16[2,256,128]{2,1,0:T(8,128)(2,1)S(1)} %get-tuple-element.136), channel_id=1, source_target_pairs={{0,2},{1,3},{2,0},{3,1},{4,6},{5,7},{6,4},{7,5},{8,10},{9,11},{10,... | collective-permute-start | bytes 393224 | tf_op jit(solution)/shard_map/ppermute | solution.py:806
  81.9 3.3 %all-to-all-done.refs_0_ = f32[8,24,128]{2,1,0:T(8,128)S(1)} async-done(((f32[8,24,128]{2,1,0:T(8,128)}), f32[8,24,128]{2,1,0:T(8,128)S(1)}, u32[]{:S(2)}, u32[]{:S(2)}) %all-to-all-start) | async-done | bytes 98336 | tf_op jit(solution)/shard_map/all_to_all | solution.py:975
  85.2 0.7 collective-permute-done.23.refs_2_
  85.9 0.3 collective-permute-start.26
  86.2 1.1 %collective-permute-start.25 = (bf16[224,128]{1,0:T(8,128)(2,1)S(1)}, bf16[224,128]{1,0:T(8,128)(2,1)S(1)}, u32[]{:S(2)}, u32[]{:S(2)}) collective-permute-start(bf16[224,128]{1,0:T(8,128)(2,1)S(1)} %last_sums.1.refs_0_), channel_id=1, source_target_pairs={{0,2},{1,3},{2,0},{3,1},{4,6},{5,7},{6,4},{7,5},{8,10},{9,11},{10,... | collective-permute-start | bytes 172040 | tf_op jit(solution)/shard_map/ppermute | solution.py:806
  87.4 0.5 collective-permute-start.24
  87.8 1.8 %layer_norm_grad.1 = bf16[2,256,512]{2,1,0:T(8,128)(2,1)} custom-call(bf16[2,256,128]{2,1,0:T(8,128)(2,1)S(1)} %get-tuple-element.134.refs_0_, bf16[2,256,128]{2,1,0:T(8,128)(2,1)S(1)} %collective-permute-done.18.refs_1_, bf16[2,256,128]{2,1,0:T(8,128)(2,1)S(1)} %collective-permute-done.19.refs_2_, bf16[2,256,128]{2,1,0:T(8,128)(2,1)S(1)} %collective-permute-done.20.refs_3_, ...), custom_call_target="tpu_custom_call" | custom-call | bytes 1000 | tf_op jit(solution)/shard_map/layer_norm_grad/pallas_call | solution.py:53
  89.7 0.5 collective-permute-done.26.refs_3_
  90.2 1.0 %collective-permute-done.25.refs_2_ = bf16[224,128]{1,0:T(8,128)(2,1)S(1)} collective-permute-done((bf16[224,128]{1,0:T(8,128)(2,1)S(1)}, bf16[224,128]{1,0:T(8,128)(2,1)S(1)}, u32[]{:S(2)}, u32[]{:S(2)}) %collective-permute-start.25) | collective-permute-done | bytes 57376 | tf_op jit(solution)/shard_map/ppermute | solution.py:806
  91.2 0.8 last.1
  (42 shorter events, 0.2 us)
Async XLA Ops:
  0.6 6.0 %copy-start.2 = (bf16[2,256,512]{2,1,0:T(8,128)(2,1)S(1)}, bf16[2,256,512]{2,1,0:T(8,128)(2,1)}, u32[]{:S(2)}) copy-start(bf16[2,256,512]{2,1,0:T(8,128)(2,1)} %refs_4_.6) | copy-start | bytes 1572868
  2.5 6.0 %copy-start.4 = (f32[1,24,128]{2,1,0:T(8,128)S(1)}, f32[1,24,128]{2,1,0:T(8,128)}, u32[]{:S(2)}) copy-start(f32[1,24,128]{2,1,0:T(8,128)} %pack.1.refs_0_) | copy-start | bytes 36868
  2.5 7.9 %copy-start.6 = (bf16[512,128]{1,0:T(8,128)(2,1)S(1)}, bf16[512,128]{1,0:T(8,128)(2,1)}, u32[]{:S(2)}) copy-start(bf16[512,128]{1,0:T(8,128)(2,1)} %param.23) | copy-start | bytes 393220
  2.5 14.7 %copy-start = (bf16[256,1536]{1,0:T(8,128)(2,1)S(1)}, bf16[256,1536]{1,0:T(8,128)(2,1)}, u32[]{:S(2)}) copy-start(bf16[256,1536]{1,0:T(8,128)(2,1)} %constant.5.clone.refs_5_.refs_8_.refs_7_.refs_11_.refs_14_.refs_10_) | copy-start | bytes 2359300
  2.5 14.7 %copy-start.1 = (bf16[512,768]{1,0:T(8,128)(2,1)S(1)}, bf16[512,768]{1,0:T(8,128)(2,1)}, u32[]{:S(2)}) copy-start(bf16[512,768]{1,0:T(8,128)(2,1)} %constant.4.clone.refs_4_.refs_7_.refs_6_.refs_10_.refs_13_.refs_9_) | copy-start | bytes 2359300
  2.5 14.7 %copy-start.3 = (bf16[2,256,512]{2,1,0:T(8,128)(2,1)S(1)}, bf16[2,256,512]{2,1,0:T(8,128)(2,1)}, u32[]{:S(2)}) copy-start(bf16[2,256,512]{2,1,0:T(8,128)(2,1)} %refs_5_.6) | copy-start | bytes 1572868
  2.5 23.2 %copy-start.5 = (s32[2,4]{1,0:T(2,128)S(1)}, s32[2,4]{1,0:T(2,128)}, u32[]{:S(2)}) copy-start(s32[2,4]{1,0:T(2,128)} %refs_5_.5) | copy-start | bytes 100
  2.5 6.0 %collective-permute-start.3 = (f32[1,24,128]{2,1,0:T(8,128)}, f32[1,24,128]{2,1,0:T(8,128)S(1)}, u32[]{:S(2)}, u32[]{:S(2)}) collective-permute-start(f32[1,24,128]{2,1,0:T(8,128)} %pack.1.refs_0_), channel_id=1, source_target_pairs={{0,16},{4,20},{8,24},{12,28},{16,0},{20,4},{24,8},{28,12},{1,17},{... | collective-permute-start | bytes 36872 | tf_op jit(solution)/shard_map/ppermute | solution.py:806
  7.9 5.2 %collective-permute-start = (bf16[2,272,128]{2,1,0:T(8,128)(2,1)S(1)}, bf16[2,272,128]{2,1,0:T(8,128)(2,1)S(1)}, u32[]{:S(2)}, u32[]{:S(2)}) collective-permute-start(bf16[2,272,128]{2,1,0:T(8,128)(2,1)S(1)} %get-tuple-element.85), channel_id=1, source_target_pairs={{0,1},{1,0},{2,3},{3,2},{4,5},{5,4},{6,7},{7,6},{8,9},{9,8},{10,11... | collective-permute-start | bytes 417800 | tf_op jit(solution)/shard_map/ppermute | solution.py:806
  8.5 4.5 %collective-permute-start.4 = (f32[2,24,128]{2,1,0:T(8,128)S(1)}, f32[2,24,128]{2,1,0:T(8,128)S(1)}, u32[]{:S(2)}, u32[]{:S(2)}) collective-permute-start(f32[2,24,128]{2,1,0:T(8,128)S(1)} %pad_maximum_fusion.3), channel_id=1, source_target_pairs={{0,8},{4,12},{8,0},{12,4},{16,24},{20,28},{24,16},{28,20},{1,9},{5... | collective-permute-start | bytes 73736 | tf_op jit(solution)/shard_map/ppermute | solution.py:806
  10.4 12.3 %collective-permute-start.6 = (bf16[1,512,128]{2,1,0:T(8,128)(2,1)S(1)}, bf16[1,512,128]{2,1,0:T(8,128)(2,1)S(1)}, u32[]{:S(2)}, u32[]{:S(2)}) collective-permute-start(bf16[1,512,128]{2,1,0:T(8,128)(2,1)S(1)} %bitcast.17), channel_id=1, source_target_pairs={{0,16},{4,20},{8,24},{12,28},{16,0},{20,4},{24,8},{28,12},{1,17},{... | collective-permute-start | bytes 393224 | tf_op jit(solution)/shard_map/ppermute | solution.py:806
  13.0 4.2 %collective-permute-start.5 = (f32[4,24,128]{2,1,0:T(8,128)S(1)}, f32[4,24,128]{2,1,0:T(8,128)S(1)}, u32[]{:S(2)}, u32[]{:S(2)}) collective-permute-start(f32[4,24,128]{2,1,0:T(8,128)S(1)} %pad_maximum_fusion.2), channel_id=1, source_target_pairs={{0,4},{4,0},{8,12},{12,8},{16,20},{20,16},{24,28},{28,24},{1,5},{5... | collective-permute-start | bytes 147464 | tf_op jit(solution)/shard_map/ppermute | solution.py:806
  14.6 11.1 %collective-permute-start.1 = (bf16[2,272,128]{2,1,0:T(8,128)(2,1)S(1)}, bf16[2,272,128]{2,1,0:T(8,128)(2,1)S(1)}, u32[]{:S(2)}, u32[]{:S(2)}) collective-permute-start(bf16[2,272,128]{2,1,0:T(8,128)(2,1)S(1)} %get-tuple-element.86), channel_id=1, source_target_pairs={{0,2},{1,3},{2,0},{3,1},{4,6},{5,7},{6,4},{7,5},{8,10},{9,11},{10,... | collective-permute-start | bytes 417800 | tf_op jit(solution)/shard_map/ppermute | solution.py:806
  16.1 9.6 %collective-permute-start.2 = (bf16[2,272,128]{2,1,0:T(8,128)(2,1)S(1)}, bf16[2,272,128]{2,1,0:T(8,128)(2,1)S(1)}, u32[]{:S(2)}, u32[]{:S(2)}) collective-permute-start(bf16[2,272,128]{2,1,0:T(8,128)(2,1)S(1)} %get-tuple-element.87), channel_id=1, source_target_pairs={{0,3},{1,2},{2,1},{3,0},{4,7},{5,6},{6,5},{7,4},{8,11},{9,10},{10,... | collective-permute-start | bytes 417800 | tf_op jit(solution)/shard_map/ppermute | solution.py:806
  22.7 10.0 %collective-permute-start.8 = (bf16[2,512,128]{2,1,0:T(8,128)(2,1)S(1)}, bf16[2,512,128]{2,1,0:T(8,128)(2,1)S(1)}, u32[]{:S(2)}, u32[]{:S(2)}) collective-permute-start(bf16[2,512,128]{2,1,0:T(8,128)(2,1)S(1)} %pad_maximum_fusion.refs_1_), channel_id=1, source_target_pairs={{0,4},{4,0},{8,12},{12,8},{16,20},{20,16},{24,28},{28,24},{1,5},{5... | collective-permute-start | bytes 786440 | tf_op jit(solution)/shard_map/ppermute | solution.py:806
  24.3 8.4 %collective-permute-start.7 = (bf16[2,512,128]{2,1,0:T(8,128)(2,1)S(1)}, bf16[2,512,128]{2,1,0:T(8,128)(2,1)S(1)}, u32[]{:S(2)}, u32[]{:S(2)}) collective-permute-start(bf16[2,512,128]{2,1,0:T(8,128)(2,1)S(1)} %pad_maximum_fusion.refs_1_), channel_id=1, source_target_pairs={{0,8},{4,12},{8,0},{12,4},{16,24},{20,28},{24,16},{28,20},{1,9},{5... | collective-permute-start | bytes 786440 | tf_op jit(solution)/shard_map/ppermute | solution.py:806
  32.7 6.9 %collective-permute-start.12 = (bf16[2,512,128]{2,1,0:T(8,128)(2,1)S(1)}, bf16[2,512,128]{2,1,0:T(8,128)(2,1)S(1)}, u32[]{:S(2)}, u32[]{:S(2)}) collective-permute-start(bf16[2,512,128]{2,1,0:T(8,128)(2,1)S(1)} %collective-permute-done.7.refs_2_), channel_id=1, source_target_pairs={{0,4},{4,0},{8,12},{12,8},{16,20},{20,16},{24,28},{28,24},{1,5},{5... | collective-permute-start | bytes 786440 | tf_op jit(solution)/shard_map/ppermute | solution.py:806
  33.3 1.9 %collective-permute-start.9 = (bf16[2,256,128]{2,1,0:T(8,128)(2,1)S(1)}, bf16[2,256,128]{2,1,0:T(8,128)(2,1)S(1)}, u32[]{:S(2)}, u32[]{:S(2)}) collective-permute-start(bf16[2,256,128]{2,1,0:T(8,128)(2,1)S(1)} %get-tuple-element.102), channel_id=1, source_target_pairs={{0,1},{1,0},{2,3},{3,2},{4,5},{5,4},{6,7},{7,6},{8,9},{9,8},{10,11... | collective-permute-start | bytes 393224 | tf_op jit(solution)/shard_map/ppermute | solution.py:806
  33.3 6.3 %collective-permute-start.10 = (bf16[2,256,128]{2,1,0:T(8,128)(2,1)S(1)}, bf16[2,256,128]{2,1,0:T(8,128)(2,1)S(1)}, u32[]{:S(2)}, u32[]{:S(2)}) collective-permute-start(bf16[2,256,128]{2,1,0:T(8,128)(2,1)S(1)} %get-tuple-element.104), channel_id=1, source_target_pairs={{0,2},{1,3},{2,0},{3,1},{4,6},{5,7},{6,4},{7,5},{8,10},{9,11},{10,... | collective-permute-start | bytes 393224 | tf_op jit(solution)/shard_map/ppermute | solution.py:806
  34.8 6.8 %collective-permute-start.11 = (bf16[2,256,128]{2,1,0:T(8,128)(2,1)S(1)}, bf16[2,256,128]{2,1,0:T(8,128)(2,1)S(1)}, u32[]{:S(2)}, u32[]{:S(2)}) collective-permute-start(bf16[2,256,128]{2,1,0:T(8,128)(2,1)S(1)} %get-tuple-element.109), channel_id=1, source_target_pairs={{0,3},{1,2},{2,1},{3,0},{4,7},{5,6},{6,5},{7,4},{8,11},{9,10},{10,... | collective-permute-start | bytes 393224 | tf_op jit(solution)/shard_map/ppermute | solution.py:806
  46.5 2.4 %collective-permute-start.15 = (bf16[2,128,1024]{2,1,0:T(8,128)(2,1)S(1)}, bf16[2,128,1024]{2,1,0:T(8,128)(2,1)S(1)}, u32[]{:S(2)}, u32[]{:S(2)}) collective-permute-start(bf16[2,128,1024]{2,1,0:T(8,128)(2,1)S(1)} %get-tuple-element.120), channel_id=1, source_target_pairs={{0,1},{1,0},{2,3},{3,2},{4,5},{5,4},{6,7},{7,6},{8,9},{9,8},{10,11... | collective-permute-start | bytes 1572872 | tf_op jit(solution)/shard_map/ppermute | solution.py:806
  46.8 6.3 %collective-permute-start.14 = (bf16[2,256,128]{2,1,0:T(8,128)(2,1)S(1)}, bf16[2,256,128]{2,1,0:T(8,128)(2,1)S(1)}, u32[]{:S(2)}, u32[]{:S(2)}) collective-permute-start(bf16[2,256,128]{2,1,0:T(8,128)(2,1)S(1)} %get-tuple-element.118), channel_id=1, source_target_pairs={{0,2},{1,3},{2,0},{3,1},{4,6},{5,7},{6,4},{7,5},{8,10},{9,11},{10,... | collective-permute-start | bytes 393224 | tf_op jit(solution)/shard_map/ppermute | solution.py:806
  48.3 4.8 %collective-permute-start.13 = (bf16[2,256,128]{2,1,0:T(8,128)(2,1)S(1)}, bf16[2,256,128]{2,1,0:T(8,128)(2,1)S(1)}, u32[]{:S(2)}, u32[]{:S(2)}) collective-permute-start(bf16[2,256,128]{2,1,0:T(8,128)(2,1)S(1)} %get-tuple-element.117), channel_id=1, source_target_pairs={{0,1},{1,0},{2,3},{3,2},{4,5},{5,4},{6,7},{7,6},{8,9},{9,8},{10,11... | collective-permute-start | bytes 393224 | tf_op jit(solution)/shard_map/ppermute | solution.py:806
  48.3 6.7 %collective-permute-start.16 = (bf16[2,256,128]{2,1,0:T(8,128)(2,1)S(1)}, bf16[2,256,128]{2,1,0:T(8,128)(2,1)S(1)}, u32[]{:S(2)}, u32[]{:S(2)}) collective-permute-start(bf16[2,256,128]{2,1,0:T(8,128)(2,1)S(1)} %get-tuple-element.123), channel_id=1, source_target_pairs={{0,3},{1,2},{2,1},{3,0},{4,7},{5,6},{6,5},{7,4},{8,11},{9,10},{10,... | collective-permute-start | bytes 393224 | tf_op jit(solution)/shard_map/ppermute | solution.py:806
  49.1 12.1 %collective-permute-start.17 = (bf16[1,128,1024]{2,1,0:T(8,128)(2,1)S(1)}, bf16[1,128,1024]{2,1,0:T(8,128)(2,1)S(1)}, u32[]{:S(2)}, u32[]{:S(2)}) collective-permute-start(bf16[1,128,1024]{2,1,0:T(8,128)(2,1)S(1)} %get-tuple-element.121), channel_id=1, source_target_pairs={{0,2},{1,3},{2,0},{3,1},{4,6},{5,7},{6,4},{7,5},{8,10},{9,11},{10,... | collective-permute-start | bytes 786440 | tf_op jit(solution)/shard_map/ppermute | solution.py:806
  61.3 10.4 %collective-permute-start.21 = (f32[4,128,128]{2,1,0:T(8,128)S(1)}, f32[4,128,128]{2,1,0:T(8,128)S(1)}, u32[]{:S(2)}, u32[]{:S(2)}) collective-permute-start(f32[4,128,128]{2,1,0:T(8,128)S(1)} %get-tuple-element.126), channel_id=1, source_target_pairs={{0,4},{4,0},{8,12},{12,8},{16,20},{20,16},{24,28},{28,24},{1,5},{5... | collective-permute-start | bytes 786440 | tf_op jit(solution)/shard_map/ppermute | solution.py:806
  71.7 6.0 %collective-permute-start.22 = (f32[2,128,128]{2,1,0:T(8,128)S(1)}, f32[2,128,128]{2,1,0:T(8,128)S(1)}, u32[]{:S(2)}, u32[]{:S(2)}) collective-permute-start(f32[2,128,128]{2,1,0:T(8,128)S(1)} %get-tuple-element.143), channel_id=1, source_target_pairs={{0,8},{4,12},{8,0},{12,4},{16,24},{20,28},{24,16},{28,20},{1,9},{5... | collective-permute-start | bytes 393224 | tf_op jit(solution)/shard_map/ppermute | solution.py:806
  72.4 12.8 %all-to-all-start = ((f32[8,24,128]{2,1,0:T(8,128)}), f32[8,24,128]{2,1,0:T(8,128)S(1)}, u32[]{:S(2)}, u32[]{:S(2)}) async-start(f32[8,24,128]{2,1,0:T(8,128)} %state_grad.1), calls=%async_computation | async-start | bytes 196608 | tf_op jit(solution)/shard_map/all_to_all | solution.py:975
  77.1 10.2 %collective-permute-start.18 = (bf16[2,256,128]{2,1,0:T(8,128)(2,1)S(1)}, bf16[2,256,128]{2,1,0:T(8,128)(2,1)S(1)}, u32[]{:S(2)}, u32[]{:S(2)}) collective-permute-start(bf16[2,256,128]{2,1,0:T(8,128)(2,1)S(1)} %get-tuple-element.135), channel_id=1, source_target_pairs={{0,1},{1,0},{2,3},{3,2},{4,5},{5,4},{6,7},{7,6},{8,9},{9,8},{10,11... | collective-permute-start | bytes 393224 | tf_op jit(solution)/shard_map/ppermute | solution.py:806
  77.7 8.2 %collective-permute-start.23 = (f32[1,128,128]{2,1,0:T(8,128)S(1)}, f32[1,128,128]{2,1,0:T(8,128)S(1)}, u32[]{:S(2)}, u32[]{:S(2)}) collective-permute-start(f32[1,128,128]{2,1,0:T(8,128)S(1)} %get-tuple-element.145), channel_id=1, source_target_pairs={{0,16},{4,20},{8,24},{12,28},{16,0},{20,4},{24,8},{28,12},{1,17},{... | collective-permute-start | bytes 196616 | tf_op jit(solution)/shard_map/ppermute | solution.py:806
  80.4 7.4 %collective-permute-start.19 = (bf16[2,256,128]{2,1,0:T(8,128)(2,1)S(1)}, bf16[2,256,128]{2,1,0:T(8,128)(2,1)S(1)}, u32[]{:S(2)}, u32[]{:S(2)}) collective-permute-start(bf16[2,256,128]{2,1,0:T(8,128)(2,1)S(1)} %get-tuple-element.136), channel_id=1, source_target_pairs={{0,2},{1,3},{2,0},{3,1},{4,6},{5,7},{6,4},{7,5},{8,10},{9,11},{10,... | collective-permute-start | bytes 393224 | tf_op jit(solution)/shard_map/ppermute | solution.py:806
  81.9 5.9 %collective-permute-start.20 = (bf16[2,256,128]{2,1,0:T(8,128)(2,1)S(1)}, bf16[2,256,128]{2,1,0:T(8,128)(2,1)S(1)}, u32[]{:S(2)}, u32[]{:S(2)}) collective-permute-start(bf16[2,256,128]{2,1,0:T(8,128)(2,1)S(1)} %get-tuple-element.137), channel_id=1, source_target_pairs={{0,3},{1,2},{2,1},{3,0},{4,7},{5,6},{6,5},{7,4},{8,11},{9,10},{10,... | collective-permute-start | bytes 393224 | tf_op jit(solution)/shard_map/ppermute | solution.py:806
  85.9 4.3 %collective-permute-start.26 = (bf16[224,128]{1,0:T(8,128)(2,1)S(1)}, bf16[224,128]{1,0:T(8,128)(2,1)S(1)}, u32[]{:S(2)}, u32[]{:S(2)}) collective-permute-start(bf16[224,128]{1,0:T(8,128)(2,1)S(1)} %last_sums.1.refs_0_), channel_id=1, source_target_pairs={{0,3},{1,2},{2,1},{3,0},{4,7},{5,6},{6,5},{7,4},{8,11},{9,10},{10,... | collective-permute-start | bytes 172040 | tf_op jit(solution)/shard_map/ppermute | solution.py:806
  86.2 4.9 %collective-permute-start.25 = (bf16[224,128]{1,0:T(8,128)(2,1)S(1)}, bf16[224,128]{1,0:T(8,128)(2,1)S(1)}, u32[]{:S(2)}, u32[]{:S(2)}) collective-permute-start(bf16[224,128]{1,0:T(8,128)(2,1)S(1)} %last_sums.1.refs_0_), channel_id=1, source_target_pairs={{0,2},{1,3},{2,0},{3,1},{4,6},{5,7},{6,4},{7,5},{8,10},{9,11},{10,... | collective-permute-start | bytes 172040 | tf_op jit(solution)/shard_map/ppermute | solution.py:806
  87.4 3.8 %collective-permute-start.24 = (bf16[224,128]{1,0:T(8,128)(2,1)S(1)}, bf16[224,128]{1,0:T(8,128)(2,1)S(1)}, u32[]{:S(2)}, u32[]{:S(2)}) collective-permute-start(bf16[224,128]{1,0:T(8,128)(2,1)S(1)} %last_sums.1.refs_0_), channel_id=1, source_target_pairs={{0,1},{1,0},{2,3},{3,2},{4,5},{5,4},{6,7},{7,6},{8,9},{9,8},{10,11... | collective-permute-start | bytes 172040 | tf_op jit(solution)/shard_map/ppermute | solution.py:806
